TPU v7x, 32 devices: a whole 2x2x4 slice. The times are simulated.
32 devices in a mesh: dp: 2 (over core), row: 4 (over y, x), col: 4 (over z).
Axes of the slice: x: 2, y: 2, z: 4, core: 2. Of those that a mesh axis runs over, the one named last changes fastest.
Arguments:
- x_in: bfloat16 [4, 768, 4096], P('dp', 'col', 'row'), may hold values from -6 to 6
- prefix: int32 [4], P('dp'), may hold values from 409 to 2048
- enc_bank: bfloat16 [4, 768, 4096], P('dp', 'col'), may hold values from -6 to 6
- bank_rows: int32 [4, 1024], P('dp'), may hold values from 0 to 4095, as said below
- w_qkv: bfloat16 [768, 3, 12, 64], P('col', None, 'row', 'dp'), may hold values from -0.3125 to 0.3125
- w_out: bfloat16 [12, 64, 768], P('row', 'dp', 'col'), may hold values from -0.625 to 0.625
- w_cross_q: bfloat16 [768, 12, 64], P('col', 'row', 'dp'), may hold values from -0.3125 to 0.3125
- w_cross_kv: bfloat16 [768, 2, 12, 64], P('col', None, 'row', 'dp'), may hold values from -0.3125 to 0.3125
- w_cross_out: bfloat16 [12, 64, 768], P('row', 'dp', 'col'), may hold values from -0.625 to 0.625
- w_up: bfloat16 [768, 3072], P('col', ('dp', 'row')), may hold values from -0.21875 to 0.21875
- w_down: bfloat16 [3072, 768], P(('dp', 'row'), 'col'), may hold values from -0.109375 to 0.109375
- ln_gains: bfloat16 [3, 768], P(None, 'col'), may hold values from 0.25 to 1.75
- out_grad: bfloat16 [4, 768, 4096], P('dp', 'col', 'row'), may hold values from -6 to 6
Outputs:
- block_out: bfloat16 [4, 768, 4096], P('dp', 'col', 'row')
- x_grad: float32 [4, 768, 4096], P('dp', 'col', 'row')
- bank_grad: float32 [4, 768, 4096], P('dp', 'col')
- w_qkv_grad: float32 [768, 3, 12, 64], P('col', None, 'row', 'dp')
- w_out_grad: float32 [12, 64, 768], P('row', 'dp', 'col')
- w_cross_q_grad: float32 [768, 12, 64], P('col', 'row', 'dp')
- w_cross_kv_grad: float32 [768, 2, 12, 64], P('col', None, 'row', 'dp')
- w_cross_out_grad: float32 [12, 64, 768], P('row', 'dp', 'col')
- w_up_grad: float32 [768, 3072], P('col', ('dp', 'row'))
- w_down_grad: float32 [3072, 768], P(('dp', 'row'), 'col')
- ln_gains_grad: float32 [3, 768], P(None, 'col')
Inputs may be any that keep to these rules, and one draw needn't show every extreme that they name: `bank_rows`: within a sequence the 1024 rows are distinct.
All inputs are finite; a program needn't handle non-finite values.
Results may differ from a plain program's by a relative error of at most 0.025.
Values may be sent and summed in bfloat16 or wider, within the bound.
No kernel may reach another device: no remote copies, remote signals or barrier semaphores. Data moves between devices by JAX's collectives and lax.ppermute only.
A program may use at most 512 MiB of HBM per device.

v0:
```python
import jax
import jax.numpy as jnp
from jax import lax
from jax.sharding import PartitionSpec as P

D = 768
HD = 64
MB = 2


NORM_EPS = 1e-05
SCORE_SCALE = 0.125
NEG_FILL = -1e30


def rows_all(value_in):
    return lax.all_gather(value_in, "row", axis=0, tiled=True)


def cols_share(value_in):
    return lax.psum_scatter(value_in, "col", scatter_dimension=0, tiled=True)


def cols_all(value_in):
    return lax.all_gather(value_in, "col", axis=0, tiled=True)


def own_from_all(all_in, weight_in):
    return (
        cols_share(
            jnp.einsum("tsd,dk->tsk", all_in, weight_in, preferred_element_type=jnp.float32)
        ),
        all_in,
    )


def b_full(own_in):
    return cols_all(own_in)


def to_resid(full_in, weight_in):
    return lax.psum_scatter(
        jnp.einsum("tsk,kd->tsd", full_in, weight_in, preferred_element_type=jnp.float32),
        "row",
        scatter_dimension=0,
        tiled=True,
    )


def col_stats(left_part, right_part):
    return lax.psum((jnp.sum(left_part, -1), jnp.sum(right_part, -1)), "col")


def norm_fwd(resid_in, gain_vec):
    row_total, row_square = col_stats(resid_in, resid_in * resid_in)
    row_mean = row_total / D
    inv_std = lax.rsqrt(row_square / D - row_mean * row_mean + NORM_EPS)
    normed = (resid_in - row_mean[..., None]) * inv_std[..., None]
    return (normed * gain_vec, normed, inv_std)


def norm_back(grad_in, gain_vec, normed, inv_std):
    scaled = grad_in * gain_vec
    grad_total, grad_cross = col_stats(scaled, scaled * normed)
    grad_resid = inv_std[..., None] * (
        scaled - grad_total[..., None] / D - normed * grad_cross[..., None] / D
    )
    return (grad_resid, jnp.sum(grad_in * normed, axis=(0, 1)))


def split_heads(value_in, head_count):
    return value_in.reshape(value_in.shape[0], value_in.shape[1], head_count, HD)


def scores_of(query_in, keys_vals, allowed):
    head_count = query_in.shape[2] // HD
    raw_scores = (
        jnp.einsum(
            "qshd,kshd->shqk",
            split_heads(query_in, head_count),
            split_heads(keys_vals[..., : head_count * HD], head_count),
            preferred_element_type=jnp.float32,
        )
        * SCORE_SCALE
    )
    if allowed is not None:
        raw_scores = jnp.where(allowed[:, None], raw_scores, NEG_FILL)
    return raw_scores


def attend_fwd(query_in, keys_vals, allowed):
    head_count = query_in.shape[2] // HD
    raw_scores = scores_of(query_in, keys_vals, allowed)
    row_max = jnp.max(raw_scores, -1, keepdims=True)
    log_total = row_max + jnp.log(jnp.sum(jnp.exp(raw_scores - row_max), -1, keepdims=True))
    low_probs = jnp.exp(raw_scores - log_total).astype(jnp.bfloat16)
    values_h = split_heads(keys_vals[..., head_count * HD :], head_count)
    mixed = jnp.einsum("shqk,kshd->qshd", low_probs, values_h, preferred_element_type=jnp.float32)
    return (mixed.reshape(query_in.shape).astype(jnp.bfloat16), log_total)


def attend_back(query_in, keys_vals, log_total, grad_out, allowed):
    head_count = query_in.shape[2] // HD
    probs_full = jnp.exp(scores_of(query_in, keys_vals, allowed) - log_total)
    low_probs = probs_full.astype(jnp.bfloat16)
    query_h = split_heads(query_in, head_count)
    keys_h = split_heads(keys_vals[..., : head_count * HD], head_count)
    values_h = split_heads(keys_vals[..., head_count * HD :], head_count)
    grad_h = split_heads(grad_out, head_count)
    grad_probs = jnp.einsum("qshd,kshd->shqk", grad_h, values_h, preferred_element_type=jnp.float32)
    row_delta = jnp.sum(probs_full * grad_probs, -1, keepdims=True)
    grad_scores = (probs_full * (grad_probs - row_delta)).astype(jnp.bfloat16)
    grad_query = (
        jnp.einsum("shqk,kshd->qshd", grad_scores, keys_h, preferred_element_type=jnp.float32)
        * SCORE_SCALE
    )
    grad_keys = (
        jnp.einsum("shqk,qshd->kshd", grad_scores, query_h, preferred_element_type=jnp.float32)
        * SCORE_SCALE
    )
    grad_values = jnp.einsum(
        "shqk,qshd->kshd", low_probs, grad_h, preferred_element_type=jnp.float32
    )
    key_rows = keys_vals.shape[0]
    seq_count = keys_vals.shape[1]
    grad_kv = jnp.concatenate(
        [grad_keys.reshape(key_rows, seq_count, -1), grad_values.reshape(key_rows, seq_count, -1)],
        -1,
    )
    return (grad_query.reshape(query_in.shape).astype(jnp.bfloat16), grad_kv)


def per_device(
    x_in,
    prefix,
    enc_bank,
    bank_rows,
    w_qkv,
    w_out,
    w_cross_q,
    w_cross_kv,
    w_cross_out,
    w_up,
    w_down,
    ln_gains,
    out_grad,
):
    x_tok = x_in.transpose(2, 0, 1)
    cot_tok = out_grad.transpose(2, 0, 1)
    bank_tok = enc_bank.transpose(0, 2, 1)
    row_len = x_tok.shape[0]
    length = row_len * lax.axis_size("row")
    queries = length // lax.axis_size("col")
    col_pos = lax.axis_index("col")
    col_width = w_qkv.shape[0]
    head_count = w_qkv.shape[2]
    split_at = head_count * HD
    per_micro = x_tok.shape[1] // MB
    gain_f = ln_gains.astype(jnp.float32)
    q_positions = col_pos * queries + jnp.arange(queries, dtype=jnp.int32)
    k_positions = jnp.arange(length, dtype=jnp.int32)
    block_outs, input_grads, bank_grads = ([], [], [])
    grad_acc = None
    gain_acc = jnp.zeros((3, col_width), jnp.float32)
    for micro_idx in range(MB):
        first_seq = micro_idx * per_micro
        after_seq = first_seq + per_micro
        flat = (
            lax.all_gather(w_qkv, "dp", axis=3, tiled=True).reshape(col_width, -1),
            lax.all_gather(w_out, "dp", axis=1, tiled=True).reshape(-1, col_width),
            lax.all_gather(w_cross_q, "dp", axis=2, tiled=True).reshape(col_width, -1),
            lax.all_gather(w_cross_kv, "dp", axis=3, tiled=True).reshape(col_width, -1),
            lax.all_gather(w_cross_out, "dp", axis=1, tiled=True).reshape(-1, col_width),
            lax.all_gather(w_up, "dp", axis=1, tiled=True),
            lax.all_gather(w_down, "dp", axis=0, tiled=True),
        )
        wt_qkv, wt_out, wt_cq, wt_ckv, wt_cout, wt_up, wt_down = flat
        x_part = x_tok[:, first_seq:after_seq]
        pre_len = prefix[first_seq:after_seq]
        allowed = (k_positions[None, None, :] <= q_positions[None, :, None]) | (
            k_positions[None, None, :] < pre_len[:, None, None]
        )
        x_all = rows_all(x_part)
        proj_f, x_left = own_from_all(x_all, wt_qkv)
        proj_own = proj_f.astype(jnp.bfloat16)
        query_own = proj_own[..., :split_at]
        kv_all = cols_all(proj_own[..., split_at:])
        attn_own, log_self = attend_fwd(query_own, kv_all, allowed)
        attn_full = b_full(attn_own)
        resid_one = x_part.astype(jnp.float32) + to_resid(attn_full, wt_out)
        h_one, normed_one, inv_one = norm_fwd(resid_one, gain_f[0])
        h_one_all = rows_all(h_one.astype(jnp.bfloat16))
        cq_f, h_one_left = own_from_all(h_one_all, wt_cq)
        cq_own = cq_f.astype(jnp.bfloat16)
        bank_part = bank_tok[first_seq:after_seq]
        row_pick = bank_rows[first_seq:after_seq]
        chosen_t = jnp.take_along_axis(bank_part, row_pick[:, :, None], axis=1).transpose(1, 0, 2)
        ckv_f, chosen_left = own_from_all(chosen_t, wt_ckv)
        ckv_all = cols_all(ckv_f.astype(jnp.bfloat16))
        catt_own, log_cross = attend_fwd(cq_own, ckv_all, None)
        catt_full = b_full(catt_own)
        resid_two = h_one + to_resid(catt_full, wt_cout)
        h_two, normed_two, inv_two = norm_fwd(resid_two, gain_f[1])
        h_two_all = rows_all(h_two.astype(jnp.bfloat16))
        upper_own, h_two_left = own_from_all(h_two_all, wt_up)
        act_full = b_full(jax.nn.gelu(upper_own, approximate=False).astype(jnp.bfloat16))
        resid_three = h_two + to_resid(act_full, wt_down)
        h_three, normed_three, inv_three = norm_fwd(resid_three, gain_f[2])
        block_outs.append(h_three.astype(jnp.bfloat16))
        dy_three, dg_three = norm_back(
            cot_tok[:, first_seq:after_seq].astype(jnp.float32), gain_f[2], normed_three, inv_three
        )
        dffn_all = rows_all(dy_three.astype(jnp.bfloat16))
        dact_own, dffn_left = own_from_all(dffn_all, wt_down.T)
        g_down = jnp.einsum("tsf,tsd->fd", act_full, dffn_left, preferred_element_type=jnp.float32)
        gelu_vals, gelu_pull = jax.vjp(
            lambda upper_in: jax.nn.gelu(upper_in, approximate=False), upper_own
        )
        dupper_full = b_full(gelu_pull(dact_own)[0].astype(jnp.bfloat16))
        g_up = jnp.einsum(
            "tsd,tsf->df", h_two_left, dupper_full, preferred_element_type=jnp.float32
        )
        dh_two = dy_three + to_resid(dupper_full, wt_up.T)
        dy_two, dg_two = norm_back(dh_two, gain_f[1], normed_two, inv_two)
        dcross_all = rows_all(dy_two.astype(jnp.bfloat16))
        dcatt_f, dcross_left = own_from_all(dcross_all, wt_cout.T)
        g_cout = jnp.einsum(
            "tsk,tsd->kd", catt_full, dcross_left, preferred_element_type=jnp.float32
        )
        dcq_own, dckv_part = attend_back(
            cq_own, ckv_all, log_cross, dcatt_f.astype(jnp.bfloat16), None
        )
        dckv_own = cols_share(dckv_part).astype(jnp.bfloat16)
        dcq_full = b_full(dcq_own)
        dckv_full = b_full(dckv_own)
        g_cq = jnp.einsum("tsd,tsk->dk", h_one_left, dcq_full, preferred_element_type=jnp.float32)
        g_ckv = jnp.einsum(
            "nsd,nsk->dk", chosen_left, dckv_full, preferred_element_type=jnp.float32
        )
        chosen_terms = jnp.einsum(
            "nsk,dk->nsd", dckv_full, wt_ckv, preferred_element_type=jnp.float32
        )
        grad_chosen = (
            lax.psum(chosen_terms.astype(jnp.bfloat16), "row")
            .astype(jnp.float32)
            .transpose(1, 0, 2)
        )
        seq_ids = jnp.arange(per_micro, dtype=jnp.int32)
        bank_grads.append(
            jnp.zeros(bank_part.shape, jnp.float32).at[seq_ids[:, None], row_pick].add(grad_chosen)
        )
        dh_one = dy_two + to_resid(dcq_full, wt_cq.T)
        dy_one, dg_one = norm_back(dh_one, gain_f[0], normed_one, inv_one)
        dattn_all = rows_all(dy_one.astype(jnp.bfloat16))
        dattn_f, dattn_left = own_from_all(dattn_all, wt_out.T)
        g_out = jnp.einsum("tsk,tsd->kd", attn_full, dattn_left, preferred_element_type=jnp.float32)
        dq_own, dkv_part = attend_back(
            query_own, kv_all, log_self, dattn_f.astype(jnp.bfloat16), allowed
        )
        dkv_own = cols_share(dkv_part).astype(jnp.bfloat16)
        dproj_full = jnp.concatenate([b_full(dq_own), b_full(dkv_own)], -1)
        g_qkv = jnp.einsum("tsd,tsk->dk", x_left, dproj_full, preferred_element_type=jnp.float32)
        input_grads.append(dy_one + to_resid(dproj_full, wt_qkv.T))
        grads_now = (g_qkv, g_out, g_cq, g_ckv, g_cout, g_up, g_down)
        shard_now = (
            lax.psum_scatter(
                grads_now[0].reshape(col_width, 3, head_count, HD).astype(jnp.bfloat16),
                "dp",
                scatter_dimension=3,
                tiled=True,
            ).astype(jnp.float32),
            lax.psum_scatter(
                grads_now[1].reshape(head_count, HD, col_width).astype(jnp.bfloat16),
                "dp",
                scatter_dimension=1,
                tiled=True,
            ).astype(jnp.float32),
            lax.psum_scatter(
                grads_now[2].reshape(col_width, head_count, HD).astype(jnp.bfloat16),
                "dp",
                scatter_dimension=2,
                tiled=True,
            ).astype(jnp.float32),
            lax.psum_scatter(
                grads_now[3].reshape(col_width, 2, head_count, HD).astype(jnp.bfloat16),
                "dp",
                scatter_dimension=3,
                tiled=True,
            ).astype(jnp.float32),
            lax.psum_scatter(
                grads_now[4].reshape(head_count, HD, col_width).astype(jnp.bfloat16),
                "dp",
                scatter_dimension=1,
                tiled=True,
            ).astype(jnp.float32),
            lax.psum_scatter(
                grads_now[5].astype(jnp.bfloat16), "dp", scatter_dimension=1, tiled=True
            ).astype(jnp.float32),
            lax.psum_scatter(
                grads_now[6].astype(jnp.bfloat16), "dp", scatter_dimension=0, tiled=True
            ).astype(jnp.float32),
        )
        grad_acc = shard_now if micro_idx == 0 else jax.tree.map(jnp.add, grad_acc, shard_now)
        gain_acc = gain_acc + jnp.stack([dg_one, dg_two, dg_three])
    gain_grads = lax.psum(gain_acc, ("dp", "row"))
    return (
        jnp.concatenate(block_outs, 1).transpose(1, 2, 0),
        jnp.concatenate(input_grads, 1).transpose(1, 2, 0),
        jnp.concatenate(bank_grads, 0).transpose(0, 2, 1),
        grad_acc[0],
        grad_acc[1],
        grad_acc[2],
        grad_acc[3],
        grad_acc[4],
        grad_acc[5],
        grad_acc[6],
        gain_grads,
    )


def solution(mesh):
    placed = (
        P("dp", "col", "row"),
        P("dp"),
        P("dp", "col", None),
        P("dp", None),
        P("col", None, "row", "dp"),
        P("row", "dp", "col"),
        P("col", "row", "dp"),
        P("col", None, "row", "dp"),
        P("row", "dp", "col"),
        P("col", ("dp", "row")),
        P(("dp", "row"), "col"),
        P(None, "col"),
        P("dp", "col", "row"),
    )
    return jax.shard_map(
        per_device,
        mesh=mesh,
        in_specs=placed,
        out_specs=(
            P("dp", "col", "row"),
            P("dp", "col", "row"),
            P("dp", "col", None),
            P("col", None, "row", "dp"),
            P("row", "dp", "col"),
            P("col", "row", "dp"),
            P("col", None, "row", "dp"),
            P("row", "dp", "col"),
            P("col", ("dp", "row")),
            P(("dp", "row"), "col"),
            P(None, "col"),
        ),
        check_vma=False,
    )
```

profile of v0, /device:TPU:0, one launch (start us, length us, event | category | flops | bytes accessed | tf_op | source)
XLA Modules:
  0.0 4516.4 jit_solution(10926181094281218415)
XLA Ops:
  12.4 31.6 all-gather.29.cloned.1.call-done
  83.9 157.0 %reduce-scatter.53.cloned.1.call-done = f32[1024,1,576]{0,2,1:T(8,128)} async-done(((f32[4096,1,576]{0,2,1:T(8,128)}), f32[1024,1,576]{0,2,1:T(8,128)}) %reduce-scatter.53.cloned.1.call-update) | async-done | bytes 2359312 | tf_op jit(solution)/shard_map/reduce_scatter | solution.py:21
  252.7 152.5 %reduce-scatter.67.cloned.1.call-done = f32[1024,1,576]{0,2,1:T(8,128)} async-done(((f32[4096,1,576]{0,2,1:T(8,128)}), f32[1024,1,576]{0,2,1:T(8,128)}) %reduce-scatter.67.cloned.1.call-update) | async-done | bytes 2359312 | tf_op jit(solution)/shard_map/reduce_scatter | solution.py:21
  408.4 63.2 %all-gather.31.cloned.1.call-done = bf16[4096,1,384]{0,2,1:T(8,128)(2,1)} async-done(((bf16[1024,1,384]{0,2,1:T(8,128)(2,1)}), bf16[4096,1,384]{0,2,1:T(8,128)(2,1)}) %all-gather.31.cloned.1.call-update) | async-done | bytes 3145744 | tf_op jit(solution)/shard_map/all_gather | solution.py:25
  612.6 30.1 all-gather.47.cloned.1.call-done
  647.0 42.0 reduce-scatter.55.cloned.1.call-done
  689.0 46.8 %reduce-scatter.69.cloned.1.call-done = f32[1024,1,192]{0,2,1:T(8,128)} async-done(((f32[4096,1,192]{0,2,1:T(8,128)}), f32[1024,1,192]{0,2,1:T(8,128)}) %reduce-scatter.69.cloned.1.call-update) | async-done | bytes 786448 | tf_op jit(solution)/shard_map/reduce_scatter | solution.py:42
  789.1 34.5 reduce-scatter.57.cloned.1.call-done
  852.7 39.5 reduce-scatter.59.cloned.1.call-done
  904.7 36.1 all-gather.37.cloned.1.call-done
  944.6 42.8 reduce-scatter.61.cloned.1.call-done
  1025.0 34.5 reduce-scatter.71.cloned.1.call-done
  1089.0 39.3 reduce-scatter.73.cloned.1.call-done
  1138.9 37.9 all-gather.51.cloned.1.call-done
  1180.6 42.9 reduce-scatter.75.cloned.1.call-done
  1281.5 211.8 %reduce-scatter.63.cloned.1.call-done = f32[1024,1,768]{2,0,1:T(8,128)} async-done(((f32[4096,1,768]{2,0,1:T(8,128)}), f32[1024,1,768]{2,0,1:T(8,128)}) %reduce-scatter.63.cloned.1.call-update) | async-done | bytes 3145744 | tf_op jit(solution)/shard_map/reduce_scatter | solution.py:21
  1505.8 112.9 %all-gather.41.cloned.1.call-done = bf16[4096,1,768]{2,0,1:T(8,128)(2,1)} async-done(((bf16[1024,1,768]{2,0,1:T(8,128)(2,1)}), bf16[4096,1,768]{2,0,1:T(8,128)(2,1)}) %all-gather.41.cloned.1.call-update) | async-done | bytes 6291472 | tf_op jit(solution)/shard_map/all_gather | solution.py:25
  1626.7 40.9 reduce-scatter.65.cloned.1.call-done
  1670.7 30.9 all-gather.53.cloned.1.call-done
  1709.5 212.0 %reduce-scatter.77.cloned.1.call-done = f32[1024,1,768]{2,0,1:T(8,128)} async-done(((f32[4096,1,768]{2,0,1:T(8,128)}), f32[1024,1,768]{2,0,1:T(8,128)}) %reduce-scatter.77.cloned.1.call-update) | async-done | bytes 3145744 | tf_op jit(solution)/shard_map/reduce_scatter | solution.py:21
  1930.5 116.5 %all-gather.55.cloned.1.call-done = bf16[4096,1,768]{2,0,1:T(8,128)(2,1)} async-done(((bf16[1024,1,768]{2,0,1:T(8,128)(2,1)}), bf16[4096,1,768]{2,0,1:T(8,128)(2,1)}) %all-gather.55.cloned.1.call-update) | async-done | bytes 6291472 | tf_op jit(solution)/shard_map/all_gather | solution.py:25
  2053.6 42.2 reduce-scatter.79.cloned.1.call-done
  2180.4 212.0 %reduce-scatter.81.cloned.1.call-done = f32[1024,1,768]{2,0,1:T(8,128)} async-done(((f32[4096,1,768]{2,0,1:T(8,128)}), f32[1024,1,768]{2,0,1:T(8,128)}) %reduce-scatter.81.cloned.1.call-update) | async-done | bytes 3145744 | tf_op jit(solution)/shard_map/reduce_scatter | solution.py:21
  2398.6 116.5 %all-gather.59.cloned.1.call-done = bf16[4096,1,768]{2,0,1:T(8,128)(2,1)} async-done(((bf16[1024,1,768]{2,0,1:T(8,128)(2,1)}), bf16[4096,1,768]{2,0,1:T(8,128)(2,1)}) %all-gather.59.cloned.1.call-update) | async-done | bytes 6291472 | tf_op jit(solution)/shard_map/all_gather | solution.py:25
  2523.1 40.9 reduce-scatter.83.cloned.1.call-done
  2568.2 30.9 all-gather.71.cloned.1.call-done
  2607.2 212.0 %reduce-scatter.95.cloned.1.call-done = f32[1024,1,768]{2,0,1:T(8,128)} async-done(((f32[4096,1,768]{2,0,1:T(8,128)}), f32[1024,1,768]{2,0,1:T(8,128)}) %reduce-scatter.95.cloned.1.call-update) | async-done | bytes 3145744 | tf_op jit(solution)/shard_map/reduce_scatter | solution.py:21
  2825.4 116.5 %all-gather.73.cloned.1.call-done = bf16[4096,1,768]{2,0,1:T(8,128)(2,1)} async-done(((bf16[1024,1,768]{2,0,1:T(8,128)(2,1)}), bf16[4096,1,768]{2,0,1:T(8,128)(2,1)}) %all-gather.73.cloned.1.call-update) | async-done | bytes 6291472 | tf_op jit(solution)/shard_map/all_gather | solution.py:25
  2948.7 42.2 reduce-scatter.97.cloned.1.call-done
  3048.0 60.5 %reduce-scatter.85.cloned.1.call-done = f32[1024,1,192]{0,2,1:T(8,128)} async-done(((f32[4096,1,192]{0,2,1:T(8,128)}), f32[1024,1,192]{0,2,1:T(8,128)}) %reduce-scatter.85.cloned.1.call-update) | async-done | bytes 786448 | tf_op jit(solution)/shard_map/reduce_scatter | solution.py:21
  3129.1 36.9 all-gather.63.cloned.1.call-done
  3169.9 42.8 reduce-scatter.87.cloned.1.call-done
  3216.9 30.9 all-gather.75.cloned.1.call-done
  3251.7 60.5 %reduce-scatter.99.cloned.1.call-done = f32[1024,1,192]{0,2,1:T(8,128)} async-done(((f32[4096,1,192]{0,2,1:T(8,128)}), f32[1024,1,192]{0,2,1:T(8,128)}) %reduce-scatter.99.cloned.1.call-update) | async-done | bytes 786448 | tf_op jit(solution)/shard_map/reduce_scatter | solution.py:21
  3331.9 37.0 all-gather.77.cloned.1.call-done
  3372.7 42.9 reduce-scatter.101.cloned.1.call-done
  3505.8 58.9 %reduce-scatter.103.cloned.1.call-done = f32[1024,1,192]{0,2,1:T(8,128)} async-done(((f32[4096,1,192]{0,2,1:T(8,128)}), f32[1024,1,192]{0,2,1:T(8,128)}) %reduce-scatter.103.cloned.1.call-update) | async-done | bytes 786448 | tf_op jit(solution)/shard_map/reduce_scatter | solution.py:21
  3565.9 36.1 multiply_reduce_fusion
  3602.0 42.4 multiply_convert_fusion
  3684.5 36.6 multiply_reduce_fusion.1
  3721.1 42.6 multiply_convert_fusion.1
  3860.6 52.4 %reduce-scatter.91.cloned.1.call-done = f32[1024,1,384]{0,2,1:T(8,128)} async-done(((f32[4096,1,384]{0,2,1:T(8,128)}), f32[1024,1,384]{0,2,1:T(8,128)}) %reduce-scatter.91.cloned.1.call-update) | async-done | bytes 1572880 | tf_op jit(solution)/shard_map/reduce_scatter | solution.py:21
  4041.8 35.8 all-gather.67.cloned.1.call-done
  4080.4 61.2 %all-gather.83.cloned.1.call-done = bf16[4096,1,384]{0,2,1:T(8,128)(2,1)} async-done(((bf16[1024,1,384]{0,2,1:T(8,128)(2,1)}), bf16[4096,1,384]{0,2,1:T(8,128)(2,1)}) %all-gather.83.cloned.1.call-update) | async-done | bytes 3145744 | tf_op jit(solution)/shard_map/all_gather | solution.py:25
  4150.1 55.8 %all-gather.69.cloned.1.call-done = bf16[4096,1,384]{0,2,1:T(8,128)(2,1)} async-done(((bf16[1024,1,384]{0,2,1:T(8,128)(2,1)}), bf16[4096,1,384]{0,2,1:T(8,128)(2,1)}) %all-gather.69.cloned.1.call-update) | async-done | bytes 3145744 | tf_op jit(solution)/shard_map/all_gather | solution.py:25
  4316.0 51.1 %all-reduce.11.cloned.1.call-done = (bf16[1,1024,192]{1,2,0:T(8,128)(2,1)}, bf16[1,1024,192]{1,2,0:T(8,128)(2,1)}) async-done(((bf16[1,1024,192]{1,2,0:T(8,128)(2,1)}, bf16[1,1024,192]{1,2,0:T(8,128)(2,1)}), (bf16[1,1024,192]{1,2,0:T(8,128)(2,1)}, bf16[1,1024,192]{1,2,0:T(8,128)(2,1)})) %all-reduce.11.cloned.1.call-update) | async-done | bytes 786448 | tf_op jit(solution)/shard_map/psum | solution.py:244
  4419.7 39.8 reduce-scatter.107.cloned.1.call-done
  4459.6 46.8 %reduce-scatter.93.cloned.1.call-done = f32[1024,1,192]{0,2,1:T(8,128)} async-done(((f32[4096,1,192]{0,2,1:T(8,128)}), f32[1024,1,192]{0,2,1:T(8,128)}) %reduce-scatter.93.cloned.1.call-update) | async-done | bytes 786448 | tf_op jit(solution)/shard_map/reduce_scatter | solution.py:42
  (703 shorter events, 1259.4 us)
Async XLA Ops:
  10.0 230.8 %reduce-scatter.53.cloned.1.call-start = ((), (), s32[]{:S(2)}) async-start(), calls=%async_computation.45 | async-start | bytes 11796480 | tf_op jit(solution)/shard_map/reduce_scatter | solution.py:21
  50.3 354.9 %reduce-scatter.67.cloned.1.call-start = ((), (), s32[]{:S(2)}) async-start(), calls=%async_computation.59 | async-start | bytes 11796480 | tf_op jit(solution)/shard_map/reduce_scatter | solution.py:21
  83.8 387.8 %all-gather.31.cloned.1.call-start = ((), (), s32[]{:S(2)}) async-start(), calls=%async_computation.46 | async-start | bytes 3932160 | tf_op jit(solution)/shard_map/all_gather | solution.py:25
  243.7 296.0 %all-gather.45.cloned.1.call-start = ((), (), s32[]{:S(2)}) async-start(), calls=%async_computation.60 | async-start | bytes 3932160 | tf_op jit(solution)/shard_map/all_gather | solution.py:25
  408.2 200.5 %all-gather.33.cloned.1.call-start = ((), (), s32[]{:S(2)}) async-start(), calls=%async_computation.47 | async-start | bytes 1966080 | tf_op jit(solution)/shard_map/all_gather | solution.py:25
  646.4 139.0 %all-gather.35.cloned.1.call-start = ((), (), s32[]{:S(2)}) async-start(), calls=%async_computation.50 | async-start | bytes 1966080 | tf_op jit(solution)/shard_map/all_gather | solution.py:17
  789.0 151.8 %all-gather.37.cloned.1.call-start = ((), (), s32[]{:S(2)}) async-start(), calls=%async_computation.52 | async-start | bytes 1966080 | tf_op jit(solution)/shard_map/all_gather | solution.py:25
  999.5 128.7 %reduce-scatter.73.cloned.1.call-start = ((), (), s32[]{:S(2)}) async-start(), calls=%async_computation.65 | async-start | bytes 3932160 | tf_op jit(solution)/shard_map/reduce_scatter | solution.py:21
  1024.9 152.0 %all-gather.51.cloned.1.call-start = ((), (), s32[]{:S(2)}) async-start(), calls=%async_computation.66 | async-start | bytes 1966080 | tf_op jit(solution)/shard_map/all_gather | solution.py:25
  1245.1 248.1 %reduce-scatter.63.cloned.1.call-start = ((), (), s32[]{:S(2)}) async-start(), calls=%async_computation.55 | async-start | bytes 15728640 | tf_op jit(solution)/shard_map/reduce_scatter | solution.py:21
  1281.2 337.5 %all-gather.41.cloned.1.call-start = ((), (), s32[]{:S(2)}) async-start(), calls=%async_computation.56 | async-start | bytes 7864320 | tf_op jit(solution)/shard_map/all_gather | solution.py:25
  1502.1 165.4 %reduce-scatter.65.cloned.1.call-start = ((), (), s32[]{:S(2)}) async-start(), calls=%async_computation.57 | async-start | bytes 3932160 | tf_op jit(solution)/shard_map/reduce_scatter | solution.py:42
  1670.6 250.9 %reduce-scatter.77.cloned.1.call-start = ((), (), s32[]{:S(2)}) async-start(), calls=%async_computation.69 | async-start | bytes 15728640 | tf_op jit(solution)/shard_map/reduce_scatter | solution.py:21
  1709.5 337.5 %all-gather.55.cloned.1.call-start = ((), (), s32[]{:S(2)}) async-start(), calls=%async_computation.70 | async-start | bytes 7864320 | tf_op jit(solution)/shard_map/all_gather | solution.py:25
  1930.4 165.4 %reduce-scatter.79.cloned.1.call-start = ((), (), s32[]{:S(2)}) async-start(), calls=%async_computation.71 | async-start | bytes 3932160 | tf_op jit(solution)/shard_map/reduce_scatter | solution.py:42
  2143.8 248.6 %reduce-scatter.81.cloned.1.call-start = ((), (), s32[]{:S(2)}) async-start(), calls=%async_computation.73 | async-start | bytes 15728640 | tf_op jit(solution)/shard_map/reduce_scatter | solution.py:21
  2180.3 334.8 %all-gather.59.cloned.1.call-start = ((), (), s32[]{:S(2)}) async-start(), calls=%async_computation.74 | async-start | bytes 7864320 | tf_op jit(solution)/shard_map/all_gather | solution.py:25
  2398.6 165.4 %reduce-scatter.83.cloned.1.call-start = ((), (), s32[]{:S(2)}) async-start(), calls=%async_computation.75 | async-start | bytes 3932160 | tf_op jit(solution)/shard_map/reduce_scatter | solution.py:42
  2568.2 250.9 %reduce-scatter.95.cloned.1.call-start = ((), (), s32[]{:S(2)}) async-start(), calls=%async_computation.87 | async-start | bytes 15728640 | tf_op jit(solution)/shard_map/reduce_scatter | solution.py:21
  2607.1 334.8 %all-gather.73.cloned.1.call-start = ((), (), s32[]{:S(2)}) async-start(), calls=%async_computation.88 | async-start | bytes 7864320 | tf_op jit(solution)/shard_map/all_gather | solution.py:25
  2825.3 165.5 %reduce-scatter.97.cloned.1.call-start = ((), (), s32[]{:S(2)}) async-start(), calls=%async_computation.89 | async-start | bytes 3932160 | tf_op jit(solution)/shard_map/reduce_scatter | solution.py:42
  3441.3 123.4 %reduce-scatter.103.cloned.1.call-start = ((), (), s32[]{:S(2)}) async-start(), calls=%async_computation.95 | async-start | bytes 3932160 | tf_op jit(solution)/shard_map/reduce_scatter | solution.py:21
  3472.6 210.7 %reduce-scatter.89.cloned.1.call-start = ((), (), s32[]{:S(2)}) async-start(), calls=%async_computation.81 | async-start | bytes 3932160 | tf_op jit(solution)/shard_map/reduce_scatter | solution.py:21
  3505.7 352.3 %reduce-scatter.105.cloned.1.call-start = ((), (), s32[]{:S(2)}) async-start(), calls=%async_computation.97 | async-start | bytes 7864320 | tf_op jit(solution)/shard_map/reduce_scatter | solution.py:21
  3682.8 230.2 %reduce-scatter.91.cloned.1.call-start = ((), (), s32[]{:S(2)}) async-start(), calls=%async_computation.83 | async-start | bytes 7864320 | tf_op jit(solution)/shard_map/reduce_scatter | solution.py:21
  3802.4 149.3 %reduce-scatter.109.cloned.1.call-start = ((), (), s32[]{:S(2)}) async-start(), calls=%async_computation.100 | async-start | bytes 1966080 | tf_op jit(solution)/shard_map/reduce_scatter | solution.py:21
  3817.0 178.4 %reduce-scatter.111.cloned.1.call-start = ((), (), s32[]{:S(2)}) async-start(), calls=%async_computation.101 | async-start | bytes 1966080 | tf_op jit(solution)/shard_map/reduce_scatter | solution.py:21
  3830.1 209.0 %all-gather.81.cloned.1.call-start = ((), (), s32[]{:S(2)}) async-start(), calls=%async_computation.96 | async-start | bytes 1966080 | tf_op jit(solution)/shard_map/all_gather | solution.py:25
  3844.2 233.5 %all-gather.67.cloned.1.call-start = ((), (), s32[]{:S(2)}) async-start(), calls=%async_computation.82 | async-start | bytes 1966080 | tf_op jit(solution)/shard_map/all_gather | solution.py:25
  3858.0 283.6 %all-gather.83.cloned.1.call-start = ((), (), s32[]{:S(2)}) async-start(), calls=%async_computation.98 | async-start | bytes 3932160 | tf_op jit(solution)/shard_map/all_gather | solution.py:25
  3860.6 345.3 %all-gather.69.cloned.1.call-start = ((), (), s32[]{:S(2)}) async-start(), calls=%async_computation.84 | async-start | bytes 3932160 | tf_op jit(solution)/shard_map/all_gather | solution.py:25
  3915.5 310.7 %reduce-scatter.137.cloned.1.call-start = ((), (), s32[]{:S(2)}) async-start(), calls=%async_computation.114 | async-start | bytes 589824
  3920.8 306.5 %reduce-scatter.133.cloned.1.call-start = ((), (), s32[]{:S(2)}) async-start(), calls=%async_computation.112 | async-start | bytes 589824
  3926.3 310.4 %reduce-scatter.139.cloned.1.call-start = ((), (), s32[]{:S(2)}) async-start(), calls=%async_computation.115 | async-start | bytes 589824
  3932.1 315.8 %reduce-scatter.135.cloned.1.call-start = ((), (), s32[]{:S(2)}) async-start(), calls=%async_computation.113 | async-start | bytes 589824
  3937.5 321.4 %reduce-scatter.129.cloned.1.call-start = ((), (), s32[]{:S(2)}) async-start(), calls=%async_computation.110 | async-start | bytes 147456 | tf_op jit(solution)/shard_map/reduce_scatter | solution.py:290
  3940.2 330.1 %reduce-scatter.131.cloned.1.call-start = ((), (), s32[]{:S(2)}) async-start(), calls=%async_computation.111 | async-start | bytes 147456 | tf_op jit(solution)/shard_map/reduce_scatter | solution.py:290
  3943.0 338.1 %reduce-scatter.121.cloned.1.call-start = ((), (), s32[]{:S(2)}) async-start(), calls=%async_computation.106 | async-start | bytes 147456 | tf_op jit(solution)/shard_map/reduce_scatter | solution.py:278
  3945.9 346.6 %reduce-scatter.123.cloned.1.call-start = ((), (), s32[]{:S(2)}) async-start(), calls=%async_computation.107 | async-start | bytes 147456 | tf_op jit(solution)/shard_map/reduce_scatter | solution.py:278
  3980.0 323.4 %reduce-scatter.125.cloned.1.call-start = ((), (), s32[]{:S(2)}) async-start(), calls=%async_computation.108 | async-start | bytes 294912 | tf_op jit(solution)/shard_map/reduce_scatter | solution.py:284
  3981.3 333.0 %reduce-scatter.127.cloned.1.call-start = ((), (), s32[]{:S(2)}) async-start(), calls=%async_computation.109 | async-start | bytes 294912 | tf_op jit(solution)/shard_map/reduce_scatter | solution.py:284
  4023.9 343.2 %all-reduce.11.cloned.1.call-start = ((), (), s32[]{:S(2)}) async-start(), calls=%async_computation.116 | async-start | bytes 1572864 | tf_op jit(solution)/shard_map/psum | solution.py:244
  4027.7 388.8 %reduce-scatter.117.cloned.1.call-start = ((), (), s32[]{:S(2)}) async-start(), calls=%async_computation.104 | async-start | bytes 147456 | tf_op jit(solution)/shard_map/reduce_scatter | solution.py:272
  4030.5 386.0 %reduce-scatter.119.cloned.1.call-start = ((), (), s32[]{:S(2)}) async-start(), calls=%async_computation.105 | async-start | bytes 147456 | tf_op jit(solution)/shard_map/reduce_scatter | solution.py:272
  4033.2 384.8 %reduce-scatter.115.cloned.1.call-start = ((), (), s32[]{:S(2)}) async-start(), calls=%async_computation.103 | async-start | bytes 442368 | tf_op jit(solution)/shard_map/reduce_scatter | solution.py:266
  4150.0 268.0 %reduce-scatter.113.cloned.1.call-start = ((), (), s32[]{:S(2)}) async-start(), calls=%async_computation.102 | async-start | bytes 442368 | tf_op jit(solution)/shard_map/reduce_scatter | solution.py:266
  4214.3 245.3 %reduce-scatter.107.cloned.1.call-start = ((), (), s32[]{:S(2)}) async-start(), calls=%async_computation.99 | async-start | bytes 3932160 | tf_op jit(solution)/shard_map/reduce_scatter | solution.py:42
  4219.8 286.6 %reduce-scatter.93.cloned.1.call-start = ((), (), s32[]{:S(2)}) async-start(), calls=%async_computation.85 | async-start | bytes 3932160 | tf_op jit(solution)/shard_map/reduce_scatter | solution.py:42
  (188 other events, 17611.6 us)
Sparse Core Ops, SparseCore 0:
  10.4 33.5 all-gather.28
  79.6 161.1 reduce-scatter.52
  243.1 162.1 reduce-scatter.66
  407.2 64.3 all-gather.30
  473.7 62.0 all-gather.44
  539.5 35.6 all-gather.32
  606.9 35.7 all-gather.46
  646.2 42.7 reduce-scatter.54
  691.9 43.8 reduce-scatter.68
  788.1 35.4 reduce-scatter.56
  826.4 65.7 reduce-scatter.58
  902.9 37.8 all-gather.36
  944.6 42.7 reduce-scatter.60
  1024.0 35.4 reduce-scatter.70
  1062.2 66.0 reduce-scatter.72
  1139.0 37.8 all-gather.50
  1180.7 42.7 reduce-scatter.74
  1281.3 211.8 reduce-scatter.62
  1502.3 116.3 all-gather.40
  1625.4 42.0 reduce-scatter.64
  1709.6 211.8 reduce-scatter.76
  1930.5 116.3 all-gather.54
  2053.7 42.0 reduce-scatter.78
  2180.5 211.8 reduce-scatter.80
  2398.7 116.3 all-gather.58
  2521.9 42.0 reduce-scatter.82
  2607.2 211.8 reduce-scatter.94
  2825.4 116.3 all-gather.72
  2948.7 42.0 reduce-scatter.96
  3048.0 60.3 reduce-scatter.84
  3129.0 36.9 all-gather.62
  3170.0 42.7 reduce-scatter.86
  3251.8 60.3 reduce-scatter.98
  3332.0 36.9 all-gather.76
  3372.8 42.7 reduce-scatter.100
  3504.2 60.3 reduce-scatter.102
  3566.8 60.3 reduce-scatter.88
  3682.9 110.6 reduce-scatter.104
  3802.5 110.4 reduce-scatter.90
  3915.8 35.9 reduce-scatter.108
  3954.6 40.7 reduce-scatter.110
  3996.9 42.2 all-gather.80
  4040.7 36.9 all-gather.66
  4079.2 62.2 all-gather.82
  4143.7 62.0 all-gather.68
  4317.2 49.7 all-reduce.10
  4414.5 45.0 reduce-scatter.106
  4462.4 43.8 reduce-scatter.92
  (25 shorter events, 443.8 us)
where the time goes:
time: 4520 us
  waiting for transfers between devices  3380 us (75%)
  matrix products  484 us (11%)
  other arithmetic  301 us (7%)
  blocking collectives  242 us (5%)
  local copies, waits for them, and re-layouts  83.8 us (2%)
    reduce_scatter x18, waiting for transfers between devices, cols_share(): return lax.psum_scatter(value_in, 'col', scatter_dimension=0, tiled=True)  1560 us
    all_gather x16, waiting for transfers between devices, cols_all(): return lax.all_gather(value_in, 'col', axis=0, tiled=True)  862 us
    reduce_scatter x12, waiting for transfers between devices, to_resid(): lax.psum_scatter(jnp.einsum('tsk,kd->tsd', full_in, weight_in, preferred_...  513 us
    all_gather x12, waiting for transfers between devices, rows_all(): return lax.all_gather(value_in, 'row', axis=0, tiled=True)  318 us
    psum x6, blocking collectives, col_stats(): return lax.psum((jnp.sum(left_part, -1), jnp.sum(right_part, -1)), 'col')  113 us
    all_gather x4, blocking collectives, cols_all(): return lax.all_gather(value_in, 'col', axis=0, tiled=True)  98.2 us
    convert_element_type x4, other arithmetic, attend_back(): grad_scores = (probs_full * (grad_probs - row_delta)).astype(jnp.bfloat16)  95.5 us
  transfers between devices with their start and end apart: 73, of which 63 were waited for; matrix products, arithmetic and copies ran while one was open for 14% of the time, Pallas kernels for 0%

commit v1 on v0

v1 whole, which is shorter than its diff:
```python
import functools

import jax
import jax.numpy as jnp
from jax import lax
from jax.experimental import pallas as pl
from jax.experimental.pallas import tpu as pltpu
from jax.sharding import PartitionSpec as P

bf16 = jnp.bfloat16
f32 = jnp.float32
HD = 64
HALF = 32
NORM_EPS = 1e-05
NEG = -1e30
LIMIT = 90.0
LN2 = 0.6931471805599453
LOG2E = 1.4426950408889634
KB = 512


def dot(left, right, left_dim, right_dim):
    return lax.dot_general(
        left, right, (((left_dim,), (right_dim,)), ((), ())), preferred_element_type=f32
    )


def ones_rows(count, shape, dim):
    return jnp.where(lax.broadcasted_iota(jnp.int32, shape, dim) < count, 1.0, 0.0).astype(bf16)


def allowed_block(meta, i, start, width, cols):
    k_pos = start + lax.broadcasted_iota(jnp.int32, (width, cols), 0)
    q_pos = meta[1 + i] + lax.broadcasted_iota(jnp.int32, (1, cols), 1)
    return k_pos <= jnp.maximum(q_pos, meta[0] - 1)


def block_range(meta, i, cols):
    full = jnp.maximum(meta[1 + i], meta[0]) // KB
    total = (jnp.maximum(meta[1 + i] + cols, meta[0]) + KB - 1) // KB
    return full, total


def over_keys(meta, i, cols, keys, masked, step, carry):
    if not masked:
        for start in range(0, keys, KB):
            carry = step(start, carry, False, KB)
        return carry
    full, total = block_range(meta, i, cols)
    pairs = full // 2
    carry = lax.fori_loop(0, pairs, lambda j, c: step(j * 2 * KB, c, False, 2 * KB), carry)
    carry = lax.fori_loop(2 * pairs, full, lambda j, c: step(j * KB, c, False, KB), carry)
    return lax.fori_loop(full, total, lambda j, c: step(j * KB, c, True, KB), carry)


def pieces(kv_refs, masked):
    out = []
    for ref in kv_refs:
        count = ref.shape[0]
        for b in range(count):
            out.append((ref, b))
    return out


def piece_start(meta, n_query, index, length, masked):
    if masked:
        return pl.multiple_of(meta[1 + n_query + index] * length, length)
    return index * length


def attend_kernel(*refs, sources, n_query, masked):
    meta, q_ref = refs[:2]
    kv_refs = refs[2 : 2 + sources]
    o_ref, l_ref, key_rows, val_cols = refs[2 + sources :]
    i = pl.program_id(1)
    cols = q_ref.shape[-1]
    keys = val_cols.shape[-1]

    @pl.when(i == 0)
    def _():
        key_rows[:, HD:] = ones_rows(1, (keys, 16), 1)
        val_cols[HD:, :] = ones_rows(1, (16, keys), 0)
        for index, (ref, b) in enumerate(pieces(kv_refs, masked)):
            length = ref.shape[-1]
            at = pl.ds(piece_start(meta, n_query, index, length, masked), length)
            key_rows[at, :HD] = ref[b, :, 0, 0].reshape(HD, length).T
            val_cols[:HD, at] = ref[b, :, 1, 0].reshape(HD, length)

    query = q_ref[0, :, 0].reshape(HD, cols)
    first = dot(key_rows[0:128, :HD], query, 1, 0)
    shift = jnp.max(first, axis=0, keepdims=True).astype(bf16).astype(f32)
    row = lax.broadcasted_iota(jnp.int32, (16, cols), 0)
    query_more = jnp.concatenate([query, jnp.where(row == 0, -shift, 0.0).astype(bf16)], axis=0)

    def step(start, carry, mask, width):
        top, acc = carry
        at = pl.ds(pl.multiple_of(start, KB), width)
        scores = dot(key_rows[at, :], query_more, 1, 0)
        if mask:
            scores = jnp.where(allowed_block(meta, i, start, width, cols), scores, NEG)
        top = jnp.maximum(top, jnp.max(scores, axis=0, keepdims=True))
        acc = acc + dot(val_cols[:, at], jnp.exp2(scores).astype(bf16), 1, 0)
        return top, acc

    def put(shift, acc):
        total = acc[HD : HD + 1, :]
        mixed = (acc[:HD] * (1.0 / total)).astype(bf16)
        o_ref[0, :, 0] = mixed.reshape(2, HALF, cols)
        l_ref[0, 0] = shift + jnp.log2(total)

    start = (jnp.full((1, cols), NEG, f32), jnp.zeros((HD + 16, cols), f32))
    top, acc = over_keys(meta, i, cols, keys, masked, step, start)
    put(shift, acc)

    @pl.when(jnp.max(top) > LIMIT)
    def _():
        def careful(j, carry):
            high, acc = carry
            at = pl.ds(pl.multiple_of(j * KB, KB), KB)
            scores = dot(key_rows[at, :HD], query, 1, 0)
            if masked:
                scores = jnp.where(allowed_block(meta, i, j * KB, KB, cols), scores, NEG)
            new = jnp.maximum(high, jnp.max(scores, axis=0, keepdims=True))
            part = dot(val_cols[:, at], jnp.exp2(scores - new).astype(bf16), 1, 0)
            return new, acc * jnp.exp2(high - new) + part

        total = block_range(meta, i, cols)[1] if masked else keys // KB
        put(*lax.fori_loop(0, total, careful, start))


def attend_back_kernel(*refs, sources, n_query, masked):
    meta, q_ref = refs[:2]
    kv_refs = refs[2 : 2 + sources]
    g_ref, o_ref, l_ref = refs[2 + sources : 5 + sources]
    dq_ref = refs[5 + sources]
    dkv_refs = refs[6 + sources : 6 + 2 * sources]
    key_rows, val_rows, key_cols, dk_acc, dv_acc = refs[6 + 2 * sources :]
    i = pl.program_id(1)
    cols = q_ref.shape[-1]
    keys = key_cols.shape[-1]

    @pl.when(i == 0)
    def _():
        key_rows[:, HD:] = ones_rows(3, (keys, 16), 1)
        val_rows[:, HD:] = ones_rows(3, (keys, 16), 1)
        for index, (ref, b) in enumerate(pieces(kv_refs, masked)):
            length = ref.shape[-1]
            at = pl.ds(piece_start(meta, n_query, index, length, masked), length)
            k_part = ref[b, :, 0, 0].reshape(HD, length)
            key_cols[:, at] = k_part
            key_rows[at, :HD] = k_part.T
            val_rows[at, :HD] = ref[b, :, 1, 0].reshape(HD, length).T
        dk_acc[...] = jnp.zeros_like(dk_acc)
        dv_acc[...] = jnp.zeros_like(dv_acc)

    query = q_ref[0, :, 0].reshape(HD, cols)
    grad = g_ref[0, :, 0].reshape(HD, cols)
    delta = jnp.sum(
        grad.astype(f32) * o_ref[0, :, 0].reshape(HD, cols).astype(f32), axis=0, keepdims=True
    )

    def with_shift(value, shift):
        high = shift.astype(bf16).astype(f32)
        mid = (shift - high).astype(bf16).astype(f32)
        low = shift - high - mid
        row = lax.broadcasted_iota(jnp.int32, (16, cols), 0)
        more = jnp.where(row == 0, -high, jnp.where(row == 1, -mid, jnp.where(row == 2, -low, 0.0)))
        return jnp.concatenate([value, more.astype(bf16)], axis=0)

    query_more = with_shift(query, l_ref[0, 0])
    grad_more = with_shift(grad, delta)

    def step(start, dq, mask, width):
        at = pl.ds(pl.multiple_of(start, KB), width)
        scores = dot(key_rows[at, :], query_more, 1, 0)
        if mask:
            scores = jnp.where(allowed_block(meta, i, start, width, cols), scores, NEG)
        probs = jnp.exp2(scores)
        grad_scores = (probs * dot(val_rows[at, :], grad_more, 1, 0)).astype(bf16)
        dv_acc[:, at] += dot(grad, probs.astype(bf16), 1, 1)
        dk_acc[:, at] += dot(query, grad_scores, 1, 1)
        return dq + dot(key_cols[:, at], grad_scores, 1, 0)

    dq = over_keys(meta, i, cols, keys, masked, step, jnp.zeros((HD, cols), f32))
    dq_ref[0, :, 0] = (dq * 0.125).astype(bf16).reshape(2, HALF, cols)

    @pl.when(i == n_query - 1)
    def _():
        for index, (ref, b) in enumerate(pieces(dkv_refs, masked)):
            length = ref.shape[-1]
            at = pl.ds(piece_start(meta, n_query, index, length, masked), length)
            ref[b, :, 0, 0] = (dk_acc[:, at] * LN2).astype(ref.dtype).reshape(2, HALF, length)
            ref[b, :, 1, 0] = dv_acc[:, at].astype(ref.dtype).reshape(2, HALF, length)


def attention_specs(query, kv_list, masked):
    cols = query.shape[-1]
    if masked:
        n_query, _, heads = query.shape[:3]
        grid = (heads, n_query)
        q_spec = pl.BlockSpec((1, 2, 1, HALF, cols), lambda h, i, m: (i, 0, h, 0, 0))
        kv_specs = [
            pl.BlockSpec(kv.shape[:3] + (1,) + kv.shape[4:], lambda h, i, m: (0, 0, 0, h, 0, 0))
            for kv in kv_list
        ]
        l_spec = pl.BlockSpec((1, 1, 1, cols), lambda h, i, m: (h, i, 0, 0))
        l_shape = (heads, n_query, 1, cols)
        keys = sum(kv.shape[0] * kv.shape[-1] for kv in kv_list)
    else:
        n_query = 1
        _, _, rows, heads = query.shape[:4]
        grid = (rows * heads, 1)
        q_spec = pl.BlockSpec(
            (1, 2, None, 1, HALF, cols), lambda g, i, m: (0, 0, g // heads, g % heads, 0, 0)
        )
        kv_specs = [
            pl.BlockSpec(
                (kv.shape[0], 2, None, 2, 1) + kv.shape[5:],
                lambda g, i, m: (0, 0, g // heads, 0, g % heads, 0, 0),
            )
            for kv in kv_list
        ]
        l_spec = pl.BlockSpec((1, 1, 1, cols), lambda g, i, m: (g, 0, 0, 0))
        l_shape = (rows * heads, 1, 1, cols)
        keys = sum(kv.shape[0] * kv.shape[-1] for kv in kv_list)
    return n_query, grid, q_spec, kv_specs, l_spec, l_shape, keys


def cost(query, keys, dots):
    pairs = query.size // HD * keys
    return pl.CostEstimate(
        flops=2 * pairs * 256 * dots // 2, bytes_accessed=query.size * 16, transcendentals=pairs
    )


def attend(meta, query, kv_list, masked, name):
    n_query, grid, q_spec, kv_specs, l_spec, l_shape, keys = attention_specs(query, kv_list, masked)
    return pl.pallas_call(
        functools.partial(attend_kernel, sources=len(kv_list), n_query=n_query, masked=masked),
        grid_spec=pltpu.PrefetchScalarGridSpec(
            num_scalar_prefetch=1,
            grid=grid,
            in_specs=[q_spec] + kv_specs,
            out_specs=[q_spec, l_spec],
            scratch_shapes=[pltpu.VMEM((keys, HD + 16), bf16), pltpu.VMEM((HD + 16, keys), bf16)],
        ),
        out_shape=[
            jax.ShapeDtypeStruct(query.shape, bf16),
            jax.ShapeDtypeStruct(l_shape, f32),
        ],
        compiler_params=pltpu.CompilerParams(vmem_limit_bytes=48 << 20),
        cost_estimate=cost(query, keys, 2),
        name=name,
    )(meta, query, *kv_list)


def attend_back(meta, query, kv_list, grad, out, lse, masked, types, name):
    n_query, grid, q_spec, kv_specs, l_spec, l_shape, keys = attention_specs(query, kv_list, masked)
    return pl.pallas_call(
        functools.partial(attend_back_kernel, sources=len(kv_list), n_query=n_query, masked=masked),
        grid_spec=pltpu.PrefetchScalarGridSpec(
            num_scalar_prefetch=1,
            grid=grid,
            in_specs=[q_spec] + kv_specs + [q_spec, q_spec, l_spec],
            out_specs=[q_spec] + kv_specs,
            scratch_shapes=[
                pltpu.VMEM((keys, HD + 16), bf16),
                pltpu.VMEM((keys, HD + 16), bf16),
                pltpu.VMEM((HD, keys), bf16),
                pltpu.VMEM((HD, keys), f32),
                pltpu.VMEM((HD, keys), f32),
            ],
        ),
        out_shape=[jax.ShapeDtypeStruct(query.shape, bf16)]
        + [jax.ShapeDtypeStruct(kv.shape, t) for kv, t in zip(kv_list, types)],
        compiler_params=pltpu.CompilerParams(vmem_limit_bytes=48 << 20),
        cost_estimate=cost(query, keys, 5),
        name=name,
    )(meta, query, *kv_list, grad, out, lse)


def norm_stats(resid, width):
    mean = jnp.sum(resid, -1, keepdims=True) / width
    square = jnp.sum(resid * resid, -1, keepdims=True) / width
    inv_std = lax.rsqrt(square - mean * mean + NORM_EPS)
    return (resid - mean) * inv_std, inv_std


def norm_back(grad, gain, normed, inv_std, width):
    scaled = grad * gain
    total = jnp.sum(scaled, -1, keepdims=True) / width
    cross = jnp.sum(scaled * normed, -1, keepdims=True) / width
    return inv_std * (scaled - total - normed * cross), jnp.sum(grad * normed, axis=0)


def mm(spec, left, right):
    return jnp.einsum(spec, left, right, preferred_element_type=f32)


def per_device(
    x_in,
    prefix,
    enc_bank,
    bank_rows,
    w_qkv,
    w_out,
    w_cross_q,
    w_cross_kv,
    w_cross_out,
    w_up,
    w_down,
    ln_gains,
    out_grad,
):
    dp, rows, cols = lax.axis_size("dp"), lax.axis_size("row"), lax.axis_size("col")
    d_pos, r_pos, c_pos = lax.axis_index("dp"), lax.axis_index("row"), lax.axis_index("col")
    own_seqs, part_width, row_len = x_in.shape
    seqs = own_seqs * dp
    sub = cols // seqs
    parts = dp * sub
    width = part_width * cols
    tokens = row_len // parts
    heads = w_qkv.shape[2]
    feat = heads * HALF
    units = w_up.shape[1]
    length = row_len * rows
    odd = (r_pos % 2) == 1
    seq_pos = c_pos // sub
    part_pos = d_pos * sub + c_pos % sub
    groups = [[s * sub + k for k in range(sub)] for s in range(seqs)]
    everywhere = ("dp", "row", "col")

    def to_tokens(value):
        take = value.shape[-1] // parts
        value = value.reshape(own_seqs, part_width, parts, take)
        value = jnp.where(odd, value[:, :, ::-1], value)
        value = value.reshape(own_seqs, part_width, dp, sub, take)
        value = lax.all_to_all(value, "dp", 2, 0, tiled=True)
        value = value.reshape(seqs, part_width, sub, take).transpose(0, 2, 1, 3)
        value = lax.all_to_all(value.reshape(cols, part_width, take), "col", 0, 1, tiled=True)
        return value.reshape(width, take)

    def to_home(value):
        take = value.shape[-1]
        value = lax.all_to_all(value.reshape(1, width, take), "col", 1, 0, tiled=True)
        value = value.reshape(seqs, sub, part_width, take).transpose(0, 2, 1, 3)
        value = value.reshape(seqs, part_width, 1, sub, take)
        value = lax.all_to_all(value, "dp", 0, 2, tiled=True)
        value = value.reshape(own_seqs, part_width, parts, take)
        value = jnp.where(odd, value[:, :, ::-1], value)
        return value.reshape(own_seqs, part_width, parts * take)

    qkv_near = lax.all_gather(w_qkv.reshape(part_width, 3 * feat), ("dp", "col"), axis=0)
    x_own = to_tokens(x_in)
    x_rows = lax.all_gather(x_own, "row", axis=0)
    small = jnp.concatenate(
        [
            w_cross_kv.reshape(part_width, 2 * feat),
            w_out.reshape(feat, part_width).T,
            w_cross_q.reshape(part_width, feat),
            w_cross_out.reshape(feat, part_width).T,
        ],
        axis=1,
    )
    small_all = lax.all_gather(small, everywhere, axis=0)
    small_all = small_all.reshape(dp, rows, cols, part_width, 5 * feat)
    large_all = lax.all_gather(jnp.stack([w_up, w_down.T]), everywhere, axis=0)
    large_all = large_all.reshape(dp, rows, cols, 2, part_width, units)
    qkv_all = lax.all_gather(qkv_near, "row", axis=0)

    def standard(first, count):
        piece = small_all[..., first * feat : (first + count) * feat]
        return piece.transpose(2, 3, 0, 1, 4).reshape(width, dp * rows * count * feat)

    wt_ckv = standard(0, 2)
    wt_out_t = standard(1 + 1, 1).reshape(width, dp, rows, feat).transpose(0, 2, 1, 3)
    wt_out_t = wt_out_t.reshape(width, width)
    wt_cq = standard(3, 1)
    wt_cout_t = standard(4, 1)
    wt_up, wt_down_t = (
        large_all[:, :, :, j].transpose(2, 3, 0, 1, 4).reshape(width, dp * rows * units)
        for j in range(2)
    )

    gains_all = lax.all_gather(ln_gains.astype(f32), "col", axis=1, tiled=True)

    near = qkv_near.reshape(dp, width, 3 * feat)
    proj = mm("dwf,rwt->rdft", near, x_rows)
    proj = proj.reshape(rows, dp, 3, heads, HALF, tokens)
    query = (proj[:, :, 0] * (0.125 * LOG2E)).astype(bf16)
    kv_own = proj[:, :, 1:].astype(bf16)

    def index_of(row, part):
        return jnp.where(row % 2 == 1, parts - 1 - part, part) + row * parts

    row_ids = jnp.arange(rows, dtype=jnp.int32)
    if sub == 1:
        kv_list = [kv_own, lax.ppermute(kv_own, "dp", [(0, 1), (1, 0)])]
        owners = [part_pos, 1 - part_pos]
    else:
        kv_all = lax.all_gather(kv_own, "col", axis=0, axis_index_groups=groups)
        kv_all = lax.all_gather(kv_all, "dp", axis=0).reshape((parts,) + kv_own.shape)
        kv_list = [kv_all[j] for j in range(parts)]
        owners = list(range(parts))
    q_start = index_of(row_ids, part_pos) * tokens
    places = [index_of(row_ids, owner) for owner in owners]
    seq_prefix = lax.all_gather(prefix, "dp", axis=0, tiled=True)[seq_pos]
    meta = jnp.concatenate([seq_prefix[None], q_start] + places).astype(jnp.int32)
    mixed, lse = attend(meta, query, kv_list, True, "self_attention")
    attn = lax.all_to_all(mixed, "row", 0, 0, tiled=True)
    attn_flat = attn.reshape(width, tokens)

    resid_one = x_own.T.astype(f32) + mm("ft,wf->tw", attn_flat, wt_out_t)
    normed_one, inv_one = norm_stats(resid_one, width)
    h_one = normed_one * gains_all[0]
    h_one_low = h_one.astype(bf16)

    picked = bank_rows.shape[1] // rows
    row_pick = lax.dynamic_slice_in_dim(bank_rows, r_pos * picked, picked, 1)
    bank_ids = jnp.arange(enc_bank.shape[2], dtype=jnp.int32)
    hot = (bank_ids[None, :, None] == row_pick[:, None, :]).astype(bf16)
    chosen = to_tokens(mm("swn,snp->swp", enc_bank, hot).astype(bf16))
    c_tokens = chosen.shape[1]
    ckv_own = mm("wf,wt->ft", wt_ckv, chosen).astype(bf16)
    ckv_own = ckv_own.reshape(dp, rows, 2, heads, HALF, c_tokens)
    if sub > 1:
        ckv_all = lax.all_gather(ckv_own, "col", axis=0, axis_index_groups=groups)
    else:
        ckv_all = ckv_own
    ckv_all = lax.all_gather(ckv_all, ("dp", "row"), axis=0)
    ckv_all = ckv_all.reshape((dp * rows * sub,) + ckv_own.shape)
    cross_q = (mm("wf,tw->ft", wt_cq, h_one_low) * (0.125 * LOG2E)).astype(bf16)
    cross_q = cross_q.reshape(1, dp, rows, heads, HALF, tokens)
    catt, lse_cross = attend(meta, cross_q, [ckv_all], False, "cross_attention")
    catt_flat = catt.reshape(width, tokens)
    resid_two = h_one + mm("ft,wf->tw", catt_flat, wt_cout_t)
    normed_two, inv_two = norm_stats(resid_two, width)
    h_two = normed_two * gains_all[1]
    h_two_low = h_two.astype(bf16)

    upper = mm("tw,wf->tf", h_two_low, wt_up)
    cdf = 0.5 * (1.0 + lax.erf(upper * 0.7071067811865476))
    act = (upper * cdf).astype(bf16)
    slope = (cdf + upper * (jnp.exp(-0.5 * upper * upper) * 0.3989422804014327)).astype(bf16)
    resid_three = h_two + mm("tf,wf->tw", act, wt_down_t)
    normed_three, inv_three = norm_stats(resid_three, width)
    block_out = to_home((normed_three * gains_all[2]).astype(bf16).T)

    cot = to_tokens(out_grad).T.astype(f32)
    dy_three, dg_three = norm_back(cot, gains_all[2], normed_three, inv_three, width)
    d_ffn = dy_three.astype(bf16)
    g_down_t = mm("tw,tf->wf", d_ffn, act)
    d_upper = (mm("tw,wf->tf", d_ffn, wt_down_t) * slope.astype(f32)).astype(bf16)
    g_up = mm("tw,tf->wf", h_two_low, d_upper)
    dh_two = dy_three + mm("tf,wf->tw", d_upper, wt_up)
    dy_two, dg_two = norm_back(dh_two, gains_all[1], normed_two, inv_two, width)
    d_cross = dy_two.astype(bf16)
    g_cout_t = mm("tw,ft->wf", d_cross, catt_flat)
    d_catt = mm("wf,tw->ft", wt_cout_t, d_cross).astype(bf16).reshape(catt.shape)
    d_cq, d_ckv = attend_back(
        meta, cross_q, [ckv_all], d_catt, catt, lse_cross, False, [bf16], "cross_attention_back"
    )
    d_cq = d_cq.reshape(width, tokens)
    if sub > 1:
        d_ckv = d_ckv.reshape(dp, rows, sub, -1)
        d_ckv = lax.psum_scatter(d_ckv, "dp", scatter_dimension=0, tiled=True)
        d_ckv = lax.psum_scatter(d_ckv, "row", scatter_dimension=1, tiled=True)
        d_ckv = lax.psum_scatter(
            d_ckv, "col", scatter_dimension=2, tiled=True, axis_index_groups=groups
        )
    else:
        d_ckv = lax.psum_scatter(d_ckv, ("dp", "row"), scatter_dimension=0, tiled=True)
    d_ckv = d_ckv.reshape(2 * width, c_tokens)
    dh_one = dy_two + mm("ft,wf->tw", d_cq, wt_cq)
    dy_one, dg_one = norm_back(dh_one, gains_all[0], normed_one, inv_one, width)
    d_attn_out = dy_one.astype(bf16)
    d_attn = mm("wf,tw->ft", wt_out_t, d_attn_out).astype(bf16).reshape(attn.shape)
    d_mixed = lax.all_to_all(d_attn, "row", 0, 0, tiled=True)
    g_cq = mm("tw,ft->wf", h_one_low, d_cq)
    g_out_t = mm("tw,ft->wf", d_attn_out, attn_flat)
    g_out_t = g_out_t.reshape(width, rows, dp, feat).transpose(0, 2, 1, 3).reshape(width, width)
    g_ckv = mm("wt,ft->wf", chosen, d_ckv)
    d_chosen = mm("wf,ft->wt", wt_ckv, d_ckv).astype(bf16)

    d_chosen = lax.all_gather(to_home(d_chosen), "row", axis=2, tiled=True)
    hot_all = (bank_rows[:, :, None] == bank_ids[None, None, :]).astype(bf16)
    bank_grad = mm("swp,spn->swn", d_chosen, hot_all)

    types = [f32] + [bf16] * (len(kv_list) - 1) if sub == 1 else [bf16] * len(kv_list)
    d_query, *d_kv = attend_back(
        meta, query, kv_list, d_mixed, mixed, lse, True, types, "self_attention_back"
    )
    if sub == 1:
        d_kv = d_kv[0] + lax.ppermute(d_kv[1], "dp", [(0, 1), (1, 0)]).astype(f32)
    else:
        d_kv = jnp.stack(d_kv).reshape((dp, sub) + kv_own.shape)
        d_kv = lax.psum_scatter(d_kv, "dp", scatter_dimension=0, tiled=True)
        d_kv = lax.psum_scatter(
            d_kv, "col", scatter_dimension=1, tiled=True, axis_index_groups=groups
        )
    d_kv = d_kv.reshape(kv_own.shape).astype(bf16)
    d_proj = jnp.concatenate([d_query[:, :, None], d_kv], axis=2)
    d_proj = d_proj.reshape(rows, dp, 3 * feat, tokens)
    g_qkv = mm("rwt,rdft->dwf", x_rows, d_proj)
    d_mine = lax.all_to_all(d_proj, "row", 0, 0, tiled=True)
    wt_qkv = qkv_all.reshape(rows, dp, width, 3 * feat)
    dx = dy_one + mm("rdft,rdwf->tw", d_mine, wt_qkv)
    x_grad = to_home(dx.astype(bf16).T).astype(f32)

    def shares(value, count):
        value = value.astype(bf16).reshape(cols, part_width, dp, rows, count)
        return value.transpose(2, 3, 0, 1, 4)

    def scatter(value):
        value = lax.psum_scatter(value, "dp", scatter_dimension=0, tiled=False)
        value = lax.psum_scatter(value, "row", scatter_dimension=0, tiled=False)
        return lax.psum_scatter(value, "col", scatter_dimension=0, tiled=False)

    big = scatter(jnp.stack([shares(g_up, units), shares(g_down_t, units)], axis=3)).astype(f32)
    rest = scatter(
        jnp.concatenate(
            [shares(g_ckv, 2 * feat), shares(g_out_t, feat), shares(g_cq, feat), shares(g_cout_t, feat)],
            axis=-1,
        )
    ).astype(f32)
    qkv_grad = g_qkv.astype(bf16).reshape(dp, cols, part_width, 3 * feat)
    qkv_grad = lax.psum_scatter(qkv_grad, "dp", scatter_dimension=0, tiled=False)
    qkv_grad = lax.psum_scatter(qkv_grad, "col", scatter_dimension=0, tiled=False).astype(f32)
    gain_grads = lax.psum(jnp.stack([dg_one, dg_two, dg_three]), everywhere)
    gain_grads = lax.dynamic_slice_in_dim(gain_grads, c_pos * part_width, part_width, 1)

    return (
        block_out,
        x_grad,
        bank_grad,
        qkv_grad.reshape(w_qkv.shape),
        rest[:, 2 * feat : 3 * feat].T.reshape(w_out.shape),
        rest[:, 3 * feat : 4 * feat].reshape(w_cross_q.shape),
        rest[:, : 2 * feat].reshape(w_cross_kv.shape),
        rest[:, 4 * feat :].T.reshape(w_cross_out.shape),
        big[0],
        big[1].T,
        gain_grads,
    )


def solution(mesh):
    placed = (
        P("dp", "col", "row"),
        P("dp"),
        P("dp", "col", None),
        P("dp", None),
        P("col", None, "row", "dp"),
        P("row", "dp", "col"),
        P("col", "row", "dp"),
        P("col", None, "row", "dp"),
        P("row", "dp", "col"),
        P("col", ("dp", "row")),
        P(("dp", "row"), "col"),
        P(None, "col"),
        P("dp", "col", "row"),
    )
    return jax.shard_map(
        per_device,
        mesh=mesh,
        in_specs=placed,
        out_specs=(
            P("dp", "col", "row"),
            P("dp", "col", "row"),
            P("dp", "col", None),
            P("col", None, "row", "dp"),
            P("row", "dp", "col"),
            P("col", "row", "dp"),
            P("col", None, "row", "dp"),
            P("row", "dp", "col"),
            P("col", ("dp", "row")),
            P(("dp", "row"), "col"),
            P(None, "col"),
        ),
        check_vma=False,
    )
```

time: 4520 us -> 859 us (0.19)
  waiting for transfers between devices: 3380 us -> 131 us
  matrix products: 484 us -> 86.2 us
  other arithmetic: 301 us -> 53.2 us
  local copies, waits for them, and re-layouts: 83.8 us -> 205 us
  Pallas kernels: 0 us -> 113 us
    reduce_scatter x40 -> x7, waiting for transfers between devices: 2130 us -> 27 us  [the longest x1 16.7 us: per_device(): lax.psum_scatter(d_ckv, ('dp', 'row'), scatter_dimension=0, tiled=True)]
    all_gather x28 -> x5, waiting for transfers between devices: 1180 us -> 72 us  [the longest x1 53.8 us: per_device(): qkv_all = lax.all_gather(qkv_near, 'row', axis=0)]
    dot_general x66 -> x23, matrix products: 484 us -> 86.2 us  [mm(): return jnp.einsum(spec, left, right, preferred_element_type=f32)]
    convert_element_type x27 -> x9, other arithmetic: 155 us -> 12.6 us  [the longest x1 2.55 us: per_device(): d_kv = d_kv.reshape(kv_own.shape).astype(bf16)]
    pallas_call x0 -> x4, Pallas kernels: none -> 113 us  [the longest x2 71.1 us: attend_back(): pl.pallas_call(functools.partial(attend_back_kernel, sources=len(kv_list)...]
    reshape x0 -> x25, local copies, waits for them, and re-layouts: none -> 99.9 us  [the longest x10 52.7 us: shares(): value = value.astype(bf16).reshape(cols, part_width, dp, rows, count)]
    reduce_sum x14 -> x1, other arithmetic: 81 us -> 0.74 us  [norm_back(): jnp.sum(grad * normed, axis=0)]
    all_to_all x0 -> x7, blocking collectives: none -> 70.8 us  [the longest x1 35.1 us: to_tokens(): lax.all_to_all(value.reshape(cols, part_width, take), 'col', 0, 1, tiled=...]
  transfers between devices with their start and end apart: 73 -> 24, of which waited for: 63 -> 10; matrix products, arithmetic and copies ran while one was open for 14% -> 30% of each run, Pallas kernels for 0% -> 11%
where the time goes in v1:
time: 859 us; the launch traced here: 847 us
  local copies, waits for them, and re-layouts  205 us (24%)
  blocking collectives  203 us (24%)
  waiting for transfers between devices  131 us (15%)
  Pallas kernels  113 us (13%)
  matrix products  86.2 us (10%)
  other arithmetic  53.2 us (6%)
  starting transfers between devices  39.9 us (5%)
  between operations  15.9 us (2%)
    dot_general x23, matrix products, mm(): return jnp.einsum(spec, left, right, preferred_element_type=f32)  86.2 us
    pallas_call x2, Pallas kernels, attend_back(): pl.pallas_call(functools.partial(attend_back_kernel, sources=len(kv_list)...  71.1 us
    psum x1, blocking collectives, per_device(): gain_grads = lax.psum(jnp.stack([dg_one, dg_two, dg_three]), everywhere)  58.1 us
    all_gather x1, waiting for transfers between devices, per_device(): qkv_all = lax.all_gather(qkv_near, 'row', axis=0)  53.8 us
    reshape x10, local copies, waits for them, and re-layouts, shares(): value = value.astype(bf16).reshape(cols, part_width, dp, rows, count)  52.7 us
    pallas_call x2, Pallas kernels, attend(): pl.pallas_call(functools.partial(attend_kernel, sources=len(kv_list), n_q...  41.6 us
    all_to_all x1, blocking collectives, to_tokens(): lax.all_to_all(value.reshape(cols, part_width, take), 'col', 0, 1, tiled=...  35.1 us
    unnamed x142, local copies, waits for them, and re-layouts  31.9 us
  transfers between devices with their start and end apart: 24, of which 10 were waited for; matrix products, arithmetic and copies ran while one was open for 30% of the time, Pallas kernels for 11%

profile of v1, /device:TPU:0, one launch (start us, length us, event | category | flops | bytes accessed | tf_op | source)
XLA Modules:
  0.0 847.2 jit_solution(2754034631383202469)
XLA Ops:
  12.5 7.9 rev.18
  26.9 35.1 %all_to_all.163 = bf16[4,192,512]{2,1,0:T(8,128)(2,1)} all-to-all(bf16[4,192,512]{2,1,0:T(8,128)(2,1)S(1)} %bitcast.382), channel_id=1, replica_groups=mesh['dp'=2,'row'=4,'col'=4] {'col'}, dimensions={0} | all-to-all | bytes 1572864 | tf_op jit(solution)/shard_map/all_to_all | solution.py:340
  64.4 4.7 all_to_all.164
  72.5 18.2 %all-gather.14.cloned.1.call-done = bf16[6144,480]{1,0:T(8,128)(2,1)} async-done(((bf16[192,480]{1,0:T(8,128)(2,1)}), bf16[6144,480]{1,0:T(8,128)(2,1)}) %all-gather.14.cloned.1.call-update) | async-done | bytes 5898256 | tf_op jit(solution)/shard_map/all_gather | solution.py:365
  96.9 6.0 reshape.324
  105.6 30.1 %all_gather.38 = bf16[8,192,288]{2,1,0:T(8,128)(2,1)S(1)} all-gather(bf16[1,192,288]{2,1,0:T(8,128)(2,1)S(1)} %copy.231), channel_id=1, replica_groups=mesh['dp'=2,'row'=4,'col'=4] {'dp','col'}, dimensions={0}, use_global_device_ids=true | all-gather | bytes 995328 | tf_op jit(solution)/shard_map/all_gather | solution.py:353
  135.7 4.7 fusion.13
  149.9 4.5 all-to-all-start.7
  162.5 24.3 %all-gather.3 = f32[4,192,3]{1,2,0:T(4,128)S(1)} all-gather(f32[1,192,3]{1,2,0:T(4,128)S(1)} %convert_bitcast_fusion), channel_id=1, replica_groups=mesh['dp'=2,'row'=4,'col'=4] {'col'}, dimensions={0}, use_global_device_ids=true | all-gather | bytes 11520 | tf_op jit(solution)/shard_map/all_gather | solution.py:385
  194.3 28.4 %self_attention.1 = (bf16[4,2,3,32,512]{4,3,2,1,0:T(8,128)(2,1)}, f32[3,4,1,512]{3,2,1,0:T(1,128)S(1)}) custom-call(s32[13]{0:T(128)S(1)} %pad_add_fusion.refs_0_, bf16[4,2,3,32,512]{4,3,2,1,0:T(8,128)(2,1)S(1)} %fusion.55.refs_1_, bf16[4,2,2,3,32,512]{5,4,3,2,1,0:T(8,128)(2,1)S(1)} %slice.107.refs_2_, ...), custom_call_target="tpu_custom_call" | custom-call | flops 12884901888 | bytes 6291456 | tf_op jit(solution)/shard_map/self_attention/pallas_call | solution.py:238
  229.7 5.7 slice_bitcast_fusion.1
  261.0 13.2 %cross_attention.1 = (bf16[1,2,4,3,32,512]{5,4,3,2,1,0:T(8,128)(2,1)S(1)}, f32[12,1,1,512]{3,2,1,0:T(1,128)S(1)}) custom-call(s32[13]{0:T(128)S(1)} %pad_add_fusion.refs_0_, bf16[1,2,4,3,32,512]{5,4,3,2,1,0:T(8,128)(2,1)S(1)} %bitcast.350, bf16[8,2,4,2,3,32,128]{6,5,4,3,2,1,0:T(8,128)(2,1)S(1)} %copy-done.3), custom_call_target="tpu_custom_call" | custom-call | flops 3221225472 | bytes 6291456 | tf_op jit(solution)/shard_map/cross_attention/pallas_call | solution.py:238
  278.3 7.1 fusion.71
  285.4 5.8 copy.319
  291.2 8.8 %reshape.331 = bf16[768,3072]{1,0:T(8,128)(2,1)} reshape(bf16[4,192,2,4,384]{4,3,2,1,0:T(4,128)(2,1)} %bitcast.353) | data formatting | bytes 9437184 | tf_op jit(solution)/shard_map/reshape | solution.py:381
  300.0 8.2 copy.318
  308.2 8.9 %reshape.332 = bf16[768,3072]{1,0:T(8,128)(2,1)} reshape(bf16[4,192,2,4,384]{4,3,2,1,0:T(4,128)(2,1)} %bitcast.354) | data formatting | bytes 9437184 | tf_op jit(solution)/shard_map/reshape | solution.py:381
  317.1 6.2 multiply_convert_fusion.1
  328.7 4.5 multiply_convert_fusion
  339.8 21.6 %cross_attention_back.1 = (bf16[1,2,4,3,32,512]{5,4,3,2,1,0:T(8,128)(2,1)S(1)}, bf16[8,2,4,2,3,32,128]{6,5,4,3,2,1,0:T(8,128)(2,1)}) custom-call(s32[13]{0:T(128)S(1)} %pad_add_fusion.refs_0_, bf16[1,2,4,3,32,512]{5,4,3,2,1,0:T(8,128)(2,1)S(1)} %bitcast.351, bf16[8,2,4,2,3,32,128]{6,5,4,3,2,1,0:T(8,128)(2,1)} %all-gather.12.cloned.1.call-done.refs_2_, ...), custom_call_target="tpu_custom_call" | custom-call | flops 8053063680 | bytes 6291456 | tf_op jit(solution)/shard_map/cross_attention_back/pallas_call | solution.py:259
  365.4 4.6 reshape.351
  375.1 4.6 reshape.352
  391.4 16.7 %reduce-scatter.14.cloned.1.call-done = bf16[1,2,4,2,3,32,128]{6,5,4,3,2,1,0:T(8,128)(2,1)} async-done(((bf16[8,2,4,2,3,32,128]{6,5,4,3,2,1,0:T(8,128)(2,1)}), bf16[1,2,4,2,3,32,128]{6,5,4,3,2,1,0:T(8,128)(2,1)}) %reduce-scatter.14.cloned.1.call-update) | async-done | bytes 393232 | tf_op jit(solution)/shard_map/reduce_scatter | solution.py:472
  417.2 5.4 pad_maximum_fusion.1
  424.0 6.4 convolution_convert_fusion.1
  430.5 9.9 %reshape.357 = bf16[4,192,2,4,384]{4,3,2,1,0:T(4,128)(2,1)} reshape(bf16[768,3072]{1,0:T(8,128)(2,1)} %convolution_convert_fusion.1) | data formatting | bytes 9437184 | tf_op jit(solution)/shard_map/reshape | solution.py:511
  440.4 5.6 copy.321
  446.0 4.4 convolution_convert_fusion
  450.4 9.6 %reshape.358 = bf16[4,192,2,4,384]{4,3,2,1,0:T(4,128)(2,1)} reshape(bf16[768,3072]{1,0:T(8,128)(2,1)} %convolution_convert_fusion) | data formatting | bytes 9437184 | tf_op jit(solution)/shard_map/reshape | solution.py:511
  460.1 5.3 copy.320
  465.4 8.5 %pad_maximum_fusion = bf16[2,4,4,2,192,384]{5,4,3,2,1,0:T(8,128)(2,1)} fusion(bf16[2,4,4,1,192,384]{5,4,3,2,1,0:T(8,128)(2,1)} %bitcast.356, bf16[2,4,4,1,192,384]{5,4,3,2,1,0:T(8,128)(2,1)} %bitcast.355), kind=kLoop, calls=%fused_computation.4 | loop fusion | flops 4718592 | bytes 18874368 | tf_op jit(solution)/shard_map/stack | solution.py:519
  477.1 13.9 %all_to_all.165.refs_4_ = bf16[4,2,3,32,512]{4,3,2,1,0:T(8,128)(2,1)S(1)} all-to-all(bf16[4,2,3,32,512]{4,3,2,1,0:T(8,128)(2,1)S(1)} %bitcast.398), channel_id=1, replica_groups=mesh['dp'=2,'row'=4,'col'=4] {'row'}, dimensions={0} | all-to-all | bytes 1572864 | tf_op jit(solution)/shard_map/all_to_all | solution.py:478
  491.0 49.5 %self_attention_back.1 = (bf16[4,2,3,32,512]{4,3,2,1,0:T(8,128)(2,1)S(1)}, f32[4,2,2,3,32,512]{5,4,3,2,1,0:T(8,128)}, bf16[4,2,2,3,32,512]{5,4,3,2,1,0:T(8,128)(2,1)S(1)}) custom-call(s32[13]{0:T(128)S(1)} %pad_add_fusion.refs_0_, bf16[4,2,3,32,512]{4,3,2,1,0:T(8,128)(2,1)S(1)} %fusion.55.refs_1_, bf16[4,2,2,3,32,512]{5,4,3,2,1,0:T(8,128)(2,1)} %copy-done.2, ...), custom_call_target="tpu_custom_call" | custom-call | flops 32212254720 | bytes 6291456 | tf_op jit(solution)/shard_map/self_attention_back/pallas_call | solution.py:259
  564.4 5.4 reduce.6
  571.2 7.7 all-to-all-start.5
  579.5 19.8 %all-to-all-done.5 = bf16[4,2,49152]{2,1,0:T(2,128)(2,1)S(1)} async-done(((bf16[4,2,49152]{2,1,0:T(2,128)(2,1)}), bf16[4,2,49152]{2,1,0:T(2,128)(2,1)S(1)}, u32[]{:S(2)}, u32[]{:S(2)}) %all-to-all-start.5) | async-done | bytes 786464 | tf_op jit(solution)/shard_map/all_to_all | solution.py:345
  604.6 4.5 all-to-all-start.10
  609.2 4.8 reduce-scatter.28.cloned.1.call-done
  614.2 58.1 %psum.7 = f32[3,768]{1,0:T(4,128)S(1)} all-reduce(f32[3,768]{1,0:T(4,128)S(1)} %pad_maximum_fusion.5), channel_id=1, replica_groups=mesh['dp'=2,'row'=4,'col'=4] {'dp','row','col'}, use_global_device_ids=true, to_apply=%region_24.25 | all-reduce | flops 2304 | bytes 18432 | tf_op jit(solution)/shard_map/psum | solution.py:529
  674.6 7.9 rev.20
  688.3 5.0 all-to-all-start.13
  693.3 53.8 %all-gather.18.cloned.1.call-done = bf16[32,192,288]{2,1,0:T(8,128)(2,1)} async-done(((bf16[8,192,288]{2,1,0:T(8,128)(2,1)}), bf16[32,192,288]{2,1,0:T(8,128)(2,1)}) %all-gather.18.cloned.1.call-update) | async-done | bytes 3538960 | tf_op jit(solution)/shard_map/all_gather | solution.py:369
  747.1 9.3 %fusion.44 = bf16[1,768,512]{1,2,0:T(8,128)(2,1)} fusion(bf16[4,2,768,288]{3,2,1,0:T(8,128)(2,1)} %bitcast.418, bf16[4,2,288,512]{3,2,1,0:T(8,128)(2,1)} %all-to-all-done.10, f32[512,768]{1,0:T(8,128)} %get-tuple-element.98, f32[512,768]{1,0:T(8,128)} %get-tuple-element.97, f32[768,512]{0,1:T(8,128)S(1)} %copy-done.7, f32[512,768]{1,0:T(8,128)} %get-tuple-element.93, ...), kind=kOutput, calls=%fused_computation.103 | convolution fusion | flops 1823735808 | bytes 17728512 | tf_op jit(solution)/shard_map/rdft,rdwf->tw/dot_general | solution.py:297
  759.9 5.4 reduce.7
  771.0 4.6 all-to-all-start.11
  779.9 18.1 %all_gather.47 = bf16[2,192,1024]{2,1,0:T(8,128)(2,1)S(1)} all-gather(bf16[2,192,256]{2,1,0:T(8,128)(2,1)S(1)} %copy_bitcast_fusion.9), channel_id=1, replica_groups=mesh['dp'=2,'row'=4,'col'=4] {'row'}, dimensions={2}, use_global_device_ids=true | all-gather | bytes 983040 | tf_op jit(solution)/shard_map/all_gather | solution.py:485
  798.0 9.4 %fusion = f32[2,192,4096]{2,1,0:T(8,128)} fusion(bf16[2,192,1024]{2,1,0:T(8,128)(2,1)S(1)} %all_gather.47, s32[2,1024]{1,0:T(2,128)S(1)} %copy-done.54), kind=kOutput, calls=%fused_computation.1 | convolution fusion | flops 3229614080 | bytes 7086080 | tf_op jit(solution)/shard_map/swp,spn->swn/dot_general | solution.py:297
  828.3 10.2 %reduce-scatter.26.cloned.1.call-done = bf16[1,2,192,384]{3,2,1,0:T(8,128)(2,1)} async-done(((bf16[4,2,192,384]{3,2,1,0:T(8,128)(2,1)}), bf16[1,2,192,384]{3,2,1,0:T(8,128)(2,1)}) %reduce-scatter.26.cloned.1.call-update) | async-done | bytes 294928 | tf_op jit(solution)/shard_map/reduce_scatter | solution.py:517
  (296 shorter events, 208.9 us)
Async XLA Ops:
  7.2 55.5 %copy-start = (bf16[2,192,4096]{2,1,0:T(8,128)(2,1)S(1)}, bf16[2,192,4096]{2,1,0:T(8,128)(2,1)}, u32[]{:S(2)}) copy-start(bf16[2,192,4096]{2,1,0:T(8,128)(2,1)} %param.15) | copy-start | bytes 9437188
  7.2 83.6 %all-gather.14.cloned.1.call-start = ((), (), s32[]{:S(2)}) async-start(), calls=%async_computation.33 | async-start | bytes 6488064 | tf_op jit(solution)/shard_map/all_gather | solution.py:365
  9.2 126.5 %all-gather.10.cloned.1.call-start = ((), (), s32[]{:S(2)}) async-start(), calls=%async_computation.24 | async-start | bytes 3932160 | tf_op jit(solution)/shard_map/all_gather | solution.py:355
  69.1 33.9 %all-to-all-start.4 = ((bf16[4,192,128]{2,1,0:T(8,128)(2,1)}), bf16[4,192,128]{2,1,0:T(8,128)(2,1)S(1)}, u32[]{:S(2)}, u32[]{:S(2)}) async-start(bf16[4,192,128]{2,1,0:T(8,128)(2,1)} %bitcast.42), calls=%async_computation.4 | async-start | bytes 393216 | tf_op jit(solution)/shard_map/all_to_all | solution.py:340
  72.5 186.6 %all-gather.12.cloned.1.call-start = ((), (), s32[]{:S(2)}) async-start(), calls=%async_computation.25 | async-start | bytes 3538944 | tf_op jit(solution)/shard_map/all_gather | solution.py:430
  104.6 173.7 %all-gather.16.cloned.1.call-start = ((), (), s32[]{:S(2)}) async-start(), calls=%async_computation.34 | async-start | bytes 9732096 | tf_op jit(solution)/shard_map/all_gather | solution.py:367
  142.6 51.7 %copy-start.2 = (bf16[4,2,2,3,32,512]{5,4,3,2,1,0:T(8,128)(2,1)}, bf16[4,2,2,3,32,512]{5,4,3,2,1,0:T(8,128)(2,1)S(1)}, u32[]{:S(2)}) copy-start(bf16[4,2,2,3,32,512]{5,4,3,2,1,0:T(8,128)(2,1)S(1)} %slice.107.refs_2_) | copy-start | bytes 4718596
  142.6 51.7 %collective-permute-start = (bf16[4,2,2,3,32,512]{5,4,3,2,1,0:T(8,128)(2,1)S(1)}, bf16[4,2,2,3,32,512]{5,4,3,2,1,0:T(8,128)(2,1)}, u32[]{:S(2)}, u32[]{:S(2)}) collective-permute-start(bf16[4,2,2,3,32,512]{5,4,3,2,1,0:T(8,128)(2,1)S(1)} %slice.107.refs_2_), channel_id=1, source_target_pairs={{0,16},{16,0},{1,17},{17,1},{2,18},{18,2},{3,19},{19,3},{4,20},{20... | collective-permute-start | bytes 4718600 | tf_op jit(solution)/shard_map/ppermute | solution.py:398
  148.9 6.7 copy-start.56
  149.9 12.6 %copy-start.53 = (bf16[3,192]{1,0:T(4,128)(2,1)S(1)}, bf16[3,192]{1,0:T(4,128)(2,1)}, u32[]{:S(2)}) copy-start(bf16[3,192]{1,0:T(4,128)(2,1)} %param.24) | copy-start | bytes 3460
  149.9 38.3 %copy-start.16 = (bf16[4,192,512]{2,1,0:T(8,128)(2,1)S(1)}, bf16[4,192,512]{2,1,0:T(8,128)(2,1)}, u32[]{:S(2)}) copy-start(bf16[4,192,512]{2,1,0:T(8,128)(2,1)} %all_to_all.163) | copy-start | bytes 2359300
  149.9 6.5 all-to-all-start.7
  156.4 66.3 %all-to-all-start.8 = ((bf16[4,192,512]{2,1,0:T(8,128)(2,1)}), bf16[4,192,512]{2,1,0:T(8,128)(2,1)}, u32[]{:S(2)}, u32[]{:S(2)}) async-start(bf16[4,192,512]{2,1,0:T(8,128)(2,1)} %bitcast.65), calls=%async_computation.8 | async-start | bytes 1572864 | tf_op jit(solution)/shard_map/all_to_all | solution.py:340
  188.2 368.2 %copy-start.42 = (f32[768]{0:T(1024)}, f32[768]{0:T(1024)S(1)}, u32[]{:S(2)}) copy-start(f32[768]{0:T(1024)S(1)} %get-tuple-element.66) | copy-start | bytes 9220
  222.7 29.7 %all-to-all-start.2 = ((bf16[4,2,3,32,512]{4,3,2,1,0:T(8,128)(2,1)}), bf16[4,2,3,32,512]{4,3,2,1,0:T(8,128)(2,1)S(1)}, u32[]{:S(2)}, u32[]{:S(2)}) async-start(bf16[4,2,3,32,512]{4,3,2,1,0:T(8,128)(2,1)} %get-tuple-element.20.refs_5_), calls=%async_computation.2 | async-start | bytes 1572864 | tf_op jit(solution)/shard_map/all_to_all | solution.py:410
  226.2 181.9 %reduce-scatter.14.cloned.1.call-start = ((), (), s32[]{:S(2)}) async-start(), calls=%async_computation.26 | async-start | bytes 3538944 | tf_op jit(solution)/shard_map/reduce_scatter | solution.py:472
  261.0 13.2 %copy-start.28 = (bf16[768,768]{1,0:T(8,128)(2,1)S(1)}, bf16[768,768]{1,0:T(8,128)(2,1)}, u32[]{:S(2)}) copy-start(bf16[768,768]{1,0:T(8,128)(2,1)} %reshape.329) | copy-start | bytes 3538948
  278.3 278.1 %copy-start.45 = (f32[512]{0:T(512)}, f32[512]{0:T(512)S(1)}, u32[]{:S(2)}) copy-start(f32[512]{0:T(512)S(1)} %get-tuple-element.88) | copy-start | bytes 6148
  278.3 278.1 %copy-start.46 = (f32[512]{0:T(512)}, f32[512]{0:T(512)S(1)}, u32[]{:S(2)}) copy-start(f32[512]{0:T(512)S(1)} %get-tuple-element.89) | copy-start | bytes 6148
  317.1 6.2 copy-start.21
  317.1 6.2 copy-start.23
  327.3 229.2 %copy-start.43 = (f32[512]{0:T(512)}, f32[512]{0:T(512)S(1)}, u32[]{:S(2)}) copy-start(f32[512]{0:T(512)S(1)} %get-tuple-element.86) | copy-start | bytes 6148
  327.3 229.2 %copy-start.44 = (f32[512]{0:T(512)}, f32[512]{0:T(512)S(1)}, u32[]{:S(2)}) copy-start(f32[512]{0:T(512)S(1)} %get-tuple-element.87) | copy-start | bytes 6148
  361.4 193.0 %reduce-scatter.20.cloned.1.call-start = ((), (), s32[]{:S(2)}) async-start(), calls=%async_computation.29 | async-start | bytes 9437184 | tf_op jit(solution)/shard_map/reduce_scatter | solution.py:515
  422.6 132.5 %reduce-scatter.24.cloned.1.call-start = ((), (), s32[]{:S(2)}) async-start(), calls=%async_computation.31 | async-start | bytes 14155776 | tf_op jit(solution)/shard_map/reduce_scatter | solution.py:515
  440.4 5.6 copy-start.35
  440.4 5.6 copy-start.59
  473.9 105.0 %reduce-scatter.16.cloned.1.call-start = ((), (), s32[]{:S(2)}) async-start(), calls=%async_computation.27 | async-start | bytes 1769472 | tf_op jit(solution)/shard_map/reduce_scatter | solution.py:527
  540.5 3.4 collective-permute-start.1
  554.3 59.7 %reduce-scatter.28.cloned.1.call-start = ((), (), s32[]{:S(2)}) async-start(), calls=%async_computation.36 | async-start | bytes 3932160
  555.1 133.2 %reduce-scatter.30.cloned.1.call-start = ((), (), s32[]{:S(2)}) async-start(), calls=%async_computation.37 | async-start | bytes 5898240
  555.7 191.4 %all-gather.18.cloned.1.call-start = ((), (), s32[]{:S(2)}) async-start(), calls=%async_computation.35 | async-start | bytes 5898240 | tf_op jit(solution)/shard_map/all_gather | solution.py:369
  571.2 28.1 %all-to-all-start.5 = ((bf16[4,2,49152]{2,1,0:T(2,128)(2,1)}), bf16[4,2,49152]{2,1,0:T(2,128)(2,1)S(1)}, u32[]{:S(2)}, u32[]{:S(2)}) async-start(bf16[4,2,49152]{2,1,0:T(2,128)(2,1)} %reshape.389), calls=%async_computation.5 | async-start | bytes 1572864 | tf_op jit(solution)/shard_map/all_to_all | solution.py:345
  578.9 199.2 %reduce-scatter.18.cloned.1.call-start = ((), (), s32[]{:S(2)}) async-start(), calls=%async_computation.28 | async-start | bytes 737280 | tf_op jit(solution)/shard_map/reduce_scatter | solution.py:528
  604.6 68.3 %copy-start.14 = (bf16[4,192,1,1,512]{4,1,3,2,0:T(8,128)(2,1)}, bf16[4,192,1,1,512]{4,1,3,2,0:T(8,128)(2,1)S(1)}, u32[]{:S(2)}) copy-start(bf16[4,192,1,1,512]{4,1,3,2,0:T(8,128)(2,1)S(1)} %all_to_all.166) | copy-start | bytes 2359300
  604.6 83.7 %all-to-all-start.10 = ((bf16[4,2,288,512]{3,2,1,0:T(8,128)(2,1)}), bf16[4,2,288,512]{3,2,1,0:T(8,128)(2,1)}, u32[]{:S(2)}, u32[]{:S(2)}) async-start(bf16[4,2,288,512]{3,2,1,0:T(8,128)(2,1)} %bitcast.76), calls=%async_computation.10 | async-start | bytes 4718592 | tf_op jit(solution)/shard_map/all_to_all | solution.py:505
  609.2 213.3 %reduce-scatter.22.cloned.1.call-start = ((), (), s32[]{:S(2)}) async-start(), calls=%async_computation.30 | async-start | bytes 983040 | tf_op jit(solution)/shard_map/reduce_scatter | solution.py:517
  614.0 224.5 %reduce-scatter.26.cloned.1.call-start = ((), (), s32[]{:S(2)}) async-start(), calls=%async_computation.32 | async-start | bytes 1474560 | tf_op jit(solution)/shard_map/reduce_scatter | solution.py:517
  672.9 9.6 %copy-start.5 = (bf16[768,1536]{1,0:T(8,128)(2,1)S(1)}, bf16[768,1536]{1,0:T(8,128)(2,1)}, u32[]{:S(2)}) copy-start(bf16[768,1536]{1,0:T(8,128)(2,1)} %copy-done.4) | copy-start | bytes 7077892
  672.9 9.6 %copy-start.38 = (bf16[1,2,4,2,3,32,128]{6,5,4,3,2,1,0:T(8,128)(2,1)S(1)}, bf16[1,2,4,2,3,32,128]{6,5,4,3,2,1,0:T(8,128)(2,1)}, u32[]{:S(2)}) copy-start(bf16[1,2,4,2,3,32,128]{6,5,4,3,2,1,0:T(8,128)(2,1)} %reduce-scatter.14.cloned.1.call-done) | copy-start | bytes 1179652
  683.3 63.8 %copy-start.7 = (f32[768,512]{0,1:T(8,128)S(1)}, f32[768,512]{0,1:T(8,128)}, u32[]{:S(2)}) copy-start(f32[768,512]{0,1:T(8,128)} %copy.251) | copy-start | bytes 4718596
  683.4 63.7 %copy-start.10 = (f32[768,512]{0,1:T(8,128)S(1)}, f32[768,512]{0,1:T(8,128)}, u32[]{:S(2)}) copy-start(f32[768,512]{0,1:T(8,128)} %copy.236) | copy-start | bytes 4718596
  688.3 78.4 %all-to-all-start.13 = ((bf16[4,2,12288]{2,1,0:T(2,128)(2,1)}), bf16[4,2,12288]{2,1,0:T(2,128)(2,1)S(1)}, u32[]{:S(2)}, u32[]{:S(2)}) async-start(bf16[4,2,12288]{2,1,0:T(2,128)(2,1)} %reshape.393), calls=%async_computation.14 | async-start | bytes 393216 | tf_op jit(solution)/shard_map/all_to_all | solution.py:345
  766.7 8.9 %copy-start.15 = (bf16[4,192,1,1,512]{4,1,3,2,0:T(8,128)(2,1)S(1)}, bf16[4,192,1,1,512]{4,1,3,2,0:T(8,128)(2,1)}, u32[]{:S(2)}) copy-start(bf16[4,192,1,1,512]{4,1,3,2,0:T(8,128)(2,1)} %copy-done.14) | copy-start | bytes 2359300
  766.7 8.9 %copy-start.30 = (bf16[2,192,2,512]{3,2,1,0:T(2,128)(2,1)S(1)}, bf16[2,192,2,512]{3,2,1,0:T(2,128)(2,1)}, u32[]{:S(2)}) copy-start(bf16[2,192,2,512]{3,2,1,0:T(2,128)(2,1)} %rev.20) | copy-start | bytes 2359300
  771.0 37.7 %all-to-all-start.11 = ((bf16[4,2,49152]{2,1,0:T(2,128)(2,1)}), bf16[4,2,49152]{2,1,0:T(2,128)(2,1)S(1)}, u32[]{:S(2)}, u32[]{:S(2)}) async-start(bf16[4,2,49152]{2,1,0:T(2,128)(2,1)} %reshape.391), calls=%async_computation.11 | async-start | bytes 1572864 | tf_op jit(solution)/shard_map/all_to_all | solution.py:345
  776.6 21.4 %copy-start.54 = (s32[2,1024]{1,0:T(2,128)S(1)}, s32[2,1024]{1,0:T(2,128)}, u32[]{:S(2)}) copy-start(s32[2,1024]{1,0:T(2,128)} %param.16) | copy-start | bytes 24580
  823.5 17.0 %copy-start.1 = (bf16[2,192,4096]{2,1,0:T(8,128)(2,1)S(1)}, bf16[2,192,4096]{2,1,0:T(8,128)(2,1)}, u32[]{:S(2)}) copy-start(bf16[2,192,4096]{2,1,0:T(8,128)(2,1)} %param.15) | copy-start | bytes 9437188
  (39 other events, 102.0 us)
Sparse Core Ops, SparseCore 0:
  11.5 79.2 all-gather.13
  92.6 42.6 all-gather.9
  137.2 32.1 all-gather.11
  172.6 90.2 all-gather.15
  361.5 46.5 reduce-scatter.13
  422.8 14.0 reduce-scatter.19
  474.0 17.5 reduce-scatter.23
  554.5 11.0 reduce-scatter.15
  568.5 45.4 reduce-scatter.27
  616.9 71.3 reduce-scatter.29
  690.1 56.9 all-gather.17
  749.2 22.1 reduce-scatter.17
  773.7 32.1 reduce-scatter.21
  808.1 30.4 reduce-scatter.25

commit v2 on v1

--- a/solution.py
+++ b/solution.py
@@ -279,18 +279,458 @@
     )(meta, query, *kv_list, grad, out, lse)
 
 
-def norm_stats(resid, width):
-    mean = jnp.sum(resid, -1, keepdims=True) / width
-    square = jnp.sum(resid * resid, -1, keepdims=True) / width
+def kernel_params():
+    return pltpu.CompilerParams(vmem_limit_bytes=60 << 20)
+
+
+def whole(value):
+    return pl.BlockSpec(value.shape, lambda *i: (0,) * value.ndim)
+
+
+def by_columns(count, body):
+    step = min(128, count)
+
+    def one(j, carry):
+        body(pl.ds(pl.multiple_of(j * step, step), step))
+        return carry
+
+    lax.fori_loop(0, count // step, one, 0)
+
+
+def norm_stats(resid):
+    width = resid.shape[0]
+    mean = jnp.sum(resid, 0, keepdims=True) / width
+    square = jnp.sum(resid * resid, 0, keepdims=True) / width
     inv_std = lax.rsqrt(square - mean * mean + NORM_EPS)
     return (resid - mean) * inv_std, inv_std
 
 
-def norm_back(grad, gain, normed, inv_std, width):
+def norm_back(grad, gain, normed, inv_std):
+    width = grad.shape[0]
     scaled = grad * gain
-    total = jnp.sum(scaled, -1, keepdims=True) / width
-    cross = jnp.sum(scaled * normed, -1, keepdims=True) / width
-    return inv_std * (scaled - total - normed * cross), jnp.sum(grad * normed, axis=0)
+    total = jnp.sum(scaled, 0, keepdims=True) / width
+    cross = jnp.sum(scaled * normed, 0, keepdims=True) / width
+    return inv_std * (scaled - total - normed * cross)
+
+
+def project_kernel(near_ref, x_ref, q_ref, kv_ref, near_t):
+    feat = q_ref.shape[2]
+
+    @pl.when(pl.program_id(0) == 0)
+    def _():
+        for d in range(near_ref.shape[0]):
+            near_t[d] = near_ref[d].T
+
+    for d in range(near_ref.shape[0]):
+        proj = dot(near_t[d], x_ref[0], 1, 0)
+        q_ref[0, d] = (proj[:feat] * (0.125 * LOG2E)).astype(bf16)
+        kv_ref[0, d, 0] = proj[feat : 2 * feat].astype(bf16)
+        kv_ref[0, d, 1] = proj[2 * feat :].astype(bf16)
+
+
+def project(near, x_rows):
+    dp, width, cols = near.shape
+    rows, _, tokens = x_rows.shape
+    feat = cols // 3
+    return pl.pallas_call(
+        project_kernel,
+        grid=(rows,),
+        in_specs=[whole(near), pl.BlockSpec((1, width, tokens), lambda r: (r, 0, 0))],
+        out_specs=[
+            pl.BlockSpec((1, dp, feat, tokens), lambda r: (r, 0, 0, 0)),
+            pl.BlockSpec((1, dp, 2, feat, tokens), lambda r: (r, 0, 0, 0, 0)),
+        ],
+        out_shape=[
+            jax.ShapeDtypeStruct((rows, dp, feat, tokens), bf16),
+            jax.ShapeDtypeStruct((rows, dp, 2, feat, tokens), bf16),
+        ],
+        scratch_shapes=[pltpu.VMEM((dp, cols, width), bf16)],
+        compiler_params=kernel_params(),
+        name="project",
+    )(near, x_rows)
+
+
+def project_back_kernel(*refs, sources):
+    near_ref, x_ref, dq_ref = refs[:3]
+    dkv_refs = refs[3 : 3 + sources]
+    dx_ref, g_ref, acc = refs[3 + sources :]
+    r = pl.program_id(0)
+
+    @pl.when(r == 0)
+    def _():
+        acc[...] = jnp.zeros_like(acc)
+
+    total = None
+    for d in range(near_ref.shape[0]):
+        parts = [dq_ref[0, d]]
+        for kind in range(2):
+            value = sum(ref[0, d, kind].astype(f32) for ref in dkv_refs)
+            parts.append(value.astype(bf16))
+        grad = jnp.concatenate(parts, axis=0)
+        acc[d] += dot(x_ref[0], grad, 1, 1)
+        part = dot(near_ref[d], grad, 1, 0)
+        total = part if total is None else total + part
+    dx_ref[0] = total.astype(bf16)
+
+    @pl.when(r == pl.num_programs(0) - 1)
+    def _():
+        g_ref[...] = acc[...].astype(bf16)
+
+
+def project_back(near, x_rows, d_query, d_kv):
+    dp, width, cols = near.shape
+    rows, _, tokens = x_rows.shape
+    feat = cols // 3
+    kv_spec = pl.BlockSpec((1, dp, 2, feat, tokens), lambda r: (r, 0, 0, 0, 0))
+    return pl.pallas_call(
+        functools.partial(project_back_kernel, sources=len(d_kv)),
+        grid=(rows,),
+        in_specs=[
+            whole(near),
+            pl.BlockSpec((1, width, tokens), lambda r: (r, 0, 0)),
+            pl.BlockSpec((1, dp, feat, tokens), lambda r: (r, 0, 0, 0)),
+        ]
+        + [kv_spec] * len(d_kv),
+        out_specs=[pl.BlockSpec((1, width, tokens), lambda r: (r, 0, 0)), whole(near)],
+        out_shape=[
+            jax.ShapeDtypeStruct(x_rows.shape, bf16),
+            jax.ShapeDtypeStruct(near.shape, bf16),
+        ],
+        scratch_shapes=[pltpu.VMEM(near.shape, f32)],
+        compiler_params=kernel_params(),
+        name="project_back",
+    )(near, x_rows, d_query, *d_kv)
+
+
+def cross_kv_kernel(w_ref, chosen_ref, o_ref):
+    feat2 = o_ref.shape[2]
+    weight = w_ref[0][:, :feat2].T
+    for n in range(chosen_ref.shape[0]):
+        o_ref[n, 0] = dot(weight, chosen_ref[n], 1, 0).astype(bf16)
+
+
+def cross_kv(small, chosen, feat):
+    groups, width, cols = small.shape
+    count, _, tokens = chosen.shape
+    return pl.pallas_call(
+        cross_kv_kernel,
+        grid=(groups,),
+        in_specs=[pl.BlockSpec((1, width, 2 * 128), lambda g: (g, 0, 0)), whole(chosen)],
+        out_specs=pl.BlockSpec((count, 1, 2 * feat, tokens), lambda g: (0, g, 0, 0)),
+        out_shape=jax.ShapeDtypeStruct((count, groups, 2 * feat, tokens), bf16),
+        compiler_params=kernel_params(),
+        name="cross_kv",
+    )(small, chosen)
+
+
+def attn_place(g, rows):
+    return g % rows, g // rows
+
+
+def after_self_kernel(x_ref, attn_ref, w_ref, gain_ref, normed_ref, inv_ref, low_ref, cq_ref, acc):
+    groups, feat, tokens = cq_ref.shape
+    rows = attn_ref.shape[0]
+    total = x_ref[...].astype(f32)
+    for g in range(groups):
+        r, d = attn_place(g, rows)
+        total = total + dot(w_ref[g, :, 2 * feat : 3 * feat], attn_ref[r, d], 1, 0)
+    acc[...] = total
+
+    def body(at):
+        normed, inv_std = norm_stats(acc[:, at])
+        normed_ref[:, at] = normed
+        inv_ref[:, at] = inv_std
+        low_ref[:, at] = (normed * gain_ref[:, 0:1]).astype(bf16)
+
+    by_columns(tokens, body)
+    low = low_ref[...]
+    for g in range(groups):
+        query = dot(w_ref[g, :, 3 * feat : 4 * feat], low, 0, 0)
+        cq_ref[g] = (query * (0.125 * LOG2E)).astype(bf16)
+
+
+def after_self(x_own, attn, small, gains, feat):
+    width, tokens = x_own.shape
+    groups = small.shape[0]
+    args = (x_own, attn, small, gains)
+    outs = [
+        jax.ShapeDtypeStruct((width, tokens), f32),
+        jax.ShapeDtypeStruct((1, tokens), f32),
+        jax.ShapeDtypeStruct((width, tokens), bf16),
+        jax.ShapeDtypeStruct((groups, feat, tokens), bf16),
+    ]
+    return pl.pallas_call(
+        after_self_kernel,
+        grid=(1,),
+        in_specs=[whole(a) for a in args],
+        out_specs=[whole(o) for o in outs],
+        out_shape=outs,
+        scratch_shapes=[pltpu.VMEM((width, tokens), f32)],
+        compiler_params=kernel_params(),
+        name="after_self",
+    )(*args)
+
+
+def middle_kernel(
+    normed_one_ref, catt_ref, wc_ref, up_ref, down_ref, cot_ref, gain_ref,
+    out_ref, dcatt_ref, dy_ref, dcross_ref, gup_ref, gdown_ref, dg_two_ref, dg_three_ref,
+    acc, normed_two, inv_two, act, slope, h_fm, h_tm, d_fm, d_tm,
+):
+    i = pl.program_id(0)
+    groups, feat, tokens = catt_ref.shape
+    units = up_ref.shape[2]
+    step = min(256, tokens)
+
+    @pl.when(i == 0)
+    def _():
+        total = normed_one_ref[...] * gain_ref[:, 0:1]
+        for g in range(groups):
+            total = total + dot(wc_ref[g, :, :feat], catt_ref[g], 1, 0)
+        acc[...] = total
+
+        def body(at):
+            normed, inv_std = norm_stats(acc[:, at])
+            normed_two[:, at] = normed
+            inv_two[:, at] = inv_std
+            value = normed * gain_ref[:, 1:2]
+            acc[:, at] = value
+            h_fm[:, at] = value.astype(bf16)
+
+        by_columns(tokens, body)
+        h_tm[...] = h_fm[...].T
+
+    @pl.when(i < groups)
+    def _():
+        for t in range(0, tokens, step):
+            upper = dot(h_tm[t : t + step, :], up_ref[0], 1, 0)
+            cdf = 0.5 * (1.0 + lax.erf(upper * 0.7071067811865476))
+            density = jnp.exp(-0.5 * upper * upper) * 0.3989422804014327
+            act[i, t : t + step, :] = (upper * cdf).astype(bf16)
+            slope[i, t : t + step, :] = (cdf + upper * density).astype(bf16)
+        acc[...] += dot(down_ref[0], act[i], 1, 1)
+
+    @pl.when(i == groups - 1)
+    def _():
+        dg_three_ref[...] = jnp.zeros_like(dg_three_ref)
+        dg_two_ref[...] = jnp.zeros_like(dg_two_ref)
+
+        def body(at):
+            normed, inv_std = norm_stats(acc[:, at])
+            gain = gain_ref[:, 2:3]
+            out_ref[:, at] = (normed * gain).astype(bf16)
+            grad = cot_ref[:, at].astype(f32)
+            dg_three_ref[...] += grad * normed
+            value = norm_back(grad, gain, normed, inv_std)
+            acc[:, at] = value
+            d_fm[:, at] = value.astype(bf16)
+
+        by_columns(tokens, body)
+        d_tm[...] = d_fm[...].T
+
+    @pl.when(i >= groups)
+    def _():
+        g = i - groups
+        for t in range(0, tokens, step):
+            at = slice(t, t + step)
+            back = dot(d_tm[at, :], down_ref[0], 1, 0) * slope[g, at, :].astype(f32)
+            slope[g, at, :] = back.astype(bf16)
+        gdown_ref[0] = dot(d_fm[...], act[g], 1, 0).astype(bf16)
+        gup_ref[0] = dot(h_fm[...], slope[g], 1, 0).astype(bf16)
+        acc[...] += dot(up_ref[0], slope[g], 1, 1)
+
+    @pl.when(i == 2 * groups - 1)
+    def _():
+        def body(at):
+            grad = acc[:, at]
+            normed = normed_two[:, at]
+            dg_two_ref[...] += grad * normed
+            value = norm_back(grad, gain_ref[:, 1:2], normed, inv_two[:, at])
+            dy_ref[:, at] = value
+            dcross_ref[:, at] = value.astype(bf16)
+
+        by_columns(tokens, body)
+        low = dcross_ref[...]
+        for g in range(groups):
+            dcatt_ref[g] = dot(wc_ref[g, :, :feat], low, 0, 0).astype(bf16)
+
+
+def middle(normed_one, catt, small, up, down, cot, gains):
+    width, tokens = normed_one.shape
+    groups, feat, _ = catt.shape
+    units = up.shape[2]
+    lanes = min(128, tokens)
+
+    def weight():
+        return pl.BlockSpec((1, width, units), lambda i: (i % groups, 0, 0))
+
+    def grad_out():
+        return pl.BlockSpec((1, width, units), lambda i: (jnp.maximum(i - groups, 0), 0, 0))
+
+    outs = [
+        jax.ShapeDtypeStruct((width, tokens), bf16),
+        jax.ShapeDtypeStruct(catt.shape, bf16),
+        jax.ShapeDtypeStruct((width, tokens), f32),
+        jax.ShapeDtypeStruct((width, tokens), bf16),
+        jax.ShapeDtypeStruct(up.shape, bf16),
+        jax.ShapeDtypeStruct(up.shape, bf16),
+        jax.ShapeDtypeStruct((width, lanes), f32),
+        jax.ShapeDtypeStruct((width, lanes), f32),
+    ]
+    specs = [whole(o) for o in outs]
+    specs[4], specs[5] = grad_out(), grad_out()
+    return pl.pallas_call(
+        middle_kernel,
+        grid=(2 * groups,),
+        in_specs=[
+            whole(normed_one),
+            whole(catt),
+            pl.BlockSpec((groups, width, 128), lambda i: (0, 0, 3)),
+            weight(),
+            weight(),
+            whole(cot),
+            whole(gains),
+        ],
+        out_specs=specs,
+        out_shape=outs,
+        scratch_shapes=[
+            pltpu.VMEM((width, tokens), f32),
+            pltpu.VMEM((width, tokens), f32),
+            pltpu.VMEM((1, tokens), f32),
+            pltpu.VMEM((groups, tokens, units), bf16),
+            pltpu.VMEM((groups, tokens, units), bf16),
+            pltpu.VMEM((width, tokens), bf16),
+            pltpu.VMEM((tokens, width), bf16),
+            pltpu.VMEM((width, tokens), bf16),
+            pltpu.VMEM((tokens, width), bf16),
+        ],
+        compiler_params=kernel_params(),
+        cost_estimate=pl.CostEstimate(
+            flops=12 * groups * width * units * tokens, bytes_accessed=4 * up.size * 2, transcendentals=0
+        ),
+        name="middle",
+    )(normed_one, catt, small, up, down, cot, gains)
+
+
+def before_self_kernel(
+    dcq_ref, w_ref, dy_ref, normed_ref, inv_ref, gain_ref,
+    dattn_ref, dlow_ref, dy_one_ref, dg_ref, acc,
+):
+    groups, feat, tokens = dcq_ref.shape
+    rows = dattn_ref.shape[0]
+    total = dy_ref[...]
+    for g in range(groups):
+        total = total + dot(w_ref[g, :, 3 * feat : 4 * feat], dcq_ref[g], 1, 0)
+    acc[...] = total
+    dg_ref[...] = jnp.zeros_like(dg_ref)
+
+    def body(at):
+        grad = acc[:, at]
+        normed = normed_ref[:, at]
+        dg_ref[...] += grad * normed
+        value = norm_back(grad, gain_ref[:, 0:1], normed, inv_ref[:, at])
+        dy_one_ref[:, at] = value
+        dlow_ref[:, at] = value.astype(bf16)
+
+    by_columns(tokens, body)
+    low = dlow_ref[...]
+    for g in range(groups):
+        r, d = attn_place(g, rows)
+        dattn_ref[r, d] = dot(w_ref[g, :, 2 * feat : 3 * feat], low, 0, 0).astype(bf16)
+
+
+def before_self(d_cq, small, dy_two, normed_one, inv_one, gains, attn_shape):
+    width, tokens = dy_two.shape
+    args = (d_cq, small, dy_two, normed_one, inv_one, gains)
+    outs = [
+        jax.ShapeDtypeStruct(attn_shape, bf16),
+        jax.ShapeDtypeStruct((width, tokens), bf16),
+        jax.ShapeDtypeStruct((width, tokens), f32),
+        jax.ShapeDtypeStruct((width, min(128, tokens)), f32),
+    ]
+    return pl.pallas_call(
+        before_self_kernel,
+        grid=(1,),
+        in_specs=[whole(a) for a in args],
+        out_specs=[whole(o) for o in outs],
+        out_shape=outs,
+        scratch_shapes=[pltpu.VMEM((width, tokens), f32)],
+        compiler_params=kernel_params(),
+        name="before_self",
+    )(*args)
+
+
+def small_grads_kernel(
+    w_ref, chosen_ref, dckv_ref, attn_ref, dcq_ref, catt_ref, dlow_ref, h_ref, dcross_ref,
+    dg_one_ref, dg_two_ref, dg_three_ref, rest_ref, dchosen_ref, acc, gain_cols,
+):
+    g = pl.program_id(0)
+    feat2 = dckv_ref.shape[2]
+    feat = feat2 // 2
+    count, width, tokens = chosen_ref.shape
+
+    @pl.when(g == 0)
+    def _():
+        col = lax.broadcasted_iota(jnp.int32, gain_cols.shape, 1)
+        total = jnp.zeros(gain_cols.shape, f32)
+        for k, ref in enumerate((dg_one_ref, dg_two_ref, dg_three_ref)):
+            total = jnp.where(col == k, jnp.sum(ref[...], axis=1, keepdims=True), total)
+        gain_cols[...] = total.astype(bf16)
+        acc[...] = jnp.zeros_like(acc)
+
+    weight = w_ref[0][:, :feat2]
+    total = None
+    for n in range(count):
+        grad = dckv_ref[n, 0]
+        acc[n] += dot(weight, grad, 1, 0)
+        part = dot(chosen_ref[n], grad, 1, 1)
+        total = part if total is None else total + part
+    rest_ref[0, :, :feat2] = total.astype(bf16)
+    pairs = ((dlow_ref, attn_ref[0, 0]), (h_ref, dcq_ref[0]), (dcross_ref, catt_ref[0]))
+    for k, (left, right) in enumerate(pairs):
+        at = feat2 + k * feat
+        rest_ref[0, :, at : at + feat] = dot(left[...], right, 1, 1).astype(bf16)
+    rest_ref[0, :, 5 * feat :] = gain_cols[...]
+
+    @pl.when(g == pl.num_programs(0) - 1)
+    def _():
+        dchosen_ref[...] = acc[...].astype(bf16)
+
+
+def small_grads(small, chosen, d_ckv, attn, d_cq, catt, d_low, h_low, d_cross, dgs):
+    groups, width, cols = small.shape
+    count, _, c_tokens = chosen.shape
+    feat2 = d_ckv.shape[2]
+    feat = feat2 // 2
+    tokens = d_low.shape[1]
+    rows = attn.shape[0]
+    piece = pl.BlockSpec((1, feat, tokens), lambda g: (g, 0, 0))
+    return pl.pallas_call(
+        small_grads_kernel,
+        grid=(groups,),
+        in_specs=[
+            pl.BlockSpec((1, width, 2 * 128), lambda g: (g, 0, 0)),
+            whole(chosen),
+            pl.BlockSpec((count, 1, feat2, c_tokens), lambda g: (0, g, 0, 0)),
+            pl.BlockSpec((1, 1, feat, tokens), lambda g: (g % rows, g // rows, 0, 0)),
+            piece,
+            piece,
+            whole(d_low),
+            whole(h_low),
+            whole(d_cross),
+        ]
+        + [whole(v) for v in dgs],
+        out_specs=[pl.BlockSpec((1, width, cols), lambda g: (g, 0, 0)), whole(chosen)],
+        out_shape=[
+            jax.ShapeDtypeStruct(small.shape, bf16),
+            jax.ShapeDtypeStruct(chosen.shape, bf16),
+        ],
+        scratch_shapes=[
+            pltpu.VMEM(chosen.shape, f32),
+            pltpu.VMEM((width, cols - 5 * feat), bf16),
+        ],
+        compiler_params=kernel_params(),
+        name="small_grads",
+    )(small, chosen, d_ckv, attn, d_cq, catt, d_low, h_low, d_cross, *dgs)
 
 
 def mm(spec, left, right):
@@ -298,19 +738,8 @@
 
 
 def per_device(
-    x_in,
-    prefix,
-    enc_bank,
-    bank_rows,
-    w_qkv,
-    w_out,
-    w_cross_q,
-    w_cross_kv,
-    w_cross_out,
-    w_up,
-    w_down,
-    ln_gains,
-    out_grad,
+    x_in, prefix, enc_bank, bank_rows, w_qkv, w_out, w_cross_q, w_cross_kv, w_cross_out,
+    w_up, w_down, ln_gains, out_grad,
 ):
     dp, rows, cols = lax.axis_size("dp"), lax.axis_size("row"), lax.axis_size("col")
     d_pos, r_pos, c_pos = lax.axis_index("dp"), lax.axis_index("row"), lax.axis_index("col")
@@ -323,79 +752,88 @@
     heads = w_qkv.shape[2]
     feat = heads * HALF
     units = w_up.shape[1]
-    length = row_len * rows
     odd = (r_pos % 2) == 1
     seq_pos = c_pos // sub
     part_pos = d_pos * sub + c_pos % sub
     groups = [[s * sub + k for k in range(sub)] for s in range(seqs)]
     everywhere = ("dp", "row", "col")
+    swap = [(0, 1), (1, 0)]
+    first_core = d_pos == 0
+
+    def flip(value):
+        return jnp.where(odd, value[:, :, ::-1], value)
 
     def to_tokens(value):
         take = value.shape[-1] // parts
-        value = value.reshape(own_seqs, part_width, parts, take)
-        value = jnp.where(odd, value[:, :, ::-1], value)
-        value = value.reshape(own_seqs, part_width, dp, sub, take)
-        value = lax.all_to_all(value, "dp", 2, 0, tiled=True)
-        value = value.reshape(seqs, part_width, sub, take).transpose(0, 2, 1, 3)
-        value = lax.all_to_all(value.reshape(cols, part_width, take), "col", 0, 1, tiled=True)
+        if parts == 2:
+            low, high = value[..., :take], value[..., take:]
+            upper = first_core == odd
+            got = lax.ppermute(jnp.where(upper, low, high), "dp", swap)
+            kept = jnp.where(upper, high, low)
+            value = jnp.concatenate(
+                [jnp.where(first_core, kept, got), jnp.where(first_core, got, kept)], axis=0
+            )
+        else:
+            value = flip(value.reshape(own_seqs, part_width, parts, take))
+            value = value.reshape(own_seqs, part_width, dp, sub, take)
+            value = lax.all_to_all(value, "dp", 2, 0, tiled=True)
+            value = value.reshape(seqs, part_width, sub, take).transpose(0, 2, 1, 3)
+        value = lax.all_to_all(value.reshape(cols, part_width, take), "col", 0, 0, tiled=True)
         return value.reshape(width, take)
 
     def to_home(value):
         take = value.shape[-1]
-        value = lax.all_to_all(value.reshape(1, width, take), "col", 1, 0, tiled=True)
+        value = lax.all_to_all(value.reshape(cols, part_width, take), "col", 0, 0, tiled=True)
+        if parts == 2:
+            early, late = value[:own_seqs], value[own_seqs:]
+            got = lax.ppermute(jnp.where(first_core, late, early), "dp", swap)
+            kept = jnp.where(first_core, early, late)
+            upper = first_core == odd
+            return jnp.concatenate(
+                [jnp.where(upper, got, kept), jnp.where(upper, kept, got)], axis=-1
+            )
         value = value.reshape(seqs, sub, part_width, take).transpose(0, 2, 1, 3)
         value = value.reshape(seqs, part_width, 1, sub, take)
         value = lax.all_to_all(value, "dp", 0, 2, tiled=True)
-        value = value.reshape(own_seqs, part_width, parts, take)
-        value = jnp.where(odd, value[:, :, ::-1], value)
+        value = flip(value.reshape(own_seqs, part_width, parts, take))
         return value.reshape(own_seqs, part_width, parts * take)
 
-    qkv_near = lax.all_gather(w_qkv.reshape(part_width, 3 * feat), ("dp", "col"), axis=0)
+    near = lax.all_gather(w_qkv.reshape(part_width, 3 * feat), ("dp", "col"), axis=0)
+    near = near.reshape(dp, width, 3 * feat)
     x_own = to_tokens(x_in)
     x_rows = lax.all_gather(x_own, "row", axis=0)
+    spare = 512 - 5 * feat
     small = jnp.concatenate(
         [
             w_cross_kv.reshape(part_width, 2 * feat),
             w_out.reshape(feat, part_width).T,
             w_cross_q.reshape(part_width, feat),
             w_cross_out.reshape(feat, part_width).T,
+            jnp.zeros((part_width, spare), bf16),
         ],
         axis=1,
     )
-    small_all = lax.all_gather(small, everywhere, axis=0)
-    small_all = small_all.reshape(dp, rows, cols, part_width, 5 * feat)
-    large_all = lax.all_gather(jnp.stack([w_up, w_down.T]), everywhere, axis=0)
-    large_all = large_all.reshape(dp, rows, cols, 2, part_width, units)
-    qkv_all = lax.all_gather(qkv_near, "row", axis=0)
-
-    def standard(first, count):
-        piece = small_all[..., first * feat : (first + count) * feat]
-        return piece.transpose(2, 3, 0, 1, 4).reshape(width, dp * rows * count * feat)
-
-    wt_ckv = standard(0, 2)
-    wt_out_t = standard(1 + 1, 1).reshape(width, dp, rows, feat).transpose(0, 2, 1, 3)
-    wt_out_t = wt_out_t.reshape(width, width)
-    wt_cq = standard(3, 1)
-    wt_cout_t = standard(4, 1)
-    wt_up, wt_down_t = (
-        large_all[:, :, :, j].transpose(2, 3, 0, 1, 4).reshape(width, dp * rows * units)
-        for j in range(2)
-    )
-
-    gains_all = lax.all_gather(ln_gains.astype(f32), "col", axis=1, tiled=True)
-
-    near = qkv_near.reshape(dp, width, 3 * feat)
-    proj = mm("dwf,rwt->rdft", near, x_rows)
-    proj = proj.reshape(rows, dp, 3, heads, HALF, tokens)
-    query = (proj[:, :, 0] * (0.125 * LOG2E)).astype(bf16)
-    kv_own = proj[:, :, 1:].astype(bf16)
+    blocks = dp * rows
+
+    def gather_all(value):
+        value = lax.all_gather(value, everywhere, axis=0)
+        return value.reshape(blocks, width, value.shape[-1])
+
+    small_all = gather_all(small)
+    up_all = gather_all(w_up)
+    down_all = gather_all(w_down.T)
+    gains = lax.all_gather(ln_gains.astype(f32).T, "col", axis=0, tiled=True)
+
+    query, kv_own = project(near, x_rows)
+    query = query.reshape(rows, dp, heads, HALF, tokens)
+    kv_own = kv_own.reshape(rows, dp, 2, heads, HALF, tokens)
 
     def index_of(row, part):
         return jnp.where(row % 2 == 1, parts - 1 - part, part) + row * parts
 
     row_ids = jnp.arange(rows, dtype=jnp.int32)
     if sub == 1:
-        kv_list = [kv_own, lax.ppermute(kv_own, "dp", [(0, 1), (1, 0)])]
+        kv_list = [kv_own, lax.ppermute(kv_own, "dp", swap)]
         owners = [part_pos, 1 - part_pos]
     else:
         kv_all = lax.all_gather(kv_own, "col", axis=0, axis_index_groups=groups)
@@ -407,13 +845,9 @@
     seq_prefix = lax.all_gather(prefix, "dp", axis=0, tiled=True)[seq_pos]
     meta = jnp.concatenate([seq_prefix[None], q_start] + places).astype(jnp.int32)
     mixed, lse = attend(meta, query, kv_list, True, "self_attention")
-    attn = lax.all_to_all(mixed, "row", 0, 0, tiled=True)
-    attn_flat = attn.reshape(width, tokens)
-
-    resid_one = x_own.T.astype(f32) + mm("ft,wf->tw", attn_flat, wt_out_t)
-    normed_one, inv_one = norm_stats(resid_one, width)
-    h_one = normed_one * gains_all[0]
-    h_one_low = h_one.astype(bf16)
+    attn = lax.all_to_all(mixed, "row", 0, 0, tiled=True).reshape(rows, dp, feat, tokens)
+    normed_one, inv_one, h_low, cross_q = after_self(x_own, attn, small_all, gains, feat)
+    cross_q = cross_q.reshape(1, dp, rows, heads, HALF, tokens)
 
     picked = bank_rows.shape[1] // rows
     row_pick = lax.dynamic_slice_in_dim(bank_rows, r_pos * picked, picked, 1)
@@ -421,67 +855,43 @@
     hot = (bank_ids[None, :, None] == row_pick[:, None, :]).astype(bf16)
     chosen = to_tokens(mm("swn,snp->swp", enc_bank, hot).astype(bf16))
     c_tokens = chosen.shape[1]
-    ckv_own = mm("wf,wt->ft", wt_ckv, chosen).astype(bf16)
-    ckv_own = ckv_own.reshape(dp, rows, 2, heads, HALF, c_tokens)
     if sub > 1:
-        ckv_all = lax.all_gather(ckv_own, "col", axis=0, axis_index_groups=groups)
-    else:
-        ckv_all = ckv_own
-    ckv_all = lax.all_gather(ckv_all, ("dp", "row"), axis=0)
-    ckv_all = ckv_all.reshape((dp * rows * sub,) + ckv_own.shape)
-    cross_q = (mm("wf,tw->ft", wt_cq, h_one_low) * (0.125 * LOG2E)).astype(bf16)
-    cross_q = cross_q.reshape(1, dp, rows, heads, HALF, tokens)
-    catt, lse_cross = attend(meta, cross_q, [ckv_all], False, "cross_attention")
-    catt_flat = catt.reshape(width, tokens)
-    resid_two = h_one + mm("ft,wf->tw", catt_flat, wt_cout_t)
-    normed_two, inv_two = norm_stats(resid_two, width)
-    h_two = normed_two * gains_all[1]
-    h_two_low = h_two.astype(bf16)
-
-    upper = mm("tw,wf->tf", h_two_low, wt_up)
-    cdf = 0.5 * (1.0 + lax.erf(upper * 0.7071067811865476))
-    act = (upper * cdf).astype(bf16)
-    slope = (cdf + upper * (jnp.exp(-0.5 * upper * upper) * 0.3989422804014327)).astype(bf16)
-    resid_three = h_two + mm("tf,wf->tw", act, wt_down_t)
-    normed_three, inv_three = norm_stats(resid_three, width)
-    block_out = to_home((normed_three * gains_all[2]).astype(bf16).T)
-
-    cot = to_tokens(out_grad).T.astype(f32)
-    dy_three, dg_three = norm_back(cot, gains_all[2], normed_three, inv_three, width)
-    d_ffn = dy_three.astype(bf16)
-    g_down_t = mm("tw,tf->wf", d_ffn, act)
-    d_upper = (mm("tw,wf->tf", d_ffn, wt_down_t) * slope.astype(f32)).astype(bf16)
-    g_up = mm("tw,tf->wf", h_two_low, d_upper)
-    dh_two = dy_three + mm("tf,wf->tw", d_upper, wt_up)
-    dy_two, dg_two = norm_back(dh_two, gains_all[1], normed_two, inv_two, width)
-    d_cross = dy_two.astype(bf16)
-    g_cout_t = mm("tw,ft->wf", d_cross, catt_flat)
-    d_catt = mm("wf,tw->ft", wt_cout_t, d_cross).astype(bf16).reshape(catt.shape)
+        chosen = lax.all_gather(chosen, "col", axis=0, axis_index_groups=groups)
+    chosen = lax.all_gather(chosen, ("dp", "row"), axis=0)
+    chosen = chosen.reshape(blocks * sub, width, c_tokens)
+    ckv = cross_kv(small_all, chosen, feat)
+    ckv = ckv.reshape(blocks * sub, dp, rows, 2, heads, HALF, c_tokens)
+    catt, lse_cross = attend(meta, cross_q, [ckv], False, "cross_attention")
+    catt_flat = catt.reshape(blocks, feat, tokens)
+
+    cot = to_tokens(out_grad)
+    block_out, d_catt, dy_two, d_cross, g_up, g_down, dg_two, dg_three = middle(
+        normed_one, catt_flat, small_all, up_all, down_all, cot, gains
+    )
+    block_out = to_home(block_out)
     d_cq, d_ckv = attend_back(
-        meta, cross_q, [ckv_all], d_catt, catt, lse_cross, False, [bf16], "cross_attention_back"
-    )
-    d_cq = d_cq.reshape(width, tokens)
+        meta, cross_q, [ckv], d_catt.reshape(catt.shape), catt, lse_cross, False, [bf16],
+        "cross_attention_back",
+    )
+    d_cq = d_cq.reshape(blocks, feat, tokens)
+    d_ckv = d_ckv.reshape(blocks * sub, blocks, 2 * feat, c_tokens)
+    d_attn, d_low, dy_one, dg_one = before_self(
+        d_cq, small_all, dy_two, normed_one, inv_one, gains, attn.shape
+    )
+    d_mixed = lax.all_to_all(d_attn, "row", 0, 0, tiled=True).reshape(mixed.shape)
+    rest, d_chosen = small_grads(
+        small_all, chosen, d_ckv, attn, d_cq, catt_flat, d_low, h_low, d_cross,
+        (dg_one, dg_two, dg_three),
+    )
+
+    d_chosen = d_chosen.reshape(dp, rows, sub, width, c_tokens)
+    d_chosen = lax.psum_scatter(d_chosen, "dp", scatter_dimension=0, tiled=False)
+    d_chosen = lax.psum_scatter(d_chosen, "row", scatter_dimension=0, tiled=False)
     if sub > 1:
-        d_ckv = d_ckv.reshape(dp, rows, sub, -1)
-        d_ckv = lax.psum_scatter(d_ckv, "dp", scatter_dimension=0, tiled=True)
-        d_ckv = lax.psum_scatter(d_ckv, "row", scatter_dimension=1, tiled=True)
-        d_ckv = lax.psum_scatter(
-            d_ckv, "col", scatter_dimension=2, tiled=True, axis_index_groups=groups
+        d_chosen = lax.psum_scatter(
+            d_chosen, "col", scatter_dimension=0, tiled=True, axis_index_groups=groups
         )
-    else:
-        d_ckv = lax.psum_scatter(d_ckv, ("dp", "row"), scatter_dimension=0, tiled=True)
-    d_ckv = d_ckv.reshape(2 * width, c_tokens)
-    dh_one = dy_two + mm("ft,wf->tw", d_cq, wt_cq)
-    dy_one, dg_one = norm_back(dh_one, gains_all[0], normed_one, inv_one, width)
-    d_attn_out = dy_one.astype(bf16)
-    d_attn = mm("wf,tw->ft", wt_out_t, d_attn_out).astype(bf16).reshape(attn.shape)
-    d_mixed = lax.all_to_all(d_attn, "row", 0, 0, tiled=True)
-    g_cq = mm("tw,ft->wf", h_one_low, d_cq)
-    g_out_t = mm("tw,ft->wf", d_attn_out, attn_flat)
-    g_out_t = g_out_t.reshape(width, rows, dp, feat).transpose(0, 2, 1, 3).reshape(width, width)
-    g_ckv = mm("wt,ft->wf", chosen, d_ckv)
-    d_chosen = mm("wf,ft->wt", wt_ckv, d_ckv).astype(bf16)
-
+    d_chosen = d_chosen.reshape(width, c_tokens)
     d_chosen = lax.all_gather(to_home(d_chosen), "row", axis=2, tiled=True)
     hot_all = (bank_rows[:, :, None] == bank_ids[None, None, :]).astype(bf16)
     bank_grad = mm("swp,spn->swn", d_chosen, hot_all)
@@ -491,43 +901,33 @@
         meta, query, kv_list, d_mixed, mixed, lse, True, types, "self_attention_back"
     )
     if sub == 1:
-        d_kv = d_kv[0] + lax.ppermute(d_kv[1], "dp", [(0, 1), (1, 0)]).astype(f32)
+        d_kv = [d_kv[0], lax.ppermute(d_kv[1], "dp", swap)]
     else:
         d_kv = jnp.stack(d_kv).reshape((dp, sub) + kv_own.shape)
         d_kv = lax.psum_scatter(d_kv, "dp", scatter_dimension=0, tiled=True)
         d_kv = lax.psum_scatter(
             d_kv, "col", scatter_dimension=1, tiled=True, axis_index_groups=groups
         )
-    d_kv = d_kv.reshape(kv_own.shape).astype(bf16)
-    d_proj = jnp.concatenate([d_query[:, :, None], d_kv], axis=2)
-    d_proj = d_proj.reshape(rows, dp, 3 * feat, tokens)
-    g_qkv = mm("rwt,rdft->dwf", x_rows, d_proj)
-    d_mine = lax.all_to_all(d_proj, "row", 0, 0, tiled=True)
-    wt_qkv = qkv_all.reshape(rows, dp, width, 3 * feat)
-    dx = dy_one + mm("rdft,rdwf->tw", d_mine, wt_qkv)
-    x_grad = to_home(dx.astype(bf16).T).astype(f32)
-
-    def shares(value, count):
-        value = value.astype(bf16).reshape(cols, part_width, dp, rows, count)
-        return value.transpose(2, 3, 0, 1, 4)
+        d_kv = [d_kv]
+    kv_shape = (rows, dp, 2, feat, tokens)
+    d_kv = [value.reshape(kv_shape) for value in d_kv]
+    dx_part, g_qkv = project_back(near, x_rows, d_query.reshape(rows, dp, feat, tokens), d_kv)
+    dx_part = lax.all_to_all(dx_part, "row", 0, 0, tiled=True)
+    dx = dy_one + jnp.sum(dx_part.astype(f32), axis=0)
+    x_grad = to_home(dx.astype(bf16)).astype(f32)
 
     def scatter(value):
-        value = lax.psum_scatter(value, "dp", scatter_dimension=0, tiled=False)
-        value = lax.psum_scatter(value, "row", scatter_dimension=0, tiled=False)
-        return lax.psum_scatter(value, "col", scatter_dimension=0, tiled=False)
-
-    big = scatter(jnp.stack([shares(g_up, units), shares(g_down_t, units)], axis=3)).astype(f32)
-    rest = scatter(
-        jnp.concatenate(
-            [shares(g_ckv, 2 * feat), shares(g_out_t, feat), shares(g_cq, feat), shares(g_cout_t, feat)],
-            axis=-1,
-        )
-    ).astype(f32)
-    qkv_grad = g_qkv.astype(bf16).reshape(dp, cols, part_width, 3 * feat)
+        value = value.reshape(dp, rows, cols, part_width, value.shape[-1])
+        for name in everywhere:
+            value = lax.psum_scatter(value, name, scatter_dimension=0, tiled=False)
+        return value.astype(f32)
+
+    up_grad = scatter(g_up)
+    down_grad = scatter(g_down).T
+    rest = scatter(rest)
+    qkv_grad = g_qkv.reshape(dp, cols, part_width, 3 * feat)
     qkv_grad = lax.psum_scatter(qkv_grad, "dp", scatter_dimension=0, tiled=False)
     qkv_grad = lax.psum_scatter(qkv_grad, "col", scatter_dimension=0, tiled=False).astype(f32)
-    gain_grads = lax.psum(jnp.stack([dg_one, dg_two, dg_three]), everywhere)
-    gain_grads = lax.dynamic_slice_in_dim(gain_grads, c_pos * part_width, part_width, 1)
 
     return (
         block_out,
@@ -537,10 +937,10 @@
         rest[:, 2 * feat : 3 * feat].T.reshape(w_out.shape),
         rest[:, 3 * feat : 4 * feat].reshape(w_cross_q.shape),
         rest[:, : 2 * feat].reshape(w_cross_kv.shape),
-        rest[:, 4 * feat :].T.reshape(w_cross_out.shape),
-        big[0],
-        big[1].T,
-        gain_grads,
+        rest[:, 4 * feat : 5 * feat].T.reshape(w_cross_out.shape),
+        up_grad,
+        down_grad,
+        rest[:, 5 * feat : 5 * feat + 3].T,
     )
 
 

time: 859 us -> 841 us (0.979)
  waiting for transfers between devices: 131 us -> 355 us
  local copies, waits for them, and re-layouts: 205 us -> 20.2 us
  Pallas kernels: 113 us -> 229 us
  matrix products: 86.2 us -> 11.1 us
  blocking collectives: 203 us -> 161 us
  other arithmetic: 53.2 us -> 19 us
  starting transfers between devices: 39.9 us -> 23.4 us
    pallas_call x0 -> x7, Pallas kernels: none -> 111 us  [the longest x1 39.1 us: middle(): pl.pallas_call(middle_kernel, grid=(2 * groups,), in_specs=[whole(normed_...]
    unnamed x16 -> x22, waiting for transfers between devices: 7.44 us -> 117 us
    reshape x25 -> x4, local copies, waits for them, and re-layouts: 99.9 us -> 0.42 us  [the longest x1 0.11 us: per_device(): w_cross_q.reshape(part_width, feat)]
    dot_general x23 -> x2, matrix products: 86.2 us -> 11.1 us  [mm(): return jnp.einsum(spec, left, right, preferred_element_type=f32)]
    psum x1 -> x0, blocking collectives: 58.1 us -> none  [per_device(): gain_grads = lax.psum(jnp.stack([dg_one, dg_two, dg_three]), everywhere)]
    reduce_scatter x5 -> x7, waiting for transfers between devices: 26.9 us -> 76.3 us  [the longest x6 76.3 us: scatter(): value = lax.psum_scatter(value, name, scatter_dimension=0, tiled=False)]
    all_gather x4, waiting for transfers between devices: 72 us -> 104 us  [the longest x3 104 us: gather_all(): value = lax.all_gather(value, everywhere, axis=0)]
    reduce_scatter x1, waiting for transfers between devices: 0.01 us -> 25.8 us  [per_device(): lax.psum_scatter(qkv_grad, 'col', scatter_dimension=0, tiled=False)]
  transfers between devices with their start and end apart: 24 -> 31, of which waited for: 10 -> 17; matrix products, arithmetic and copies ran while one was open for 30% -> 4% of each run, Pallas kernels for 11% -> 23%
where the time goes in v2:
time: 841 us; the launch traced here: 834 us
  waiting for transfers between devices  355 us (42%)
  Pallas kernels  229 us (27%)
  blocking collectives  161 us (19%)
  starting transfers between devices  23.4 us (3%)
  local copies, waits for them, and re-layouts  20.2 us (2%)
  other arithmetic  19 us (2%)
  between operations  15.9 us (2%)
  matrix products  11.1 us (1%)
    unnamed x22, waiting for transfers between devices  117 us
    all_gather x3, waiting for transfers between devices, gather_all(): value = lax.all_gather(value, everywhere, axis=0)  104 us
    reduce_scatter x6, waiting for transfers between devices, scatter(): value = lax.psum_scatter(value, name, scatter_dimension=0, tiled=False)  76.3 us
    pallas_call x2, Pallas kernels, attend_back(): pl.pallas_call(functools.partial(attend_back_kernel, sources=len(kv_list)...  75.8 us
    pallas_call x2, Pallas kernels, attend(): pl.pallas_call(functools.partial(attend_kernel, sources=len(kv_list), n_q...  42.1 us
    pallas_call x1, Pallas kernels, middle(): pl.pallas_call(middle_kernel, grid=(2 * groups,), in_specs=[whole(normed_...  39.1 us
    all_to_all x2, blocking collectives, to_tokens(): lax.all_to_all(value.reshape(cols, part_width, take), 'col', 0, 0, tiled=...  37.7 us
    all_gather x1, blocking collectives, per_device(): lax.all_gather(w_qkv.reshape(part_width, 3 * feat), ('dp', 'col'), axis=0)  31.5 us
  transfers between devices with their start and end apart: 31, of which 17 were waited for; matrix products, arithmetic and copies ran while one was open for 4% of the time, Pallas kernels for 23%

profile of v2, /device:TPU:0, one launch (start us, length us, event | category | flops | bytes accessed | tf_op | source)
XLA Modules:
  0.0 834.3 jit_solution(11763407620471499333)
XLA Ops:
  11.8 26.5 %all_to_all.45 = bf16[4,192,512]{2,1,0:T(8,128)(2,1)} all-to-all(bf16[4,192,512]{2,1,0:T(8,128)(2,1)S(1)} %pad_maximum_fusion), channel_id=1, replica_groups=mesh['dp'=2,'row'=4,'col'=4] {'col'}, dimensions={0} | all-to-all | bytes 1572864 | tf_op jit(solution)/shard_map/all_to_all | solution.py:781
  39.9 1.6 fusion.5
  43.0 11.1 %all_to_all.46 = bf16[4,192,128]{2,1,0:T(8,128)(2,1)} all-to-all(bf16[4,192,128]{2,1,0:T(8,128)(2,1)S(1)} %pad_maximum_fusion.3), channel_id=1, replica_groups=mesh['dp'=2,'row'=4,'col'=4] {'col'}, dimensions={0} | all-to-all | bytes 393216 | tf_op jit(solution)/shard_map/all_to_all | solution.py:781
  55.4 31.5 %all_gather.37 = bf16[8,192,288]{2,1,0:T(8,128)(2,1)} all-gather(bf16[1,192,288]{2,1,0:T(8,128)(2,1)S(1)} %copy.45), channel_id=1, replica_groups=mesh['dp'=2,'row'=4,'col'=4] {'dp','col'}, dimensions={0}, use_global_device_ids=true | all-gather | bytes 995328 | tf_op jit(solution)/shard_map/all_gather | solution.py:801
  87.0 6.0 project.1
  95.1 2.1 all-reduce
  98.5 2.0 copy-done.7
  101.6 29.1 %self_attention.1 = (bf16[4,2,3,32,512]{4,3,2,1,0:T(8,128)(2,1)}, f32[3,4,1,512]{3,2,1,0:T(1,128)S(1)}) custom-call(s32[13]{0:T(128)S(1)} %pad_add_fusion.refs_0_, bf16[4,2,3,32,512]{4,3,2,1,0:T(8,128)(2,1)S(1)} %bitcast.97, bf16[4,2,2,3,32,512]{5,4,3,2,1,0:T(8,128)(2,1)S(1)} %bitcast.96, bf16[4,2,2,3,32,512]{5,4,3,2,1,0:T(8,128)(2,1)S(1)} %collective-permute-done.1.refs_3_), custom_call_target="tpu_custom_call" | custom-call | flops 12884901888 | bytes 6291456 | tf_op jit(solution)/shard_map/self_attention/pallas_call | solution.py:238
  130.7 3.7 all-to-all-start.1
  136.6 15.6 %all-to-all-done.1 = bf16[4,2,3,32,512]{4,3,2,1,0:T(8,128)(2,1)S(1)} async-done(((bf16[4,2,3,32,512]{4,3,2,1,0:T(8,128)(2,1)}), bf16[4,2,3,32,512]{4,3,2,1,0:T(8,128)(2,1)S(1)}, u32[]{:S(2)}, u32[]{:S(2)}) %all-to-all-start.1) | async-done | bytes 786464 | tf_op jit(solution)/shard_map/all_to_all | solution.py:848
  152.2 4.6 all-to-all-start.3
  156.8 26.7 %all-gather.3 = f32[4,192,3]{1,2,0:T(4,128)S(1)} all-gather(f32[1,192,3]{1,2,0:T(4,128)S(1)} %convert_bitcast_fusion.1), channel_id=1, replica_groups=mesh['dp'=2,'row'=4,'col'=4] {'col'}, dimensions={0}, use_global_device_ids=true | all-gather | bytes 11520 | tf_op jit(solution)/shard_map/all_gather | solution.py:825
  184.4 8.8 %after_self.1 = (f32[768,512]{1,0:T(8,128)}, f32[1,512]{1,0:T(1,128)}, bf16[768,512]{1,0:T(8,128)(2,1)}, bf16[8,96,512]{2,1,0:T(8,128)(2,1)}) custom-call(bf16[768,512]{1,0:T(8,128)(2,1)} %bitcast.112, bf16[4,2,96,512]{3,2,1,0:T(8,128)(2,1)} %bitcast.109, bf16[8,768,512]{2,1,0:T(8,128)(2,1)} %bitcast.102, f32[768,3]{1,0:T(8,128)} %bitcast.117), custom_call_target="tpu_custom_call" | custom-call | tf_op jit(solution)/shard_map/after_self/pallas_call | solution.py:462
  193.2 10.0 %cross_kv.1 = bf16[8,8,192,128]{3,2,1,0:T(8,128)(2,1)} custom-call(bf16[8,768,512]{2,1,0:T(8,128)(2,1)} %bitcast.103, bf16[8,768,128]{2,1,0:T(8,128)(2,1)} %all-gather.12.cloned.1.call-done.chosen_ref), custom_call_target="tpu_custom_call" | custom-call | tf_op jit(solution)/shard_map/cross_kv/pallas_call | solution.py:415
  203.3 1.9 copy-done.3
  205.2 13.0 %cross_attention.1 = (bf16[1,2,4,3,32,512]{5,4,3,2,1,0:T(8,128)(2,1)S(1)}, f32[12,1,1,512]{3,2,1,0:T(1,128)S(1)}) custom-call(s32[13]{0:T(128)S(1)} %pad_add_fusion.refs_0_, bf16[1,2,4,3,32,512]{5,4,3,2,1,0:T(8,128)(2,1)S(1)} %bitcast.99, bf16[8,2,4,2,3,32,128]{6,5,4,3,2,1,0:T(8,128)(2,1)S(1)} %bitcast.89), custom_call_target="tpu_custom_call" | custom-call | flops 3221225472 | bytes 6291456 | tf_op jit(solution)/shard_map/cross_attention/pallas_call | solution.py:238
  219.1 39.5 %all-gather.16.cloned.1.call-done = bf16[6144,384]{1,0:T(8,128)(2,1)} async-done(((bf16[192,384]{1,0:T(8,128)(2,1)}), bf16[6144,384]{1,0:T(8,128)(2,1)}) %all-gather.16.cloned.1.call-update) | async-done | bytes 4718608 | tf_op jit(solution)/shard_map/all_gather | solution.py:819
  258.6 64.6 %all-gather.18.cloned.1.call-done = bf16[6144,384]{1,0:T(8,128)(2,1)} async-done(((bf16[192,384]{1,0:T(8,128)(2,1)}), bf16[6144,384]{1,0:T(8,128)(2,1)}) %all-gather.18.cloned.1.call-update) | async-done | bytes 4718608 | tf_op jit(solution)/shard_map/all_gather | solution.py:819
  323.2 39.1 %middle.1 = (bf16[768,512]{1,0:T(8,128)(2,1)}, bf16[8,96,512]{2,1,0:T(8,128)(2,1)}, f32[768,512]{1,0:T(8,128)}, bf16[768,512]{1,0:T(8,128)(2,1)}, bf16[8,768,384...) custom-call(f32[768,512]{1,0:T(8,128)} %get-tuple-element.45.normed_one_ref.normed_ref, ...), custom_call_target="tpu_custom_call" | custom-call | flops 14495514624 | bytes 18874368 | tf_op jit(solution)/shard_map/middle/pallas_call | solution.py:581
  363.7 21.6 %cross_attention_back.1 = (bf16[1,2,4,3,32,512]{5,4,3,2,1,0:T(8,128)(2,1)S(1)}, bf16[8,2,4,2,3,32,128]{6,5,4,3,2,1,0:T(8,128)(2,1)}) custom-call(s32[13]{0:T(128)S(1)} %pad_add_fusion.refs_0_, bf16[1,2,4,3,32,512]{5,4,3,2,1,0:T(8,128)(2,1)S(1)} %bitcast.100, bf16[8,2,4,2,3,32,128]{6,5,4,3,2,1,0:T(8,128)(2,1)} %bitcast.88, ...), custom_call_target="tpu_custom_call" | custom-call | flops 8053063680 | bytes 6291456 | tf_op jit(solution)/shard_map/cross_attention_back/pallas_call | solution.py:259
  386.3 10.5 %before_self.1 = (bf16[4,2,96,512]{3,2,1,0:T(8,128)(2,1)}, bf16[768,512]{1,0:T(8,128)(2,1)}, f32[768,512]{1,0:T(8,128)}, f32[768,128]{1,0:T(8,128)}) custom-call(bf16[8,96,512]{2,1,0:T(8,128)(2,1)} %bitcast.86, bf16[8,768,512]{2,1,0:T(8,128)(2,1)} %bitcast.105, f32[768,512]{1,0:T(8,128)} %get-tuple-element.52.dy_ref, ...), custom_call_target="tpu_custom_call" | custom-call | tf_op jit(solution)/shard_map/before_self/pallas_call | solution.py:650
  396.8 25.4 %small_grads.1 = (bf16[8,768,512]{2,1,0:T(8,128)(2,1)}, bf16[8,768,128]{2,1,0:T(8,128)(2,1)}) custom-call(bf16[8,768,512]{2,1,0:T(8,128)(2,1)} %bitcast.106, bf16[8,768,128]{2,1,0:T(8,128)(2,1)} %all-gather.12.cloned.1.call-done.chosen_ref, bf16[8,8,192,128]{3,2,1,0:T(8,128)(2,1)} %bitcast.120, bf16[4,2,96,512]{3,2,1,0:T(8,128)(2,1)} %bitcast.110, ...), custom_call_target="tpu_custom_call" | custom-call | tf_op jit(solution)/shard_map/small_grads/pallas_call | solution.py:707
  423.4 14.7 %all_to_all.47 = bf16[4,2,96,512]{3,2,1,0:T(8,128)(2,1)S(1)} all-to-all(bf16[4,2,96,512]{3,2,1,0:T(8,128)(2,1)S(1)} %copy-done.19), channel_id=1, replica_groups=mesh['dp'=2,'row'=4,'col'=4] {'row'}, dimensions={0} | all-to-all | bytes 1572864 | tf_op jit(solution)/shard_map/all_to_all | solution.py:881
  438.1 54.2 %self_attention_back.1 = (bf16[4,2,3,32,512]{4,3,2,1,0:T(8,128)(2,1)S(1)}, f32[4,2,2,3,32,512]{5,4,3,2,1,0:T(8,128)}, bf16[4,2,2,3,32,512]{5,4,3,2,1,0:T(8,128)(2,1)S(1)}) custom-call(s32[13]{0:T(128)S(1)} %pad_add_fusion.refs_0_, bf16[4,2,3,32,512]{4,3,2,1,0:T(8,128)(2,1)S(1)} %bitcast.98, bf16[4,2,2,3,32,512]{5,4,3,2,1,0:T(8,128)(2,1)} %bitcast.95, ...), custom_call_target="tpu_custom_call" | custom-call | flops 32212254720 | bytes 6291456 | tf_op jit(solution)/shard_map/self_attention_back/pallas_call | solution.py:259
  493.2 3.4 collective-permute-done.5
  497.7 11.2 %project_back.1 = (bf16[4,768,512]{2,1,0:T(8,128)(2,1)}, bf16[2,768,288]{2,1,0:T(8,128)(2,1)}) custom-call(bf16[2,768,288]{2,1,0:T(8,128)(2,1)} %bitcast.108, bf16[4,768,512]{2,1,0:T(8,128)(2,1)} %all-gather.10.cloned.1.call-done.x_ref.refs_1_, bf16[4,2,96,512]{3,2,1,0:T(8,128)(2,1)} %bitcast.92, f32[4,2,2,96,512]{4,3,2,1,0:T(8,128)} %bitcast.122, ...), custom_call_target="tpu_custom_call" | custom-call | tf_op jit(solution)/shard_map/project_back/pallas_call | solution.py:385
  511.7 3.4 reduce-scatter.27.cloned.1.call-done
  515.2 18.0 %reduce-scatter.31.cloned.1.call-done = bf16[1,4,4,192,512]{4,3,2,1,0:T(8,128)(2,1)} async-done(((bf16[2,4,4,192,512]{4,3,2,1,0:T(8,128)(2,1)}), bf16[1,4,4,192,512]{4,3,2,1,0:T(8,128)(2,1)}) %reduce-scatter.31.cloned.1.call-update) | async-done | bytes 3145744 | tf_op jit(solution)/shard_map/reduce_scatter | solution.py:922
  533.2 25.3 %all_to_all.48 = bf16[4,192,512]{2,1,0:T(8,128)(2,1)} all-to-all(bf16[4,192,512]{2,1,0:T(8,128)(2,1)S(1)} %bitcast.128), channel_id=1, replica_groups=mesh['dp'=2,'row'=4,'col'=4] {'col'}, dimensions={0} | all-to-all | bytes 1572864 | tf_op jit(solution)/shard_map/all_to_all | solution.py:786
  558.5 3.7 all-to-all-start.6
  562.3 33.0 %reduce-scatter.49.cloned.1.call-done = bf16[1,4,192,384]{3,2,1,0:T(8,128)(2,1)} async-done(((bf16[4,4,192,384]{3,2,1,0:T(8,128)(2,1)}), bf16[1,4,192,384]{3,2,1,0:T(8,128)(2,1)}) %reduce-scatter.49.cloned.1.call-update) | async-done | bytes 589840
  595.4 1.9 broadcast_select_fusion.3
  597.3 6.3 all-to-all-done.6
  605.3 17.1 %reduce-scatter.43.cloned.1.call-done = bf16[1,1,768,128]{3,2,0,1:T(8,128)(2,1)} async-done(((bf16[4,1,768,128]{3,2,0,1:T(8,128)(2,1)}), bf16[1,1,768,128]{3,2,0,1:T(8,128)(2,1)}) %reduce-scatter.43.cloned.1.call-update) | async-done | bytes 196624
  622.4 4.6 all-to-all-start.8
  627.0 3.1 add_convert_fusion
  630.1 32.8 %reduce-scatter.47.cloned.1.call-done = bf16[1,4,192,384]{3,2,1,0:T(8,128)(2,1)} async-done(((bf16[4,4,192,384]{3,2,1,0:T(8,128)(2,1)}), bf16[1,4,192,384]{3,2,1,0:T(8,128)(2,1)}) %reduce-scatter.47.cloned.1.call-update) | async-done | bytes 589840
  662.8 4.6 all-to-all-start.7
  668.6 25.8 %reduce-scatter.29.cloned.1.call-done = bf16[1,192,288]{2,1,0:T(8,128)(2,1)} async-done(((bf16[4,192,288]{2,1,0:T(8,128)(2,1)}), bf16[1,192,288]{2,1,0:T(8,128)(2,1)}) %reduce-scatter.29.cloned.1.call-update) | async-done | bytes 110608 | tf_op jit(solution)/shard_map/reduce_scatter | solution.py:930
  694.5 1.7 copy.52
  696.2 23.0 %all_gather.47 = bf16[2,192,1024]{2,1,0:T(8,128)(2,1)S(1)} all-gather(bf16[2,192,256]{2,1,0:T(8,128)(2,1)S(1)} %pad_maximum_fusion.4), channel_id=1, replica_groups=mesh['dp'=2,'row'=4,'col'=4] {'row'}, dimensions={2}, use_global_device_ids=true | all-gather | bytes 983040 | tf_op jit(solution)/shard_map/all_gather | solution.py:895
  719.3 30.0 %reduce-scatter.45.cloned.1.call-done = bf16[1,4,192,512]{3,2,1,0:T(8,128)(2,1)} async-done(((bf16[4,4,192,512]{3,2,1,0:T(8,128)(2,1)}), bf16[1,4,192,512]{3,2,1,0:T(8,128)(2,1)}) %reduce-scatter.45.cloned.1.call-update) | async-done | bytes 786448
  749.3 2.2 copy.53
  751.7 9.4 %fusion = f32[2,192,4096]{2,1,0:T(8,128)} fusion(bf16[2,192,1024]{2,1,0:T(8,128)(2,1)S(1)} %all_gather.47, s32[2,1024]{1,0:T(2,128)S(1)} %copy-done.26), kind=kOutput, calls=%fused_computation.1 | convolution fusion | flops 3229614080 | bytes 7086080 | tf_op jit(solution)/shard_map/swp,spn->swn/dot_general | solution.py:737
  762.5 11.1 %reduce-scatter.41.cloned.1.call-done = bf16[1,192,384]{2,1,0:T(8,128)(2,1)} async-done(((bf16[4,192,384]{2,1,0:T(8,128)(2,1)}), bf16[1,192,384]{2,1,0:T(8,128)(2,1)}) %reduce-scatter.41.cloned.1.call-update) | async-done | bytes 147472 | tf_op jit(solution)/shard_map/reduce_scatter | solution.py:922
  773.6 1.6 convert_bitcast_fusion
  775.2 21.0 %reduce-scatter.37.cloned.1.call-done = bf16[1,192,384]{2,1,0:T(8,128)(2,1)} async-done(((bf16[4,192,384]{2,1,0:T(8,128)(2,1)}), bf16[1,192,384]{2,1,0:T(8,128)(2,1)}) %reduce-scatter.37.cloned.1.call-update) | async-done | bytes 147472 | tf_op jit(solution)/shard_map/reduce_scatter | solution.py:922
  797.9 26.2 %reduce-scatter.33.cloned.1.call-done = bf16[1,192,512]{1,2,0:T(8,128)(2,1)} async-done(((bf16[4,192,512]{1,2,0:T(8,128)(2,1)}), bf16[1,192,512]{1,2,0:T(8,128)(2,1)}) %reduce-scatter.33.cloned.1.call-update) | async-done | bytes 196624 | tf_op jit(solution)/shard_map/reduce_scatter | solution.py:922
  (156 shorter events, 33.9 us)
Async XLA Ops:
  7.2 32.7 %copy-start = (bf16[2,192,4096]{2,1,0:T(8,128)(2,1)S(1)}, bf16[2,192,4096]{2,1,0:T(8,128)(2,1)}, u32[]{:S(2)}) copy-start(bf16[2,192,4096]{2,1,0:T(8,128)(2,1)} %param.15) | copy-start | bytes 9437188
  7.2 79.8 %all-gather.10.cloned.1.call-start = ((), (), s32[]{:S(2)}) async-start(), calls=%async_computation.22 | async-start | bytes 3932160 | tf_op jit(solution)/shard_map/all_gather | solution.py:804
  8.6 1.9 collective-permute-start
  11.7 26.8 %copy-start.22 = (bf16[3,32,192]{2,1,0:T(8,128)(2,1)S(1)}, bf16[3,32,192]{2,1,0:T(8,128)(2,1)}, u32[]{:S(2)}) copy-start(bf16[3,32,192]{2,1,0:T(8,128)(2,1)} %param.18) | copy-start | bytes 110596
  11.7 26.9 %copy-start.23 = (bf16[192,3,32]{0,2,1:T(8,128)(2,1)S(1)}, bf16[192,3,32]{0,2,1:T(8,128)(2,1)}, u32[]{:S(2)}) copy-start(bf16[192,3,32]{0,2,1:T(8,128)(2,1)} %param.19) | copy-start | bytes 110596
  11.7 27.0 %copy-start.24 = (bf16[3,32,192]{2,1,0:T(8,128)(2,1)S(1)}, bf16[3,32,192]{2,1,0:T(8,128)(2,1)}, u32[]{:S(2)}) copy-start(bf16[3,32,192]{2,1,0:T(8,128)(2,1)} %param.21) | copy-start | bytes 110596
  11.7 27.1 %copy-start.21 = (bf16[192,2,3,32]{0,3,2,1:T(8,128)(2,1)S(1)}, bf16[192,2,3,32]{0,3,2,1:T(8,128)(2,1)}, u32[]{:S(2)}) copy-start(bf16[192,2,3,32]{0,3,2,1:T(8,128)(2,1)} %param.20) | copy-start | bytes 221188
  11.7 28.1 %copy-start.26 = (s32[2,1024]{1,0:T(2,128)S(1)}, s32[2,1024]{1,0:T(2,128)}, u32[]{:S(2)}) copy-start(s32[2,1024]{1,0:T(2,128)} %param.16) | copy-start | bytes 24580
  38.4 146.1 %all-gather.14.cloned.1.call-start = ((), (), s32[]{:S(2)}) async-start(), calls=%async_computation.33 | async-start | bytes 6488064 | tf_op jit(solution)/shard_map/all_gather | solution.py:819
  39.8 153.5 %all-gather.12.cloned.1.call-start = ((), (), s32[]{:S(2)}) async-start(), calls=%async_computation.23 | async-start | bytes 1769472 | tf_op jit(solution)/shard_map/all_gather | solution.py:860
  39.9 15.4 %copy-start.20 = (bf16[192,3,3,32]{0,3,2,1:T(8,128)(2,1)S(1)}, bf16[192,3,3,32]{0,3,2,1:T(8,128)(2,1)}, u32[]{:S(2)}) copy-start(bf16[192,3,3,32]{0,3,2,1:T(8,128)(2,1)} %param.17) | copy-start | bytes 331780
  41.6 1.4 collective-permute-start.2
  54.1 204.5 %all-gather.16.cloned.1.call-start = ((), (), s32[]{:S(2)}) async-start(), calls=%async_computation.34 | async-start | bytes 4866048 | tf_op jit(solution)/shard_map/all_gather | solution.py:819
  54.7 268.5 %all-gather.18.cloned.1.call-start = ((), (), s32[]{:S(2)}) async-start(), calls=%async_computation.35 | async-start | bytes 4866048 | tf_op jit(solution)/shard_map/all_gather | solution.py:819
  86.9 7.5 copy-start.15
  92.9 5.5 collective-permute-start.1
  94.5 39.9 %collective-permute-start.3 = (bf16[2,192,512]{2,1,0:T(8,128)(2,1)S(1)}, bf16[2,192,512]{2,1,0:T(8,128)(2,1)S(1)}, u32[]{:S(2)}, u32[]{:S(2)}) collective-permute-start(bf16[2,192,512]{2,1,0:T(8,128)(2,1)S(1)} %broadcast_select_fusion.12), channel_id=1, source_target_pairs={{0,16},{16,0},{1,17},{17,1},{2,18},{18,2},{3,19},{19,3},{4,20},{20... | collective-permute-start | bytes 1179656 | tf_op jit(solution)/shard_map/ppermute | solution.py:771
  98.4 32.2 %copy-start.8 = (bf16[4,2,2,3,32,512]{5,4,3,2,1,0:T(8,128)(2,1)}, bf16[4,2,2,3,32,512]{5,4,3,2,1,0:T(8,128)(2,1)S(1)}, u32[]{:S(2)}) copy-start(bf16[4,2,2,3,32,512]{5,4,3,2,1,0:T(8,128)(2,1)S(1)} %collective-permute-done.1.refs_3_) | copy-start | bytes 4718596
  130.7 21.5 %all-to-all-start.1 = ((bf16[4,2,3,32,512]{4,3,2,1,0:T(8,128)(2,1)}), bf16[4,2,3,32,512]{4,3,2,1,0:T(8,128)(2,1)S(1)}, u32[]{:S(2)}, u32[]{:S(2)}) async-start(bf16[4,2,3,32,512]{4,3,2,1,0:T(8,128)(2,1)} %get-tuple-element.44.refs_5_), calls=%async_computation.1 | async-start | bytes 1572864 | tf_op jit(solution)/shard_map/all_to_all | solution.py:848
  134.4 22.4 %copy-start.25 = (bf16[3,192]{1,0:T(4,128)(2,1)S(1)}, bf16[3,192]{1,0:T(4,128)(2,1)}, u32[]{:S(2)}) copy-start(bf16[3,192]{1,0:T(4,128)(2,1)} %param.24) | copy-start | bytes 3460
  152.2 32.3 %copy-start.13 = (bf16[4,2,3,32,512]{4,3,2,1,0:T(8,128)(2,1)}, bf16[4,2,3,32,512]{4,3,2,1,0:T(8,128)(2,1)S(1)}, u32[]{:S(2)}) copy-start(bf16[4,2,3,32,512]{4,3,2,1,0:T(8,128)(2,1)S(1)} %all-to-all-done.1) | copy-start | bytes 2359300
  152.2 67.0 %all-to-all-start.3 = ((bf16[4,192,512]{2,1,0:T(8,128)(2,1)}), bf16[4,192,512]{2,1,0:T(8,128)(2,1)S(1)}, u32[]{:S(2)}, u32[]{:S(2)}) async-start(bf16[4,192,512]{2,1,0:T(8,128)(2,1)} %pad_maximum_fusion.1), calls=%async_computation.3 | async-start | bytes 1572864 | tf_op jit(solution)/shard_map/all_to_all | solution.py:781
  156.7 352.9 %reduce-scatter.39.cloned.1.call-start = ((), (), s32[]{:S(2)}) async-start(), calls=%async_computation.31 | async-start | bytes 7077888 | tf_op jit(solution)/shard_map/reduce_scatter | solution.py:922
  193.2 10.0 %copy-start.11 = (bf16[8,96,512]{2,1,0:T(8,128)(2,1)S(1)}, bf16[8,96,512]{2,1,0:T(8,128)(2,1)}, u32[]{:S(2)}) copy-start(bf16[8,96,512]{2,1,0:T(8,128)(2,1)} %get-tuple-element.46) | copy-start | bytes 2359300
  219.1 104.0 %copy-start.18 = (bf16[4,192,512]{2,1,0:T(8,128)(2,1)}, bf16[4,192,512]{2,1,0:T(8,128)(2,1)S(1)}, u32[]{:S(2)}) copy-start(bf16[4,192,512]{2,1,0:T(8,128)(2,1)S(1)} %all-to-all-done.3) | copy-start | bytes 2359300
  362.4 148.0 %reduce-scatter.25.cloned.1.call-start = ((), (), s32[]{:S(2)}) async-start(), calls=%async_computation.24 | async-start | bytes 2359296 | tf_op jit(solution)/shard_map/reduce_scatter | solution.py:888
  422.3 88.7 %reduce-scatter.35.cloned.1.call-start = ((), (), s32[]{:S(2)}) async-start(), calls=%async_computation.29 | async-start | bytes 7077888 | tf_op jit(solution)/shard_map/reduce_scatter | solution.py:922
  422.3 15.8 %copy-start.10 = (bf16[4,2,96,512]{3,2,1,0:T(8,128)(2,1)S(1)}, bf16[4,2,96,512]{3,2,1,0:T(8,128)(2,1)}, u32[]{:S(2)}) copy-start(bf16[4,2,96,512]{3,2,1,0:T(8,128)(2,1)} %get-tuple-element.42) | copy-start | bytes 2359300
  423.0 92.1 %reduce-scatter.27.cloned.1.call-start = ((), (), s32[]{:S(2)}) async-start(), calls=%async_computation.25 | async-start | bytes 1769472 | tf_op jit(solution)/shard_map/reduce_scatter | solution.py:929
  493.2 3.4 collective-permute-start.5
  509.0 24.2 %reduce-scatter.31.cloned.1.call-start = ((), (), s32[]{:S(2)}) async-start(), calls=%async_computation.27 | async-start | bytes 9437184 | tf_op jit(solution)/shard_map/reduce_scatter | solution.py:922
  509.6 85.8 %reduce-scatter.49.cloned.1.call-start = ((), (), s32[]{:S(2)}) async-start(), calls=%async_computation.39 | async-start | bytes 2949120
  510.3 112.1 %reduce-scatter.43.cloned.1.call-start = ((), (), s32[]{:S(2)}) async-start(), calls=%async_computation.36 | async-start | bytes 983040
  510.9 151.9 %reduce-scatter.47.cloned.1.call-start = ((), (), s32[]{:S(2)}) async-start(), calls=%async_computation.38 | async-start | bytes 2949120
  511.6 21.6 %copy-start.17 = (bf16[768,512]{1,0:T(8,128)(2,1)S(1)}, bf16[768,512]{1,0:T(8,128)(2,1)}, u32[]{:S(2)}) copy-start(bf16[768,512]{1,0:T(8,128)(2,1)} %get-tuple-element.48) | copy-start | bytes 2359300
  511.6 182.8 %reduce-scatter.29.cloned.1.call-start = ((), (), s32[]{:S(2)}) async-start(), calls=%async_computation.26 | async-start | bytes 737280 | tf_op jit(solution)/shard_map/reduce_scatter | solution.py:930
  515.1 234.1 %reduce-scatter.45.cloned.1.call-start = ((), (), s32[]{:S(2)}) async-start(), calls=%async_computation.37 | async-start | bytes 3932160
  558.5 45.1 %all-to-all-start.6 = ((bf16[4,768,512]{2,1,0:T(8,128)(2,1)}), bf16[4,768,512]{2,1,0:T(8,128)(2,1)S(1)}, u32[]{:S(2)}, u32[]{:S(2)}) async-start(bf16[4,768,512]{2,1,0:T(8,128)(2,1)} %get-tuple-element.60), calls=%async_computation.6 | async-start | bytes 6291456 | tf_op jit(solution)/shard_map/all_to_all | solution.py:915
  562.2 211.3 %reduce-scatter.41.cloned.1.call-start = ((), (), s32[]{:S(2)}) async-start(), calls=%async_computation.32 | async-start | bytes 737280 | tf_op jit(solution)/shard_map/reduce_scatter | solution.py:922
  597.3 70.2 %collective-permute-start.4 = (bf16[2,192,512]{2,1,0:T(8,128)(2,1)}, bf16[2,192,512]{2,1,0:T(8,128)(2,1)S(1)}, u32[]{:S(2)}, u32[]{:S(2)}) collective-permute-start(bf16[2,192,512]{2,1,0:T(8,128)(2,1)} %broadcast_select_fusion.3), channel_id=1, source_target_pairs={{0,16},{16,0},{1,17},{17,1},{2,18},{18,2},{3,19},{19,3},{4,20},{20... | collective-permute-start | bytes 1179656 | tf_op jit(solution)/shard_map/ppermute | solution.py:789
  622.4 40.5 %all-to-all-start.8 = ((bf16[4,192,128]{2,1,0:T(8,128)(2,1)}), bf16[4,192,128]{2,1,0:T(8,128)(2,1)S(1)}, u32[]{:S(2)}, u32[]{:S(2)}) async-start(bf16[4,192,128]{2,1,0:T(8,128)(2,1)} %bitcast.136), calls=%async_computation.9 | async-start | bytes 393216 | tf_op jit(solution)/shard_map/all_to_all | solution.py:786
  627.0 169.2 %reduce-scatter.37.cloned.1.call-start = ((), (), s32[]{:S(2)}) async-start(), calls=%async_computation.30 | async-start | bytes 737280 | tf_op jit(solution)/shard_map/reduce_scatter | solution.py:922
  627.0 40.5 %copy-start.14 = (bf16[4,192,512]{2,1,0:T(8,128)(2,1)S(1)}, bf16[4,192,512]{2,1,0:T(8,128)(2,1)}, u32[]{:S(2)}) copy-start(bf16[4,192,512]{2,1,0:T(8,128)(2,1)} %all_to_all.48) | copy-start | bytes 2359300
  662.8 88.7 %all-to-all-start.7 = ((bf16[4,192,512]{2,1,0:T(8,128)(2,1)}), bf16[4,192,512]{2,1,0:T(8,128)(2,1)S(1)}, u32[]{:S(2)}, u32[]{:S(2)}) async-start(bf16[4,192,512]{2,1,0:T(8,128)(2,1)} %bitcast.34), calls=%async_computation.7 | async-start | bytes 1572864 | tf_op jit(solution)/shard_map/all_to_all | solution.py:786
  667.4 156.6 %reduce-scatter.33.cloned.1.call-start = ((), (), s32[]{:S(2)}) async-start(), calls=%async_computation.28 | async-start | bytes 1310720 | tf_op jit(solution)/shard_map/reduce_scatter | solution.py:922
  667.6 28.6 %collective-permute-start.7 = (bf16[2,192,128]{2,1,0:T(8,128)(2,1)S(1)}, bf16[2,192,128]{2,1,0:T(8,128)(2,1)S(1)}, u32[]{:S(2)}, u32[]{:S(2)}) collective-permute-start(bf16[2,192,128]{2,1,0:T(8,128)(2,1)S(1)} %broadcast_select_fusion.21), channel_id=1, source_target_pairs={{0,16},{16,0},{1,17},{17,1},{2,18},{18,2},{3,19},{19,3},{4,20},{20... | collective-permute-start | bytes 294920 | tf_op jit(solution)/shard_map/ppermute | solution.py:789
  751.6 9.5 %collective-permute-start.6 = (bf16[2,192,512]{2,1,0:T(8,128)(2,1)S(1)}, bf16[2,192,512]{2,1,0:T(8,128)(2,1)S(1)}, u32[]{:S(2)}, u32[]{:S(2)}) collective-permute-start(bf16[2,192,512]{2,1,0:T(8,128)(2,1)S(1)} %broadcast_select_fusion.1), channel_id=1, source_target_pairs={{0,16},{16,0},{1,17},{17,1},{2,18},{18,2},{3,19},{19,3},{4,20},{20... | collective-permute-start | bytes 1179656 | tf_op jit(solution)/shard_map/ppermute | solution.py:789
  761.2 65.9 %copy-start.1 = (bf16[2,192,4096]{2,1,0:T(8,128)(2,1)S(1)}, bf16[2,192,4096]{2,1,0:T(8,128)(2,1)}, u32[]{:S(2)}) copy-start(bf16[2,192,4096]{2,1,0:T(8,128)(2,1)} %param.15) | copy-start | bytes 9437188
  (12 other events, 25.8 us)
Sparse Core Ops, SparseCore 0:
  38.5 42.9 all-gather.9
  84.9 78.0 all-gather.13
  164.9 27.4 all-gather.11
  195.0 63.5 all-gather.15
  261.3 61.8 all-gather.17
  362.5 10.8 reduce-scatter.38
  422.4 7.3 reduce-scatter.24
  432.1 13.7 reduce-scatter.34
  509.1 5.9 reduce-scatter.26
  517.8 15.3 reduce-scatter.30
  536.3 59.0 reduce-scatter.48
  598.1 24.2 reduce-scatter.42
  625.4 37.3 reduce-scatter.46
  665.0 29.4 reduce-scatter.28
  697.3 51.9 reduce-scatter.44
  751.4 22.1 reduce-scatter.40
  775.7 20.4 reduce-scatter.36
  798.4 25.6 reduce-scatter.32

commit v3 on v2

--- a/solution.py
+++ b/solution.py
@@ -313,111 +313,140 @@
     return inv_std * (scaled - total - normed * cross)
 
 
-def project_kernel(near_ref, x_ref, q_ref, kv_ref, near_t):
+def project_kernel(place_ref, near_ref, *refs, rows):
+    x_refs = refs[:rows]
+    q_ref, kv_ref, near_t = refs[rows:]
     feat = q_ref.shape[2]
-
-    @pl.when(pl.program_id(0) == 0)
+    step = pl.program_id(0)
+
+    @pl.when(step == 0)
     def _():
         for d in range(near_ref.shape[0]):
             near_t[d] = near_ref[d].T
 
-    for d in range(near_ref.shape[0]):
-        proj = dot(near_t[d], x_ref[0], 1, 0)
-        q_ref[0, d] = (proj[:feat] * (0.125 * LOG2E)).astype(bf16)
-        kv_ref[0, d, 0] = proj[feat : 2 * feat].astype(bf16)
-        kv_ref[0, d, 1] = proj[2 * feat :].astype(bf16)
-
-
-def project(near, x_rows):
+    for k, x_ref in enumerate(x_refs):
+
+        @pl.when(step == k)
+        def _():
+            for d in range(near_ref.shape[0]):
+                proj = dot(near_t[d, : 3 * feat, :], x_ref[...], 1, 0)
+                q_ref[0, d] = (proj[:feat] * (0.125 * LOG2E)).astype(bf16)
+                kv_ref[0, d, 0] = proj[feat : 2 * feat].astype(bf16)
+                kv_ref[0, d, 1] = proj[2 * feat :].astype(bf16)
+
+
+def project(place, near, x_rows, feat):
     dp, width, cols = near.shape
-    rows, _, tokens = x_rows.shape
-    feat = cols // 3
+    rows = len(x_rows)
+    tokens = x_rows[0].shape[1]
     return pl.pallas_call(
-        project_kernel,
-        grid=(rows,),
-        in_specs=[whole(near), pl.BlockSpec((1, width, tokens), lambda r: (r, 0, 0))],
-        out_specs=[
-            pl.BlockSpec((1, dp, feat, tokens), lambda r: (r, 0, 0, 0)),
-            pl.BlockSpec((1, dp, 2, feat, tokens), lambda r: (r, 0, 0, 0, 0)),
-        ],
+        functools.partial(project_kernel, rows=rows),
+        grid_spec=pltpu.PrefetchScalarGridSpec(
+            num_scalar_prefetch=1,
+            grid=(rows,),
+            in_specs=[whole(near)] + [whole(x) for x in x_rows],
+            out_specs=[
+                pl.BlockSpec((1, dp, feat, tokens), lambda k, p: (p[0] ^ k, 0, 0, 0)),
+                pl.BlockSpec((1, dp, 2, feat, tokens), lambda k, p: (p[0] ^ k, 0, 0, 0, 0)),
+            ],
+            scratch_shapes=[pltpu.VMEM((dp, cols, width), bf16)],
+        ),
         out_shape=[
             jax.ShapeDtypeStruct((rows, dp, feat, tokens), bf16),
             jax.ShapeDtypeStruct((rows, dp, 2, feat, tokens), bf16),
         ],
-        scratch_shapes=[pltpu.VMEM((dp, cols, width), bf16)],
         compiler_params=kernel_params(),
         name="project",
-    )(near, x_rows)
-
-
-def project_back_kernel(*refs, sources):
-    near_ref, x_ref, dq_ref = refs[:3]
-    dkv_refs = refs[3 : 3 + sources]
-    dx_ref, g_ref, acc = refs[3 + sources :]
-    r = pl.program_id(0)
-
-    @pl.when(r == 0)
+    )(place, near, *x_rows)
+
+
+def project_back_kernel(place_ref, near_ref, *refs, rows, sources):
+    x_refs, dq_ref = refs[:rows], refs[rows]
+    dkv_refs = refs[rows + 1 : rows + 1 + sources]
+    dx_ref, g_ref, acc = refs[rows + 1 + sources :]
+    step = pl.program_id(0)
+    feat = dq_ref.shape[2]
+
+    @pl.when(step == 0)
     def _():
         acc[...] = jnp.zeros_like(acc)
 
-    total = None
-    for d in range(near_ref.shape[0]):
-        parts = [dq_ref[0, d]]
-        for kind in range(2):
-            value = sum(ref[0, d, kind].astype(f32) for ref in dkv_refs)
-            parts.append(value.astype(bf16))
-        grad = jnp.concatenate(parts, axis=0)
-        acc[d] += dot(x_ref[0], grad, 1, 1)
-        part = dot(near_ref[d], grad, 1, 0)
-        total = part if total is None else total + part
-    dx_ref[0] = total.astype(bf16)
-
-    @pl.when(r == pl.num_programs(0) - 1)
+    for k, x_ref in enumerate(x_refs):
+
+        @pl.when(step == k)
+        def _():
+            total = None
+            for d in range(near_ref.shape[0]):
+                parts = [dq_ref[0, d]]
+                for kind in range(2):
+                    value = sum(ref[0, d, kind].astype(f32) for ref in dkv_refs)
+                    parts.append(value.astype(bf16))
+                grad = jnp.concatenate(parts, axis=0)
+                acc[d, :, : 3 * feat] += dot(x_ref[...], grad, 1, 1)
+                part = dot(near_ref[d, :, : 3 * feat], grad, 1, 0)
+                total = part if total is None else total + part
+            dx_ref[0] = total.astype(bf16)
+
+    @pl.when(step == rows - 1)
     def _():
         g_ref[...] = acc[...].astype(bf16)
 
 
-def project_back(near, x_rows, d_query, d_kv):
+def project_back(place, near, x_rows, d_query, d_kv):
     dp, width, cols = near.shape
-    rows, _, tokens = x_rows.shape
-    feat = cols // 3
-    kv_spec = pl.BlockSpec((1, dp, 2, feat, tokens), lambda r: (r, 0, 0, 0, 0))
+    rows = len(x_rows)
+    tokens = x_rows[0].shape[1]
+    feat = d_query.shape[2]
+    kv_spec = pl.BlockSpec((1, dp, 2, feat, tokens), lambda k, p: (p[0] ^ k, 0, 0, 0, 0))
     return pl.pallas_call(
-        functools.partial(project_back_kernel, sources=len(d_kv)),
-        grid=(rows,),
-        in_specs=[
-            whole(near),
-            pl.BlockSpec((1, width, tokens), lambda r: (r, 0, 0)),
-            pl.BlockSpec((1, dp, feat, tokens), lambda r: (r, 0, 0, 0)),
-        ]
-        + [kv_spec] * len(d_kv),
-        out_specs=[pl.BlockSpec((1, width, tokens), lambda r: (r, 0, 0)), whole(near)],
+        functools.partial(project_back_kernel, rows=rows, sources=len(d_kv)),
+        grid_spec=pltpu.PrefetchScalarGridSpec(
+            num_scalar_prefetch=1,
+            grid=(rows,),
+            in_specs=[whole(near)]
+            + [whole(x) for x in x_rows]
+            + [pl.BlockSpec((1, dp, feat, tokens), lambda k, p: (p[0] ^ k, 0, 0, 0))]
+            + [kv_spec] * len(d_kv),
+            out_specs=[
+                pl.BlockSpec((1, width, tokens), lambda k, p: (p[0] ^ k, 0, 0)),
+                whole(near),
+            ],
+            scratch_shapes=[pltpu.VMEM(near.shape, f32)],
+        ),
         out_shape=[
-            jax.ShapeDtypeStruct(x_rows.shape, bf16),
+            jax.ShapeDtypeStruct((rows, width, tokens), bf16),
             jax.ShapeDtypeStruct(near.shape, bf16),
         ],
-        scratch_shapes=[pltpu.VMEM(near.shape, f32)],
         compiler_params=kernel_params(),
         name="project_back",
-    )(near, x_rows, d_query, *d_kv)
-
-
-def cross_kv_kernel(w_ref, chosen_ref, o_ref):
-    feat2 = o_ref.shape[2]
-    weight = w_ref[0][:, :feat2].T
-    for n in range(chosen_ref.shape[0]):
-        o_ref[n, 0] = dot(weight, chosen_ref[n], 1, 0).astype(bf16)
+    )(place, near, *x_rows, d_query, *d_kv)
+
+
+def side_by_side(chosen_ref, wide):
+    count, _, tokens = chosen_ref.shape
+    for n in range(count):
+        wide[:, n * tokens : (n + 1) * tokens] = chosen_ref[n]
+
+
+def cross_kv_kernel(w_ref, chosen_ref, o_ref, wide):
+    @pl.when(pl.program_id(0) == 0)
+    def _():
+        side_by_side(chosen_ref, wide)
+
+    weight = w_ref[0][:, : o_ref.shape[1]].T
+    o_ref[0] = dot(weight, wide[...], 1, 0).astype(bf16)
 
 
 def cross_kv(small, chosen, feat):
     groups, width, cols = small.shape
-    count, _, tokens = chosen.shape
+    keys = chosen.shape[0] * chosen.shape[2]
     return pl.pallas_call(
         cross_kv_kernel,
         grid=(groups,),
         in_specs=[pl.BlockSpec((1, width, 2 * 128), lambda g: (g, 0, 0)), whole(chosen)],
-        out_specs=pl.BlockSpec((count, 1, 2 * feat, tokens), lambda g: (0, g, 0, 0)),
-        out_shape=jax.ShapeDtypeStruct((count, groups, 2 * feat, tokens), bf16),
+        out_specs=pl.BlockSpec((1, 2 * feat, keys), lambda g: (g, 0, 0)),
+        out_shape=jax.ShapeDtypeStruct((groups, 2 * feat, keys), bf16),
+        scratch_shapes=[pltpu.VMEM((width, keys), bf16)],
         compiler_params=kernel_params(),
         name="cross_kv",
     )(small, chosen)
@@ -473,7 +502,7 @@
 
 def middle_kernel(
     normed_one_ref, catt_ref, wc_ref, up_ref, down_ref, cot_ref, gain_ref,
-    out_ref, dcatt_ref, dy_ref, dcross_ref, gup_ref, gdown_ref, dg_two_ref, dg_three_ref,
+    out_ref, dcatt_ref, dy_ref, dcross_ref, glarge_ref, dg_two_ref, dg_three_ref,
     acc, normed_two, inv_two, act, slope, h_fm, h_tm, d_fm, d_tm,
 ):
     i = pl.program_id(0)
@@ -534,8 +563,8 @@
             at = slice(t, t + step)
             back = dot(d_tm[at, :], down_ref[0], 1, 0) * slope[g, at, :].astype(f32)
             slope[g, at, :] = back.astype(bf16)
-        gdown_ref[0] = dot(d_fm[...], act[g], 1, 0).astype(bf16)
-        gup_ref[0] = dot(h_fm[...], slope[g], 1, 0).astype(bf16)
+        glarge_ref[0, :, units:] = dot(d_fm[...], act[g], 1, 0).astype(bf16)
+        glarge_ref[0, :, :units] = dot(h_fm[...], slope[g], 1, 0).astype(bf16)
         acc[...] += dot(up_ref[0], slope[g], 1, 1)
 
     @pl.when(i == 2 * groups - 1)
@@ -554,30 +583,28 @@
             dcatt_ref[g] = dot(wc_ref[g, :, :feat], low, 0, 0).astype(bf16)
 
 
-def middle(normed_one, catt, small, up, down, cot, gains):
+def middle(normed_one, catt, small, large, cot, gains):
     width, tokens = normed_one.shape
     groups, feat, _ = catt.shape
-    units = up.shape[2]
+    units = large.shape[2] // 2
     lanes = min(128, tokens)
 
-    def weight():
-        return pl.BlockSpec((1, width, units), lambda i: (i % groups, 0, 0))
-
-    def grad_out():
-        return pl.BlockSpec((1, width, units), lambda i: (jnp.maximum(i - groups, 0), 0, 0))
+    def weight(kind):
+        return pl.BlockSpec((1, width, units), lambda i: (i % groups, 0, kind))
 
     outs = [
         jax.ShapeDtypeStruct((width, tokens), bf16),
         jax.ShapeDtypeStruct(catt.shape, bf16),
         jax.ShapeDtypeStruct((width, tokens), f32),
         jax.ShapeDtypeStruct((width, tokens), bf16),
-        jax.ShapeDtypeStruct(up.shape, bf16),
-        jax.ShapeDtypeStruct(up.shape, bf16),
+        jax.ShapeDtypeStruct(large.shape, bf16),
         jax.ShapeDtypeStruct((width, lanes), f32),
         jax.ShapeDtypeStruct((width, lanes), f32),
     ]
     specs = [whole(o) for o in outs]
-    specs[4], specs[5] = grad_out(), grad_out()
+    specs[4] = pl.BlockSpec(
+        (1, width, 2 * units), lambda i: (jnp.maximum(i - groups, 0), 0, 0)
+    )
     return pl.pallas_call(
         middle_kernel,
         grid=(2 * groups,),
@@ -585,8 +612,8 @@
             whole(normed_one),
             whole(catt),
             pl.BlockSpec((groups, width, 128), lambda i: (0, 0, 3)),
-            weight(),
-            weight(),
+            weight(0),
+            weight(1),
             whole(cot),
             whole(gains),
         ],
@@ -605,10 +632,10 @@
         ],
         compiler_params=kernel_params(),
         cost_estimate=pl.CostEstimate(
-            flops=12 * groups * width * units * tokens, bytes_accessed=4 * up.size * 2, transcendentals=0
+            flops=12 * groups * width * units * tokens, bytes_accessed=8 * large.size, transcendentals=0
         ),
         name="middle",
-    )(normed_one, catt, small, up, down, cot, gains)
+    )(normed_one, catt, small, large, large, cot, gains)
 
 
 def before_self_kernel(
@@ -660,16 +687,19 @@
 
 
 def small_grads_kernel(
-    w_ref, chosen_ref, dckv_ref, attn_ref, dcq_ref, catt_ref, dlow_ref, h_ref, dcross_ref,
-    dg_one_ref, dg_two_ref, dg_three_ref, rest_ref, dchosen_ref, acc, gain_cols,
+    place_ref, w_ref, chosen_ref, dckv_ref, attn_ref, dcq_ref, catt_ref, dlow_ref, h_ref,
+    dcross_ref, dg_one_ref, dg_two_ref, dg_three_ref, rest_ref, dchosen_ref, wide, acc, gain_cols,
+    *, paired,
 ):
     g = pl.program_id(0)
-    feat2 = dckv_ref.shape[2]
+    feat2 = dckv_ref.shape[1]
     feat = feat2 // 2
     count, width, tokens = chosen_ref.shape
+    rows = count // 2
 
     @pl.when(g == 0)
     def _():
+        side_by_side(chosen_ref, wide)
         col = lax.broadcasted_iota(jnp.int32, gain_cols.shape, 1)
         total = jnp.zeros(gain_cols.shape, f32)
         for k, ref in enumerate((dg_one_ref, dg_two_ref, dg_three_ref)):
@@ -677,14 +707,9 @@
         gain_cols[...] = total.astype(bf16)
         acc[...] = jnp.zeros_like(acc)
 
-    weight = w_ref[0][:, :feat2]
-    total = None
-    for n in range(count):
-        grad = dckv_ref[n, 0]
-        acc[n] += dot(weight, grad, 1, 0)
-        part = dot(chosen_ref[n], grad, 1, 1)
-        total = part if total is None else total + part
-    rest_ref[0, :, :feat2] = total.astype(bf16)
+    grad = dckv_ref[0]
+    acc[...] += dot(w_ref[0][:, :feat2], grad, 1, 0)
+    rest_ref[0, :, :feat2] = dot(wide[...], grad, 1, 1).astype(bf16)
     pairs = ((dlow_ref, attn_ref[0, 0]), (h_ref, dcq_ref[0]), (dcross_ref, catt_ref[0]))
     for k, (left, right) in enumerate(pairs):
         at = feat2 + k * feat
@@ -693,44 +718,51 @@
 
     @pl.when(g == pl.num_programs(0) - 1)
     def _():
-        dchosen_ref[...] = acc[...].astype(bf16)
-
-
-def small_grads(small, chosen, d_ckv, attn, d_cq, catt, d_low, h_low, d_cross, dgs):
+        for n in range(count):
+            at = n
+            if paired:
+                at = (place_ref[1] ^ (n % 2)) * rows + (place_ref[0] ^ (n // 2))
+            dchosen_ref[at] = acc[:, n * tokens : (n + 1) * tokens].astype(bf16)
+
+
+def small_grads(place, small, chosen, d_ckv, attn, d_cq, catt, d_low, h_low, d_cross, dgs, paired):
     groups, width, cols = small.shape
-    count, _, c_tokens = chosen.shape
-    feat2 = d_ckv.shape[2]
+    _, feat2, keys = d_ckv.shape
     feat = feat2 // 2
     tokens = d_low.shape[1]
     rows = attn.shape[0]
-    piece = pl.BlockSpec((1, feat, tokens), lambda g: (g, 0, 0))
+    piece = pl.BlockSpec((1, feat, tokens), lambda g, p: (g, 0, 0))
     return pl.pallas_call(
-        small_grads_kernel,
-        grid=(groups,),
-        in_specs=[
-            pl.BlockSpec((1, width, 2 * 128), lambda g: (g, 0, 0)),
-            whole(chosen),
-            pl.BlockSpec((count, 1, feat2, c_tokens), lambda g: (0, g, 0, 0)),
-            pl.BlockSpec((1, 1, feat, tokens), lambda g: (g % rows, g // rows, 0, 0)),
-            piece,
-            piece,
-            whole(d_low),
-            whole(h_low),
-            whole(d_cross),
-        ]
-        + [whole(v) for v in dgs],
-        out_specs=[pl.BlockSpec((1, width, cols), lambda g: (g, 0, 0)), whole(chosen)],
+        functools.partial(small_grads_kernel, paired=paired),
+        grid_spec=pltpu.PrefetchScalarGridSpec(
+            num_scalar_prefetch=1,
+            grid=(groups,),
+            in_specs=[
+                pl.BlockSpec((1, width, 2 * 128), lambda g, p: (g, 0, 0)),
+                whole(chosen),
+                pl.BlockSpec((1, feat2, keys), lambda g, p: (g, 0, 0)),
+                pl.BlockSpec((1, 1, feat, tokens), lambda g, p: (g % rows, g // rows, 0, 0)),
+                piece,
+                piece,
+                whole(d_low),
+                whole(h_low),
+                whole(d_cross),
+            ]
+            + [whole(v) for v in dgs],
+            out_specs=[pl.BlockSpec((1, width, cols), lambda g, p: (g, 0, 0)), whole(chosen)],
+            scratch_shapes=[
+                pltpu.VMEM((width, keys), bf16),
+                pltpu.VMEM((width, keys), f32),
+                pltpu.VMEM((width, cols - 5 * feat), bf16),
+            ],
+        ),
         out_shape=[
             jax.ShapeDtypeStruct(small.shape, bf16),
             jax.ShapeDtypeStruct(chosen.shape, bf16),
         ],
-        scratch_shapes=[
-            pltpu.VMEM(chosen.shape, f32),
-            pltpu.VMEM((width, cols - 5 * feat), bf16),
-        ],
         compiler_params=kernel_params(),
         name="small_grads",
-    )(small, chosen, d_ckv, attn, d_cq, catt, d_low, h_low, d_cross, *dgs)
+    )(place, small, chosen, d_ckv, attn, d_cq, catt, d_low, h_low, d_cross, *dgs)
 
 
 def mm(spec, left, right):
@@ -763,7 +795,7 @@
     def flip(value):
         return jnp.where(odd, value[:, :, ::-1], value)
 
-    def to_tokens(value):
+    def swap_cores(value):
         take = value.shape[-1] // parts
         if parts == 2:
             low, high = value[..., :take], value[..., take:]
@@ -778,8 +810,26 @@
             value = value.reshape(own_seqs, part_width, dp, sub, take)
             value = lax.all_to_all(value, "dp", 2, 0, tiled=True)
             value = value.reshape(seqs, part_width, sub, take).transpose(0, 2, 1, 3)
-        value = lax.all_to_all(value.reshape(cols, part_width, take), "col", 0, 0, tiled=True)
-        return value.reshape(width, take)
+        return value.reshape(cols, part_width, take)
+
+    def across_cols(value):
+        return lax.all_to_all(value, "col", 0, 0, tiled=True).reshape(width, value.shape[-1])
+
+    def to_tokens(value):
+        return across_cols(swap_cores(value))
+
+    def row_gather(value):
+        if rows != 4:
+            every = lax.all_gather(value, "row", axis=0)
+            return [lax.dynamic_index_in_dim(every, r_pos ^ k, 0, False) for k in range(rows)]
+
+        def send(v, k):
+            return lax.ppermute(v, "row", [(i, i ^ k) for i in range(rows)])
+
+        near_one, near_two = send(value, 1), send(value, 2)
+        half = value.shape[0] // 2
+        far = jnp.concatenate([send(near_two[:half], 1), send(near_one[half:], 2)], axis=0)
+        return [value, near_one, near_two, far]
 
     def to_home(value):
         take = value.shape[-1]
@@ -798,10 +848,12 @@
         value = flip(value.reshape(own_seqs, part_width, parts, take))
         return value.reshape(own_seqs, part_width, parts * take)
 
-    near = lax.all_gather(w_qkv.reshape(part_width, 3 * feat), ("dp", "col"), axis=0)
-    near = near.reshape(dp, width, 3 * feat)
-    x_own = to_tokens(x_in)
-    x_rows = lax.all_gather(x_own, "row", axis=0)
+    place = jnp.stack([r_pos, d_pos]).astype(jnp.int32)
+    qkv = jnp.pad(w_qkv.reshape(part_width, 3 * feat), ((0, 0), (0, 384 - 3 * feat)))
+    near = lax.all_gather(qkv, ("dp", "col"), axis=0).reshape(dp, width, qkv.shape[1])
+    x_swapped = swap_cores(x_in)
+    x_own = across_cols(x_swapped)
+    x_rows = row_gather(x_own)
     spare = 512 - 5 * feat
     small = jnp.concatenate(
         [
@@ -819,12 +871,13 @@
         value = lax.all_gather(value, everywhere, axis=0)
         return value.reshape(blocks, width, value.shape[-1])
 
+    small, _ = lax.optimization_barrier((small, x_swapped))
     small_all = gather_all(small)
-    up_all = gather_all(w_up)
-    down_all = gather_all(w_down.T)
+    large, _ = lax.optimization_barrier((jnp.concatenate([w_up, w_down.T], axis=1), x_own))
+    large_all = gather_all(large)
     gains = lax.all_gather(ln_gains.astype(f32).T, "col", axis=0, tiled=True)
 
-    query, kv_own = project(near, x_rows)
+    query, kv_own = project(place, near, x_rows, feat)
     query = query.reshape(rows, dp, heads, HALF, tokens)
     kv_own = kv_own.reshape(rows, dp, 2, heads, HALF, tokens)
 
@@ -857,32 +910,68 @@
     c_tokens = chosen.shape[1]
     if sub > 1:
         chosen = lax.all_gather(chosen, "col", axis=0, axis_index_groups=groups)
-    chosen = lax.all_gather(chosen, ("dp", "row"), axis=0)
-    chosen = chosen.reshape(blocks * sub, width, c_tokens)
+        chosen = lax.all_gather(chosen, ("dp", "row"), axis=0)
+        chosen = chosen.reshape(blocks * sub, width, c_tokens)
+    else:
+        pair = jnp.stack([chosen, lax.ppermute(chosen, "dp", swap)])
+        chosen = jnp.concatenate(row_gather(pair), axis=0)
     ckv = cross_kv(small_all, chosen, feat)
-    ckv = ckv.reshape(blocks * sub, dp, rows, 2, heads, HALF, c_tokens)
+    ckv = ckv.reshape(1, dp, rows, 2, heads, HALF, ckv.shape[-1])
     catt, lse_cross = attend(meta, cross_q, [ckv], False, "cross_attention")
     catt_flat = catt.reshape(blocks, feat, tokens)
 
     cot = to_tokens(out_grad)
-    block_out, d_catt, dy_two, d_cross, g_up, g_down, dg_two, dg_three = middle(
-        normed_one, catt_flat, small_all, up_all, down_all, cot, gains
+    block_out, d_catt, dy_two, d_cross, g_large, dg_two, dg_three = middle(
+        normed_one, catt_flat, small_all, large_all, cot, gains
     )
     block_out = to_home(block_out)
+
+    def scatter(value):
+        value = value.reshape(dp, rows, cols, part_width, value.shape[-1])
+        for name in everywhere:
+            value = lax.psum_scatter(value, name, scatter_dimension=0, tiled=False)
+        return value
+
+    large_grad = scatter(g_large)
     d_cq, d_ckv = attend_back(
         meta, cross_q, [ckv], d_catt.reshape(catt.shape), catt, lse_cross, False, [bf16],
         "cross_attention_back",
     )
     d_cq = d_cq.reshape(blocks, feat, tokens)
-    d_ckv = d_ckv.reshape(blocks * sub, blocks, 2 * feat, c_tokens)
+    d_ckv = d_ckv.reshape(blocks, 2 * feat, d_ckv.shape[-1])
     d_attn, d_low, dy_one, dg_one = before_self(
         d_cq, small_all, dy_two, normed_one, inv_one, gains, attn.shape
     )
     d_mixed = lax.all_to_all(d_attn, "row", 0, 0, tiled=True).reshape(mixed.shape)
     rest, d_chosen = small_grads(
-        small_all, chosen, d_ckv, attn, d_cq, catt_flat, d_low, h_low, d_cross,
-        (dg_one, dg_two, dg_three),
-    )
+        place, small_all, chosen, d_ckv, attn, d_cq, catt_flat, d_low, h_low, d_cross,
+        (dg_one, dg_two, dg_three), sub == 1,
+    )
+
+    types = [f32] + [bf16] * (len(kv_list) - 1) if sub == 1 else [bf16] * len(kv_list)
+    d_query, *d_kv = attend_back(
+        meta, query, kv_list, d_mixed, mixed, lse, True, types, "self_attention_back"
+    )
+    d_query, large_grad, d_chosen, rest = lax.optimization_barrier(
+        (d_query, large_grad, d_chosen, rest)
+    )
+    if sub == 1:
+        d_kv = [d_kv[0], lax.ppermute(d_kv[1], "dp", swap)]
+    else:
+        d_kv = jnp.stack(d_kv).reshape((dp, sub) + kv_own.shape)
+        d_kv = lax.psum_scatter(d_kv, "dp", scatter_dimension=0, tiled=True)
+        d_kv = lax.psum_scatter(
+            d_kv, "col", scatter_dimension=1, tiled=True, axis_index_groups=groups
+        )
+        d_kv = [d_kv]
+    kv_shape = (rows, dp, 2, feat, tokens)
+    d_kv = [value.reshape(kv_shape) for value in d_kv]
+    dx_part, g_qkv = project_back(
+        place, near, x_rows, d_query.reshape(rows, dp, feat, tokens), d_kv
+    )
+    dx_part = lax.all_to_all(dx_part, "row", 0, 0, tiled=True)
+    dx = dy_one + jnp.sum(dx_part.astype(f32), axis=0)
+    x_grad = to_home(dx.astype(bf16)).astype(f32)
 
     d_chosen = d_chosen.reshape(dp, rows, sub, width, c_tokens)
     d_chosen = lax.psum_scatter(d_chosen, "dp", scatter_dimension=0, tiled=False)
@@ -896,36 +985,9 @@
     hot_all = (bank_rows[:, :, None] == bank_ids[None, None, :]).astype(bf16)
     bank_grad = mm("swp,spn->swn", d_chosen, hot_all)
 
-    types = [f32] + [bf16] * (len(kv_list) - 1) if sub == 1 else [bf16] * len(kv_list)
-    d_query, *d_kv = attend_back(
-        meta, query, kv_list, d_mixed, mixed, lse, True, types, "self_attention_back"
-    )
-    if sub == 1:
-        d_kv = [d_kv[0], lax.ppermute(d_kv[1], "dp", swap)]
-    else:
-        d_kv = jnp.stack(d_kv).reshape((dp, sub) + kv_own.shape)
-        d_kv = lax.psum_scatter(d_kv, "dp", scatter_dimension=0, tiled=True)
-        d_kv = lax.psum_scatter(
-            d_kv, "col", scatter_dimension=1, tiled=True, axis_index_groups=groups
-        )
-        d_kv = [d_kv]
-    kv_shape = (rows, dp, 2, feat, tokens)
-    d_kv = [value.reshape(kv_shape) for value in d_kv]
-    dx_part, g_qkv = project_back(near, x_rows, d_query.reshape(rows, dp, feat, tokens), d_kv)
-    dx_part = lax.all_to_all(dx_part, "row", 0, 0, tiled=True)
-    dx = dy_one + jnp.sum(dx_part.astype(f32), axis=0)
-    x_grad = to_home(dx.astype(bf16)).astype(f32)
-
-    def scatter(value):
-        value = value.reshape(dp, rows, cols, part_width, value.shape[-1])
-        for name in everywhere:
-            value = lax.psum_scatter(value, name, scatter_dimension=0, tiled=False)
-        return value.astype(f32)
-
-    up_grad = scatter(g_up)
-    down_grad = scatter(g_down).T
-    rest = scatter(rest)
-    qkv_grad = g_qkv.reshape(dp, cols, part_width, 3 * feat)
+    large_grad = large_grad.astype(f32)
+    rest = scatter(rest).astype(f32)
+    qkv_grad = g_qkv.reshape(dp, cols, part_width, g_qkv.shape[-1])
     qkv_grad = lax.psum_scatter(qkv_grad, "dp", scatter_dimension=0, tiled=False)
     qkv_grad = lax.psum_scatter(qkv_grad, "col", scatter_dimension=0, tiled=False).astype(f32)
 
@@ -933,13 +995,13 @@
         block_out,
         x_grad,
         bank_grad,
-        qkv_grad.reshape(w_qkv.shape),
+        qkv_grad[:, : 3 * feat].reshape(w_qkv.shape),
         rest[:, 2 * feat : 3 * feat].T.reshape(w_out.shape),
         rest[:, 3 * feat : 4 * feat].reshape(w_cross_q.shape),
         rest[:, : 2 * feat].reshape(w_cross_kv.shape),
         rest[:, 4 * feat : 5 * feat].T.reshape(w_cross_out.shape),
-        up_grad,
-        down_grad,
+        large_grad[:, :units],
+        large_grad[:, units:].T,
         rest[:, 5 * feat : 5 * feat + 3].T,
     )
 

time: 841 us -> 642 us (0.76)
  waiting for transfers between devices: 355 us -> 170 us
  blocking collectives: 161 us -> 108 us
  starting transfers between devices: 23.4 us -> 46.5 us
  local copies, waits for them, and re-layouts: 20.2 us -> 35.1 us
    all_gather x3 -> x2, waiting for transfers between devices: 104 us -> 0.02 us  [gather_all(): value = lax.all_gather(value, everywhere, axis=0)]
    unnamed x22 -> x16, waiting for transfers between devices: 117 us -> 20.4 us
    reduce_scatter x6 -> x4, waiting for transfers between devices: 76.3 us -> 32.8 us  [scatter(): value = lax.psum_scatter(value, name, scatter_dimension=0, tiled=False)]
    all_to_all x2 -> x3, waiting for transfers between devices: 0.01 us -> 38.7 us  [to_home(): lax.all_to_all(value.reshape(cols, part_width, take), 'col', 0, 0, tiled=...]
    all_gather x1 -> x0, blocking collectives: 31.5 us -> none  [per_device(): lax.all_gather(w_qkv.reshape(part_width, 3 * feat), ('dp', 'col'), axis=0)]
    all_to_all x4 -> x1, blocking collectives: 77.6 us -> 48.1 us  [per_device(): dx_part = lax.all_to_all(dx_part, 'row', 0, 0, tiled=True)]
    ppermute x3 -> x12, waiting for transfers between devices: 2.64 us -> 32.1 us  [the longest x8 32.1 us: send(): return lax.ppermute(v, 'row', [(i, i ^ k) for i in range(rows)])]
    reduce_scatter x1, waiting for transfers between devices: 25.8 us -> 0.02 us  [per_device(): lax.psum_scatter(qkv_grad, 'col', scatter_dimension=0, tiled=False)]
  transfers between devices with their start and end apart: 31 -> 38, of which waited for: 17 -> 16; matrix products, arithmetic and copies ran while one was open for 4% -> 8% of each run, Pallas kernels for 23% -> 29%
where the time goes in v3:
time: 642 us; the launch traced here: 630 us
  Pallas kernels  223 us (35%)
  waiting for transfers between devices  170 us (26%)
  blocking collectives  108 us (17%)
  starting transfers between devices  46.5 us (7%)
  local copies, waits for them, and re-layouts  35.1 us (5%)
  other arithmetic  20.1 us (3%)
  between operations  15.6 us (2%)
  matrix products  11 us (2%)
    pallas_call x2, Pallas kernels, attend_back(): pl.pallas_call(functools.partial(attend_back_kernel, sources=len(kv_list)...  74.9 us
    all_to_all x1, blocking collectives, per_device(): dx_part = lax.all_to_all(dx_part, 'row', 0, 0, tiled=True)  48.1 us
    pallas_call x2, Pallas kernels, attend(): pl.pallas_call(functools.partial(attend_kernel, sources=len(kv_list), n_q...  41 us
    pallas_call x1, Pallas kernels, middle(): pl.pallas_call(middle_kernel, grid=(2 * groups,), in_specs=[whole(normed_...  39.1 us
    all_gather x1, blocking collectives, per_device(): gains = lax.all_gather(ln_gains.astype(f32).T, 'col', axis=0, tiled=True)  38.8 us
    all_to_all x3, waiting for transfers between devices, to_home(): lax.all_to_all(value.reshape(cols, part_width, take), 'col', 0, 0, tiled=...  38.7 us
    reduce_scatter x4, waiting for transfers between devices, scatter(): value = lax.psum_scatter(value, name, scatter_dimension=0, tiled=False)  32.8 us
    ppermute x8, waiting for transfers between devices, send(): return lax.ppermute(v, 'row', [(i, i ^ k) for i in range(rows)])  32.1 us
  transfers between devices with their start and end apart: 38, of which 16 were waited for; matrix products, arithmetic and copies ran while one was open for 8% of the time, Pallas kernels for 29%

profile of v3, /device:TPU:0, one launch (start us, length us, event | category | flops | bytes accessed | tf_op | source)
XLA Modules:
  0.0 630.3 jit_solution(2874599475062617932)
XLA Ops:
  9.2 1.9 broadcast_select_fusion.14
  16.2 1.6 copy.48
  18.4 1.8 concatenate.37
  22.5 5.8 all-to-all-start
  29.0 22.1 %all-to-all-done = bf16[4,192,512]{2,1,0:T(8,128)(2,1)} async-done(((bf16[4,192,512]{2,1,0:T(8,128)(2,1)}), bf16[4,192,512]{2,1,0:T(8,128)(2,1)}, u32[]{:S(2)}, u32[]{:S(2)}) %all-to-all-start) | async-done | bytes 786464 | tf_op jit(solution)/shard_map/all_to_all | solution.py:816
  54.1 18.9 %collective-permute-done.2.refs_2_ = bf16[768,512]{1,0:T(8,128)(2,1)S(1)} collective-permute-done((bf16[768,512]{1,0:T(8,128)(2,1)}, bf16[768,512]{1,0:T(8,128)(2,1)S(1)}, u32[]{:S(2)}, u32[]{:S(2)}) %collective-permute-start.2) | collective-permute-done | bytes 786464 | tf_op jit(solution)/shard_map/ppermute | solution.py:827
  79.3 7.0 %collective-permute-done.3 = bf16[384,512]{1,0:T(8,128)(2,1)S(1)} collective-permute-done((bf16[384,512]{1,0:T(8,128)(2,1)}, bf16[384,512]{1,0:T(8,128)(2,1)S(1)}, u32[]{:S(2)}, u32[]{:S(2)}) %collective-permute-start.3) | collective-permute-done | bytes 393248 | tf_op jit(solution)/shard_map/ppermute | solution.py:827
  87.8 1.8 constant_dynamic-update-slice_fusion.refs_3_
  89.6 7.1 %project.1 = (bf16[4,2,96,512]{3,2,1,0:T(8,128)(2,1)}, bf16[4,2,2,96,512]{4,3,2,1,0:T(8,128)(2,1)}) custom-call(s32[2]{0:T(128)} %pad_add_fusion.1.place_ref, bf16[2,768,384]{2,1,0:T(8,128)(2,1)} %bitcast.109, bf16[768,512]{1,0:T(8,128)(2,1)} %bitcast.refs_0_.x_ref, bf16[768,512]{1,0:T(8,128)(2,1)} %copy-done.16, bf16[768,512]{1,0:T(8,128)(2,1)} %copy-done.15, ...), custom_call_target="tpu_custom_call" | custom-call | tf_op jit(solution)/shard_map/project/pallas_call | solution.py:342
  96.8 1.6 fusion.5
  100.5 1.9 broadcast_select_fusion.12
  102.5 2.0 all-reduce.1
  106.5 3.4 all-to-all-start.2
  110.0 28.1 %self_attention.1 = (bf16[4,2,3,32,512]{4,3,2,1,0:T(8,128)(2,1)}, f32[3,4,1,512]{3,2,1,0:T(1,128)S(1)}) custom-call(s32[13]{0:T(128)S(1)} %pad_add_fusion.refs_0_, bf16[4,2,3,32,512]{4,3,2,1,0:T(8,128)(2,1)S(1)} %bitcast.95, bf16[4,2,2,3,32,512]{5,4,3,2,1,0:T(8,128)(2,1)S(1)} %bitcast.94, bf16[4,2,2,3,32,512]{5,4,3,2,1,0:T(8,128)(2,1)} %collective-permute-done.5.refs_3_), custom_call_target="tpu_custom_call" | custom-call | flops 12884901888 | bytes 6291456 | tf_op jit(solution)/shard_map/self_attention/pallas_call | solution.py:238
  138.0 3.6 all-to-all-start.1
  144.9 1.6 collective-permute-start.9
  148.0 13.8 %all-to-all-done.1 = bf16[4,2,3,32,512]{4,3,2,1,0:T(8,128)(2,1)S(1)} async-done(((bf16[4,2,3,32,512]{4,3,2,1,0:T(8,128)(2,1)}), bf16[4,2,3,32,512]{4,3,2,1,0:T(8,128)(2,1)S(1)}, u32[]{:S(2)}, u32[]{:S(2)}) %all-to-all-start.1) | async-done | bytes 786464 | tf_op jit(solution)/shard_map/all_to_all | solution.py:901
  161.7 4.9 all-to-all-start.3
  166.6 38.8 %all-gather.3 = f32[4,192,3]{1,2,0:T(4,128)S(1)} all-gather(f32[1,192,3]{1,2,0:T(4,128)S(1)} %convert_bitcast_fusion), channel_id=1, replica_groups=mesh['dp'=2,'row'=4,'col'=4] {'col'}, dimensions={0}, use_global_device_ids=true | all-gather | bytes 11520 | tf_op jit(solution)/shard_map/all_gather | solution.py:878
  207.4 2.7 collective-permute-start.10
  210.4 3.4 collective-permute-done.10
  213.8 2.1 collective-permute-done.11
  217.1 8.9 %cross_kv.1 = bf16[8,192,1024]{2,1,0:T(8,128)(2,1)} custom-call(bf16[8,768,512]{2,1,0:T(8,128)(2,1)} %bitcast.100, bf16[8,768,128]{2,1,0:T(8,128)(2,1)} %copy-done.13), custom_call_target="tpu_custom_call" | custom-call | tf_op jit(solution)/shard_map/cross_kv/pallas_call | solution.py:443
  226.0 8.9 %after_self.1 = (f32[768,512]{1,0:T(8,128)}, f32[1,512]{1,0:T(1,128)}, bf16[768,512]{1,0:T(8,128)(2,1)}, bf16[8,96,512]{2,1,0:T(8,128)(2,1)}) custom-call(bf16[768,512]{1,0:T(8,128)(2,1)} %bitcast.refs_0_.x_ref, bf16[4,2,96,512]{3,2,1,0:T(8,128)(2,1)} %bitcast.106, bf16[8,768,512]{2,1,0:T(8,128)(2,1)} %bitcast.101, f32[768,3]{1,0:T(8,128)} %bitcast.113), custom_call_target="tpu_custom_call" | custom-call | tf_op jit(solution)/shard_map/after_self/pallas_call | solution.py:491
  236.0 12.9 %cross_attention.1 = (bf16[1,2,4,3,32,512]{5,4,3,2,1,0:T(8,128)(2,1)S(1)}, f32[12,1,1,512]{3,2,1,0:T(1,128)S(1)}) custom-call(s32[13]{0:T(128)S(1)} %pad_add_fusion.refs_0_, bf16[1,2,4,3,32,512]{5,4,3,2,1,0:T(8,128)(2,1)S(1)} %bitcast.97, bf16[1,2,4,2,3,32,1024]{6,5,4,3,2,1,0:T(8,128)(2,1)S(1)} %bitcast.87), custom_call_target="tpu_custom_call" | custom-call | flops 3221225472 | bytes 6291456 | tf_op jit(solution)/shard_map/cross_attention/pallas_call | solution.py:238
  249.9 39.1 %middle.1 = (bf16[768,512]{1,0:T(8,128)(2,1)}, bf16[8,96,512]{2,1,0:T(8,128)(2,1)}, f32[768,512]{1,0:T(8,128)}, bf16[768,512]{1,0:T(8,128)(2,1)}, bf16[8,768,768...) custom-call(f32[768,512]{1,0:T(8,128)} %get-tuple-element.51.normed_one_ref.normed_ref, ...), custom_call_target="tpu_custom_call" | custom-call | flops 14495514624 | bytes 37748736 | tf_op jit(solution)/shard_map/middle/pallas_call | solution.py:608
  289.3 14.7 %reduce-scatter.20.cloned.1.call-done = bf16[1,4,4,192,768]{4,3,2,1,0:T(8,128)(2,1)} async-done(((bf16[2,4,4,192,768]{4,3,2,1,0:T(8,128)(2,1)}), bf16[1,4,4,192,768]{4,3,2,1,0:T(8,128)(2,1)}) %reduce-scatter.20.cloned.1.call-update) | async-done | bytes 4718608 | tf_op jit(solution)/shard_map/reduce_scatter | solution.py:932
  305.5 21.4 %cross_attention_back.1 = (bf16[1,2,4,3,32,512]{5,4,3,2,1,0:T(8,128)(2,1)S(1)}, bf16[1,2,4,2,3,32,1024]{6,5,4,3,2,1,0:T(8,128)(2,1)}) custom-call(s32[13]{0:T(128)S(1)} %pad_add_fusion.refs_0_, bf16[1,2,4,3,32,512]{5,4,3,2,1,0:T(8,128)(2,1)S(1)} %bitcast.98, bf16[1,2,4,2,3,32,1024]{6,5,4,3,2,1,0:T(8,128)(2,1)} %bitcast.86, ...), custom_call_target="tpu_custom_call" | custom-call | flops 8053063680 | bytes 6291456 | tf_op jit(solution)/shard_map/cross_attention_back/pallas_call | solution.py:259
  327.9 10.8 %before_self.1 = (bf16[4,2,96,512]{3,2,1,0:T(8,128)(2,1)}, bf16[768,512]{1,0:T(8,128)(2,1)}, f32[768,512]{1,0:T(8,128)}, f32[768,128]{1,0:T(8,128)}) custom-call(bf16[8,96,512]{2,1,0:T(8,128)(2,1)} %bitcast.84, bf16[8,768,512]{2,1,0:T(8,128)(2,1)} %bitcast.103, f32[768,512]{1,0:T(8,128)} %get-tuple-element.59.dy_ref, ...), custom_call_target="tpu_custom_call" | custom-call | tf_op jit(solution)/shard_map/before_self/pallas_call | solution.py:677
  338.7 4.0 all-to-all-start.5
  342.6 20.2 %small_grads.1 = (bf16[8,768,512]{2,1,0:T(8,128)(2,1)}, bf16[8,768,128]{2,1,0:T(8,128)(2,1)}) custom-call(s32[2]{0:T(128)} %pad_add_fusion.1.place_ref, bf16[8,768,512]{2,1,0:T(8,128)(2,1)} %bitcast.104, bf16[8,768,128]{2,1,0:T(8,128)(2,1)} %copy-done.13, bf16[8,192,1024]{2,1,0:T(8,128)(2,1)} %bitcast.117, bf16[4,2,96,512]{3,2,1,0:T(8,128)(2,1)} %bitcast.107, ...), custom_call_target="tpu_custom_call" | custom-call | tf_op jit(solution)/shard_map/small_grads/pallas_call | solution.py:735
  362.8 5.2 reduce-scatter.34.cloned.1.call-done
  368.1 53.4 %self_attention_back.1 = (bf16[4,2,3,32,512]{4,3,2,1,0:T(8,128)(2,1)S(1)}, f32[4,2,2,3,32,512]{5,4,3,2,1,0:T(8,128)}, bf16[4,2,2,3,32,512]{5,4,3,2,1,0:T(8,128)(2,1)S(1)}) custom-call(s32[13]{0:T(128)S(1)} %pad_add_fusion.refs_0_, bf16[4,2,3,32,512]{4,3,2,1,0:T(8,128)(2,1)S(1)} %bitcast.96, bf16[4,2,2,3,32,512]{5,4,3,2,1,0:T(8,128)(2,1)} %bitcast.93, ...), custom_call_target="tpu_custom_call" | custom-call | flops 32212254720 | bytes 6291456 | tf_op jit(solution)/shard_map/self_attention_back/pallas_call | solution.py:259
  422.8 3.6 collective-permute-done.14
  427.6 12.5 %project_back.1 = (bf16[4,768,512]{2,1,0:T(8,128)(2,1)}, bf16[2,768,384]{2,1,0:T(8,128)(2,1)}) custom-call(s32[2]{0:T(128)} %pad_add_fusion.1.place_ref, bf16[2,768,384]{2,1,0:T(8,128)(2,1)} %bitcast.110, bf16[768,512]{1,0:T(8,128)(2,1)} %bitcast.refs_0_.x_ref, bf16[768,512]{1,0:T(8,128)(2,1)} %copy-done.16, bf16[768,512]{1,0:T(8,128)(2,1)} %copy-done.15, ...), custom_call_target="tpu_custom_call" | custom-call | tf_op jit(solution)/shard_map/project_back/pallas_call | solution.py:401
  441.5 5.0 reduce-scatter.26.cloned.1.call-done
  446.5 18.2 %reduce-scatter.30.cloned.1.call-done = bf16[1,4,4,192,512]{4,3,2,1,0:T(8,128)(2,1)} async-done(((bf16[2,4,4,192,512]{4,3,2,1,0:T(8,128)(2,1)}), bf16[1,4,4,192,512]{4,3,2,1,0:T(8,128)(2,1)}) %reduce-scatter.30.cloned.1.call-update) | async-done | bytes 3145744 | tf_op jit(solution)/shard_map/reduce_scatter | solution.py:932
  464.7 48.1 %all_to_all.45 = bf16[4,768,512]{2,1,0:T(8,128)(2,1)S(1)} all-to-all(bf16[4,768,512]{2,1,0:T(8,128)(2,1)} %get-tuple-element.78), channel_id=1, replica_groups=mesh['dp'=2,'row'=4,'col'=4] {'row'}, dimensions={0} | all-to-all | bytes 6291456 | tf_op jit(solution)/shard_map/all_to_all | solution.py:972
  512.9 4.2 all-to-all-start.4
  519.6 24.5 %all-to-all-done.4 = bf16[4,192,512]{2,1,0:T(8,128)(2,1)} async-done(((bf16[4,192,512]{2,1,0:T(8,128)(2,1)}), bf16[4,192,512]{2,1,0:T(8,128)(2,1)}, u32[]{:S(2)}, u32[]{:S(2)}) %all-to-all-start.4) | async-done | bytes 786464 | tf_op jit(solution)/shard_map/all_to_all | solution.py:836
  544.1 3.5 all-to-all-start.7
  548.8 1.7 collective-permute-done.13
  553.5 14.2 %all-to-all-done.7 = bf16[4,192,512]{2,1,0:T(8,128)(2,1)S(1)} async-done(((bf16[4,192,512]{2,1,0:T(8,128)(2,1)}), bf16[4,192,512]{2,1,0:T(8,128)(2,1)S(1)}, u32[]{:S(2)}, u32[]{:S(2)}) %all-to-all-start.7) | async-done | bytes 786464 | tf_op jit(solution)/shard_map/all_to_all | solution.py:836
  568.6 3.4 all-to-all-start.8
  573.8 13.8 %reduce-scatter.38.cloned.1.call-done = bf16[1,4,192,512]{3,2,1,0:T(8,128)(2,1)} async-done(((bf16[4,4,192,512]{3,2,1,0:T(8,128)(2,1)}), bf16[1,4,192,512]{3,2,1,0:T(8,128)(2,1)}) %reduce-scatter.38.cloned.1.call-update) | async-done | bytes 786448
  587.6 2.2 copy.53
  591.5 19.4 %all_gather.35 = bf16[2,192,1024]{2,1,0:T(8,128)(2,1)S(1)} all-gather(bf16[2,192,256]{2,1,0:T(8,128)(2,1)S(1)} %pad_maximum_fusion.6), channel_id=1, replica_groups=mesh['dp'=2,'row'=4,'col'=4] {'row'}, dimensions={2}, use_global_device_ids=true | all-gather | bytes 983040 | tf_op jit(solution)/shard_map/all_gather | solution.py:984
  610.9 9.4 %fusion = f32[2,192,4096]{2,1,0:T(8,128)} fusion(bf16[2,192,1024]{2,1,0:T(8,128)(2,1)S(1)} %all_gather.35, s32[2,1024]{1,0:T(2,128)S(1)} %copy-done.25), kind=kOutput, calls=%fused_computation.1 | convolution fusion | flops 3229614080 | bytes 7086080 | tf_op jit(solution)/shard_map/swp,spn->swn/dot_general | solution.py:769
  (177 shorter events, 55.6 us)
Async XLA Ops:
  7.2 89.6 %copy-start = (bf16[2,192,4096]{2,1,0:T(8,128)(2,1)S(1)}, bf16[2,192,4096]{2,1,0:T(8,128)(2,1)}, u32[]{:S(2)}) copy-start(bf16[2,192,4096]{2,1,0:T(8,128)(2,1)} %param.15) | copy-start | bytes 9437188
  7.2 82.4 %all-gather.8.cloned.1.call-start = ((), (), s32[]{:S(2)}) async-start(), calls=%async_computation.26 | async-start | bytes 1327104 | tf_op jit(solution)/shard_map/all_gather | solution.py:853
  9.2 206.8 %all-gather.10.cloned.1.call-start = ((), (), s32[]{:S(2)}) async-start(), calls=%async_computation.27 | async-start | bytes 6488064 | tf_op jit(solution)/shard_map/all_gather | solution.py:871
  11.1 9.1 %collective-permute-start = (bf16[2,192,512]{2,1,0:T(8,128)(2,1)}, bf16[2,192,512]{2,1,0:T(8,128)(2,1)S(1)}, u32[]{:S(2)}, u32[]{:S(2)}) collective-permute-start(bf16[2,192,512]{2,1,0:T(8,128)(2,1)} %broadcast_select_fusion.14), channel_id=1, source_target_pairs={{0,16},{16,0},{1,17},{17,1},{2,18},{18,2},{3,19},{19,3},{4,20},{20... | collective-permute-start | bytes 1179656 | tf_op jit(solution)/shard_map/ppermute | solution.py:803
  21.5 6.8 %copy-start.22 = (bf16[384,192]{0,1:T(8,128)(2,1)S(1)}, bf16[384,192]{0,1:T(8,128)(2,1)}, u32[]{:S(2)}) copy-start(bf16[384,192]{0,1:T(8,128)(2,1)} %param.23) | copy-start | bytes 442372
  22.5 28.6 %all-to-all-start = ((bf16[4,192,512]{2,1,0:T(8,128)(2,1)}), bf16[4,192,512]{2,1,0:T(8,128)(2,1)}, u32[]{:S(2)}, u32[]{:S(2)}) async-start(bf16[4,192,512]{2,1,0:T(8,128)(2,1)} %pad_maximum_fusion), calls=%async_computation | async-start | bytes 1572864 | tf_op jit(solution)/shard_map/all_to_all | solution.py:816
  28.3 221.6 %all-gather.12.cloned.1.call-start = ((), (), s32[]{:S(2)}) async-start(), calls=%async_computation.28 | async-start | bytes 9732096 | tf_op jit(solution)/shard_map/all_gather | solution.py:871
  51.1 21.9 %collective-permute-start.2 = (bf16[768,512]{1,0:T(8,128)(2,1)}, bf16[768,512]{1,0:T(8,128)(2,1)S(1)}, u32[]{:S(2)}, u32[]{:S(2)}) collective-permute-start(bf16[768,512]{1,0:T(8,128)(2,1)} %bitcast.refs_0_.x_ref), channel_id=1, source_target_pairs={{0,8},{4,12},{8,0},{12,4},{1,9},{5,13},{9,1},{13,5},{2,10},{6,14},... | collective-permute-start | bytes 2359304 | tf_op jit(solution)/shard_map/ppermute | solution.py:827
  52.6 23.4 %collective-permute-start.1 = (bf16[768,512]{1,0:T(8,128)(2,1)}, bf16[768,512]{1,0:T(8,128)(2,1)S(1)}, u32[]{:S(2)}, u32[]{:S(2)}) collective-permute-start(bf16[768,512]{1,0:T(8,128)(2,1)} %bitcast.refs_0_.x_ref), channel_id=1, source_target_pairs={{0,4},{4,0},{8,12},{12,8},{1,5},{5,1},{9,13},{13,9},{2,6},{6,2},{1... | collective-permute-start | bytes 2359304 | tf_op jit(solution)/shard_map/ppermute | solution.py:827
  74.7 11.7 %collective-permute-start.3 = (bf16[384,512]{1,0:T(8,128)(2,1)}, bf16[384,512]{1,0:T(8,128)(2,1)S(1)}, u32[]{:S(2)}, u32[]{:S(2)}) collective-permute-start(bf16[384,512]{1,0:T(8,128)(2,1)} %slice.97), channel_id=1, source_target_pairs={{0,4},{4,0},{8,12},{12,8},{1,5},{5,1},{9,13},{13,9},{2,6},{6,2},{1... | collective-permute-start | bytes 1179656 | tf_op jit(solution)/shard_map/ppermute | solution.py:827
  77.7 10.1 %collective-permute-start.4 = (bf16[384,512]{1,0:T(8,128)(2,1)}, bf16[384,512]{1,0:T(8,128)(2,1)}, u32[]{:S(2)}, u32[]{:S(2)}) collective-permute-start(bf16[384,512]{1,0:T(8,128)(2,1)} %slice.98), channel_id=1, source_target_pairs={{0,8},{4,12},{8,0},{12,4},{1,9},{5,13},{9,1},{13,5},{2,10},{6,14},... | collective-permute-start | bytes 1179656 | tf_op jit(solution)/shard_map/ppermute | solution.py:827
  89.6 7.2 %copy-start.25 = (s32[2,1024]{1,0:T(2,128)S(1)}, s32[2,1024]{1,0:T(2,128)}, u32[]{:S(2)}) copy-start(s32[2,1024]{1,0:T(2,128)} %param.16) | copy-start | bytes 24580
  96.7 13.2 %collective-permute-start.5 = (bf16[4,2,2,3,32,512]{5,4,3,2,1,0:T(8,128)(2,1)}, bf16[4,2,2,3,32,512]{5,4,3,2,1,0:T(8,128)(2,1)}, u32[]{:S(2)}, u32[]{:S(2)}) collective-permute-start(bf16[4,2,2,3,32,512]{5,4,3,2,1,0:T(8,128)(2,1)} %bitcast.92), channel_id=1, source_target_pairs={{0,16},{16,0},{1,17},{17,1},{2,18},{18,2},{3,19},{19,3},{4,20},{20... | collective-permute-start | bytes 4718600 | tf_op jit(solution)/shard_map/ppermute | solution.py:889
  98.4 11.5 %copy-start.7 = (bf16[4,2,2,96,512]{4,3,2,1,0:T(8,128)(2,1)S(1)}, bf16[4,2,2,96,512]{4,3,2,1,0:T(8,128)(2,1)}, u32[]{:S(2)}) copy-start(bf16[4,2,2,96,512]{4,3,2,1,0:T(8,128)(2,1)} %get-tuple-element.48) | copy-start | bytes 4718596
  98.4 11.5 %copy-start.8 = (bf16[4,2,96,512]{3,2,1,0:T(8,128)(2,1)S(1)}, bf16[4,2,96,512]{3,2,1,0:T(8,128)(2,1)}, u32[]{:S(2)}) copy-start(bf16[4,2,96,512]{3,2,1,0:T(8,128)(2,1)} %get-tuple-element.47) | copy-start | bytes 2359300
  98.5 7.3 %collective-permute-start.6 = (bf16[2,192,128]{2,1,0:T(8,128)(2,1)S(1)}, bf16[2,192,128]{2,1,0:T(8,128)(2,1)S(1)}, u32[]{:S(2)}, u32[]{:S(2)}) collective-permute-start(bf16[2,192,128]{2,1,0:T(8,128)(2,1)S(1)} %broadcast_select_fusion.18), channel_id=1, source_target_pairs={{0,16},{16,0},{1,17},{17,1},{2,18},{18,2},{3,19},{19,3},{4,20},{20... | collective-permute-start | bytes 294920 | tf_op jit(solution)/shard_map/ppermute | solution.py:803
  102.4 39.6 %collective-permute-start.12 = (bf16[2,192,512]{2,1,0:T(8,128)(2,1)}, bf16[2,192,512]{2,1,0:T(8,128)(2,1)}, u32[]{:S(2)}, u32[]{:S(2)}) collective-permute-start(bf16[2,192,512]{2,1,0:T(8,128)(2,1)} %broadcast_select_fusion.12), channel_id=1, source_target_pairs={{0,16},{16,0},{1,17},{17,1},{2,18},{18,2},{3,19},{19,3},{4,20},{20... | collective-permute-start | bytes 1179656 | tf_op jit(solution)/shard_map/ppermute | solution.py:803
  106.5 31.5 %all-to-all-start.2 = ((bf16[4,192,128]{2,1,0:T(8,128)(2,1)}), bf16[4,192,128]{2,1,0:T(8,128)(2,1)S(1)}, u32[]{:S(2)}, u32[]{:S(2)}) async-start(bf16[4,192,128]{2,1,0:T(8,128)(2,1)} %pad_maximum_fusion.5), calls=%async_computation.2 | async-start | bytes 393216 | tf_op jit(solution)/shard_map/all_to_all | solution.py:816
  138.0 23.7 %all-to-all-start.1 = ((bf16[4,2,3,32,512]{4,3,2,1,0:T(8,128)(2,1)}), bf16[4,2,3,32,512]{4,3,2,1,0:T(8,128)(2,1)S(1)}, u32[]{:S(2)}, u32[]{:S(2)}) async-start(bf16[4,2,3,32,512]{4,3,2,1,0:T(8,128)(2,1)} %get-tuple-element.49.refs_5_), calls=%async_computation.1 | async-start | bytes 1572864 | tf_op jit(solution)/shard_map/all_to_all | solution.py:901
  141.7 2.4 collective-permute-start.7
  144.1 22.6 %copy-start.24 = (bf16[3,192]{1,0:T(4,128)(2,1)S(1)}, bf16[3,192]{1,0:T(4,128)(2,1)}, u32[]{:S(2)}) copy-start(bf16[3,192]{1,0:T(4,128)(2,1)} %param.24) | copy-start | bytes 3460
  144.9 62.5 %collective-permute-start.9 = (bf16[2,768,128]{2,1,0:T(8,128)(2,1)}, bf16[2,768,128]{2,1,0:T(8,128)(2,1)S(1)}, u32[]{:S(2)}, u32[]{:S(2)}) collective-permute-start(bf16[2,768,128]{2,1,0:T(8,128)(2,1)} %pad_maximum_fusion.3), channel_id=1, source_target_pairs={{0,8},{4,12},{8,0},{12,4},{1,9},{5,13},{9,1},{13,5},{2,10},{6,14},... | collective-permute-start | bytes 1179656 | tf_op jit(solution)/shard_map/ppermute | solution.py:827
  146.5 63.6 %collective-permute-start.8 = (bf16[2,768,128]{2,1,0:T(8,128)(2,1)}, bf16[2,768,128]{2,1,0:T(8,128)(2,1)S(1)}, u32[]{:S(2)}, u32[]{:S(2)}) collective-permute-start(bf16[2,768,128]{2,1,0:T(8,128)(2,1)} %pad_maximum_fusion.3), channel_id=1, source_target_pairs={{0,4},{4,0},{8,12},{12,8},{1,5},{5,1},{9,13},{13,9},{2,6},{6,2},{1... | collective-permute-start | bytes 1179656 | tf_op jit(solution)/shard_map/ppermute | solution.py:827
  161.7 45.7 %copy-start.14 = (bf16[4,2,3,32,512]{4,3,2,1,0:T(8,128)(2,1)}, bf16[4,2,3,32,512]{4,3,2,1,0:T(8,128)(2,1)S(1)}, u32[]{:S(2)}) copy-start(bf16[4,2,3,32,512]{4,3,2,1,0:T(8,128)(2,1)S(1)} %all-to-all-done.1) | copy-start | bytes 2359300
  161.7 88.1 %all-to-all-start.3 = ((bf16[4,192,512]{2,1,0:T(8,128)(2,1)}), bf16[4,192,512]{2,1,0:T(8,128)(2,1)}, u32[]{:S(2)}, u32[]{:S(2)}) async-start(bf16[4,192,512]{2,1,0:T(8,128)(2,1)} %pad_maximum_fusion.1), calls=%async_computation.3 | async-start | bytes 1572864 | tf_op jit(solution)/shard_map/all_to_all | solution.py:816
  166.6 137.3 %reduce-scatter.20.cloned.1.call-start = ((), (), s32[]{:S(2)}) async-start(), calls=%async_computation.19 | async-start | bytes 14155776 | tf_op jit(solution)/shard_map/reduce_scatter | solution.py:932
  207.4 6.4 %collective-permute-start.10 = (bf16[1,768,128]{2,1,0:T(8,128)(2,1)S(1)}, bf16[1,768,128]{2,1,0:T(8,128)(2,1)S(1)}, u32[]{:S(2)}, u32[]{:S(2)}) collective-permute-start(bf16[1,768,128]{2,1,0:T(8,128)(2,1)S(1)} %slice.101), channel_id=1, source_target_pairs={{0,4},{4,0},{8,12},{12,8},{1,5},{5,1},{9,13},{13,9},{2,6},{6,2},{1... | collective-permute-start | bytes 589832 | tf_op jit(solution)/shard_map/ppermute | solution.py:827
  210.2 5.7 collective-permute-start.11
  226.0 8.9 %copy-start.3 = (bf16[8,192,1024]{2,1,0:T(8,128)(2,1)S(1)}, bf16[8,192,1024]{2,1,0:T(8,128)(2,1)}, u32[]{:S(2)}) copy-start(bf16[8,192,1024]{2,1,0:T(8,128)(2,1)} %cross_kv.1) | copy-start | bytes 9437188
  289.0 79.0 %reduce-scatter.34.cloned.1.call-start = ((), (), s32[]{:S(2)}) async-start(), calls=%async_computation.29 | async-start | bytes 5898240
  338.7 29.4 %all-to-all-start.5 = ((bf16[4,2,96,512]{3,2,1,0:T(8,128)(2,1)}), bf16[4,2,96,512]{3,2,1,0:T(8,128)(2,1)S(1)}, u32[]{:S(2)}, u32[]{:S(2)}) async-start(bf16[4,2,96,512]{3,2,1,0:T(8,128)(2,1)} %get-tuple-element.62), calls=%async_computation.5 | async-start | bytes 1572864 | tf_op jit(solution)/shard_map/all_to_all | solution.py:945
  342.6 79.8 %reduce-scatter.22.cloned.1.call-start = ((), (), s32[]{:S(2)}) async-start(), calls=%async_computation.20 | async-start | bytes 1474560 | tf_op jit(solution)/shard_map/reduce_scatter | solution.py:932
  342.6 25.4 %copy-start.9 = (bf16[4,2,96,512]{3,2,1,0:T(8,128)(2,1)S(1)}, bf16[4,2,96,512]{3,2,1,0:T(8,128)(2,1)}, u32[]{:S(2)}) copy-start(bf16[4,2,96,512]{3,2,1,0:T(8,128)(2,1)} %get-tuple-element.47) | copy-start | bytes 2359300
  368.0 72.9 %reduce-scatter.24.cloned.1.call-start = ((), (), s32[]{:S(2)}) async-start(), calls=%async_computation.21 | async-start | bytes 2359296 | tf_op jit(solution)/shard_map/reduce_scatter | solution.py:977
  422.5 24.0 %reduce-scatter.26.cloned.1.call-start = ((), (), s32[]{:S(2)}) async-start(), calls=%async_computation.22 | async-start | bytes 1769472 | tf_op jit(solution)/shard_map/reduce_scatter | solution.py:991
  422.8 3.7 collective-permute-start.14
  440.1 24.6 %reduce-scatter.30.cloned.1.call-start = ((), (), s32[]{:S(2)}) async-start(), calls=%async_computation.24 | async-start | bytes 9437184 | tf_op jit(solution)/shard_map/reduce_scatter | solution.py:932
  440.9 127.7 %reduce-scatter.36.cloned.1.call-start = ((), (), s32[]{:S(2)}) async-start(), calls=%async_computation.30 | async-start | bytes 983040
  441.4 130.6 %reduce-scatter.28.cloned.1.call-start = ((), (), s32[]{:S(2)}) async-start(), calls=%async_computation.23 | async-start | bytes 737280 | tf_op jit(solution)/shard_map/reduce_scatter | solution.py:992
  446.5 141.1 %reduce-scatter.38.cloned.1.call-start = ((), (), s32[]{:S(2)}) async-start(), calls=%async_computation.31 | async-start | bytes 3932160
  512.9 31.2 %all-to-all-start.4 = ((bf16[4,192,512]{2,1,0:T(8,128)(2,1)}), bf16[4,192,512]{2,1,0:T(8,128)(2,1)}, u32[]{:S(2)}, u32[]{:S(2)}) async-start(bf16[4,192,512]{2,1,0:T(8,128)(2,1)} %bitcast.128), calls=%async_computation.4 | async-start | bytes 1572864 | tf_op jit(solution)/shard_map/all_to_all | solution.py:836
  544.1 23.6 %all-to-all-start.7 = ((bf16[4,192,512]{2,1,0:T(8,128)(2,1)}), bf16[4,192,512]{2,1,0:T(8,128)(2,1)S(1)}, u32[]{:S(2)}, u32[]{:S(2)}) async-start(bf16[4,192,512]{2,1,0:T(8,128)(2,1)} %bitcast.41), calls=%async_computation.9 | async-start | bytes 1572864 | tf_op jit(solution)/shard_map/all_to_all | solution.py:836
  548.8 1.8 collective-permute-start.13
  567.8 22.1 %collective-permute-start.15 = (bf16[2,192,512]{2,1,0:T(8,128)(2,1)S(1)}, bf16[2,192,512]{2,1,0:T(8,128)(2,1)S(1)}, u32[]{:S(2)}, u32[]{:S(2)}) collective-permute-start(bf16[2,192,512]{2,1,0:T(8,128)(2,1)S(1)} %broadcast_select_fusion.1), channel_id=1, source_target_pairs={{0,16},{16,0},{1,17},{17,1},{2,18},{18,2},{3,19},{19,3},{4,20},{20... | collective-permute-start | bytes 1179656 | tf_op jit(solution)/shard_map/ppermute | solution.py:839
  568.6 21.4 %all-to-all-start.8 = ((bf16[4,192,128]{2,1,0:T(8,128)(2,1)}), bf16[4,192,128]{2,1,0:T(8,128)(2,1)S(1)}, u32[]{:S(2)}, u32[]{:S(2)}) async-start(bf16[4,192,128]{2,1,0:T(8,128)(2,1)} %bitcast.133), calls=%async_computation.11 | async-start | bytes 393216 | tf_op jit(solution)/shard_map/all_to_all | solution.py:836
  571.9 48.3 %reduce-scatter.32.cloned.1.call-start = ((), (), s32[]{:S(2)}) async-start(), calls=%async_computation.25 | async-start | bytes 1310720 | tf_op jit(solution)/shard_map/reduce_scatter | solution.py:932
  590.0 1.4 collective-permute-start.16
  610.9 12.4 %copy-start.1 = (bf16[2,192,4096]{2,1,0:T(8,128)(2,1)S(1)}, bf16[2,192,4096]{2,1,0:T(8,128)(2,1)}, u32[]{:S(2)}) copy-start(bf16[2,192,4096]{2,1,0:T(8,128)(2,1)} %param.15) | copy-start | bytes 9437188
  (18 other events, 36.4 us)
Sparse Core Ops, SparseCore 0:
  10.2 30.9 all-gather.7
  44.6 70.0 all-gather.9
  118.2 96.7 all-gather.11
  289.1 14.7 reduce-scatter.19
  306.8 61.1 reduce-scatter.33
  370.2 29.3 reduce-scatter.21
  422.6 6.3 reduce-scatter.23
  440.2 6.1 reduce-scatter.25
  449.3 15.3 reduce-scatter.29
  467.4 38.9 reduce-scatter.35
  508.7 26.7 reduce-scatter.27
  538.4 49.1 reduce-scatter.37
  590.0 27.2 reduce-scatter.31

commit v4 on v3

--- a/solution.py
+++ b/solution.py
@@ -279,6 +279,14 @@
     )(meta, query, *kv_list, grad, out, lse)
 
 
+def gain_of(w_ref, first, k):
+    return w_ref[0, :, first + k : first + k + 1].astype(f32)
+
+
+def other_first(i, place, half):
+    return jnp.where(i < half, (1 - place[1]) * half + i, place[1] * half + i - half)
+
+
 def kernel_params():
     return pltpu.CompilerParams(vmem_limit_bytes=60 << 20)
 
@@ -363,7 +371,7 @@
 def project_back_kernel(place_ref, near_ref, *refs, rows, sources):
     x_refs, dq_ref = refs[:rows], refs[rows]
     dkv_refs = refs[rows + 1 : rows + 1 + sources]
-    dx_ref, g_ref, acc = refs[rows + 1 + sources :]
+    dx_ref, gother_ref, gown_ref, acc = refs[rows + 1 + sources :]
     step = pl.program_id(0)
     feat = dq_ref.shape[2]
 
@@ -389,7 +397,8 @@
 
     @pl.when(step == rows - 1)
     def _():
-        g_ref[...] = acc[...].astype(bf16)
+        gown_ref[...] = acc[place_ref[1]].astype(bf16)
+        gother_ref[...] = acc[1 - place_ref[1]].astype(bf16)
 
 
 def project_back(place, near, x_rows, d_query, d_kv):
@@ -398,6 +407,7 @@
     tokens = x_rows[0].shape[1]
     feat = d_query.shape[2]
     kv_spec = pl.BlockSpec((1, dp, 2, feat, tokens), lambda k, p: (p[0] ^ k, 0, 0, 0, 0))
+    half = jax.ShapeDtypeStruct((width, cols), bf16)
     return pl.pallas_call(
         functools.partial(project_back_kernel, rows=rows, sources=len(d_kv)),
         grid_spec=pltpu.PrefetchScalarGridSpec(
@@ -409,13 +419,15 @@
             + [kv_spec] * len(d_kv),
             out_specs=[
                 pl.BlockSpec((1, width, tokens), lambda k, p: (p[0] ^ k, 0, 0)),
-                whole(near),
+                whole(half),
+                whole(half),
             ],
             scratch_shapes=[pltpu.VMEM(near.shape, f32)],
         ),
         out_shape=[
             jax.ShapeDtypeStruct((rows, width, tokens), bf16),
-            jax.ShapeDtypeStruct(near.shape, bf16),
+            half,
+            half,
         ],
         compiler_params=kernel_params(),
         name="project_back",
@@ -456,7 +468,7 @@
     return g % rows, g // rows
 
 
-def after_self_kernel(x_ref, attn_ref, w_ref, gain_ref, normed_ref, inv_ref, low_ref, cq_ref, acc):
+def after_self_kernel(x_ref, attn_ref, w_ref, normed_ref, inv_ref, low_ref, cq_ref, acc):
     groups, feat, tokens = cq_ref.shape
     rows = attn_ref.shape[0]
     total = x_ref[...].astype(f32)
@@ -469,7 +481,7 @@
         normed, inv_std = norm_stats(acc[:, at])
         normed_ref[:, at] = normed
         inv_ref[:, at] = inv_std
-        low_ref[:, at] = (normed * gain_ref[:, 0:1]).astype(bf16)
+        low_ref[:, at] = (normed * gain_of(w_ref, 5 * feat, 0)).astype(bf16)
 
     by_columns(tokens, body)
     low = low_ref[...]
@@ -478,10 +490,10 @@
         cq_ref[g] = (query * (0.125 * LOG2E)).astype(bf16)
 
 
-def after_self(x_own, attn, small, gains, feat):
+def after_self(x_own, attn, small, feat):
     width, tokens = x_own.shape
     groups = small.shape[0]
-    args = (x_own, attn, small, gains)
+    args = (x_own, attn, small)
     outs = [
         jax.ShapeDtypeStruct((width, tokens), f32),
         jax.ShapeDtypeStruct((1, tokens), f32),
@@ -501,18 +513,19 @@
 
 
 def middle_kernel(
-    normed_one_ref, catt_ref, wc_ref, up_ref, down_ref, cot_ref, gain_ref,
-    out_ref, dcatt_ref, dy_ref, dcross_ref, glarge_ref, dg_two_ref, dg_three_ref,
+    place_ref, normed_one_ref, catt_ref, wc_ref, up_ref, down_ref, cot_ref,
+    out_ref, dcatt_ref, dy_ref, dcross_ref, gother_ref, gown_ref, dg_two_ref, dg_three_ref,
     acc, normed_two, inv_two, act, slope, h_fm, h_tm, d_fm, d_tm,
 ):
     i = pl.program_id(0)
     groups, feat, tokens = catt_ref.shape
+    half = groups // 2
     units = up_ref.shape[2]
     step = min(256, tokens)
 
     @pl.when(i == 0)
     def _():
-        total = normed_one_ref[...] * gain_ref[:, 0:1]
+        total = normed_one_ref[...] * gain_of(wc_ref, feat, 0)
         for g in range(groups):
             total = total + dot(wc_ref[g, :, :feat], catt_ref[g], 1, 0)
         acc[...] = total
@@ -521,7 +534,7 @@
             normed, inv_std = norm_stats(acc[:, at])
             normed_two[:, at] = normed
             inv_two[:, at] = inv_std
-            value = normed * gain_ref[:, 1:2]
+            value = normed * gain_of(wc_ref, feat, 1)
             acc[:, at] = value
             h_fm[:, at] = value.astype(bf16)
 
@@ -545,7 +558,7 @@
 
         def body(at):
             normed, inv_std = norm_stats(acc[:, at])
-            gain = gain_ref[:, 2:3]
+            gain = gain_of(wc_ref, feat, 2)
             out_ref[:, at] = (normed * gain).astype(bf16)
             grad = cot_ref[:, at].astype(f32)
             dg_three_ref[...] += grad * normed
@@ -558,13 +571,24 @@
 
     @pl.when(i >= groups)
     def _():
-        g = i - groups
+        g = other_first(i - groups, place_ref, half)
         for t in range(0, tokens, step):
             at = slice(t, t + step)
             back = dot(d_tm[at, :], down_ref[0], 1, 0) * slope[g, at, :].astype(f32)
             slope[g, at, :] = back.astype(bf16)
-        glarge_ref[0, :, units:] = dot(d_fm[...], act[g], 1, 0).astype(bf16)
-        glarge_ref[0, :, :units] = dot(h_fm[...], slope[g], 1, 0).astype(bf16)
+        g_down = dot(d_fm[...], act[g], 1, 0).astype(bf16)
+        g_up = dot(h_fm[...], slope[g], 1, 0).astype(bf16)
+
+        @pl.when(i < groups + half)
+        def _():
+            gother_ref[0, :, units:] = g_down
+            gother_ref[0, :, :units] = g_up
+
+        @pl.when(i >= groups + half)
+        def _():
+            gown_ref[0, :, units:] = g_down
+            gown_ref[0, :, :units] = g_up
+
         acc[...] += dot(up_ref[0], slope[g], 1, 1)
 
     @pl.when(i == 2 * groups - 1)
@@ -573,7 +597,7 @@
             grad = acc[:, at]
             normed = normed_two[:, at]
             dg_two_ref[...] += grad * normed
-            value = norm_back(grad, gain_ref[:, 1:2], normed, inv_two[:, at])
+            value = norm_back(grad, gain_of(wc_ref, feat, 1), normed, inv_two[:, at])
             dy_ref[:, at] = value
             dcross_ref[:, at] = value.astype(bf16)
 
@@ -583,63 +607,73 @@
             dcatt_ref[g] = dot(wc_ref[g, :, :feat], low, 0, 0).astype(bf16)
 
 
-def middle(normed_one, catt, small, large, cot, gains):
+def middle(place, normed_one, catt, small, large, cot):
     width, tokens = normed_one.shape
     groups, feat, _ = catt.shape
+    half = groups // 2
     units = large.shape[2] // 2
     lanes = min(128, tokens)
 
     def weight(kind):
-        return pl.BlockSpec((1, width, units), lambda i: (i % groups, 0, kind))
+        def index(i, p):
+            return jnp.where(i < groups, i, other_first(i - groups, p, half)), 0, kind
+
+        return pl.BlockSpec((1, width, units), index)
+
+    def grad_out(first):
+        return pl.BlockSpec(
+            (1, width, 2 * units), lambda i, p: (jnp.clip(i - first, 0, half - 1), 0, 0)
+        )
 
     outs = [
         jax.ShapeDtypeStruct((width, tokens), bf16),
         jax.ShapeDtypeStruct(catt.shape, bf16),
         jax.ShapeDtypeStruct((width, tokens), f32),
         jax.ShapeDtypeStruct((width, tokens), bf16),
-        jax.ShapeDtypeStruct(large.shape, bf16),
+        jax.ShapeDtypeStruct((half, width, 2 * units), bf16),
+        jax.ShapeDtypeStruct((half, width, 2 * units), bf16),
         jax.ShapeDtypeStruct((width, lanes), f32),
         jax.ShapeDtypeStruct((width, lanes), f32),
     ]
     specs = [whole(o) for o in outs]
-    specs[4] = pl.BlockSpec(
-        (1, width, 2 * units), lambda i: (jnp.maximum(i - groups, 0), 0, 0)
-    )
+    specs[4], specs[5] = grad_out(groups), grad_out(groups + half)
     return pl.pallas_call(
         middle_kernel,
-        grid=(2 * groups,),
-        in_specs=[
-            whole(normed_one),
-            whole(catt),
-            pl.BlockSpec((groups, width, 128), lambda i: (0, 0, 3)),
-            weight(0),
-            weight(1),
-            whole(cot),
-            whole(gains),
-        ],
-        out_specs=specs,
+        grid_spec=pltpu.PrefetchScalarGridSpec(
+            num_scalar_prefetch=1,
+            grid=(2 * groups,),
+            in_specs=[
+                whole(normed_one),
+                whole(catt),
+                pl.BlockSpec((groups, width, 128), lambda i, p: (0, 0, 3)),
+                weight(0),
+                weight(1),
+                whole(cot),
+            ],
+            out_specs=specs,
+            scratch_shapes=[
+                pltpu.VMEM((width, tokens), f32),
+                pltpu.VMEM((width, tokens), f32),
+                pltpu.VMEM((1, tokens), f32),
+                pltpu.VMEM((groups, tokens, units), bf16),
+                pltpu.VMEM((groups, tokens, units), bf16),
+                pltpu.VMEM((width, tokens), bf16),
+                pltpu.VMEM((tokens, width), bf16),
+                pltpu.VMEM((width, tokens), bf16),
+                pltpu.VMEM((tokens, width), bf16),
+            ],
+        ),
         out_shape=outs,
-        scratch_shapes=[
-            pltpu.VMEM((width, tokens), f32),
-            pltpu.VMEM((width, tokens), f32),
-            pltpu.VMEM((1, tokens), f32),
-            pltpu.VMEM((groups, tokens, units), bf16),
-            pltpu.VMEM((groups, tokens, units), bf16),
-            pltpu.VMEM((width, tokens), bf16),
-            pltpu.VMEM((tokens, width), bf16),
-            pltpu.VMEM((width, tokens), bf16),
-            pltpu.VMEM((tokens, width), bf16),
-        ],
         compiler_params=kernel_params(),
         cost_estimate=pl.CostEstimate(
             flops=12 * groups * width * units * tokens, bytes_accessed=8 * large.size, transcendentals=0
         ),
         name="middle",
-    )(normed_one, catt, small, large, large, cot, gains)
+    )(place, normed_one, catt, small, large, large, cot)
 
 
 def before_self_kernel(
-    dcq_ref, w_ref, dy_ref, normed_ref, inv_ref, gain_ref,
+    dcq_ref, w_ref, dy_ref, normed_ref, inv_ref,
     dattn_ref, dlow_ref, dy_one_ref, dg_ref, acc,
 ):
     groups, feat, tokens = dcq_ref.shape
@@ -654,7 +688,7 @@
         grad = acc[:, at]
         normed = normed_ref[:, at]
         dg_ref[...] += grad * normed
-        value = norm_back(grad, gain_ref[:, 0:1], normed, inv_ref[:, at])
+        value = norm_back(grad, gain_of(w_ref, 5 * feat, 0), normed, inv_ref[:, at])
         dy_one_ref[:, at] = value
         dlow_ref[:, at] = value.astype(bf16)
 
@@ -665,9 +699,9 @@
         dattn_ref[r, d] = dot(w_ref[g, :, 2 * feat : 3 * feat], low, 0, 0).astype(bf16)
 
 
-def before_self(d_cq, small, dy_two, normed_one, inv_one, gains, attn_shape):
+def before_self(d_cq, small, dy_two, normed_one, inv_one, attn_shape):
     width, tokens = dy_two.shape
-    args = (d_cq, small, dy_two, normed_one, inv_one, gains)
+    args = (d_cq, small, dy_two, normed_one, inv_one)
     outs = [
         jax.ShapeDtypeStruct(attn_shape, bf16),
         jax.ShapeDtypeStruct((width, tokens), bf16),
@@ -688,14 +722,15 @@
 
 def small_grads_kernel(
     place_ref, w_ref, chosen_ref, dckv_ref, attn_ref, dcq_ref, catt_ref, dlow_ref, h_ref,
-    dcross_ref, dg_one_ref, dg_two_ref, dg_three_ref, rest_ref, dchosen_ref, wide, acc, gain_cols,
-    *, paired,
+    dcross_ref, dg_one_ref, dg_two_ref, dg_three_ref, rother_ref, rown_ref, cother_ref, cown_ref,
+    wide, acc, gain_cols, *, paired,
 ):
     g = pl.program_id(0)
     feat2 = dckv_ref.shape[1]
     feat = feat2 // 2
     count, width, tokens = chosen_ref.shape
-    rows = count // 2
+    share = count // 2
+    half = pl.num_programs(0) // 2
 
     @pl.when(g == 0)
     def _():
@@ -709,20 +744,43 @@
 
     grad = dckv_ref[0]
     acc[...] += dot(w_ref[0][:, :feat2], grad, 1, 0)
-    rest_ref[0, :, :feat2] = dot(wide[...], grad, 1, 1).astype(bf16)
+    parts = [dot(wide[...], grad, 1, 1).astype(bf16)]
     pairs = ((dlow_ref, attn_ref[0, 0]), (h_ref, dcq_ref[0]), (dcross_ref, catt_ref[0]))
-    for k, (left, right) in enumerate(pairs):
-        at = feat2 + k * feat
-        rest_ref[0, :, at : at + feat] = dot(left[...], right, 1, 1).astype(bf16)
-    rest_ref[0, :, 5 * feat :] = gain_cols[...]
+    for left, right in pairs:
+        parts.append(dot(left[...], right, 1, 1).astype(bf16))
+    parts.append(gain_cols[...])
+
+    def put(ref):
+        at = 0
+        for part in parts:
+            ref[0, :, at : at + part.shape[1]] = part
+            at += part.shape[1]
+
+    @pl.when(g < half)
+    def _():
+        put(rother_ref)
+
+    @pl.when(g >= half)
+    def _():
+        put(rown_ref)
 
     @pl.when(g == pl.num_programs(0) - 1)
     def _():
         for n in range(count):
-            at = n
+            piece = acc[:, n * tokens : (n + 1) * tokens].astype(bf16)
             if paired:
-                at = (place_ref[1] ^ (n % 2)) * rows + (place_ref[0] ^ (n // 2))
-            dchosen_ref[at] = acc[:, n * tokens : (n + 1) * tokens].astype(bf16)
+                ref = cother_ref if n % 2 else cown_ref
+                ref[place_ref[0] ^ (n // 2)] = piece
+                continue
+            mine = place_ref[1] == n // share
+
+            @pl.when(mine)
+            def _():
+                cown_ref[n % share] = piece
+
+            @pl.when(jnp.logical_not(mine))
+            def _():
+                cother_ref[n % share] = piece
 
 
 def small_grads(place, small, chosen, d_ckv, attn, d_cq, catt, d_low, h_low, d_cross, dgs, paired):
@@ -731,17 +789,30 @@
     feat = feat2 // 2
     tokens = d_low.shape[1]
     rows = attn.shape[0]
-    piece = pl.BlockSpec((1, feat, tokens), lambda g, p: (g, 0, 0))
+    half = groups // 2
+
+    def order(g, p):
+        return other_first(g, p, half)
+
+    def rest_out(first):
+        return pl.BlockSpec((1, width, cols), lambda g, p: (jnp.clip(g - first, 0, half - 1), 0, 0))
+
+    piece = pl.BlockSpec((1, feat, tokens), lambda g, p: (order(g, p), 0, 0))
+    share = jax.ShapeDtypeStruct((chosen.shape[0] // 2,) + chosen.shape[1:], bf16)
+    rest_shape = jax.ShapeDtypeStruct((half, width, cols), bf16)
     return pl.pallas_call(
         functools.partial(small_grads_kernel, paired=paired),
         grid_spec=pltpu.PrefetchScalarGridSpec(
             num_scalar_prefetch=1,
             grid=(groups,),
             in_specs=[
-                pl.BlockSpec((1, width, 2 * 128), lambda g, p: (g, 0, 0)),
+                pl.BlockSpec((1, width, 2 * 128), lambda g, p: (order(g, p), 0, 0)),
                 whole(chosen),
-                pl.BlockSpec((1, feat2, keys), lambda g, p: (g, 0, 0)),
-                pl.BlockSpec((1, 1, feat, tokens), lambda g, p: (g % rows, g // rows, 0, 0)),
+                pl.BlockSpec((1, feat2, keys), lambda g, p: (order(g, p), 0, 0)),
+                pl.BlockSpec(
+                    (1, 1, feat, tokens),
+                    lambda g, p: (order(g, p) % rows, order(g, p) // rows, 0, 0),
+                ),
                 piece,
                 piece,
                 whole(d_low),
@@ -749,17 +820,14 @@
                 whole(d_cross),
             ]
             + [whole(v) for v in dgs],
-            out_specs=[pl.BlockSpec((1, width, cols), lambda g, p: (g, 0, 0)), whole(chosen)],
+            out_specs=[rest_out(0), rest_out(half), whole(share), whole(share)],
             scratch_shapes=[
                 pltpu.VMEM((width, keys), bf16),
                 pltpu.VMEM((width, keys), f32),
                 pltpu.VMEM((width, cols - 5 * feat), bf16),
             ],
         ),
-        out_shape=[
-            jax.ShapeDtypeStruct(small.shape, bf16),
-            jax.ShapeDtypeStruct(chosen.shape, bf16),
-        ],
+        out_shape=[rest_shape, rest_shape, share, share],
         compiler_params=kernel_params(),
         name="small_grads",
     )(place, small, chosen, d_ckv, attn, d_cq, catt, d_low, h_low, d_cross, *dgs)
@@ -854,14 +922,17 @@
     x_swapped = swap_cores(x_in)
     x_own = across_cols(x_swapped)
     x_rows = row_gather(x_own)
-    spare = 512 - 5 * feat
+    tied, _ = lax.optimization_barrier(
+        ((w_cross_kv, w_out, w_cross_q, w_cross_out, w_up, w_down, ln_gains), x_swapped)
+    )
     small = jnp.concatenate(
         [
-            w_cross_kv.reshape(part_width, 2 * feat),
-            w_out.reshape(feat, part_width).T,
-            w_cross_q.reshape(part_width, feat),
-            w_cross_out.reshape(feat, part_width).T,
-            jnp.zeros((part_width, spare), bf16),
+            tied[0].reshape(part_width, 2 * feat),
+            tied[1].reshape(feat, part_width).T,
+            tied[2].reshape(part_width, feat),
+            tied[3].reshape(feat, part_width).T,
+            tied[6].T,
+            jnp.zeros((part_width, 512 - 5 * feat - 3), bf16),
         ],
         axis=1,
     )
@@ -871,11 +942,9 @@
         value = lax.all_gather(value, everywhere, axis=0)
         return value.reshape(blocks, width, value.shape[-1])
 
-    small, _ = lax.optimization_barrier((small, x_swapped))
     small_all = gather_all(small)
-    large, _ = lax.optimization_barrier((jnp.concatenate([w_up, w_down.T], axis=1), x_own))
+    large, _ = lax.optimization_barrier((jnp.concatenate([tied[4], tied[5].T], axis=1), x_own))
     large_all = gather_all(large)
-    gains = lax.all_gather(ln_gains.astype(f32).T, "col", axis=0, tiled=True)
 
     query, kv_own = project(place, near, x_rows, feat)
     query = query.reshape(rows, dp, heads, HALF, tokens)
@@ -899,7 +968,7 @@
     meta = jnp.concatenate([seq_prefix[None], q_start] + places).astype(jnp.int32)
     mixed, lse = attend(meta, query, kv_list, True, "self_attention")
     attn = lax.all_to_all(mixed, "row", 0, 0, tiled=True).reshape(rows, dp, feat, tokens)
-    normed_one, inv_one, h_low, cross_q = after_self(x_own, attn, small_all, gains, feat)
+    normed_one, inv_one, h_low, cross_q = after_self(x_own, attn, small_all, feat)
     cross_q = cross_q.reshape(1, dp, rows, heads, HALF, tokens)
 
     picked = bank_rows.shape[1] // rows
@@ -921,40 +990,47 @@
     catt_flat = catt.reshape(blocks, feat, tokens)
 
     cot = to_tokens(out_grad)
-    block_out, d_catt, dy_two, d_cross, g_large, dg_two, dg_three = middle(
-        normed_one, catt_flat, small_all, large_all, cot, gains
+    block_out, d_catt, dy_two, d_cross, g_other, g_own, dg_two, dg_three = middle(
+        place, normed_one, catt_flat, small_all, large_all, cot
     )
     block_out = to_home(block_out)
 
-    def scatter(value):
-        value = value.reshape(dp, rows, cols, part_width, value.shape[-1])
-        for name in everywhere:
-            value = lax.psum_scatter(value, name, scatter_dimension=0, tiled=False)
-        return value
-
-    large_grad = scatter(g_large)
+
+    def with_core(own, got):
+        return (own.astype(f32) + got.astype(f32)).astype(bf16)
+
+    g_other = lax.ppermute(g_other, "dp", swap)
     d_cq, d_ckv = attend_back(
         meta, cross_q, [ckv], d_catt.reshape(catt.shape), catt, lse_cross, False, [bf16],
         "cross_attention_back",
     )
+    g_other, d_cq = lax.optimization_barrier((g_other, d_cq))
+    large_grad = with_core(g_own, g_other).reshape(rows * cols, part_width, 2 * units)
+    large_grad = lax.psum_scatter(large_grad, ("row", "col"), scatter_dimension=0, tiled=False)
     d_cq = d_cq.reshape(blocks, feat, tokens)
     d_ckv = d_ckv.reshape(blocks, 2 * feat, d_ckv.shape[-1])
     d_attn, d_low, dy_one, dg_one = before_self(
-        d_cq, small_all, dy_two, normed_one, inv_one, gains, attn.shape
+        d_cq, small_all, dy_two, normed_one, inv_one, attn.shape
     )
     d_mixed = lax.all_to_all(d_attn, "row", 0, 0, tiled=True).reshape(mixed.shape)
-    rest, d_chosen = small_grads(
+    rest_other, rest, chosen_other, d_chosen = small_grads(
         place, small_all, chosen, d_ckv, attn, d_cq, catt_flat, d_low, h_low, d_cross,
         (dg_one, dg_two, dg_three), sub == 1,
     )
+    rest_other = lax.ppermute(rest_other, "dp", swap)
+    d_chosen = with_core(d_chosen, lax.ppermute(chosen_other, "dp", swap))
+    d_chosen = d_chosen.reshape(rows, sub * width, c_tokens)
+    d_chosen = lax.all_to_all(d_chosen, "row", 0, 0, tiled=True)
 
     types = [f32] + [bf16] * (len(kv_list) - 1) if sub == 1 else [bf16] * len(kv_list)
     d_query, *d_kv = attend_back(
         meta, query, kv_list, d_mixed, mixed, lse, True, types, "self_attention_back"
     )
-    d_query, large_grad, d_chosen, rest = lax.optimization_barrier(
-        (d_query, large_grad, d_chosen, rest)
-    )
+    d_query, d_chosen, rest_other, block_out = lax.optimization_barrier(
+        (d_query, d_chosen, rest_other, block_out)
+    )
+    rest = with_core(rest, rest_other).reshape(rows, cols, part_width, -1)
+    rest = lax.psum_scatter(rest, "row", scatter_dimension=0, tiled=False)
     if sub == 1:
         d_kv = [d_kv[0], lax.ppermute(d_kv[1], "dp", swap)]
     else:
@@ -966,30 +1042,36 @@
         d_kv = [d_kv]
     kv_shape = (rows, dp, 2, feat, tokens)
     d_kv = [value.reshape(kv_shape) for value in d_kv]
-    dx_part, g_qkv = project_back(
+    dx_part, qkv_other, g_qkv = project_back(
         place, near, x_rows, d_query.reshape(rows, dp, feat, tokens), d_kv
     )
     dx_part = lax.all_to_all(dx_part, "row", 0, 0, tiled=True)
     dx = dy_one + jnp.sum(dx_part.astype(f32), axis=0)
     x_grad = to_home(dx.astype(bf16)).astype(f32)
 
-    d_chosen = d_chosen.reshape(dp, rows, sub, width, c_tokens)
-    d_chosen = lax.psum_scatter(d_chosen, "dp", scatter_dimension=0, tiled=False)
-    d_chosen = lax.psum_scatter(d_chosen, "row", scatter_dimension=0, tiled=False)
+    d_chosen = jnp.sum(d_chosen.astype(f32), axis=0).astype(bf16)
     if sub > 1:
         d_chosen = lax.psum_scatter(
-            d_chosen, "col", scatter_dimension=0, tiled=True, axis_index_groups=groups
+            d_chosen.reshape(sub, width, c_tokens), "col", scatter_dimension=0, tiled=True,
+            axis_index_groups=groups,
         )
     d_chosen = d_chosen.reshape(width, c_tokens)
-    d_chosen = lax.all_gather(to_home(d_chosen), "row", axis=2, tiled=True)
-    hot_all = (bank_rows[:, :, None] == bank_ids[None, None, :]).astype(bf16)
+    d_chosen = jnp.concatenate(row_gather(to_home(d_chosen)), axis=2)
+    pick_rows = jnp.concatenate(
+        [
+            lax.dynamic_slice_in_dim(bank_rows, (r_pos ^ k) * picked, picked, 1)
+            for k in range(rows)
+        ],
+        axis=1,
+    )
+    hot_all = (pick_rows[:, :, None] == bank_ids[None, None, :]).astype(bf16)
     bank_grad = mm("swp,spn->swn", d_chosen, hot_all)
 
+    qkv = with_core(g_qkv, lax.ppermute(qkv_other, "dp", swap))
+    last = jnp.concatenate([rest, qkv.reshape(cols, part_width, -1)], axis=2)
+    last = lax.psum_scatter(last, "col", scatter_dimension=0, tiled=False).astype(f32)
+    rest, qkv_grad = last[:, :512], last[:, 512:]
     large_grad = large_grad.astype(f32)
-    rest = scatter(rest).astype(f32)
-    qkv_grad = g_qkv.reshape(dp, cols, part_width, g_qkv.shape[-1])
-    qkv_grad = lax.psum_scatter(qkv_grad, "dp", scatter_dimension=0, tiled=False)
-    qkv_grad = lax.psum_scatter(qkv_grad, "col", scatter_dimension=0, tiled=False).astype(f32)
 
     return (
         block_out,

time: 642 us -> 707 us (1.10)
  waiting for transfers between devices: 170 us -> 295 us
  blocking collectives: 108 us -> 26.7 us
  other arithmetic: 20.1 us -> 38.2 us
  starting transfers between devices: 46.5 us -> 59.3 us
  local copies, waits for them, and re-layouts: 35.1 us -> 26 us
    reduce_scatter x7 -> x2, waiting for transfers between devices: 37.8 us -> 136 us  [the longest x1 97.3 us: per_device(): lax.psum_scatter(large_grad, ('row', 'col'), scatter_dimension=0, tiled=F...]
    all_gather x2 -> x0, blocking collectives: 58.2 us -> none  [the longest x1 38.8 us: per_device(): gains = lax.all_gather(ln_gains.astype(f32).T, 'col', axis=0, tiled=True)]
    all_to_all x0 -> x2, waiting for transfers between devices: none -> 38.4 us  [the longest x1 38.4 us: per_device(): dx_part = lax.all_to_all(dx_part, 'row', 0, 0, tiled=True)]
    all_to_all x3 -> x2, waiting for transfers between devices: 38.7 us -> 13.8 us  [to_home(): lax.all_to_all(value.reshape(cols, part_width, take), 'col', 0, 0, tiled=...]
    all_to_all x1, blocking collectives: 48.1 us -> 24.6 us  [to_home(): lax.all_to_all(value.reshape(cols, part_width, take), 'col', 0, 0, tiled=...]
    ppermute x8 -> x12, waiting for transfers between devices: 32.1 us -> 54.6 us  [send(): return lax.ppermute(v, 'row', [(i, i ^ k) for i in range(rows)])]
    unnamed x16 -> x7, waiting for transfers between devices: 20.4 us -> 0.12 us
    convert_element_type x1 -> x5, other arithmetic: 0.99 us -> 18.1 us  [the longest x4 17 us: with_core(): return (own.astype(f32) + got.astype(f32)).astype(bf16)]
  transfers between devices with their start and end apart: 38 -> 40, of which waited for: 16 -> 20; matrix products, arithmetic and copies ran while one was open for 8% -> 8% of each run, Pallas kernels for 29% -> 26%
where the time goes in v4:
time: 707 us; the launch traced here: 698 us
  waiting for transfers between devices  295 us (42%)
  Pallas kernels  226 us (32%)
  starting transfers between devices  59.3 us (8%)
  other arithmetic  38.2 us (5%)
  blocking collectives  26.7 us (4%)
  local copies, waits for them, and re-layouts  26 us (4%)
  between operations  15.6 us (2%)
  matrix products  11.1 us (2%)
    reduce_scatter x1, waiting for transfers between devices, per_device(): lax.psum_scatter(large_grad, ('row', 'col'), scatter_dimension=0, tiled=F...  97.3 us
    pallas_call x2, Pallas kernels, attend_back(): pl.pallas_call(functools.partial(attend_back_kernel, sources=len(kv_list)...  70.9 us
    ppermute x12, waiting for transfers between devices, send(): return lax.ppermute(v, 'row', [(i, i ^ k) for i in range(rows)])  54.6 us
    pallas_call x1, Pallas kernels, middle(): pl.pallas_call(middle_kernel, grid_spec=pltpu.PrefetchScalarGridSpec(num_...  43.1 us
    pallas_call x2, Pallas kernels, attend(): pl.pallas_call(functools.partial(attend_kernel, sources=len(kv_list), n_q...  41.3 us
    reduce_scatter x1, waiting for transfers between devices, per_device(): lax.psum_scatter(last, 'col', scatter_dimension=0, tiled=False).astype(f32)  38.6 us
    all_to_all x1, waiting for transfers between devices, per_device(): dx_part = lax.all_to_all(dx_part, 'row', 0, 0, tiled=True)  38.4 us
    all_to_all x3, waiting for transfers between devices, across_cols(): lax.all_to_all(value, 'col', 0, 0, tiled=True)  27.3 us
  transfers between devices with their start and end apart: 40, of which 20 were waited for; matrix products, arithmetic and copies ran while one was open for 8% of the time, Pallas kernels for 26%

profile of v4, /device:TPU:0, one launch (start us, length us, event | category | flops | bytes accessed | tf_op | source)
XLA Modules:
  0.0 697.9 jit_solution(1002955811037480392)
XLA Ops:
  16.0 6.4 all-to-all-start
  23.1 27.3 %all-to-all-done = bf16[4,192,512]{2,1,0:T(8,128)(2,1)} async-done(((bf16[4,192,512]{2,1,0:T(8,128)(2,1)}), bf16[4,192,512]{2,1,0:T(8,128)(2,1)}, u32[]{:S(2)}, u32[]{:S(2)}) %all-to-all-start) | async-done | bytes 786464 | tf_op jit(solution)/shard_map/all_to_all | solution.py:884
  53.5 18.0 %collective-permute-done.2.refs_2_ = bf16[768,512]{1,0:T(8,128)(2,1)S(1)} collective-permute-done((bf16[768,512]{1,0:T(8,128)(2,1)}, bf16[768,512]{1,0:T(8,128)(2,1)S(1)}, u32[]{:S(2)}, u32[]{:S(2)}) %collective-permute-start.2) | collective-permute-done | bytes 786464 | tf_op jit(solution)/shard_map/ppermute | solution.py:895
  78.3 10.7 %collective-permute-done.3 = bf16[384,512]{1,0:T(8,128)(2,1)S(1)} collective-permute-done((bf16[384,512]{1,0:T(8,128)(2,1)}, bf16[384,512]{1,0:T(8,128)(2,1)S(1)}, u32[]{:S(2)}, u32[]{:S(2)}) %collective-permute-start.3) | collective-permute-done | bytes 393248 | tf_op jit(solution)/shard_map/ppermute | solution.py:895
  89.9 1.8 constant_dynamic-update-slice_fusion.refs_3_
  91.7 6.6 project.1
  102.1 1.9 broadcast_select_fusion.4
  104.1 2.0 all-reduce.1
  108.1 3.4 all-to-all-start.2
  111.5 28.3 %self_attention.1 = (bf16[4,2,3,32,512]{4,3,2,1,0:T(8,128)(2,1)}, f32[3,4,1,512]{3,2,1,0:T(1,128)S(1)}) custom-call(s32[13]{0:T(128)S(1)} %pad_add_fusion.1.refs_0_, bf16[4,2,3,32,512]{4,3,2,1,0:T(8,128)(2,1)S(1)} %bitcast.78, bf16[4,2,2,3,32,512]{5,4,3,2,1,0:T(8,128)(2,1)S(1)} %bitcast.77, bf16[4,2,2,3,32,512]{5,4,3,2,1,0:T(8,128)(2,1)} %collective-permute-done.5.refs_3_), custom_call_target="tpu_custom_call" | custom-call | flops 12884901888 | bytes 6291456 | tf_op jit(solution)/shard_map/self_attention/pallas_call | solution.py:238
  139.9 3.8 all-to-all-start.1
  145.7 8.0 %all-to-all-done.1 = bf16[4,2,3,32,512]{4,3,2,1,0:T(8,128)(2,1)S(1)} async-done(((bf16[4,2,3,32,512]{4,3,2,1,0:T(8,128)(2,1)}), bf16[4,2,3,32,512]{4,3,2,1,0:T(8,128)(2,1)S(1)}, u32[]{:S(2)}, u32[]{:S(2)}) %all-to-all-start.1) | async-done | bytes 786464 | tf_op jit(solution)/shard_map/all_to_all | solution.py:970
  153.7 5.1 all-to-all-start.3
  161.9 9.3 %collective-permute-done.9 = bf16[2,768,128]{2,1,0:T(8,128)(2,1)S(1)} collective-permute-done((bf16[2,768,128]{2,1,0:T(8,128)(2,1)S(1)}, bf16[2,768,128]{2,1,0:T(8,128)(2,1)S(1)}, u32[]{:S(2)}, u32[]{:S(2)}) %collective-permute-start.9) | collective-permute-done | bytes 393248 | tf_op jit(solution)/shard_map/ppermute | solution.py:895
  172.7 3.5 collective-permute-done.8
  177.9 1.8 collective-permute-done.10
  179.6 2.3 collective-permute-done.11
  183.2 8.9 %cross_kv.1 = bf16[8,192,1024]{2,1,0:T(8,128)(2,1)} custom-call(bf16[8,768,512]{2,1,0:T(8,128)(2,1)} %bitcast.83, bf16[8,768,128]{2,1,0:T(8,128)(2,1)} %copy-done.13), custom_call_target="tpu_custom_call" | custom-call | tf_op jit(solution)/shard_map/cross_kv/pallas_call | solution.py:455
  192.1 9.0 %after_self.1 = (f32[768,512]{1,0:T(8,128)}, f32[1,512]{1,0:T(1,128)}, bf16[768,512]{1,0:T(8,128)(2,1)}, bf16[8,96,512]{2,1,0:T(8,128)(2,1)}) custom-call(bf16[768,512]{1,0:T(8,128)(2,1)} %bitcast.5.refs_0_.x_ref, bf16[4,2,96,512]{3,2,1,0:T(8,128)(2,1)} %bitcast.90, bf16[8,768,512]{2,1,0:T(8,128)(2,1)} %bitcast.84), custom_call_target="tpu_custom_call" | custom-call | tf_op jit(solution)/shard_map/after_self/pallas_call | solution.py:503
  202.2 12.9 %cross_attention.1 = (bf16[1,2,4,3,32,512]{5,4,3,2,1,0:T(8,128)(2,1)S(1)}, f32[12,1,1,512]{3,2,1,0:T(1,128)S(1)}) custom-call(s32[13]{0:T(128)S(1)} %pad_add_fusion.1.refs_0_, bf16[1,2,4,3,32,512]{5,4,3,2,1,0:T(8,128)(2,1)S(1)} %bitcast.80, bf16[1,2,4,2,3,32,1024]{6,5,4,3,2,1,0:T(8,128)(2,1)S(1)} %bitcast.70), custom_call_target="tpu_custom_call" | custom-call | flops 3221225472 | bytes 6291456 | tf_op jit(solution)/shard_map/cross_attention/pallas_call | solution.py:238
  216.0 8.1 %all-gather.11.cloned.1.call-done = bf16[6144,768]{1,0:T(8,128)(2,1)} async-done(((bf16[192,768]{1,0:T(8,128)(2,1)}), bf16[6144,768]{1,0:T(8,128)(2,1)}) %all-gather.11.cloned.1.call-update) | async-done | bytes 9437200 | tf_op jit(solution)/shard_map/all_gather | solution.py:942
  224.1 43.1 %middle.1 = (bf16[768,512]{1,0:T(8,128)(2,1)}, bf16[8,96,512]{2,1,0:T(8,128)(2,1)}, f32[768,512]{1,0:T(8,128)}, bf16[768,512]{1,0:T(8,128)(2,1)}, bf16[4,768,768...) custom-call(s32[2]{0:T(128)} %pad_add_fusion.2.place_ref, ...), custom_call_target="tpu_custom_call" | custom-call | flops 14495514624 | bytes 37748736 | tf_op jit(solution)/shard_map/middle/pallas_call | solution.py:640
  267.6 24.6 %all_to_all.50 = bf16[4,192,512]{2,1,0:T(8,128)(2,1)S(1)} all-to-all(bf16[4,192,512]{2,1,0:T(8,128)(2,1)} %bitcast.101), channel_id=1, replica_groups=mesh['dp'=2,'row'=4,'col'=4] {'col'}, dimensions={0} | all-to-all | bytes 1572864 | tf_op jit(solution)/shard_map/all_to_all | solution.py:904
  292.3 21.4 %cross_attention_back.1 = (bf16[1,2,4,3,32,512]{5,4,3,2,1,0:T(8,128)(2,1)S(1)}, bf16[1,2,4,2,3,32,1024]{6,5,4,3,2,1,0:T(8,128)(2,1)}) custom-call(s32[13]{0:T(128)S(1)} %pad_add_fusion.1.refs_0_, bf16[1,2,4,3,32,512]{5,4,3,2,1,0:T(8,128)(2,1)S(1)} %bitcast.81, bf16[1,2,4,2,3,32,1024]{6,5,4,3,2,1,0:T(8,128)(2,1)} %bitcast.69, ...), custom_call_target="tpu_custom_call" | custom-call | flops 8053063680 | bytes 6291456 | tf_op jit(solution)/shard_map/cross_attention_back/pallas_call | solution.py:259
  314.6 10.3 %before_self.1 = (bf16[4,2,96,512]{3,2,1,0:T(8,128)(2,1)}, bf16[768,512]{1,0:T(8,128)(2,1)}, f32[768,512]{1,0:T(8,128)}, f32[768,128]{1,0:T(8,128)}) custom-call(bf16[8,96,512]{2,1,0:T(8,128)(2,1)} %bitcast.67, bf16[8,768,512]{2,1,0:T(8,128)(2,1)} %bitcast.86, f32[768,512]{1,0:T(8,128)} %get-tuple-element.78.dy_ref, ...), custom_call_target="tpu_custom_call" | custom-call | tf_op jit(solution)/shard_map/before_self/pallas_call | solution.py:711
  325.0 23.2 %small_grads.1 = (bf16[4,768,512]{2,1,0:T(8,128)(2,1)}, bf16[4,768,512]{2,1,0:T(8,128)(2,1)}, bf16[4,768,128]{2,1,0:T(8,128)(2,1)}, bf16[4,768,128]{2,1,0:T(8,128)(2,1)}) custom-call(s32[2]{0:T(128)} %pad_add_fusion.2.place_ref, bf16[8,768,512]{2,1,0:T(8,128)(2,1)} %bitcast.87, bf16[8,768,128]{2,1,0:T(8,128)(2,1)} %copy-done.13, ...), custom_call_target="tpu_custom_call" | custom-call | tf_op jit(solution)/shard_map/small_grads/pallas_call | solution.py:803
  348.7 3.5 all-to-all-start.4
  355.4 2.3 add_convert_fusion.3
  357.7 5.8 all-to-all-done.4
  363.5 4.2 all-to-all-start.5
  368.0 49.5 %self_attention_back.1 = (bf16[4,2,3,32,512]{4,3,2,1,0:T(8,128)(2,1)S(1)}, f32[4,2,2,3,32,512]{5,4,3,2,1,0:T(8,128)}, bf16[4,2,2,3,32,512]{5,4,3,2,1,0:T(8,128)(2,1)S(1)}) custom-call(s32[13]{0:T(128)S(1)} %pad_add_fusion.1.refs_0_, bf16[4,2,3,32,512]{4,3,2,1,0:T(8,128)(2,1)S(1)} %bitcast.79, bf16[4,2,2,3,32,512]{5,4,3,2,1,0:T(8,128)(2,1)} %bitcast.76, ...), custom_call_target="tpu_custom_call" | custom-call | flops 32212254720 | bytes 6291456 | tf_op jit(solution)/shard_map/self_attention_back/pallas_call | solution.py:259
  418.4 5.5 add_convert_fusion.1
  424.0 7.1 %add_convert_fusion = bf16[4,768,768]{2,1,0:T(8,128)(2,1)} fusion(bf16[4,768,768]{2,1,0:T(8,128)(2,1)} %collective-permute-done.13, bf16[4,768,768]{2,1,0:T(8,128)(2,1)} %get-tuple-element.105), kind=kLoop, calls=%fused_computation.3 | loop fusion | flops 9437184 | bytes 14155776 | tf_op jit(solution)/shard_map/convert_element_type | solution.py:1000
  431.2 2.0 reduce_sum.22
  433.2 5.8 all-to-all-start.9
  439.1 12.7 %project_back.1 = (bf16[4,768,512]{2,1,0:T(8,128)(2,1)}, bf16[768,384]{1,0:T(8,128)(2,1)}, bf16[768,384]{1,0:T(8,128)(2,1)}) custom-call(s32[2]{0:T(128)} %pad_add_fusion.2.place_ref, bf16[2,768,384]{2,1,0:T(8,128)(2,1)} %bitcast.93, bf16[768,512]{1,0:T(8,128)(2,1)} %bitcast.5.refs_0_.x_ref, bf16[768,512]{1,0:T(8,128)(2,1)} %copy-done.16, ...), custom_call_target="tpu_custom_call" | custom-call | tf_op jit(solution)/shard_map/project_back/pallas_call | solution.py:411
  451.8 4.1 all-to-all-start.7
  458.0 2.1 add_convert_fusion.4
  460.1 2.2 copy.51
  462.4 38.4 %all-to-all-done.7 = bf16[4,768,512]{2,1,0:T(8,128)(2,1)S(1)} async-done(((bf16[4,768,512]{2,1,0:T(8,128)(2,1)}), bf16[4,768,512]{2,1,0:T(8,128)(2,1)S(1)}, u32[]{:S(2)}, u32[]{:S(2)}) %all-to-all-start.7) | async-done | bytes 3145760 | tf_op jit(solution)/shard_map/all_to_all | solution.py:1048
  503.3 4.9 all-to-all-start.8
  513.7 3.7 collective-permute-done.21
  519.6 2.5 collective-permute-done.22
  522.1 2.3 collective-permute-done.23
  524.4 13.8 %all-to-all-done.8 = bf16[4,192,512]{2,1,0:T(8,128)(2,1)S(1)} async-done(((bf16[4,192,512]{2,1,0:T(8,128)(2,1)}), bf16[4,192,512]{2,1,0:T(8,128)(2,1)S(1)}, u32[]{:S(2)}, u32[]{:S(2)}) %all-to-all-start.8) | async-done | bytes 786464 | tf_op jit(solution)/shard_map/all_to_all | solution.py:904
  538.3 9.4 %fusion = f32[2,192,4096]{2,1,0:T(8,128)} fusion(bf16[2,192,1024]{2,1,0:T(8,128)(2,1)S(1)} %maximum_dynamic-update-slice_fusion, s32[2,1024]{1,0:T(2,128)S(1)} %pad_add_fusion), kind=kOutput, calls=%fused_computation.1 | convolution fusion | flops 3229614080 | bytes 7086080 | tf_op jit(solution)/shard_map/swp,spn->swn/dot_general | solution.py:837
  549.2 97.3 %reduce-scatter.8.cloned.1.call-done = bf16[1,192,768]{2,1,0:T(8,128)(2,1)} async-done(((bf16[16,192,768]{2,1,0:T(8,128)(2,1)}), bf16[1,192,768]{2,1,0:T(8,128)(2,1)}) %reduce-scatter.8.cloned.1.call-update) | async-done | bytes 294928 | tf_op jit(solution)/shard_map/reduce_scatter | solution.py:1009
  648.5 38.6 %reduce-scatter.6.cloned.1.call-done = bf16[1,192,896]{1,2,0:T(8,128)(2,1)} async-done(((bf16[4,192,896]{1,2,0:T(8,128)(2,1)}), bf16[1,192,896]{1,2,0:T(8,128)(2,1)}) %reduce-scatter.6.cloned.1.call-update) | async-done | bytes 344080 | tf_op jit(solution)/shard_map/reduce_scatter | solution.py:1072
  (193 shorter events, 62.7 us)
Async XLA Ops:
  7.2 91.2 %copy-start = (bf16[2,192,4096]{2,1,0:T(8,128)(2,1)S(1)}, bf16[2,192,4096]{2,1,0:T(8,128)(2,1)}, u32[]{:S(2)}) copy-start(bf16[2,192,4096]{2,1,0:T(8,128)(2,1)} %param.15) | copy-start | bytes 9437188
  7.2 84.5 %all-gather.7.cloned.1.call-start = ((), (), s32[]{:S(2)}) async-start(), calls=%async_computation.15 | async-start | bytes 1327104 | tf_op jit(solution)/shard_map/all_gather | solution.py:921
  9.2 172.9 %all-gather.9.cloned.1.call-start = ((), (), s32[]{:S(2)}) async-start(), calls=%async_computation.16 | async-start | bytes 6488064 | tf_op jit(solution)/shard_map/all_gather | solution.py:942
  10.4 1.9 collective-permute-start
  16.0 34.4 %all-to-all-start = ((bf16[4,192,512]{2,1,0:T(8,128)(2,1)}), bf16[4,192,512]{2,1,0:T(8,128)(2,1)}, u32[]{:S(2)}, u32[]{:S(2)}) async-start(bf16[4,192,512]{2,1,0:T(8,128)(2,1)} %pad_maximum_fusion.1), calls=%async_computation | async-start | bytes 1572864 | tf_op jit(solution)/shard_map/all_to_all | solution.py:884
  22.4 201.7 %all-gather.11.cloned.1.call-start = ((), (), s32[]{:S(2)}) async-start(), calls=%async_computation.17 | async-start | bytes 9732096 | tf_op jit(solution)/shard_map/all_gather | solution.py:942
  50.5 21.0 %collective-permute-start.2 = (bf16[768,512]{1,0:T(8,128)(2,1)}, bf16[768,512]{1,0:T(8,128)(2,1)S(1)}, u32[]{:S(2)}, u32[]{:S(2)}) collective-permute-start(bf16[768,512]{1,0:T(8,128)(2,1)} %bitcast.5.refs_0_.x_ref), channel_id=1, source_target_pairs={{0,8},{4,12},{8,0},{12,4},{1,9},{5,13},{9,1},{13,5},{2,10},{6,14},... | collective-permute-start | bytes 2359304 | tf_op jit(solution)/shard_map/ppermute | solution.py:895
  52.0 22.6 %collective-permute-start.1 = (bf16[768,512]{1,0:T(8,128)(2,1)}, bf16[768,512]{1,0:T(8,128)(2,1)S(1)}, u32[]{:S(2)}, u32[]{:S(2)}) collective-permute-start(bf16[768,512]{1,0:T(8,128)(2,1)} %bitcast.5.refs_0_.x_ref), channel_id=1, source_target_pairs={{0,4},{4,0},{8,12},{12,8},{1,5},{5,1},{9,13},{13,9},{2,6},{6,2},{1... | collective-permute-start | bytes 2359304 | tf_op jit(solution)/shard_map/ppermute | solution.py:895
  73.1 16.0 %collective-permute-start.3 = (bf16[384,512]{1,0:T(8,128)(2,1)}, bf16[384,512]{1,0:T(8,128)(2,1)S(1)}, u32[]{:S(2)}, u32[]{:S(2)}) collective-permute-start(bf16[384,512]{1,0:T(8,128)(2,1)} %slice.112), channel_id=1, source_target_pairs={{0,4},{4,0},{8,12},{12,8},{1,5},{5,1},{9,13},{13,9},{2,6},{6,2},{1... | collective-permute-start | bytes 1179656 | tf_op jit(solution)/shard_map/ppermute | solution.py:895
  76.3 13.6 %collective-permute-start.4 = (bf16[384,512]{1,0:T(8,128)(2,1)}, bf16[384,512]{1,0:T(8,128)(2,1)}, u32[]{:S(2)}, u32[]{:S(2)}) collective-permute-start(bf16[384,512]{1,0:T(8,128)(2,1)} %slice.113), channel_id=1, source_target_pairs={{0,8},{4,12},{8,0},{12,4},{1,9},{5,13},{9,1},{13,5},{2,10},{6,14},... | collective-permute-start | bytes 1179656 | tf_op jit(solution)/shard_map/ppermute | solution.py:895
  98.3 13.2 %collective-permute-start.5 = (bf16[4,2,2,3,32,512]{5,4,3,2,1,0:T(8,128)(2,1)}, bf16[4,2,2,3,32,512]{5,4,3,2,1,0:T(8,128)(2,1)}, u32[]{:S(2)}, u32[]{:S(2)}) collective-permute-start(bf16[4,2,2,3,32,512]{5,4,3,2,1,0:T(8,128)(2,1)} %bitcast.75), channel_id=1, source_target_pairs={{0,16},{16,0},{1,17},{17,1},{2,18},{18,2},{3,19},{19,3},{4,20},{20... | collective-permute-start | bytes 4718600 | tf_op jit(solution)/shard_map/ppermute | solution.py:958
  100.0 11.5 %copy-start.7 = (bf16[4,2,2,96,512]{4,3,2,1,0:T(8,128)(2,1)S(1)}, bf16[4,2,2,96,512]{4,3,2,1,0:T(8,128)(2,1)}, u32[]{:S(2)}) copy-start(bf16[4,2,2,96,512]{4,3,2,1,0:T(8,128)(2,1)} %get-tuple-element.60) | copy-start | bytes 4718596
  100.1 7.3 %collective-permute-start.6 = (bf16[2,192,128]{2,1,0:T(8,128)(2,1)S(1)}, bf16[2,192,128]{2,1,0:T(8,128)(2,1)S(1)}, u32[]{:S(2)}, u32[]{:S(2)}) collective-permute-start(bf16[2,192,128]{2,1,0:T(8,128)(2,1)S(1)} %broadcast_select_fusion.18), channel_id=1, source_target_pairs={{0,16},{16,0},{1,17},{17,1},{2,18},{18,2},{3,19},{19,3},{4,20},{20... | collective-permute-start | bytes 294920 | tf_op jit(solution)/shard_map/ppermute | solution.py:871
  104.0 39.7 %collective-permute-start.12 = (bf16[2,192,512]{2,1,0:T(8,128)(2,1)}, bf16[2,192,512]{2,1,0:T(8,128)(2,1)}, u32[]{:S(2)}, u32[]{:S(2)}) collective-permute-start(bf16[2,192,512]{2,1,0:T(8,128)(2,1)} %broadcast_select_fusion.4), channel_id=1, source_target_pairs={{0,16},{16,0},{1,17},{17,1},{2,18},{18,2},{3,19},{19,3},{4,20},{20... | collective-permute-start | bytes 1179656 | tf_op jit(solution)/shard_map/ppermute | solution.py:871
  108.1 31.8 %all-to-all-start.2 = ((bf16[4,192,128]{2,1,0:T(8,128)(2,1)}), bf16[4,192,128]{2,1,0:T(8,128)(2,1)S(1)}, u32[]{:S(2)}, u32[]{:S(2)}) async-start(bf16[4,192,128]{2,1,0:T(8,128)(2,1)} %pad_maximum_fusion.6), calls=%async_computation.2 | async-start | bytes 393216 | tf_op jit(solution)/shard_map/all_to_all | solution.py:884
  139.9 13.8 %all-to-all-start.1 = ((bf16[4,2,3,32,512]{4,3,2,1,0:T(8,128)(2,1)}), bf16[4,2,3,32,512]{4,3,2,1,0:T(8,128)(2,1)S(1)}, u32[]{:S(2)}, u32[]{:S(2)}) async-start(bf16[4,2,3,32,512]{4,3,2,1,0:T(8,128)(2,1)} %get-tuple-element.61.refs_5_), calls=%async_computation.1 | async-start | bytes 1572864 | tf_op jit(solution)/shard_map/all_to_all | solution.py:970
  143.7 15.1 %collective-permute-start.7 = (bf16[768,128]{1,0:T(8,128)(2,1)S(1)}, bf16[768,128]{1,0:T(8,128)(2,1)S(1)}, u32[]{:S(2)}, u32[]{:S(2)}) collective-permute-start(bf16[768,128]{1,0:T(8,128)(2,1)S(1)} %bitcast.98), channel_id=1, source_target_pairs={{0,16},{16,0},{1,17},{17,1},{2,18},{18,2},{3,19},{19,3},{4,20},{20... | collective-permute-start | bytes 589832 | tf_op jit(solution)/shard_map/ppermute | solution.py:985
  153.7 22.5 %copy-start.14 = (bf16[4,2,3,32,512]{4,3,2,1,0:T(8,128)(2,1)}, bf16[4,2,3,32,512]{4,3,2,1,0:T(8,128)(2,1)S(1)}, u32[]{:S(2)}) copy-start(bf16[4,2,3,32,512]{4,3,2,1,0:T(8,128)(2,1)S(1)} %all-to-all-done.1) | copy-start | bytes 2359300
  153.7 62.3 %all-to-all-start.3 = ((bf16[4,192,512]{2,1,0:T(8,128)(2,1)}), bf16[4,192,512]{2,1,0:T(8,128)(2,1)}, u32[]{:S(2)}, u32[]{:S(2)}) async-start(bf16[4,192,512]{2,1,0:T(8,128)(2,1)} %pad_maximum_fusion.2), calls=%async_computation.3 | async-start | bytes 1572864 | tf_op jit(solution)/shard_map/all_to_all | solution.py:884
  158.9 12.3 %collective-permute-start.9 = (bf16[2,768,128]{2,1,0:T(8,128)(2,1)S(1)}, bf16[2,768,128]{2,1,0:T(8,128)(2,1)S(1)}, u32[]{:S(2)}, u32[]{:S(2)}) collective-permute-start(bf16[2,768,128]{2,1,0:T(8,128)(2,1)S(1)} %pad_maximum_fusion.4), channel_id=1, source_target_pairs={{0,8},{4,12},{8,0},{12,4},{1,9},{5,13},{9,1},{13,5},{2,10},{6,14},... | collective-permute-start | bytes 1179656 | tf_op jit(solution)/shard_map/ppermute | solution.py:895
  160.4 15.8 %collective-permute-start.8 = (bf16[2,768,128]{2,1,0:T(8,128)(2,1)S(1)}, bf16[2,768,128]{2,1,0:T(8,128)(2,1)S(1)}, u32[]{:S(2)}, u32[]{:S(2)}) collective-permute-start(bf16[2,768,128]{2,1,0:T(8,128)(2,1)S(1)} %pad_maximum_fusion.4), channel_id=1, source_target_pairs={{0,4},{4,0},{8,12},{12,8},{1,5},{5,1},{9,13},{13,9},{2,6},{6,2},{1... | collective-permute-start | bytes 1179656 | tf_op jit(solution)/shard_map/ppermute | solution.py:895
  171.2 8.4 %collective-permute-start.10 = (bf16[1,768,128]{2,1,0:T(8,128)(2,1)S(1)}, bf16[1,768,128]{2,1,0:T(8,128)(2,1)S(1)}, u32[]{:S(2)}, u32[]{:S(2)}) collective-permute-start(bf16[1,768,128]{2,1,0:T(8,128)(2,1)S(1)} %slice.116), channel_id=1, source_target_pairs={{0,4},{4,0},{8,12},{12,8},{1,5},{5,1},{9,13},{13,9},{2,6},{6,2},{1... | collective-permute-start | bytes 589832 | tf_op jit(solution)/shard_map/ppermute | solution.py:895
  176.2 5.7 collective-permute-start.11
  267.2 25.1 %copy-start.5 = (bf16[1,2,4,3,32,512]{5,4,3,2,1,0:T(8,128)(2,1)S(1)}, bf16[1,2,4,3,32,512]{5,4,3,2,1,0:T(8,128)(2,1)}, u32[]{:S(2)}) copy-start(bf16[1,2,4,3,32,512]{5,4,3,2,1,0:T(8,128)(2,1)} %copy-done.4) | copy-start | bytes 2359300
  267.2 25.1 %copy-start.11 = (bf16[8,96,512]{2,1,0:T(8,128)(2,1)S(1)}, bf16[8,96,512]{2,1,0:T(8,128)(2,1)}, u32[]{:S(2)}) copy-start(bf16[8,96,512]{2,1,0:T(8,128)(2,1)} %get-tuple-element.68) | copy-start | bytes 2359300
  267.2 25.1 %copy-start.12 = (bf16[8,96,512]{2,1,0:T(8,128)(2,1)S(1)}, bf16[8,96,512]{2,1,0:T(8,128)(2,1)}, u32[]{:S(2)}) copy-start(bf16[8,96,512]{2,1,0:T(8,128)(2,1)} %get-tuple-element.74) | copy-start | bytes 2359300
  267.3 47.4 %collective-permute-start.13 = (bf16[4,768,768]{2,1,0:T(8,128)(2,1)}, bf16[4,768,768]{2,1,0:T(8,128)(2,1)}, u32[]{:S(2)}, u32[]{:S(2)}) collective-permute-start(bf16[4,768,768]{2,1,0:T(8,128)(2,1)} %get-tuple-element.73), channel_id=1, source_target_pairs={{0,16},{16,0},{1,17},{17,1},{2,18},{18,2},{3,19},{19,3},{4,20},{20... | collective-permute-start | bytes 14155784 | tf_op jit(solution)/shard_map/ppermute | solution.py:1002
  292.2 60.0 %collective-permute-start.16 = (bf16[2,192,512]{2,1,0:T(8,128)(2,1)S(1)}, bf16[2,192,512]{2,1,0:T(8,128)(2,1)}, u32[]{:S(2)}, u32[]{:S(2)}) collective-permute-start(bf16[2,192,512]{2,1,0:T(8,128)(2,1)S(1)} %broadcast_select_fusion.11), channel_id=1, source_target_pairs={{0,16},{16,0},{1,17},{17,1},{2,18},{18,2},{3,19},{19,3},{4,20},{20... | collective-permute-start | bytes 1179656 | tf_op jit(solution)/shard_map/ppermute | solution.py:907
  348.2 6.2 collective-permute-start.14
  348.7 14.8 %all-to-all-start.4 = ((bf16[4,2,96,512]{3,2,1,0:T(8,128)(2,1)}), bf16[4,2,96,512]{3,2,1,0:T(8,128)(2,1)S(1)}, u32[]{:S(2)}, u32[]{:S(2)}) async-start(bf16[4,2,96,512]{3,2,1,0:T(8,128)(2,1)} %get-tuple-element.80), calls=%async_computation.4 | async-start | bytes 1572864 | tf_op jit(solution)/shard_map/all_to_all | solution.py:1015
  354.4 64.1 %collective-permute-start.15 = (bf16[4,768,512]{2,1,0:T(8,128)(2,1)}, bf16[4,768,512]{2,1,0:T(8,128)(2,1)}, u32[]{:S(2)}, u32[]{:S(2)}) collective-permute-start(bf16[4,768,512]{2,1,0:T(8,128)(2,1)} %get-tuple-element.92), channel_id=1, source_target_pairs={{0,16},{16,0},{1,17},{17,1},{2,18},{18,2},{3,19},{19,3},{4,20},{20... | collective-permute-start | bytes 9437192 | tf_op jit(solution)/shard_map/ppermute | solution.py:1020
  355.4 12.6 %copy-start.9 = (bf16[4,2,96,512]{3,2,1,0:T(8,128)(2,1)S(1)}, bf16[4,2,96,512]{3,2,1,0:T(8,128)(2,1)}, u32[]{:S(2)}) copy-start(bf16[4,2,96,512]{3,2,1,0:T(8,128)(2,1)} %get-tuple-element.59) | copy-start | bytes 2359300
  363.5 54.9 %all-to-all-start.5 = ((bf16[4,768,128]{2,1,0:T(8,128)(2,1)}), bf16[4,768,128]{2,1,0:T(8,128)(2,1)}, u32[]{:S(2)}, u32[]{:S(2)}) async-start(bf16[4,768,128]{2,1,0:T(8,128)(2,1)} %add_convert_fusion.3), calls=%async_computation.5 | async-start | bytes 1572864 | tf_op jit(solution)/shard_map/all_to_all | solution.py:1023
  367.7 140.8 %reduce-scatter.10.cloned.1.call-start = ((), (), s32[]{:S(2)}) async-start(), calls=%async_computation.18 | async-start | bytes 3932160
  424.0 222.5 %reduce-scatter.8.cloned.1.call-start = ((), (), s32[]{:S(2)}) async-start(), calls=%async_computation.14 | async-start | bytes 5013504 | tf_op jit(solution)/shard_map/reduce_scatter | solution.py:1009
  431.1 7.9 %collective-permute-start.17 = (bf16[4,2,2,3,32,512]{5,4,3,2,1,0:T(8,128)(2,1)S(1)}, bf16[4,2,2,3,32,512]{5,4,3,2,1,0:T(8,128)(2,1)}, u32[]{:S(2)}, u32[]{:S(2)}) collective-permute-start(bf16[4,2,2,3,32,512]{5,4,3,2,1,0:T(8,128)(2,1)S(1)} %get-tuple-element.98), channel_id=1, source_target_pairs={{0,16},{16,0},{1,17},{17,1},{2,18},{18,2},{3,19},{19,3},{4,20},{20... | collective-permute-start | bytes 4718600 | tf_op jit(solution)/shard_map/ppermute | solution.py:1035
  433.2 18.5 %all-to-all-start.9 = ((bf16[4,192,128]{2,1,0:T(8,128)(2,1)}), bf16[4,192,128]{2,1,0:T(8,128)(2,1)S(1)}, u32[]{:S(2)}, u32[]{:S(2)}) async-start(bf16[4,192,128]{2,1,0:T(8,128)(2,1)} %bitcast.36), calls=%async_computation.9 | async-start | bytes 393216 | tf_op jit(solution)/shard_map/all_to_all | solution.py:904
  451.8 49.0 %all-to-all-start.7 = ((bf16[4,768,512]{2,1,0:T(8,128)(2,1)}), bf16[4,768,512]{2,1,0:T(8,128)(2,1)S(1)}, u32[]{:S(2)}, u32[]{:S(2)}) async-start(bf16[4,768,512]{2,1,0:T(8,128)(2,1)} %get-tuple-element.99), calls=%async_computation.7 | async-start | bytes 6291456 | tf_op jit(solution)/shard_map/all_to_all | solution.py:1048
  455.8 2.2 collective-permute-start.24
  455.8 55.7 %collective-permute-start.19 = (bf16[2,192,128]{2,1,0:T(8,128)(2,1)S(1)}, bf16[2,192,128]{2,1,0:T(8,128)(2,1)S(1)}, u32[]{:S(2)}, u32[]{:S(2)}) collective-permute-start(bf16[2,192,128]{2,1,0:T(8,128)(2,1)S(1)} %broadcast_select_fusion.21), channel_id=1, source_target_pairs={{0,16},{16,0},{1,17},{17,1},{2,18},{18,2},{3,19},{19,3},{4,20},{20... | collective-permute-start | bytes 294920 | tf_op jit(solution)/shard_map/ppermute | solution.py:907
  503.3 34.9 %all-to-all-start.8 = ((bf16[4,192,512]{2,1,0:T(8,128)(2,1)}), bf16[4,192,512]{2,1,0:T(8,128)(2,1)S(1)}, u32[]{:S(2)}, u32[]{:S(2)}) async-start(bf16[4,192,512]{2,1,0:T(8,128)(2,1)} %bitcast.35), calls=%async_computation.8 | async-start | bytes 1572864 | tf_op jit(solution)/shard_map/all_to_all | solution.py:904
  508.3 178.8 %reduce-scatter.6.cloned.1.call-start = ((), (), s32[]{:S(2)}) async-start(), calls=%async_computation.13 | async-start | bytes 2293760 | tf_op jit(solution)/shard_map/reduce_scatter | solution.py:1072
  511.6 5.7 collective-permute-start.21
  513.1 6.3 collective-permute-start.20
  517.4 4.7 collective-permute-start.22
  519.4 4.9 collective-permute-start.23
  538.2 9.5 %collective-permute-start.18 = (bf16[2,192,512]{2,1,0:T(8,128)(2,1)S(1)}, bf16[2,192,512]{2,1,0:T(8,128)(2,1)S(1)}, u32[]{:S(2)}, u32[]{:S(2)}) collective-permute-start(bf16[2,192,512]{2,1,0:T(8,128)(2,1)S(1)} %broadcast_select_fusion.9), channel_id=1, source_target_pairs={{0,16},{16,0},{1,17},{17,1},{2,18},{18,2},{3,19},{19,3},{4,20},{20... | collective-permute-start | bytes 1179656 | tf_op jit(solution)/shard_map/ppermute | solution.py:907
  646.4 44.4 %copy-start.1 = (bf16[2,192,4096]{2,1,0:T(8,128)(2,1)S(1)}, bf16[2,192,4096]{2,1,0:T(8,128)(2,1)}, u32[]{:S(2)}) copy-start(bf16[2,192,4096]{2,1,0:T(8,128)(2,1)} %param.15) | copy-start | bytes 9437188
  (25 other events, 92.1 us)
Sparse Core Ops, SparseCore 0:
  10.2 32.6 all-gather.6
  46.3 81.2 all-gather.8
  131.0 93.1 all-gather.10
  424.1 70.4 reduce-scatter.9
  499.7 146.7 reduce-scatter.7
  648.6 38.3 reduce-scatter.5

commit v5 on v4

--- a/solution.py
+++ b/solution.py
@@ -829,6 +829,11 @@
         ),
         out_shape=[rest_shape, rest_shape, share, share],
         compiler_params=kernel_params(),
+        cost_estimate=pl.CostEstimate(
+            flops=groups * width * (4 * feat2 * keys + 6 * feat * tokens),
+            bytes_accessed=4 * small.size,
+            transcendentals=0,
+        ),
         name="small_grads",
     )(place, small, chosen, d_ckv, attn, d_cq, catt, d_low, h_low, d_cross, *dgs)
 
@@ -899,9 +904,15 @@
         far = jnp.concatenate([send(near_two[:half], 1), send(near_one[half:], 2)], axis=0)
         return [value, near_one, near_two, far]
 
+    def home_cols(value):
+        value = value.reshape(cols, part_width, value.shape[-1])
+        return lax.all_to_all(value, "col", 0, 0, tiled=True)
+
     def to_home(value):
+        return home_cores(home_cols(value))
+
+    def home_cores(value):
         take = value.shape[-1]
-        value = lax.all_to_all(value.reshape(cols, part_width, take), "col", 0, 0, tiled=True)
         if parts == 2:
             early, late = value[:own_seqs], value[own_seqs:]
             got = lax.ppermute(jnp.where(first_core, late, early), "dp", swap)
@@ -993,7 +1004,7 @@
     block_out, d_catt, dy_two, d_cross, g_other, g_own, dg_two, dg_three = middle(
         place, normed_one, catt_flat, small_all, large_all, cot
     )
-    block_out = to_home(block_out)
+    block_out = home_cols(block_out)
 
 
     def with_core(own, got):
@@ -1004,8 +1015,9 @@
         meta, cross_q, [ckv], d_catt.reshape(catt.shape), catt, lse_cross, False, [bf16],
         "cross_attention_back",
     )
-    g_other, d_cq = lax.optimization_barrier((g_other, d_cq))
-    large_grad = with_core(g_own, g_other).reshape(rows * cols, part_width, 2 * units)
+    g_other, d_cq, block_out = lax.optimization_barrier((g_other, d_cq, block_out))
+    large_grad, d_cq = lax.optimization_barrier((with_core(g_own, g_other), d_cq))
+    large_grad = large_grad.reshape(rows * cols, part_width, 2 * units)
     large_grad = lax.psum_scatter(large_grad, ("row", "col"), scatter_dimension=0, tiled=False)
     d_cq = d_cq.reshape(blocks, feat, tokens)
     d_ckv = d_ckv.reshape(blocks, 2 * feat, d_ckv.shape[-1])
@@ -1017,6 +1029,9 @@
         place, small_all, chosen, d_ckv, attn, d_cq, catt_flat, d_low, h_low, d_cross,
         (dg_one, dg_two, dg_three), sub == 1,
     )
+    d_mixed, rest_other, rest, chosen_other, d_chosen = lax.optimization_barrier(
+        (d_mixed, rest_other, rest, chosen_other, d_chosen)
+    )
     rest_other = lax.ppermute(rest_other, "dp", swap)
     d_chosen = with_core(d_chosen, lax.ppermute(chosen_other, "dp", swap))
     d_chosen = d_chosen.reshape(rows, sub * width, c_tokens)
@@ -1026,8 +1041,8 @@
     d_query, *d_kv = attend_back(
         meta, query, kv_list, d_mixed, mixed, lse, True, types, "self_attention_back"
     )
-    d_query, d_chosen, rest_other, block_out = lax.optimization_barrier(
-        (d_query, d_chosen, rest_other, block_out)
+    d_query, d_chosen, rest_other, large_grad = lax.optimization_barrier(
+        (d_query, d_chosen, rest_other, large_grad)
     )
     rest = with_core(rest, rest_other).reshape(rows, cols, part_width, -1)
     rest = lax.psum_scatter(rest, "row", scatter_dimension=0, tiled=False)
@@ -1074,7 +1089,7 @@
     large_grad = large_grad.astype(f32)
 
     return (
-        block_out,
+        home_cores(block_out),
         x_grad,
         bank_grad,
         qkv_grad[:, : 3 * feat].reshape(w_qkv.shape),

time: 707 us -> 603 us (0.85)
  waiting for transfers between devices: 295 us -> 216 us
  blocking collectives: 26.7 us -> 1.94 us
    reduce_scatter x1, waiting for transfers between devices: 97.3 us -> 49.5 us  [per_device(): lax.psum_scatter(large_grad, ('row', 'col'), scatter_dimension=0, tiled=F...]
    reduce_scatter x1, waiting for transfers between devices: 38.6 us -> 0.01 us  [per_device(): lax.psum_scatter(last, 'col', scatter_dimension=0, tiled=False).astype(f32)]
    all_to_all x1 -> x0, blocking collectives: 24.6 us -> none  [to_home(): lax.all_to_all(value.reshape(cols, part_width, take), 'col', 0, 0, tiled=...]
    all_to_all x2 -> x3, waiting for transfers between devices: 13.8 us -> 26.8 us  [home_cols(): return lax.all_to_all(value, 'col', 0, 0, tiled=True)]
  transfers between devices with their start and end apart: 40 -> 41, of which waited for: 20 -> 19; matrix products, arithmetic and copies ran while one was open for 8% -> 8% of each run, Pallas kernels for 26% -> 30%
where the time goes in v5:
time: 603 us; the launch traced here: 596 us
  Pallas kernels  223 us (37%)
  waiting for transfers between devices  216 us (36%)
  starting transfers between devices  61.1 us (10%)
  other arithmetic  40 us (7%)
  local copies, waits for them, and re-layouts  27.3 us (5%)
  between operations  15.7 us (3%)
  matrix products  11.1 us (2%)
    pallas_call x2, Pallas kernels, attend_back(): pl.pallas_call(functools.partial(attend_back_kernel, sources=len(kv_list)...  68.7 us
    ppermute x12, waiting for transfers between devices, send(): return lax.ppermute(v, 'row', [(i, i ^ k) for i in range(rows)])  53.2 us
    reduce_scatter x1, waiting for transfers between devices, per_device(): lax.psum_scatter(large_grad, ('row', 'col'), scatter_dimension=0, tiled=F...  49.5 us
    pallas_call x1, Pallas kernels, middle(): pl.pallas_call(middle_kernel, grid_spec=pltpu.PrefetchScalarGridSpec(num_...  43.3 us
    pallas_call x2, Pallas kernels, attend(): pl.pallas_call(functools.partial(attend_kernel, sources=len(kv_list), n_q...  39.9 us
    all_to_all x1, waiting for transfers between devices, per_device(): dx_part = lax.all_to_all(dx_part, 'row', 0, 0, tiled=True)  36.2 us
    all_to_all x3, waiting for transfers between devices, across_cols(): lax.all_to_all(value, 'col', 0, 0, tiled=True)  27.3 us
    all_to_all x3, waiting for transfers between devices, home_cols(): return lax.all_to_all(value, 'col', 0, 0, tiled=True)  26.8 us
  transfers between devices with their start and end apart: 41, of which 19 were waited for; matrix products, arithmetic and copies ran while one was open for 8% of the time, Pallas kernels for 30%

profile of v5, /device:TPU:0, one launch (start us, length us, event | category | flops | bytes accessed | tf_op | source)
XLA Modules:
  0.0 595.6 jit_solution(18341892829711887033)
XLA Ops:
  16.0 6.4 %all-to-all-start = ((bf16[4,192,512]{2,1,0:T(8,128)(2,1)}), bf16[4,192,512]{2,1,0:T(8,128)(2,1)}, u32[]{:S(2)}, u32[]{:S(2)}) async-start(bf16[4,192,512]{2,1,0:T(8,128)(2,1)} %pad_maximum_fusion.1), calls=%async_computation | async-start | bytes 1572864 | tf_op jit(solution)/shard_map/all_to_all | solution.py:889
  23.1 27.3 %all-to-all-done = bf16[4,192,512]{2,1,0:T(8,128)(2,1)} async-done(((bf16[4,192,512]{2,1,0:T(8,128)(2,1)}), bf16[4,192,512]{2,1,0:T(8,128)(2,1)}, u32[]{:S(2)}, u32[]{:S(2)}) %all-to-all-start) | async-done | bytes 786464 | tf_op jit(solution)/shard_map/all_to_all | solution.py:889
  53.5 18.0 %collective-permute-done.2.refs_2_ = bf16[768,512]{1,0:T(8,128)(2,1)S(1)} collective-permute-done((bf16[768,512]{1,0:T(8,128)(2,1)}, bf16[768,512]{1,0:T(8,128)(2,1)S(1)}, u32[]{:S(2)}, u32[]{:S(2)}) %collective-permute-start.2) | collective-permute-done | bytes 786464 | tf_op jit(solution)/shard_map/ppermute | solution.py:900
  78.3 10.8 %collective-permute-done.3 = bf16[384,512]{1,0:T(8,128)(2,1)S(1)} collective-permute-done((bf16[384,512]{1,0:T(8,128)(2,1)}, bf16[384,512]{1,0:T(8,128)(2,1)S(1)}, u32[]{:S(2)}, u32[]{:S(2)}) %collective-permute-start.3) | collective-permute-done | bytes 393248 | tf_op jit(solution)/shard_map/ppermute | solution.py:900
  89.9 1.8 constant_dynamic-update-slice_fusion.refs_3_
  91.7 6.6 %project.1 = (bf16[4,2,96,512]{3,2,1,0:T(8,128)(2,1)}, bf16[4,2,2,96,512]{4,3,2,1,0:T(8,128)(2,1)}) custom-call(s32[2]{0:T(128)} %pad_add_fusion.1.place_ref, bf16[2,768,384]{2,1,0:T(8,128)(2,1)} %bitcast.88, bf16[768,512]{1,0:T(8,128)(2,1)} %bitcast.2.refs_0_.x_ref, bf16[768,512]{1,0:T(8,128)(2,1)} %copy-done.16, bf16[768,512]{1,0:T(8,128)(2,1)} %copy-done.15, ...), custom_call_target="tpu_custom_call" | custom-call | tf_op jit(solution)/shard_map/project/pallas_call | solution.py:350
  102.1 1.9 broadcast_select_fusion.12
  104.1 1.9 all-reduce.1
  108.0 3.4 all-to-all-start.2
  111.5 27.0 %self_attention.1 = (bf16[4,2,3,32,512]{4,3,2,1,0:T(8,128)(2,1)}, f32[3,4,1,512]{3,2,1,0:T(1,128)S(1)}) custom-call(s32[13]{0:T(128)S(1)} %pad_add_fusion.2.refs_0_, bf16[4,2,3,32,512]{4,3,2,1,0:T(8,128)(2,1)S(1)} %bitcast.74, bf16[4,2,2,3,32,512]{5,4,3,2,1,0:T(8,128)(2,1)S(1)} %bitcast.73, bf16[4,2,2,3,32,512]{5,4,3,2,1,0:T(8,128)(2,1)} %collective-permute-done.5.refs_3_), custom_call_target="tpu_custom_call" | custom-call | flops 12884901888 | bytes 6291456 | tf_op jit(solution)/shard_map/self_attention/pallas_call | solution.py:238
  138.4 3.8 all-to-all-start.1
  143.6 10.1 %all-to-all-done.1 = bf16[4,2,3,32,512]{4,3,2,1,0:T(8,128)(2,1)S(1)} async-done(((bf16[4,2,3,32,512]{4,3,2,1,0:T(8,128)(2,1)}), bf16[4,2,3,32,512]{4,3,2,1,0:T(8,128)(2,1)S(1)}, u32[]{:S(2)}, u32[]{:S(2)}) %all-to-all-start.1) | async-done | bytes 786464 | tf_op jit(solution)/shard_map/all_to_all | solution.py:981
  153.7 5.2 all-to-all-start.3
  162.1 8.9 %collective-permute-done.9 = bf16[2,768,128]{2,1,0:T(8,128)(2,1)S(1)} collective-permute-done((bf16[2,768,128]{2,1,0:T(8,128)(2,1)S(1)}, bf16[2,768,128]{2,1,0:T(8,128)(2,1)S(1)}, u32[]{:S(2)}, u32[]{:S(2)}) %collective-permute-start.9) | collective-permute-done | bytes 393248 | tf_op jit(solution)/shard_map/ppermute | solution.py:900
  172.5 3.5 collective-permute-done.8
  177.6 1.8 collective-permute-done.10
  179.4 2.3 collective-permute-done.11
  182.9 9.0 %cross_kv.1 = bf16[8,192,1024]{2,1,0:T(8,128)(2,1)} custom-call(bf16[8,768,512]{2,1,0:T(8,128)(2,1)} %bitcast.81, bf16[8,768,128]{2,1,0:T(8,128)(2,1)} %copy-done.20), custom_call_target="tpu_custom_call" | custom-call | tf_op jit(solution)/shard_map/cross_kv/pallas_call | solution.py:455
  191.9 9.0 %after_self.1 = (f32[768,512]{1,0:T(8,128)}, f32[1,512]{1,0:T(1,128)}, bf16[768,512]{1,0:T(8,128)(2,1)}, bf16[8,96,512]{2,1,0:T(8,128)(2,1)}) custom-call(bf16[768,512]{1,0:T(8,128)(2,1)} %bitcast.2.refs_0_.x_ref, bf16[4,2,96,512]{3,2,1,0:T(8,128)(2,1)} %bitcast.92, bf16[8,768,512]{2,1,0:T(8,128)(2,1)} %bitcast.82), custom_call_target="tpu_custom_call" | custom-call | tf_op jit(solution)/shard_map/after_self/pallas_call | solution.py:503
  202.0 12.9 %cross_attention.1 = (bf16[1,2,4,3,32,512]{5,4,3,2,1,0:T(8,128)(2,1)S(1)}, f32[12,1,1,512]{3,2,1,0:T(1,128)S(1)}) custom-call(s32[13]{0:T(128)S(1)} %pad_add_fusion.2.refs_0_, bf16[1,2,4,3,32,512]{5,4,3,2,1,0:T(8,128)(2,1)S(1)} %bitcast.76, bf16[1,2,4,2,3,32,1024]{6,5,4,3,2,1,0:T(8,128)(2,1)S(1)} %bitcast.66), custom_call_target="tpu_custom_call" | custom-call | flops 3221225472 | bytes 6291456 | tf_op jit(solution)/shard_map/cross_attention/pallas_call | solution.py:238
  215.8 7.9 %all-gather.11.cloned.1.call-done = bf16[6144,768]{1,0:T(8,128)(2,1)} async-done(((bf16[192,768]{1,0:T(8,128)(2,1)}), bf16[6144,768]{1,0:T(8,128)(2,1)}) %all-gather.11.cloned.1.call-update) | async-done | bytes 9437200 | tf_op jit(solution)/shard_map/all_gather | solution.py:953
  223.7 43.3 %middle.1 = (bf16[768,512]{1,0:T(8,128)(2,1)}, bf16[8,96,512]{2,1,0:T(8,128)(2,1)}, f32[768,512]{1,0:T(8,128)}, bf16[768,512]{1,0:T(8,128)(2,1)}, bf16[4,768,768...) custom-call(s32[2]{0:T(128)} %pad_add_fusion.1.place_ref, ...), custom_call_target="tpu_custom_call" | custom-call | flops 14495514624 | bytes 37748736 | tf_op jit(solution)/shard_map/middle/pallas_call | solution.py:640
  267.3 3.5 all-to-all-start.4
  272.2 21.4 %cross_attention_back.1 = (bf16[1,2,4,3,32,512]{5,4,3,2,1,0:T(8,128)(2,1)S(1)}, bf16[1,2,4,2,3,32,1024]{6,5,4,3,2,1,0:T(8,128)(2,1)}) custom-call(s32[13]{0:T(128)S(1)} %pad_add_fusion.2.refs_0_, bf16[1,2,4,3,32,512]{5,4,3,2,1,0:T(8,128)(2,1)S(1)} %bitcast.77, bf16[1,2,4,2,3,32,1024]{6,5,4,3,2,1,0:T(8,128)(2,1)} %bitcast.65, ...), custom_call_target="tpu_custom_call" | custom-call | flops 8053063680 | bytes 6291456 | tf_op jit(solution)/shard_map/cross_attention_back/pallas_call | solution.py:259
  294.5 7.3 %add_convert_fusion = bf16[4,768,768]{2,1,0:T(8,128)(2,1)} fusion(bf16[4,768,768]{2,1,0:T(8,128)(2,1)} %collective-permute-done.13, bf16[4,768,768]{2,1,0:T(8,128)(2,1)} %get-tuple-element.87), kind=kLoop, calls=%fused_computation.3 | loop fusion | flops 9437184 | bytes 14155776 | tf_op jit(solution)/shard_map/convert_element_type | solution.py:1011
  301.8 10.4 %before_self.1 = (bf16[4,2,96,512]{3,2,1,0:T(8,128)(2,1)}, bf16[768,512]{1,0:T(8,128)(2,1)}, f32[768,512]{1,0:T(8,128)}, f32[768,128]{1,0:T(8,128)}) custom-call(bf16[8,96,512]{2,1,0:T(8,128)(2,1)} %bitcast.69, bf16[8,768,512]{2,1,0:T(8,128)(2,1)} %bitcast.84, f32[768,512]{1,0:T(8,128)} %get-tuple-element.91.dy_ref, ...), custom_call_target="tpu_custom_call" | custom-call | tf_op jit(solution)/shard_map/before_self/pallas_call | solution.py:711
  312.3 3.5 all-to-all-start.5
  315.8 23.3 %small_grads.1 = (bf16[4,768,512]{2,1,0:T(8,128)(2,1)}, bf16[4,768,512]{2,1,0:T(8,128)(2,1)}, bf16[4,768,128]{2,1,0:T(8,128)(2,1)}, bf16[4,768,128]{2,1,0:T(8,128)(2,1)}) custom-call(s32[2]{0:T(128)} %pad_add_fusion.1.place_ref, bf16[8,768,512]{2,1,0:T(8,128)(2,1)} %bitcast.85, bf16[8,768,128]{2,1,0:T(8,128)(2,1)} %copy-done.20, ...), custom_call_target="tpu_custom_call" | custom-call | flops 6643777536 | bytes 12582912 | tf_op jit(solution)/shard_map/small_grads/pallas_call | solution.py:803
  339.7 2.0 collective-permute-done.15
  341.6 2.2 add_convert_fusion.3
  343.9 4.2 all-to-all-start.6
  348.4 47.3 %self_attention_back.1 = (bf16[4,2,3,32,512]{4,3,2,1,0:T(8,128)(2,1)S(1)}, f32[4,2,2,3,32,512]{5,4,3,2,1,0:T(8,128)}, bf16[4,2,2,3,32,512]{5,4,3,2,1,0:T(8,128)(2,1)S(1)}) custom-call(s32[13]{0:T(128)S(1)} %pad_add_fusion.2.refs_0_, bf16[4,2,3,32,512]{4,3,2,1,0:T(8,128)(2,1)S(1)} %bitcast.75, bf16[4,2,2,3,32,512]{5,4,3,2,1,0:T(8,128)(2,1)} %bitcast.72, ...), custom_call_target="tpu_custom_call" | custom-call | flops 32212254720 | bytes 6291456 | tf_op jit(solution)/shard_map/self_attention_back/pallas_call | solution.py:259
  396.5 49.5 %reduce-scatter.6.cloned.1.call-done = bf16[1,192,768]{2,1,0:T(8,128)(2,1)} async-done(((bf16[16,192,768]{2,1,0:T(8,128)(2,1)}), bf16[1,192,768]{2,1,0:T(8,128)(2,1)}) %reduce-scatter.6.cloned.1.call-update) | async-done | bytes 294928 | tf_op jit(solution)/shard_map/reduce_scatter | solution.py:1021
  446.0 5.4 add_convert_fusion.1
  451.6 2.0 reduce_sum.22
  453.6 3.5 all-to-all-start.9
  457.1 12.5 %project_back.1 = (bf16[4,768,512]{2,1,0:T(8,128)(2,1)}, bf16[768,384]{1,0:T(8,128)(2,1)}, bf16[768,384]{1,0:T(8,128)(2,1)}) custom-call(s32[2]{0:T(128)} %pad_add_fusion.1.place_ref, bf16[2,768,384]{2,1,0:T(8,128)(2,1)} %bitcast.89, bf16[768,512]{1,0:T(8,128)(2,1)} %bitcast.2.refs_0_.x_ref, bf16[768,512]{1,0:T(8,128)(2,1)} %copy-done.16, ...), custom_call_target="tpu_custom_call" | custom-call | tf_op jit(solution)/shard_map/project_back/pallas_call | solution.py:411
  469.6 3.7 all-to-all-start.7
  476.6 2.1 broadcast_select_fusion.11
  480.1 2.2 copy.51
  482.4 36.2 %all-to-all-done.7 = bf16[4,768,512]{2,1,0:T(8,128)(2,1)S(1)} async-done(((bf16[4,768,512]{2,1,0:T(8,128)(2,1)}), bf16[4,768,512]{2,1,0:T(8,128)(2,1)S(1)}, u32[]{:S(2)}, u32[]{:S(2)}) %all-to-all-start.7) | async-done | bytes 3145760 | tf_op jit(solution)/shard_map/all_to_all | solution.py:1063
  524.7 2.6 add_convert_fusion.2
  527.3 4.9 all-to-all-start.8
  536.9 3.0 collective-permute-done.21
  542.1 2.5 collective-permute-done.22
  544.6 2.1 collective-permute-done.23
  546.7 26.8 %all-to-all-done.8 = bf16[4,192,512]{2,1,0:T(8,128)(2,1)S(1)} async-done(((bf16[4,192,512]{2,1,0:T(8,128)(2,1)}), bf16[4,192,512]{2,1,0:T(8,128)(2,1)S(1)}, u32[]{:S(2)}, u32[]{:S(2)}) %all-to-all-start.8) | async-done | bytes 786464 | tf_op jit(solution)/shard_map/all_to_all | solution.py:909
  573.6 9.4 %fusion = f32[2,192,4096]{2,1,0:T(8,128)} fusion(bf16[2,192,1024]{2,1,0:T(8,128)(2,1)S(1)} %maximum_dynamic-update-slice_fusion, s32[2,1024]{1,0:T(2,128)S(1)} %pad_add_fusion), kind=kOutput, calls=%fused_computation.1 | convolution fusion | flops 3229614080 | bytes 7086080 | tf_op jit(solution)/shard_map/swp,spn->swn/dot_general | solution.py:842
  (201 shorter events, 63.6 us)
Async XLA Ops:
  7.2 91.2 %copy-start = (bf16[2,192,4096]{2,1,0:T(8,128)(2,1)S(1)}, bf16[2,192,4096]{2,1,0:T(8,128)(2,1)}, u32[]{:S(2)}) copy-start(bf16[2,192,4096]{2,1,0:T(8,128)(2,1)} %param.15) | copy-start | bytes 9437188
  7.2 84.5 %all-gather.7.cloned.1.call-start = ((), (), s32[]{:S(2)}) async-start(), calls=%async_computation.15 | async-start | bytes 1327104 | tf_op jit(solution)/shard_map/all_gather | solution.py:932
  9.2 172.6 %all-gather.9.cloned.1.call-start = ((), (), s32[]{:S(2)}) async-start(), calls=%async_computation.16 | async-start | bytes 6488064 | tf_op jit(solution)/shard_map/all_gather | solution.py:953
  10.4 1.9 collective-permute-start
  16.0 34.4 %all-to-all-start = ((bf16[4,192,512]{2,1,0:T(8,128)(2,1)}), bf16[4,192,512]{2,1,0:T(8,128)(2,1)}, u32[]{:S(2)}, u32[]{:S(2)}) async-start(bf16[4,192,512]{2,1,0:T(8,128)(2,1)} %pad_maximum_fusion.1), calls=%async_computation | async-start | bytes 1572864 | tf_op jit(solution)/shard_map/all_to_all | solution.py:889
  22.4 201.3 %all-gather.11.cloned.1.call-start = ((), (), s32[]{:S(2)}) async-start(), calls=%async_computation.17 | async-start | bytes 9732096 | tf_op jit(solution)/shard_map/all_gather | solution.py:953
  50.5 21.0 %collective-permute-start.2 = (bf16[768,512]{1,0:T(8,128)(2,1)}, bf16[768,512]{1,0:T(8,128)(2,1)S(1)}, u32[]{:S(2)}, u32[]{:S(2)}) collective-permute-start(bf16[768,512]{1,0:T(8,128)(2,1)} %bitcast.2.refs_0_.x_ref), channel_id=1, source_target_pairs={{0,8},{4,12},{8,0},{12,4},{1,9},{5,13},{9,1},{13,5},{2,10},{6,14},... | collective-permute-start | bytes 2359304 | tf_op jit(solution)/shard_map/ppermute | solution.py:900
  52.0 22.6 %collective-permute-start.1 = (bf16[768,512]{1,0:T(8,128)(2,1)}, bf16[768,512]{1,0:T(8,128)(2,1)S(1)}, u32[]{:S(2)}, u32[]{:S(2)}) collective-permute-start(bf16[768,512]{1,0:T(8,128)(2,1)} %bitcast.2.refs_0_.x_ref), channel_id=1, source_target_pairs={{0,4},{4,0},{8,12},{12,8},{1,5},{5,1},{9,13},{13,9},{2,6},{6,2},{1... | collective-permute-start | bytes 2359304 | tf_op jit(solution)/shard_map/ppermute | solution.py:900
  73.1 16.0 %collective-permute-start.3 = (bf16[384,512]{1,0:T(8,128)(2,1)}, bf16[384,512]{1,0:T(8,128)(2,1)S(1)}, u32[]{:S(2)}, u32[]{:S(2)}) collective-permute-start(bf16[384,512]{1,0:T(8,128)(2,1)} %slice.112), channel_id=1, source_target_pairs={{0,4},{4,0},{8,12},{12,8},{1,5},{5,1},{9,13},{13,9},{2,6},{6,2},{1... | collective-permute-start | bytes 1179656 | tf_op jit(solution)/shard_map/ppermute | solution.py:900
  76.3 13.6 %collective-permute-start.4 = (bf16[384,512]{1,0:T(8,128)(2,1)}, bf16[384,512]{1,0:T(8,128)(2,1)}, u32[]{:S(2)}, u32[]{:S(2)}) collective-permute-start(bf16[384,512]{1,0:T(8,128)(2,1)} %slice.113), channel_id=1, source_target_pairs={{0,8},{4,12},{8,0},{12,4},{1,9},{5,13},{9,1},{13,5},{2,10},{6,14},... | collective-permute-start | bytes 1179656 | tf_op jit(solution)/shard_map/ppermute | solution.py:900
  98.3 13.1 %collective-permute-start.5 = (bf16[4,2,2,3,32,512]{5,4,3,2,1,0:T(8,128)(2,1)}, bf16[4,2,2,3,32,512]{5,4,3,2,1,0:T(8,128)(2,1)}, u32[]{:S(2)}, u32[]{:S(2)}) collective-permute-start(bf16[4,2,2,3,32,512]{5,4,3,2,1,0:T(8,128)(2,1)} %bitcast.71), channel_id=1, source_target_pairs={{0,16},{16,0},{1,17},{17,1},{2,18},{18,2},{3,19},{19,3},{4,20},{20... | collective-permute-start | bytes 4718600 | tf_op jit(solution)/shard_map/ppermute | solution.py:969
  100.0 11.4 %copy-start.5 = (bf16[4,2,2,96,512]{4,3,2,1,0:T(8,128)(2,1)S(1)}, bf16[4,2,2,96,512]{4,3,2,1,0:T(8,128)(2,1)}, u32[]{:S(2)}) copy-start(bf16[4,2,2,96,512]{4,3,2,1,0:T(8,128)(2,1)} %get-tuple-element.68) | copy-start | bytes 4718596
  100.0 11.4 %copy-start.6 = (bf16[4,2,96,512]{3,2,1,0:T(8,128)(2,1)S(1)}, bf16[4,2,96,512]{3,2,1,0:T(8,128)(2,1)}, u32[]{:S(2)}) copy-start(bf16[4,2,96,512]{3,2,1,0:T(8,128)(2,1)} %get-tuple-element.67) | copy-start | bytes 2359300
  100.1 7.3 %collective-permute-start.6 = (bf16[2,192,128]{2,1,0:T(8,128)(2,1)S(1)}, bf16[2,192,128]{2,1,0:T(8,128)(2,1)S(1)}, u32[]{:S(2)}, u32[]{:S(2)}) collective-permute-start(bf16[2,192,128]{2,1,0:T(8,128)(2,1)S(1)} %broadcast_select_fusion.18), channel_id=1, source_target_pairs={{0,16},{16,0},{1,17},{17,1},{2,18},{18,2},{3,19},{19,3},{4,20},{20... | collective-permute-start | bytes 294920 | tf_op jit(solution)/shard_map/ppermute | solution.py:876
  104.0 38.5 %collective-permute-start.12 = (bf16[2,192,512]{2,1,0:T(8,128)(2,1)}, bf16[2,192,512]{2,1,0:T(8,128)(2,1)S(1)}, u32[]{:S(2)}, u32[]{:S(2)}) collective-permute-start(bf16[2,192,512]{2,1,0:T(8,128)(2,1)} %broadcast_select_fusion.12), channel_id=1, source_target_pairs={{0,16},{16,0},{1,17},{17,1},{2,18},{18,2},{3,19},{19,3},{4,20},{20... | collective-permute-start | bytes 1179656 | tf_op jit(solution)/shard_map/ppermute | solution.py:876
  108.0 30.4 %all-to-all-start.2 = ((bf16[4,192,128]{2,1,0:T(8,128)(2,1)}), bf16[4,192,128]{2,1,0:T(8,128)(2,1)S(1)}, u32[]{:S(2)}, u32[]{:S(2)}) async-start(bf16[4,192,128]{2,1,0:T(8,128)(2,1)} %pad_maximum_fusion.6), calls=%async_computation.2 | async-start | bytes 393216 | tf_op jit(solution)/shard_map/all_to_all | solution.py:889
  138.4 15.3 %all-to-all-start.1 = ((bf16[4,2,3,32,512]{4,3,2,1,0:T(8,128)(2,1)}), bf16[4,2,3,32,512]{4,3,2,1,0:T(8,128)(2,1)S(1)}, u32[]{:S(2)}, u32[]{:S(2)}) async-start(bf16[4,2,3,32,512]{4,3,2,1,0:T(8,128)(2,1)} %get-tuple-element.69.refs_5_), calls=%async_computation.1 | async-start | bytes 1572864 | tf_op jit(solution)/shard_map/all_to_all | solution.py:981
  142.2 16.7 %collective-permute-start.7 = (bf16[768,128]{1,0:T(8,128)(2,1)S(1)}, bf16[768,128]{1,0:T(8,128)(2,1)S(1)}, u32[]{:S(2)}, u32[]{:S(2)}) collective-permute-start(bf16[768,128]{1,0:T(8,128)(2,1)S(1)} %bitcast.95), channel_id=1, source_target_pairs={{0,16},{16,0},{1,17},{17,1},{2,18},{18,2},{3,19},{19,3},{4,20},{20... | collective-permute-start | bytes 589832 | tf_op jit(solution)/shard_map/ppermute | solution.py:996
  153.7 22.3 %copy-start.19 = (bf16[4,2,3,32,512]{4,3,2,1,0:T(8,128)(2,1)}, bf16[4,2,3,32,512]{4,3,2,1,0:T(8,128)(2,1)S(1)}, u32[]{:S(2)}) copy-start(bf16[4,2,3,32,512]{4,3,2,1,0:T(8,128)(2,1)S(1)} %all-to-all-done.1) | copy-start | bytes 2359300
  153.7 62.1 %all-to-all-start.3 = ((bf16[4,192,512]{2,1,0:T(8,128)(2,1)}), bf16[4,192,512]{2,1,0:T(8,128)(2,1)}, u32[]{:S(2)}, u32[]{:S(2)}) async-start(bf16[4,192,512]{2,1,0:T(8,128)(2,1)} %pad_maximum_fusion.2), calls=%async_computation.3 | async-start | bytes 1572864 | tf_op jit(solution)/shard_map/all_to_all | solution.py:889
  159.0 11.9 %collective-permute-start.9 = (bf16[2,768,128]{2,1,0:T(8,128)(2,1)S(1)}, bf16[2,768,128]{2,1,0:T(8,128)(2,1)S(1)}, u32[]{:S(2)}, u32[]{:S(2)}) collective-permute-start(bf16[2,768,128]{2,1,0:T(8,128)(2,1)S(1)} %pad_maximum_fusion.4), channel_id=1, source_target_pairs={{0,8},{4,12},{8,0},{12,4},{1,9},{5,13},{9,1},{13,5},{2,10},{6,14},... | collective-permute-start | bytes 1179656 | tf_op jit(solution)/shard_map/ppermute | solution.py:900
  160.5 15.4 %collective-permute-start.8 = (bf16[2,768,128]{2,1,0:T(8,128)(2,1)S(1)}, bf16[2,768,128]{2,1,0:T(8,128)(2,1)S(1)}, u32[]{:S(2)}, u32[]{:S(2)}) collective-permute-start(bf16[2,768,128]{2,1,0:T(8,128)(2,1)S(1)} %pad_maximum_fusion.4), channel_id=1, source_target_pairs={{0,4},{4,0},{8,12},{12,8},{1,5},{5,1},{9,13},{13,9},{2,6},{6,2},{1... | collective-permute-start | bytes 1179656 | tf_op jit(solution)/shard_map/ppermute | solution.py:900
  171.0 8.4 %collective-permute-start.10 = (bf16[1,768,128]{2,1,0:T(8,128)(2,1)S(1)}, bf16[1,768,128]{2,1,0:T(8,128)(2,1)S(1)}, u32[]{:S(2)}, u32[]{:S(2)}) collective-permute-start(bf16[1,768,128]{2,1,0:T(8,128)(2,1)S(1)} %slice.116), channel_id=1, source_target_pairs={{0,4},{4,0},{8,12},{12,8},{1,5},{5,1},{9,13},{13,9},{2,6},{6,2},{1... | collective-permute-start | bytes 589832 | tf_op jit(solution)/shard_map/ppermute | solution.py:900
  176.0 5.7 collective-permute-start.11
  223.7 47.3 %copy-start.9 = (bf16[8,96,512]{2,1,0:T(8,128)(2,1)S(1)}, bf16[8,96,512]{2,1,0:T(8,128)(2,1)}, u32[]{:S(2)}) copy-start(bf16[8,96,512]{2,1,0:T(8,128)(2,1)} %get-tuple-element.76) | copy-start | bytes 2359300
  223.7 47.3 %copy-start.11 = (bf16[1,2,4,3,32,512]{5,4,3,2,1,0:T(8,128)(2,1)S(1)}, bf16[1,2,4,3,32,512]{5,4,3,2,1,0:T(8,128)(2,1)}, u32[]{:S(2)}) copy-start(bf16[1,2,4,3,32,512]{5,4,3,2,1,0:T(8,128)(2,1)} %copy-done.10) | copy-start | bytes 2359300
  267.0 27.5 %collective-permute-start.13 = (bf16[4,768,768]{2,1,0:T(8,128)(2,1)}, bf16[4,768,768]{2,1,0:T(8,128)(2,1)}, u32[]{:S(2)}, u32[]{:S(2)}) collective-permute-start(bf16[4,768,768]{2,1,0:T(8,128)(2,1)} %get-tuple-element.81), channel_id=1, source_target_pairs={{0,16},{16,0},{1,17},{17,1},{2,18},{18,2},{3,19},{19,3},{4,20},{20... | collective-permute-start | bytes 14155784 | tf_op jit(solution)/shard_map/ppermute | solution.py:1013
  267.3 27.2 %all-to-all-start.4 = ((bf16[4,192,512]{2,1,0:T(8,128)(2,1)}), bf16[4,192,512]{2,1,0:T(8,128)(2,1)S(1)}, u32[]{:S(2)}, u32[]{:S(2)}) async-start(bf16[4,192,512]{2,1,0:T(8,128)(2,1)} %bitcast.100), calls=%async_computation.4 | async-start | bytes 1572864 | tf_op jit(solution)/shard_map/all_to_all | solution.py:909
  270.8 175.2 %reduce-scatter.6.cloned.1.call-start = ((), (), s32[]{:S(2)}) async-start(), calls=%async_computation.13 | async-start | bytes 5013504 | tf_op jit(solution)/shard_map/reduce_scatter | solution.py:1021
  312.3 26.8 %all-to-all-start.5 = ((bf16[4,2,96,512]{3,2,1,0:T(8,128)(2,1)}), bf16[4,2,96,512]{3,2,1,0:T(8,128)(2,1)S(1)}, u32[]{:S(2)}, u32[]{:S(2)}) async-start(bf16[4,2,96,512]{3,2,1,0:T(8,128)(2,1)} %get-tuple-element.94), calls=%async_computation.5 | async-start | bytes 1572864 | tf_op jit(solution)/shard_map/all_to_all | solution.py:1027
  339.1 9.3 %copy-start.7 = (bf16[4,2,96,512]{3,2,1,0:T(8,128)(2,1)S(1)}, bf16[4,2,96,512]{3,2,1,0:T(8,128)(2,1)}, u32[]{:S(2)}) copy-start(bf16[4,2,96,512]{3,2,1,0:T(8,128)(2,1)} %get-tuple-element.67) | copy-start | bytes 2359300
  339.1 2.6 collective-permute-start.15
  339.5 57.0 %collective-permute-start.16 = (bf16[4,768,512]{2,1,0:T(8,128)(2,1)}, bf16[4,768,512]{2,1,0:T(8,128)(2,1)}, u32[]{:S(2)}, u32[]{:S(2)}) collective-permute-start(bf16[4,768,512]{2,1,0:T(8,128)(2,1)} %get-tuple-element.111), channel_id=1, source_target_pairs={{0,16},{16,0},{1,17},{17,1},{2,18},{18,2},{3,19},{19,3},{4,20},{20... | collective-permute-start | bytes 9437192 | tf_op jit(solution)/shard_map/ppermute | solution.py:1035
  343.9 52.6 %all-to-all-start.6 = ((bf16[4,768,128]{2,1,0:T(8,128)(2,1)}), bf16[4,768,128]{2,1,0:T(8,128)(2,1)}, u32[]{:S(2)}, u32[]{:S(2)}) async-start(bf16[4,768,128]{2,1,0:T(8,128)(2,1)} %add_convert_fusion.3), calls=%async_computation.6 | async-start | bytes 1572864 | tf_op jit(solution)/shard_map/all_to_all | solution.py:1038
  348.1 172.2 %reduce-scatter.10.cloned.1.call-start = ((), (), s32[]{:S(2)}) async-start(), calls=%async_computation.18 | async-start | bytes 3932160
  451.5 5.6 collective-permute-start.17
  453.6 16.0 %all-to-all-start.9 = ((bf16[4,192,128]{2,1,0:T(8,128)(2,1)}), bf16[4,192,128]{2,1,0:T(8,128)(2,1)S(1)}, u32[]{:S(2)}, u32[]{:S(2)}) async-start(bf16[4,192,128]{2,1,0:T(8,128)(2,1)} %bitcast.38), calls=%async_computation.10 | async-start | bytes 393216 | tf_op jit(solution)/shard_map/all_to_all | solution.py:909
  469.6 49.0 %all-to-all-start.7 = ((bf16[4,768,512]{2,1,0:T(8,128)(2,1)}), bf16[4,768,512]{2,1,0:T(8,128)(2,1)S(1)}, u32[]{:S(2)}, u32[]{:S(2)}) async-start(bf16[4,768,512]{2,1,0:T(8,128)(2,1)} %get-tuple-element.116), calls=%async_computation.8 | async-start | bytes 6291456 | tf_op jit(solution)/shard_map/all_to_all | solution.py:1063
  473.3 111.2 %reduce-scatter.8.cloned.1.call-start = ((), (), s32[]{:S(2)}) async-start(), calls=%async_computation.14 | async-start | bytes 2293760 | tf_op jit(solution)/shard_map/reduce_scatter | solution.py:1087
  474.8 1.8 collective-permute-start.14
  475.3 3.9 collective-permute-start.24
  478.8 55.2 %collective-permute-start.19 = (bf16[2,192,128]{2,1,0:T(8,128)(2,1)S(1)}, bf16[2,192,128]{2,1,0:T(8,128)(2,1)S(1)}, u32[]{:S(2)}, u32[]{:S(2)}) collective-permute-start(bf16[2,192,128]{2,1,0:T(8,128)(2,1)S(1)} %broadcast_select_fusion.21), channel_id=1, source_target_pairs={{0,16},{16,0},{1,17},{17,1},{2,18},{18,2},{3,19},{19,3},{4,20},{20... | collective-permute-start | bytes 294920 | tf_op jit(solution)/shard_map/ppermute | solution.py:918
  527.3 46.2 %all-to-all-start.8 = ((bf16[4,192,512]{2,1,0:T(8,128)(2,1)}), bf16[4,192,512]{2,1,0:T(8,128)(2,1)S(1)}, u32[]{:S(2)}, u32[]{:S(2)}) async-start(bf16[4,192,512]{2,1,0:T(8,128)(2,1)} %bitcast.37), calls=%async_computation.9 | async-start | bytes 1572864 | tf_op jit(solution)/shard_map/all_to_all | solution.py:909
  534.1 5.8 collective-permute-start.21
  535.7 6.3 %collective-permute-start.20 = (bf16[2,192,256]{2,1,0:T(8,128)(2,1)S(1)}, bf16[2,192,256]{2,1,0:T(8,128)(2,1)S(1)}, u32[]{:S(2)}, u32[]{:S(2)}) collective-permute-start(bf16[2,192,256]{2,1,0:T(8,128)(2,1)S(1)} %pad_maximum_fusion.7), channel_id=1, source_target_pairs={{0,4},{4,0},{8,12},{12,8},{1,5},{5,1},{9,13},{13,9},{2,6},{6,2},{1... | collective-permute-start | bytes 589832 | tf_op jit(solution)/shard_map/ppermute | solution.py:900
  539.9 4.7 collective-permute-start.22
  542.0 4.7 collective-permute-start.23
  573.5 9.5 %collective-permute-start.18 = (bf16[2,192,512]{2,1,0:T(8,128)(2,1)S(1)}, bf16[2,192,512]{2,1,0:T(8,128)(2,1)S(1)}, u32[]{:S(2)}, u32[]{:S(2)}) collective-permute-start(bf16[2,192,512]{2,1,0:T(8,128)(2,1)S(1)} %broadcast_select_fusion.1), channel_id=1, source_target_pairs={{0,16},{16,0},{1,17},{17,1},{2,18},{18,2},{3,19},{19,3},{4,20},{20... | collective-permute-start | bytes 1179656 | tf_op jit(solution)/shard_map/ppermute | solution.py:918
  (29 other events, 112.0 us)
Sparse Core Ops, SparseCore 0:
  10.2 32.6 all-gather.6
  46.3 81.1 all-gather.8
  130.9 92.7 all-gather.10
  301.9 144.0 reduce-scatter.5
  451.6 60.8 reduce-scatter.9
  523.4 53.8 reduce-scatter.7

commit v6 on v5

--- a/solution.py
+++ b/solution.py
@@ -430,6 +430,9 @@
             half,
         ],
         compiler_params=kernel_params(),
+        cost_estimate=pl.CostEstimate(
+            flops=12 * rows * dp * width * feat * tokens, bytes_accessed=16 << 20, transcendentals=0
+        ),
         name="project_back",
     )(place, near, *x_rows, d_query, *d_kv)
 
@@ -1017,8 +1020,8 @@
     )
     g_other, d_cq, block_out = lax.optimization_barrier((g_other, d_cq, block_out))
     large_grad, d_cq = lax.optimization_barrier((with_core(g_own, g_other), d_cq))
-    large_grad = large_grad.reshape(rows * cols, part_width, 2 * units)
-    large_grad = lax.psum_scatter(large_grad, ("row", "col"), scatter_dimension=0, tiled=False)
+    large_grad = large_grad.reshape(rows, cols, part_width, 2 * units)
+    large_grad = lax.psum_scatter(large_grad, "row", scatter_dimension=0, tiled=False)
     d_cq = d_cq.reshape(blocks, feat, tokens)
     d_ckv = d_ckv.reshape(blocks, 2 * feat, d_ckv.shape[-1])
     d_attn, d_low, dy_one, dg_one = before_self(
@@ -1032,8 +1035,11 @@
     d_mixed, rest_other, rest, chosen_other, d_chosen = lax.optimization_barrier(
         (d_mixed, rest_other, rest, chosen_other, d_chosen)
     )
-    rest_other = lax.ppermute(rest_other, "dp", swap)
+    rest = with_core(rest, lax.ppermute(rest_other, "dp", swap))
     d_chosen = with_core(d_chosen, lax.ppermute(chosen_other, "dp", swap))
+    rest, d_mixed, d_chosen = lax.optimization_barrier((rest, d_mixed, d_chosen))
+    rest = rest.reshape(rows, cols, part_width, -1)
+    rest = lax.psum_scatter(rest, "row", scatter_dimension=0, tiled=False)
     d_chosen = d_chosen.reshape(rows, sub * width, c_tokens)
     d_chosen = lax.all_to_all(d_chosen, "row", 0, 0, tiled=True)
 
@@ -1041,11 +1047,12 @@
     d_query, *d_kv = attend_back(
         meta, query, kv_list, d_mixed, mixed, lse, True, types, "self_attention_back"
     )
-    d_query, d_chosen, rest_other, large_grad = lax.optimization_barrier(
-        (d_query, d_chosen, rest_other, large_grad)
-    )
-    rest = with_core(rest, rest_other).reshape(rows, cols, part_width, -1)
-    rest = lax.psum_scatter(rest, "row", scatter_dimension=0, tiled=False)
+    d_query, d_chosen, rest, large_grad = lax.optimization_barrier(
+        (d_query, d_chosen, rest, large_grad)
+    )
+    joined = jnp.concatenate([large_grad, rest], axis=2)
+    joined, d_query = lax.optimization_barrier((joined, d_query))
+    joined = lax.psum_scatter(joined, "col", scatter_dimension=0, tiled=False)
     if sub == 1:
         d_kv = [d_kv[0], lax.ppermute(d_kv[1], "dp", swap)]
     else:
@@ -1061,8 +1068,10 @@
         place, near, x_rows, d_query.reshape(rows, dp, feat, tokens), d_kv
     )
     dx_part = lax.all_to_all(dx_part, "row", 0, 0, tiled=True)
+    dx_part, joined = lax.optimization_barrier((dx_part, joined))
+    joined = joined.astype(f32)
     dx = dy_one + jnp.sum(dx_part.astype(f32), axis=0)
-    x_grad = to_home(dx.astype(bf16)).astype(f32)
+    x_moved = home_cols(dx.astype(bf16))
 
     d_chosen = jnp.sum(d_chosen.astype(f32), axis=0).astype(bf16)
     if sub > 1:
@@ -1081,12 +1090,14 @@
     )
     hot_all = (pick_rows[:, :, None] == bank_ids[None, None, :]).astype(bf16)
     bank_grad = mm("swp,spn->swn", d_chosen, hot_all)
+    x_moved, bank_grad = lax.optimization_barrier((x_moved, bank_grad))
+    x_grad = home_cores(x_moved).astype(f32)
 
     qkv = with_core(g_qkv, lax.ppermute(qkv_other, "dp", swap))
-    last = jnp.concatenate([rest, qkv.reshape(cols, part_width, -1)], axis=2)
-    last = lax.psum_scatter(last, "col", scatter_dimension=0, tiled=False).astype(f32)
-    rest, qkv_grad = last[:, :512], last[:, 512:]
-    large_grad = large_grad.astype(f32)
+    qkv_grad = lax.psum_scatter(
+        qkv.reshape(cols, part_width, -1), "col", scatter_dimension=0, tiled=False
+    ).astype(f32)
+    large_grad, rest = joined[:, : 2 * units], joined[:, 2 * units :]
 
     return (
         home_cores(block_out),

time: 603 us -> 542 us (0.90)
  waiting for transfers between devices: 216 us -> 143 us
    reduce_scatter x2, waiting for transfers between devices: 49.5 us -> 0.01 us  [the longest x1 0.01 us: per_device(): joined = lax.psum_scatter(joined, 'col', scatter_dimension=0, tiled=False)]
    all_to_all x1, waiting for transfers between devices: 36.2 us -> 0.01 us  [per_device(): dx_part = lax.all_to_all(dx_part, 'row', 0, 0, tiled=True)]
    all_to_all x3, waiting for transfers between devices: 26.8 us -> 4.95 us  [home_cols(): return lax.all_to_all(value, 'col', 0, 0, tiled=True)]
    ppermute x12, waiting for transfers between devices: 53.2 us -> 72.6 us  [send(): return lax.ppermute(v, 'row', [(i, i ^ k) for i in range(rows)])]
    unnamed x7 -> x9, waiting for transfers between devices: 0.1 us -> 9.47 us
    unnamed x83 -> x87, local copies, waits for them, and re-layouts: 12 us -> 14.8 us
  transfers between devices with their start and end apart: 41 -> 42, of which waited for: 19 -> 18; matrix products, arithmetic and copies ran while one was open for 8% -> 11% of each run, Pallas kernels for 30% -> 35%
where the time goes in v6:
time: 542 us; the launch traced here: 534 us
  Pallas kernels  229 us (42%)
  waiting for transfers between devices  143 us (26%)
  starting transfers between devices  63.2 us (12%)
  other arithmetic  40.3 us (7%)
  local copies, waits for them, and re-layouts  30.2 us (6%)
  between operations  15.9 us (3%)
  matrix products  11.1 us (2%)
    pallas_call x2, Pallas kernels, attend_back(): pl.pallas_call(functools.partial(attend_back_kernel, sources=len(kv_list)...  73 us
    ppermute x12, waiting for transfers between devices, send(): return lax.ppermute(v, 'row', [(i, i ^ k) for i in range(rows)])  72.6 us
    pallas_call x1, Pallas kernels, middle(): pl.pallas_call(middle_kernel, grid_spec=pltpu.PrefetchScalarGridSpec(num_...  43.1 us
    pallas_call x2, Pallas kernels, attend(): pl.pallas_call(functools.partial(attend_kernel, sources=len(kv_list), n_q...  41.7 us
    all_to_all x3, waiting for transfers between devices, across_cols(): lax.all_to_all(value, 'col', 0, 0, tiled=True)  28.3 us
    pallas_call x1, Pallas kernels, small_grads(): pl.pallas_call(functools.partial(small_grads_kernel, paired=paired), grid...  23.4 us
    ppermute x12, starting transfers between devices, send(): return lax.ppermute(v, 'row', [(i, i ^ k) for i in range(rows)])  16.4 us
    convert_element_type x4, other arithmetic, with_core(): return (own.astype(f32) + got.astype(f32)).astype(bf16)  15.1 us
  transfers between devices with their start and end apart: 42, of which 18 were waited for; matrix products, arithmetic and copies ran while one was open for 11% of the time, Pallas kernels for 35%

profile of v6, /device:TPU:0, one launch (start us, length us, event | category | flops | bytes accessed | tf_op | source)
XLA Modules:
  0.0 534.2 jit_solution(13079916750886871732)
XLA Ops:
  15.0 6.4 %all-to-all-start = ((bf16[4,192,512]{2,1,0:T(8,128)(2,1)}), bf16[4,192,512]{2,1,0:T(8,128)(2,1)}, u32[]{:S(2)}, u32[]{:S(2)}) async-start(bf16[4,192,512]{2,1,0:T(8,128)(2,1)} %pad_maximum_fusion.1), calls=%async_computation | async-start | bytes 1572864 | tf_op jit(solution)/shard_map/all_to_all | solution.py:892
  22.1 28.3 %all-to-all-done = bf16[4,192,512]{2,1,0:T(8,128)(2,1)} async-done(((bf16[4,192,512]{2,1,0:T(8,128)(2,1)}), bf16[4,192,512]{2,1,0:T(8,128)(2,1)}, u32[]{:S(2)}, u32[]{:S(2)}) %all-to-all-start) | async-done | bytes 786464 | tf_op jit(solution)/shard_map/all_to_all | solution.py:892
  50.5 1.5 collective-permute-start.2
  53.5 18.0 %collective-permute-done.2.refs_2_ = bf16[768,512]{1,0:T(8,128)(2,1)S(1)} collective-permute-done((bf16[768,512]{1,0:T(8,128)(2,1)}, bf16[768,512]{1,0:T(8,128)(2,1)S(1)}, u32[]{:S(2)}, u32[]{:S(2)}) %collective-permute-start.2) | collective-permute-done | bytes 786464 | tf_op jit(solution)/shard_map/ppermute | solution.py:903
  78.4 10.5 %collective-permute-done.3 = bf16[384,512]{1,0:T(8,128)(2,1)S(1)} collective-permute-done((bf16[384,512]{1,0:T(8,128)(2,1)}, bf16[384,512]{1,0:T(8,128)(2,1)S(1)}, u32[]{:S(2)}, u32[]{:S(2)}) %collective-permute-start.3) | collective-permute-done | bytes 393248 | tf_op jit(solution)/shard_map/ppermute | solution.py:903
  89.7 1.8 constant_dynamic-update-slice_fusion.refs_3_
  91.5 6.6 %project.1 = (bf16[4,2,96,512]{3,2,1,0:T(8,128)(2,1)}, bf16[4,2,2,96,512]{4,3,2,1,0:T(8,128)(2,1)}) custom-call(s32[2]{0:T(128)} %pad_add_fusion.1.place_ref, bf16[2,768,384]{2,1,0:T(8,128)(2,1)} %bitcast.99, bf16[768,512]{1,0:T(8,128)(2,1)} %bitcast.2.refs_0_.x_ref, bf16[768,512]{1,0:T(8,128)(2,1)} %copy-done.21, bf16[768,512]{1,0:T(8,128)(2,1)} %copy-done.20, ...), custom_call_target="tpu_custom_call" | custom-call | tf_op jit(solution)/shard_map/project/pallas_call | solution.py:350
  98.2 1.6 fusion.5
  102.0 1.9 broadcast_select_fusion.12
  103.9 2.0 all-reduce.1
  108.0 3.4 all-to-all-start.2
  111.4 28.8 %self_attention.1 = (bf16[4,2,3,32,512]{4,3,2,1,0:T(8,128)(2,1)}, f32[3,4,1,512]{3,2,1,0:T(1,128)S(1)}) custom-call(s32[13]{0:T(128)S(1)} %pad_add_fusion.2.refs_0_, bf16[4,2,3,32,512]{4,3,2,1,0:T(8,128)(2,1)S(1)} %bitcast.72, bf16[4,2,2,3,32,512]{5,4,3,2,1,0:T(8,128)(2,1)S(1)} %bitcast.71, bf16[4,2,2,3,32,512]{5,4,3,2,1,0:T(8,128)(2,1)} %collective-permute-done.5.refs_3_), custom_call_target="tpu_custom_call" | custom-call | flops 12884901888 | bytes 6291456 | tf_op jit(solution)/shard_map/self_attention/pallas_call | solution.py:238
  140.1 4.0 all-to-all-start.1
  145.2 8.9 %all-to-all-done.1 = bf16[4,2,3,32,512]{4,3,2,1,0:T(8,128)(2,1)S(1)} async-done(((bf16[4,2,3,32,512]{4,3,2,1,0:T(8,128)(2,1)}), bf16[4,2,3,32,512]{4,3,2,1,0:T(8,128)(2,1)S(1)}, u32[]{:S(2)}, u32[]{:S(2)}) %all-to-all-start.1) | async-done | bytes 786464 | tf_op jit(solution)/shard_map/all_to_all | solution.py:984
  154.1 5.2 all-to-all-start.3
  162.5 8.3 %collective-permute-done.9 = bf16[2,768,128]{2,1,0:T(8,128)(2,1)S(1)} collective-permute-done((bf16[2,768,128]{2,1,0:T(8,128)(2,1)S(1)}, bf16[2,768,128]{2,1,0:T(8,128)(2,1)S(1)}, u32[]{:S(2)}, u32[]{:S(2)}) %collective-permute-start.9) | collective-permute-done | bytes 393248 | tf_op jit(solution)/shard_map/ppermute | solution.py:903
  172.4 3.6 collective-permute-done.8
  177.5 1.8 collective-permute-done.10
  179.3 2.4 collective-permute-done.11
  182.9 9.0 %cross_kv.1 = bf16[8,192,1024]{2,1,0:T(8,128)(2,1)} custom-call(bf16[8,768,512]{2,1,0:T(8,128)(2,1)} %bitcast.80, bf16[8,768,128]{2,1,0:T(8,128)(2,1)} %copy-done.19), custom_call_target="tpu_custom_call" | custom-call | tf_op jit(solution)/shard_map/cross_kv/pallas_call | solution.py:458
  191.8 9.0 %after_self.1 = (f32[768,512]{1,0:T(8,128)}, f32[1,512]{1,0:T(1,128)}, bf16[768,512]{1,0:T(8,128)(2,1)}, bf16[8,96,512]{2,1,0:T(8,128)(2,1)}) custom-call(bf16[768,512]{1,0:T(8,128)(2,1)} %bitcast.2.refs_0_.x_ref, bf16[4,2,96,512]{3,2,1,0:T(8,128)(2,1)} %bitcast.93, bf16[8,768,512]{2,1,0:T(8,128)(2,1)} %bitcast.81), custom_call_target="tpu_custom_call" | custom-call | tf_op jit(solution)/shard_map/after_self/pallas_call | solution.py:506
  201.9 12.9 %cross_attention.1 = (bf16[1,2,4,3,32,512]{5,4,3,2,1,0:T(8,128)(2,1)S(1)}, f32[12,1,1,512]{3,2,1,0:T(1,128)S(1)}) custom-call(s32[13]{0:T(128)S(1)} %pad_add_fusion.2.refs_0_, bf16[1,2,4,3,32,512]{5,4,3,2,1,0:T(8,128)(2,1)S(1)} %bitcast.74, bf16[1,2,4,2,3,32,1024]{6,5,4,3,2,1,0:T(8,128)(2,1)S(1)} %bitcast.65), custom_call_target="tpu_custom_call" | custom-call | flops 3221225472 | bytes 6291456 | tf_op jit(solution)/shard_map/cross_attention/pallas_call | solution.py:238
  215.8 7.9 %all-gather.11.cloned.1.call-done = bf16[6144,768]{1,0:T(8,128)(2,1)} async-done(((bf16[192,768]{1,0:T(8,128)(2,1)}), bf16[6144,768]{1,0:T(8,128)(2,1)}) %all-gather.11.cloned.1.call-update) | async-done | bytes 9437200 | tf_op jit(solution)/shard_map/all_gather | solution.py:956
  223.7 43.1 %middle.1 = (bf16[768,512]{1,0:T(8,128)(2,1)}, bf16[8,96,512]{2,1,0:T(8,128)(2,1)}, f32[768,512]{1,0:T(8,128)}, bf16[768,512]{1,0:T(8,128)(2,1)}, bf16[4,768,768...) custom-call(s32[2]{0:T(128)} %pad_add_fusion.1.place_ref, ...), custom_call_target="tpu_custom_call" | custom-call | flops 14495514624 | bytes 37748736 | tf_op jit(solution)/shard_map/middle/pallas_call | solution.py:643
  267.2 3.6 all-to-all-start.4
  272.2 21.4 %cross_attention_back.1 = (bf16[1,2,4,3,32,512]{5,4,3,2,1,0:T(8,128)(2,1)S(1)}, bf16[1,2,4,2,3,32,1024]{6,5,4,3,2,1,0:T(8,128)(2,1)}) custom-call(s32[13]{0:T(128)S(1)} %pad_add_fusion.2.refs_0_, bf16[1,2,4,3,32,512]{5,4,3,2,1,0:T(8,128)(2,1)S(1)} %bitcast.75, bf16[1,2,4,2,3,32,1024]{6,5,4,3,2,1,0:T(8,128)(2,1)} %bitcast.64, ...), custom_call_target="tpu_custom_call" | custom-call | flops 8053063680 | bytes 6291456 | tf_op jit(solution)/shard_map/cross_attention_back/pallas_call | solution.py:259
  294.5 7.3 %add_convert_fusion = bf16[4,768,768]{2,1,0:T(8,128)(2,1)} fusion(bf16[4,768,768]{2,1,0:T(8,128)(2,1)} %collective-permute-done.13, bf16[4,768,768]{2,1,0:T(8,128)(2,1)} %get-tuple-element.96), kind=kLoop, calls=%fused_computation.3 | loop fusion | flops 9437184 | bytes 14155776 | tf_op jit(solution)/shard_map/convert_element_type | solution.py:1014
  301.8 10.5 %before_self.1 = (bf16[4,2,96,512]{3,2,1,0:T(8,128)(2,1)}, bf16[768,512]{1,0:T(8,128)(2,1)}, f32[768,512]{1,0:T(8,128)}, f32[768,128]{1,0:T(8,128)}) custom-call(bf16[8,96,512]{2,1,0:T(8,128)(2,1)} %bitcast.67, bf16[8,768,512]{2,1,0:T(8,128)(2,1)} %bitcast.83, f32[768,512]{1,0:T(8,128)} %get-tuple-element.100.dy_ref, ...), custom_call_target="tpu_custom_call" | custom-call | tf_op jit(solution)/shard_map/before_self/pallas_call | solution.py:714
  312.3 3.5 all-to-all-start.5
  315.9 23.4 %small_grads.1 = (bf16[4,768,512]{2,1,0:T(8,128)(2,1)}, bf16[4,768,512]{2,1,0:T(8,128)(2,1)}, bf16[4,768,128]{2,1,0:T(8,128)(2,1)}, bf16[4,768,128]{2,1,0:T(8,128)(2,1)}) custom-call(s32[2]{0:T(128)} %pad_add_fusion.1.place_ref, bf16[8,768,512]{2,1,0:T(8,128)(2,1)} %bitcast.84, bf16[8,768,128]{2,1,0:T(8,128)(2,1)} %copy-done.19, ...), custom_call_target="tpu_custom_call" | custom-call | flops 6643777536 | bytes 12582912 | tf_op jit(solution)/shard_map/small_grads/pallas_call | solution.py:806
  339.9 6.5 %collective-permute-done.16 = bf16[4,768,128]{2,1,0:T(8,128)(2,1)S(1)} collective-permute-done((bf16[4,768,128]{2,1,0:T(8,128)(2,1)}, bf16[4,768,128]{2,1,0:T(8,128)(2,1)S(1)}, u32[]{:S(2)}, u32[]{:S(2)}) %collective-permute-start.16) | collective-permute-done | bytes 786464 | tf_op jit(solution)/shard_map/ppermute | solution.py:1039
  346.4 2.2 add_convert_fusion.3
  348.7 4.4 add_convert_fusion.1
  353.2 4.3 all-to-all-start.6
  357.8 51.6 %self_attention_back.1 = (bf16[4,2,3,32,512]{4,3,2,1,0:T(8,128)(2,1)S(1)}, f32[4,2,2,3,32,512]{5,4,3,2,1,0:T(8,128)}, bf16[4,2,2,3,32,512]{5,4,3,2,1,0:T(8,128)(2,1)S(1)}) custom-call(s32[13]{0:T(128)S(1)} %pad_add_fusion.2.refs_0_, bf16[4,2,3,32,512]{4,3,2,1,0:T(8,128)(2,1)S(1)} %bitcast.73, bf16[4,2,2,3,32,512]{5,4,3,2,1,0:T(8,128)(2,1)} %bitcast.70, ...), custom_call_target="tpu_custom_call" | custom-call | flops 32212254720 | bytes 6291456 | tf_op jit(solution)/shard_map/self_attention_back/pallas_call | solution.py:259
  410.3 2.5 copy.54
  412.8 9.4 %reduce-scatter.13.cloned.1.call-done = bf16[1,4,192,512]{3,2,1,0:T(8,128)(2,1)} async-done(((bf16[4,4,192,512]{3,2,1,0:T(8,128)(2,1)}), bf16[1,4,192,512]{3,2,1,0:T(8,128)(2,1)}) %reduce-scatter.13.cloned.1.call-update) | async-done | bytes 786448
  423.6 3.4 pad_maximum_fusion
  427.0 2.0 reduce_sum.22
  428.9 4.6 all-to-all-start.9
  433.5 12.4 %project_back.1 = (bf16[4,768,512]{2,1,0:T(8,128)(2,1)}, bf16[768,384]{1,0:T(8,128)(2,1)}, bf16[768,384]{1,0:T(8,128)(2,1)}) custom-call(s32[2]{0:T(128)} %pad_add_fusion.1.place_ref, bf16[2,768,384]{2,1,0:T(8,128)(2,1)} %bitcast.100, bf16[768,512]{1,0:T(8,128)(2,1)} %bitcast.2.refs_0_.x_ref, bf16[768,512]{1,0:T(8,128)(2,1)} %copy-done.21, ...), custom_call_target="tpu_custom_call" | custom-call | flops 3623878656 | bytes 16777216 | tf_op jit(solution)/shard_map/project_back/pallas_call | solution.py:411
  446.6 3.7 all-to-all-start.7
  452.0 1.7 collective-permute-done.14
  458.1 1.9 collective-permute-start.20
  462.6 27.9 %collective-permute-done.20 = bf16[2,192,256]{2,1,0:T(8,128)(2,1)S(1)} collective-permute-done((bf16[2,192,256]{2,1,0:T(8,128)(2,1)}, bf16[2,192,256]{2,1,0:T(8,128)(2,1)S(1)}, u32[]{:S(2)}, u32[]{:S(2)}) %collective-permute-start.20) | collective-permute-done | bytes 196640 | tf_op jit(solution)/shard_map/ppermute | solution.py:903
  497.8 4.3 all-to-all-start.8
  503.2 9.4 %fusion = f32[2,192,4096]{2,1,0:T(8,128)} fusion(bf16[2,192,1024]{2,1,0:T(8,128)(2,1)S(1)} %maximum_dynamic-update-slice_fusion, s32[2,1024]{1,0:T(2,128)S(1)} %pad_add_fusion), kind=kOutput, calls=%fused_computation.1 | convolution fusion | flops 3229614080 | bytes 7086080 | tf_op jit(solution)/shard_map/swp,spn->swn/dot_general | solution.py:845
  517.0 4.3 all-to-all-done.8
  (208 shorter events, 64.7 us)
Async XLA Ops:
  7.2 91.0 %copy-start = (bf16[2,192,4096]{2,1,0:T(8,128)(2,1)S(1)}, bf16[2,192,4096]{2,1,0:T(8,128)(2,1)}, u32[]{:S(2)}) copy-start(bf16[2,192,4096]{2,1,0:T(8,128)(2,1)} %param.15) | copy-start | bytes 9437188
  7.2 84.3 %all-gather.7.cloned.1.call-start = ((), (), s32[]{:S(2)}) async-start(), calls=%async_computation.16 | async-start | bytes 1327104 | tf_op jit(solution)/shard_map/all_gather | solution.py:935
  9.2 172.6 %all-gather.9.cloned.1.call-start = ((), (), s32[]{:S(2)}) async-start(), calls=%async_computation.17 | async-start | bytes 6488064 | tf_op jit(solution)/shard_map/all_gather | solution.py:956
  10.5 1.9 collective-permute-start
  15.0 35.5 %all-to-all-start = ((bf16[4,192,512]{2,1,0:T(8,128)(2,1)}), bf16[4,192,512]{2,1,0:T(8,128)(2,1)}, u32[]{:S(2)}, u32[]{:S(2)}) async-start(bf16[4,192,512]{2,1,0:T(8,128)(2,1)} %pad_maximum_fusion.1), calls=%async_computation | async-start | bytes 1572864 | tf_op jit(solution)/shard_map/all_to_all | solution.py:892
  21.4 202.3 %all-gather.11.cloned.1.call-start = ((), (), s32[]{:S(2)}) async-start(), calls=%async_computation.18 | async-start | bytes 9732096 | tf_op jit(solution)/shard_map/all_gather | solution.py:956
  50.5 21.1 %collective-permute-start.2 = (bf16[768,512]{1,0:T(8,128)(2,1)}, bf16[768,512]{1,0:T(8,128)(2,1)S(1)}, u32[]{:S(2)}, u32[]{:S(2)}) collective-permute-start(bf16[768,512]{1,0:T(8,128)(2,1)} %bitcast.2.refs_0_.x_ref), channel_id=1, source_target_pairs={{0,8},{4,12},{8,0},{12,4},{1,9},{5,13},{9,1},{13,5},{2,10},{6,14},... | collective-permute-start | bytes 2359304 | tf_op jit(solution)/shard_map/ppermute | solution.py:903
  52.0 22.7 %collective-permute-start.1 = (bf16[768,512]{1,0:T(8,128)(2,1)}, bf16[768,512]{1,0:T(8,128)(2,1)S(1)}, u32[]{:S(2)}, u32[]{:S(2)}) collective-permute-start(bf16[768,512]{1,0:T(8,128)(2,1)} %bitcast.2.refs_0_.x_ref), channel_id=1, source_target_pairs={{0,4},{4,0},{8,12},{12,8},{1,5},{5,1},{9,13},{13,9},{2,6},{6,2},{1... | collective-permute-start | bytes 2359304 | tf_op jit(solution)/shard_map/ppermute | solution.py:903
  73.2 15.7 %collective-permute-start.3 = (bf16[384,512]{1,0:T(8,128)(2,1)}, bf16[384,512]{1,0:T(8,128)(2,1)S(1)}, u32[]{:S(2)}, u32[]{:S(2)}) collective-permute-start(bf16[384,512]{1,0:T(8,128)(2,1)} %slice.114), channel_id=1, source_target_pairs={{0,4},{4,0},{8,12},{12,8},{1,5},{5,1},{9,13},{13,9},{2,6},{6,2},{1... | collective-permute-start | bytes 1179656 | tf_op jit(solution)/shard_map/ppermute | solution.py:903
  76.3 13.4 %collective-permute-start.4 = (bf16[384,512]{1,0:T(8,128)(2,1)}, bf16[384,512]{1,0:T(8,128)(2,1)}, u32[]{:S(2)}, u32[]{:S(2)}) collective-permute-start(bf16[384,512]{1,0:T(8,128)(2,1)} %slice.115), channel_id=1, source_target_pairs={{0,8},{4,12},{8,0},{12,4},{1,9},{5,13},{9,1},{13,5},{2,10},{6,14},... | collective-permute-start | bytes 1179656 | tf_op jit(solution)/shard_map/ppermute | solution.py:903
  98.2 13.2 %collective-permute-start.5 = (bf16[4,2,2,3,32,512]{5,4,3,2,1,0:T(8,128)(2,1)}, bf16[4,2,2,3,32,512]{5,4,3,2,1,0:T(8,128)(2,1)}, u32[]{:S(2)}, u32[]{:S(2)}) collective-permute-start(bf16[4,2,2,3,32,512]{5,4,3,2,1,0:T(8,128)(2,1)} %bitcast.69), channel_id=1, source_target_pairs={{0,16},{16,0},{1,17},{17,1},{2,18},{18,2},{3,19},{19,3},{4,20},{20... | collective-permute-start | bytes 4718600 | tf_op jit(solution)/shard_map/ppermute | solution.py:972
  99.9 11.5 %copy-start.4 = (bf16[4,2,2,96,512]{4,3,2,1,0:T(8,128)(2,1)S(1)}, bf16[4,2,2,96,512]{4,3,2,1,0:T(8,128)(2,1)}, u32[]{:S(2)}) copy-start(bf16[4,2,2,96,512]{4,3,2,1,0:T(8,128)(2,1)} %get-tuple-element.77) | copy-start | bytes 4718596
  99.9 11.5 %copy-start.5 = (bf16[4,2,96,512]{3,2,1,0:T(8,128)(2,1)S(1)}, bf16[4,2,96,512]{3,2,1,0:T(8,128)(2,1)}, u32[]{:S(2)}) copy-start(bf16[4,2,96,512]{3,2,1,0:T(8,128)(2,1)} %get-tuple-element.76) | copy-start | bytes 2359300
  99.9 7.3 %collective-permute-start.6 = (bf16[2,192,128]{2,1,0:T(8,128)(2,1)S(1)}, bf16[2,192,128]{2,1,0:T(8,128)(2,1)S(1)}, u32[]{:S(2)}, u32[]{:S(2)}) collective-permute-start(bf16[2,192,128]{2,1,0:T(8,128)(2,1)S(1)} %broadcast_select_fusion.18), channel_id=1, source_target_pairs={{0,16},{16,0},{1,17},{17,1},{2,18},{18,2},{3,19},{19,3},{4,20},{20... | collective-permute-start | bytes 294920 | tf_op jit(solution)/shard_map/ppermute | solution.py:879
  103.9 40.3 %collective-permute-start.12 = (bf16[2,192,512]{2,1,0:T(8,128)(2,1)}, bf16[2,192,512]{2,1,0:T(8,128)(2,1)S(1)}, u32[]{:S(2)}, u32[]{:S(2)}) collective-permute-start(bf16[2,192,512]{2,1,0:T(8,128)(2,1)} %broadcast_select_fusion.12), channel_id=1, source_target_pairs={{0,16},{16,0},{1,17},{17,1},{2,18},{18,2},{3,19},{19,3},{4,20},{20... | collective-permute-start | bytes 1179656 | tf_op jit(solution)/shard_map/ppermute | solution.py:879
  108.0 32.2 %all-to-all-start.2 = ((bf16[4,192,128]{2,1,0:T(8,128)(2,1)}), bf16[4,192,128]{2,1,0:T(8,128)(2,1)S(1)}, u32[]{:S(2)}, u32[]{:S(2)}) async-start(bf16[4,192,128]{2,1,0:T(8,128)(2,1)} %pad_maximum_fusion.6), calls=%async_computation.2 | async-start | bytes 393216 | tf_op jit(solution)/shard_map/all_to_all | solution.py:892
  140.1 14.0 %all-to-all-start.1 = ((bf16[4,2,3,32,512]{4,3,2,1,0:T(8,128)(2,1)}), bf16[4,2,3,32,512]{4,3,2,1,0:T(8,128)(2,1)S(1)}, u32[]{:S(2)}, u32[]{:S(2)}) async-start(bf16[4,2,3,32,512]{4,3,2,1,0:T(8,128)(2,1)} %get-tuple-element.78.refs_5_), calls=%async_computation.1 | async-start | bytes 1572864 | tf_op jit(solution)/shard_map/all_to_all | solution.py:984
  144.2 15.2 %collective-permute-start.7 = (bf16[768,128]{1,0:T(8,128)(2,1)S(1)}, bf16[768,128]{1,0:T(8,128)(2,1)S(1)}, u32[]{:S(2)}, u32[]{:S(2)}) collective-permute-start(bf16[768,128]{1,0:T(8,128)(2,1)S(1)} %bitcast.96), channel_id=1, source_target_pairs={{0,16},{16,0},{1,17},{17,1},{2,18},{18,2},{3,19},{19,3},{4,20},{20... | collective-permute-start | bytes 589832 | tf_op jit(solution)/shard_map/ppermute | solution.py:999
  154.1 8.3 %copy-start.18 = (bf16[4,2,3,32,512]{4,3,2,1,0:T(8,128)(2,1)}, bf16[4,2,3,32,512]{4,3,2,1,0:T(8,128)(2,1)S(1)}, u32[]{:S(2)}) copy-start(bf16[4,2,3,32,512]{4,3,2,1,0:T(8,128)(2,1)S(1)} %all-to-all-done.1) | copy-start | bytes 2359300
  154.1 61.6 %all-to-all-start.3 = ((bf16[4,192,512]{2,1,0:T(8,128)(2,1)}), bf16[4,192,512]{2,1,0:T(8,128)(2,1)}, u32[]{:S(2)}, u32[]{:S(2)}) async-start(bf16[4,192,512]{2,1,0:T(8,128)(2,1)} %pad_maximum_fusion.2), calls=%async_computation.3 | async-start | bytes 1572864 | tf_op jit(solution)/shard_map/all_to_all | solution.py:892
  159.5 11.4 %collective-permute-start.9 = (bf16[2,768,128]{2,1,0:T(8,128)(2,1)S(1)}, bf16[2,768,128]{2,1,0:T(8,128)(2,1)S(1)}, u32[]{:S(2)}, u32[]{:S(2)}) collective-permute-start(bf16[2,768,128]{2,1,0:T(8,128)(2,1)S(1)} %pad_maximum_fusion.4), channel_id=1, source_target_pairs={{0,8},{4,12},{8,0},{12,4},{1,9},{5,13},{9,1},{13,5},{2,10},{6,14},... | collective-permute-start | bytes 1179656 | tf_op jit(solution)/shard_map/ppermute | solution.py:903
  161.0 14.9 %collective-permute-start.8 = (bf16[2,768,128]{2,1,0:T(8,128)(2,1)S(1)}, bf16[2,768,128]{2,1,0:T(8,128)(2,1)S(1)}, u32[]{:S(2)}, u32[]{:S(2)}) collective-permute-start(bf16[2,768,128]{2,1,0:T(8,128)(2,1)S(1)} %pad_maximum_fusion.4), channel_id=1, source_target_pairs={{0,4},{4,0},{8,12},{12,8},{1,5},{5,1},{9,13},{13,9},{2,6},{6,2},{1... | collective-permute-start | bytes 1179656 | tf_op jit(solution)/shard_map/ppermute | solution.py:903
  170.8 8.4 %collective-permute-start.10 = (bf16[1,768,128]{2,1,0:T(8,128)(2,1)S(1)}, bf16[1,768,128]{2,1,0:T(8,128)(2,1)S(1)}, u32[]{:S(2)}, u32[]{:S(2)}) collective-permute-start(bf16[1,768,128]{2,1,0:T(8,128)(2,1)S(1)} %slice.118), channel_id=1, source_target_pairs={{0,4},{4,0},{8,12},{12,8},{1,5},{5,1},{9,13},{13,9},{2,6},{6,2},{1... | collective-permute-start | bytes 589832 | tf_op jit(solution)/shard_map/ppermute | solution.py:903
  175.9 5.7 %collective-permute-start.11 = (bf16[1,768,128]{2,1,0:T(8,128)(2,1)S(1)}, bf16[1,768,128]{2,1,0:T(8,128)(2,1)S(1)}, u32[]{:S(2)}, u32[]{:S(2)}) collective-permute-start(bf16[1,768,128]{2,1,0:T(8,128)(2,1)S(1)} %slice.119), channel_id=1, source_target_pairs={{0,8},{4,12},{8,0},{12,4},{1,9},{5,13},{9,1},{13,5},{2,10},{6,14},... | collective-permute-start | bytes 589832 | tf_op jit(solution)/shard_map/ppermute | solution.py:903
  191.8 9.0 %copy-start.2 = (bf16[8,192,1024]{2,1,0:T(8,128)(2,1)S(1)}, bf16[8,192,1024]{2,1,0:T(8,128)(2,1)}, u32[]{:S(2)}) copy-start(bf16[8,192,1024]{2,1,0:T(8,128)(2,1)} %cross_kv.1) | copy-start | bytes 9437188
  266.8 27.6 %collective-permute-start.13 = (bf16[4,768,768]{2,1,0:T(8,128)(2,1)}, bf16[4,768,768]{2,1,0:T(8,128)(2,1)}, u32[]{:S(2)}, u32[]{:S(2)}) collective-permute-start(bf16[4,768,768]{2,1,0:T(8,128)(2,1)} %get-tuple-element.90), channel_id=1, source_target_pairs={{0,16},{16,0},{1,17},{17,1},{2,18},{18,2},{3,19},{19,3},{4,20},{20... | collective-permute-start | bytes 14155784 | tf_op jit(solution)/shard_map/ppermute | solution.py:1016
  267.2 27.3 %all-to-all-start.4 = ((bf16[4,192,512]{2,1,0:T(8,128)(2,1)}), bf16[4,192,512]{2,1,0:T(8,128)(2,1)S(1)}, u32[]{:S(2)}, u32[]{:S(2)}) async-start(bf16[4,192,512]{2,1,0:T(8,128)(2,1)} %bitcast.101), calls=%async_computation.4 | async-start | bytes 1572864 | tf_op jit(solution)/shard_map/all_to_all | solution.py:912
  270.8 139.5 %reduce-scatter.15.cloned.1.call-start = ((), (), s32[]{:S(2)}) async-start(), calls=%async_computation.20 | async-start | bytes 5898240
  312.3 27.0 %all-to-all-start.5 = ((bf16[4,2,96,512]{3,2,1,0:T(8,128)(2,1)}), bf16[4,2,96,512]{3,2,1,0:T(8,128)(2,1)S(1)}, u32[]{:S(2)}, u32[]{:S(2)}) async-start(bf16[4,2,96,512]{3,2,1,0:T(8,128)(2,1)} %get-tuple-element.103), calls=%async_computation.5 | async-start | bytes 1572864 | tf_op jit(solution)/shard_map/all_to_all | solution.py:1030
  315.8 106.3 %reduce-scatter.13.cloned.1.call-start = ((), (), s32[]{:S(2)}) async-start(), calls=%async_computation.19 | async-start | bytes 3932160
  339.3 9.4 %collective-permute-start.15 = (bf16[4,768,512]{2,1,0:T(8,128)(2,1)}, bf16[4,768,512]{2,1,0:T(8,128)(2,1)S(1)}, u32[]{:S(2)}, u32[]{:S(2)}) collective-permute-start(bf16[4,768,512]{2,1,0:T(8,128)(2,1)} %get-tuple-element.116), channel_id=1, source_target_pairs={{0,16},{16,0},{1,17},{17,1},{2,18},{18,2},{3,19},{19,3},{4,20},{20... | collective-permute-start | bytes 9437192 | tf_op jit(solution)/shard_map/ppermute | solution.py:1038
  339.8 6.6 %collective-permute-start.16 = (bf16[4,768,128]{2,1,0:T(8,128)(2,1)}, bf16[4,768,128]{2,1,0:T(8,128)(2,1)S(1)}, u32[]{:S(2)}, u32[]{:S(2)}) collective-permute-start(bf16[4,768,128]{2,1,0:T(8,128)(2,1)} %get-tuple-element.119), channel_id=1, source_target_pairs={{0,16},{16,0},{1,17},{17,1},{2,18},{18,2},{3,19},{19,3},{4,20},{20... | collective-permute-start | bytes 2359304 | tf_op jit(solution)/shard_map/ppermute | solution.py:1039
  353.2 70.4 %all-to-all-start.6 = ((bf16[4,768,128]{2,1,0:T(8,128)(2,1)}), bf16[4,768,128]{2,1,0:T(8,128)(2,1)}, u32[]{:S(2)}, u32[]{:S(2)}) async-start(bf16[4,768,128]{2,1,0:T(8,128)(2,1)} %add_convert_fusion.3), calls=%async_computation.6 | async-start | bytes 1572864 | tf_op jit(solution)/shard_map/all_to_all | solution.py:1044
  357.5 137.8 %reduce-scatter.9.cloned.1.call-start = ((), (), s32[]{:S(2)}) async-start(), calls=%async_computation.14 | async-start | bytes 3276800 | tf_op jit(solution)/shard_map/reduce_scatter | solution.py:1055
  410.2 23.3 %collective-permute-start.17 = (bf16[4,2,2,3,32,512]{5,4,3,2,1,0:T(8,128)(2,1)S(1)}, bf16[4,2,2,3,32,512]{5,4,3,2,1,0:T(8,128)(2,1)}, u32[]{:S(2)}, u32[]{:S(2)}) collective-permute-start(bf16[4,2,2,3,32,512]{5,4,3,2,1,0:T(8,128)(2,1)S(1)} %get-tuple-element.131), channel_id=1, source_target_pairs={{0,16},{16,0},{1,17},{17,1},{2,18},{18,2},{3,19},{19,3},{4,20},{20... | collective-permute-start | bytes 4718600 | tf_op jit(solution)/shard_map/ppermute | solution.py:1057
  428.9 17.7 %all-to-all-start.9 = ((bf16[4,192,128]{2,1,0:T(8,128)(2,1)}), bf16[4,192,128]{2,1,0:T(8,128)(2,1)S(1)}, u32[]{:S(2)}, u32[]{:S(2)}) async-start(bf16[4,192,128]{2,1,0:T(8,128)(2,1)} %bitcast.41), calls=%async_computation.10 | async-start | bytes 393216 | tf_op jit(solution)/shard_map/all_to_all | solution.py:912
  446.6 48.7 %all-to-all-start.7 = ((bf16[4,768,512]{2,1,0:T(8,128)(2,1)}), bf16[4,768,512]{2,1,0:T(8,128)(2,1)S(1)}, u32[]{:S(2)}, u32[]{:S(2)}) async-start(bf16[4,768,512]{2,1,0:T(8,128)(2,1)} %get-tuple-element.132), calls=%async_computation.7 | async-start | bytes 6291456 | tf_op jit(solution)/shard_map/all_to_all | solution.py:1070
  450.3 62.3 %reduce-scatter.11.cloned.1.call-start = ((), (), s32[]{:S(2)}) async-start(), calls=%async_computation.15 | async-start | bytes 737280 | tf_op jit(solution)/shard_map/reduce_scatter | solution.py:1097
  451.9 1.8 collective-permute-start.14
  453.8 7.7 %collective-permute-start.24 = (bf16[768,384]{1,0:T(8,128)(2,1)S(1)}, bf16[768,384]{1,0:T(8,128)(2,1)S(1)}, u32[]{:S(2)}, u32[]{:S(2)}) collective-permute-start(bf16[768,384]{1,0:T(8,128)(2,1)S(1)} %copy-done.34), channel_id=1, source_target_pairs={{0,16},{16,0},{1,17},{17,1},{2,18},{18,2},{3,19},{19,3},{4,20},{20... | collective-permute-start | bytes 1769480 | tf_op jit(solution)/shard_map/ppermute | solution.py:1096
  454.0 2.0 collective-permute-start.18
  458.1 32.4 %collective-permute-start.20 = (bf16[2,192,256]{2,1,0:T(8,128)(2,1)}, bf16[2,192,256]{2,1,0:T(8,128)(2,1)S(1)}, u32[]{:S(2)}, u32[]{:S(2)}) collective-permute-start(bf16[2,192,256]{2,1,0:T(8,128)(2,1)} %pad_maximum_fusion.7), channel_id=1, source_target_pairs={{0,8},{4,12},{8,0},{12,4},{1,9},{5,13},{9,1},{13,5},{2,10},{6,14},... | collective-permute-start | bytes 589832 | tf_op jit(solution)/shard_map/ppermute | solution.py:903
  460.1 32.6 %collective-permute-start.19 = (bf16[2,192,256]{2,1,0:T(8,128)(2,1)}, bf16[2,192,256]{2,1,0:T(8,128)(2,1)S(1)}, u32[]{:S(2)}, u32[]{:S(2)}) collective-permute-start(bf16[2,192,256]{2,1,0:T(8,128)(2,1)} %pad_maximum_fusion.7), channel_id=1, source_target_pairs={{0,4},{4,0},{8,12},{12,8},{1,5},{5,1},{9,13},{13,9},{2,6},{6,2},{1... | collective-permute-start | bytes 589832 | tf_op jit(solution)/shard_map/ppermute | solution.py:903
  491.2 11.0 %collective-permute-start.21 = (bf16[1,192,256]{2,1,0:T(8,128)(2,1)}, bf16[1,192,256]{2,1,0:T(8,128)(2,1)}, u32[]{:S(2)}, u32[]{:S(2)}) collective-permute-start(bf16[1,192,256]{2,1,0:T(8,128)(2,1)} %slice.122), channel_id=1, source_target_pairs={{0,4},{4,0},{8,12},{12,8},{1,5},{5,1},{9,13},{13,9},{2,6},{6,2},{1... | collective-permute-start | bytes 294920 | tf_op jit(solution)/shard_map/ppermute | solution.py:903
  493.3 8.9 %collective-permute-start.22 = (bf16[1,192,256]{2,1,0:T(8,128)(2,1)}, bf16[1,192,256]{2,1,0:T(8,128)(2,1)}, u32[]{:S(2)}, u32[]{:S(2)}) collective-permute-start(bf16[1,192,256]{2,1,0:T(8,128)(2,1)} %slice.123), channel_id=1, source_target_pairs={{0,8},{4,12},{8,0},{12,4},{1,9},{5,13},{9,1},{13,5},{2,10},{6,14},... | collective-permute-start | bytes 294920 | tf_op jit(solution)/shard_map/ppermute | solution.py:903
  497.8 23.4 %all-to-all-start.8 = ((bf16[4,192,512]{2,1,0:T(8,128)(2,1)}), bf16[4,192,512]{2,1,0:T(8,128)(2,1)}, u32[]{:S(2)}, u32[]{:S(2)}) async-start(bf16[4,192,512]{2,1,0:T(8,128)(2,1)} %bitcast.40), calls=%async_computation.9 | async-start | bytes 1572864 | tf_op jit(solution)/shard_map/all_to_all | solution.py:912
  503.2 11.2 %copy-start.15 = (bf16[1,192,1280]{1,2,0:T(8,128)(2,1)S(1)}, bf16[1,192,1280]{1,2,0:T(8,128)(2,1)}, u32[]{:S(2)}) copy-start(bf16[1,192,1280]{1,2,0:T(8,128)(2,1)} %reduce-scatter.9.cloned.1.call-done) | copy-start | bytes 1474564
  522.5 1.8 collective-permute-start.23
  (31 other events, 101.3 us)
Sparse Core Ops, SparseCore 0:
  10.2 32.9 all-gather.6
  46.6 80.7 all-gather.8
  130.8 92.8 all-gather.10
  302.0 74.1 reduce-scatter.14
  379.0 43.0 reduce-scatter.12
  427.1 55.3 reduce-scatter.8
  484.8 21.5 reduce-scatter.10

commit v7 on v6

--- a/solution.py
+++ b/solution.py
@@ -4,6 +4,7 @@
 import jax.numpy as jnp
 from jax import lax
 from jax.experimental import pallas as pl
+from jax.experimental.layout import Layout, with_layout_constraint
 from jax.experimental.pallas import tpu as pltpu
 from jax.sharding import PartitionSpec as P
 
@@ -516,13 +517,12 @@
 
 
 def middle_kernel(
-    place_ref, normed_one_ref, catt_ref, wc_ref, up_ref, down_ref, cot_ref,
-    out_ref, dcatt_ref, dy_ref, dcross_ref, gother_ref, gown_ref, dg_two_ref, dg_three_ref,
+    normed_one_ref, catt_ref, wc_ref, up_ref, down_ref, cot_ref,
+    out_ref, dcatt_ref, dy_ref, dcross_ref, glarge_ref, dg_two_ref, dg_three_ref,
     acc, normed_two, inv_two, act, slope, h_fm, h_tm, d_fm, d_tm,
 ):
     i = pl.program_id(0)
     groups, feat, tokens = catt_ref.shape
-    half = groups // 2
     units = up_ref.shape[2]
     step = min(256, tokens)
 
@@ -574,24 +574,13 @@
 
     @pl.when(i >= groups)
     def _():
-        g = other_first(i - groups, place_ref, half)
+        g = i - groups
         for t in range(0, tokens, step):
             at = slice(t, t + step)
             back = dot(d_tm[at, :], down_ref[0], 1, 0) * slope[g, at, :].astype(f32)
             slope[g, at, :] = back.astype(bf16)
-        g_down = dot(d_fm[...], act[g], 1, 0).astype(bf16)
-        g_up = dot(h_fm[...], slope[g], 1, 0).astype(bf16)
-
-        @pl.when(i < groups + half)
-        def _():
-            gother_ref[0, :, units:] = g_down
-            gother_ref[0, :, :units] = g_up
-
-        @pl.when(i >= groups + half)
-        def _():
-            gown_ref[0, :, units:] = g_down
-            gown_ref[0, :, :units] = g_up
-
+        glarge_ref[0, :, units:] = dot(d_fm[...], act[g], 1, 0).astype(bf16)
+        glarge_ref[0, :, :units] = dot(h_fm[...], slope[g], 1, 0).astype(bf16)
         acc[...] += dot(up_ref[0], slope[g], 1, 1)
 
     @pl.when(i == 2 * groups - 1)
@@ -610,69 +599,58 @@
             dcatt_ref[g] = dot(wc_ref[g, :, :feat], low, 0, 0).astype(bf16)
 
 
-def middle(place, normed_one, catt, small, large, cot):
+def middle(normed_one, catt, small, large, cot):
     width, tokens = normed_one.shape
     groups, feat, _ = catt.shape
-    half = groups // 2
     units = large.shape[2] // 2
     lanes = min(128, tokens)
 
     def weight(kind):
-        def index(i, p):
-            return jnp.where(i < groups, i, other_first(i - groups, p, half)), 0, kind
-
-        return pl.BlockSpec((1, width, units), index)
-
-    def grad_out(first):
-        return pl.BlockSpec(
-            (1, width, 2 * units), lambda i, p: (jnp.clip(i - first, 0, half - 1), 0, 0)
-        )
+        return pl.BlockSpec((1, width, units), lambda i: (i % groups, 0, kind))
 
     outs = [
         jax.ShapeDtypeStruct((width, tokens), bf16),
         jax.ShapeDtypeStruct(catt.shape, bf16),
         jax.ShapeDtypeStruct((width, tokens), f32),
         jax.ShapeDtypeStruct((width, tokens), bf16),
-        jax.ShapeDtypeStruct((half, width, 2 * units), bf16),
-        jax.ShapeDtypeStruct((half, width, 2 * units), bf16),
+        jax.ShapeDtypeStruct(large.shape, bf16),
         jax.ShapeDtypeStruct((width, lanes), f32),
         jax.ShapeDtypeStruct((width, lanes), f32),
     ]
     specs = [whole(o) for o in outs]
-    specs[4], specs[5] = grad_out(groups), grad_out(groups + half)
+    specs[4] = pl.BlockSpec(
+        (1, width, 2 * units), lambda i: (jnp.maximum(i - groups, 0), 0, 0)
+    )
     return pl.pallas_call(
         middle_kernel,
-        grid_spec=pltpu.PrefetchScalarGridSpec(
-            num_scalar_prefetch=1,
-            grid=(2 * groups,),
-            in_specs=[
-                whole(normed_one),
-                whole(catt),
-                pl.BlockSpec((groups, width, 128), lambda i, p: (0, 0, 3)),
-                weight(0),
-                weight(1),
-                whole(cot),
-            ],
-            out_specs=specs,
-            scratch_shapes=[
-                pltpu.VMEM((width, tokens), f32),
-                pltpu.VMEM((width, tokens), f32),
-                pltpu.VMEM((1, tokens), f32),
-                pltpu.VMEM((groups, tokens, units), bf16),
-                pltpu.VMEM((groups, tokens, units), bf16),
-                pltpu.VMEM((width, tokens), bf16),
-                pltpu.VMEM((tokens, width), bf16),
-                pltpu.VMEM((width, tokens), bf16),
-                pltpu.VMEM((tokens, width), bf16),
-            ],
-        ),
+        grid=(2 * groups,),
+        in_specs=[
+            whole(normed_one),
+            whole(catt),
+            pl.BlockSpec((groups, width, 128), lambda i: (0, 0, 3)),
+            weight(0),
+            weight(1),
+            whole(cot),
+        ],
+        out_specs=specs,
+        scratch_shapes=[
+            pltpu.VMEM((width, tokens), f32),
+            pltpu.VMEM((width, tokens), f32),
+            pltpu.VMEM((1, tokens), f32),
+            pltpu.VMEM((groups, tokens, units), bf16),
+            pltpu.VMEM((groups, tokens, units), bf16),
+            pltpu.VMEM((width, tokens), bf16),
+            pltpu.VMEM((tokens, width), bf16),
+            pltpu.VMEM((width, tokens), bf16),
+            pltpu.VMEM((tokens, width), bf16),
+        ],
         out_shape=outs,
         compiler_params=kernel_params(),
         cost_estimate=pl.CostEstimate(
             flops=12 * groups * width * units * tokens, bytes_accessed=8 * large.size, transcendentals=0
         ),
         name="middle",
-    )(place, normed_one, catt, small, large, large, cot)
+    )(normed_one, catt, small, large, large, cot)
 
 
 def before_self_kernel(
@@ -773,7 +751,7 @@
             piece = acc[:, n * tokens : (n + 1) * tokens].astype(bf16)
             if paired:
                 ref = cother_ref if n % 2 else cown_ref
-                ref[place_ref[0] ^ (n // 2)] = piece
+                ref[n // 2] = piece
                 continue
             mine = place_ref[1] == n // share
 
@@ -841,6 +819,10 @@
     )(place, small, chosen, d_ckv, attn, d_cq, catt, d_low, h_low, d_cross, *dgs)
 
 
+def row_major(value):
+    return with_layout_constraint(value, Layout(tuple(range(value.ndim))))
+
+
 def mm(spec, left, right):
     return jnp.einsum(spec, left, right, preferred_element_type=f32)
 
@@ -1004,8 +986,8 @@
     catt_flat = catt.reshape(blocks, feat, tokens)
 
     cot = to_tokens(out_grad)
-    block_out, d_catt, dy_two, d_cross, g_other, g_own, dg_two, dg_three = middle(
-        place, normed_one, catt_flat, small_all, large_all, cot
+    block_out, d_catt, dy_two, d_cross, g_large, dg_two, dg_three = middle(
+        normed_one, catt_flat, small_all, large_all, cot
     )
     block_out = home_cols(block_out)
 
@@ -1013,14 +995,13 @@
     def with_core(own, got):
         return (own.astype(f32) + got.astype(f32)).astype(bf16)
 
-    g_other = lax.ppermute(g_other, "dp", swap)
+    large_grad = g_large.reshape(dp, rows, cols, part_width, 2 * units)
+    large_grad = lax.psum_scatter(large_grad, "dp", scatter_dimension=0, tiled=False)
     d_cq, d_ckv = attend_back(
         meta, cross_q, [ckv], d_catt.reshape(catt.shape), catt, lse_cross, False, [bf16],
         "cross_attention_back",
     )
-    g_other, d_cq, block_out = lax.optimization_barrier((g_other, d_cq, block_out))
-    large_grad, d_cq = lax.optimization_barrier((with_core(g_own, g_other), d_cq))
-    large_grad = large_grad.reshape(rows, cols, part_width, 2 * units)
+    large_grad, d_cq, block_out = lax.optimization_barrier((large_grad, d_cq, block_out))
     large_grad = lax.psum_scatter(large_grad, "row", scatter_dimension=0, tiled=False)
     d_cq = d_cq.reshape(blocks, feat, tokens)
     d_ckv = d_ckv.reshape(blocks, 2 * feat, d_ckv.shape[-1])
@@ -1040,19 +1021,24 @@
     rest, d_mixed, d_chosen = lax.optimization_barrier((rest, d_mixed, d_chosen))
     rest = rest.reshape(rows, cols, part_width, -1)
     rest = lax.psum_scatter(rest, "row", scatter_dimension=0, tiled=False)
-    d_chosen = d_chosen.reshape(rows, sub * width, c_tokens)
-    d_chosen = lax.all_to_all(d_chosen, "row", 0, 0, tiled=True)
+    if sub == 1:
+        d_chosen = [d_chosen[0]] + [
+            lax.ppermute(d_chosen[k], "row", [(i, i ^ k) for i in range(rows)])
+            for k in range(1, rows)
+        ]
+    else:
+        d_chosen = d_chosen.reshape(rows, sub * width, c_tokens)
+        d_chosen = list(lax.all_to_all(d_chosen, "row", 0, 0, tiled=True))
 
     types = [f32] + [bf16] * (len(kv_list) - 1) if sub == 1 else [bf16] * len(kv_list)
     d_query, *d_kv = attend_back(
         meta, query, kv_list, d_mixed, mixed, lse, True, types, "self_attention_back"
     )
-    d_query, d_chosen, rest, large_grad = lax.optimization_barrier(
-        (d_query, d_chosen, rest, large_grad)
-    )
-    joined = jnp.concatenate([large_grad, rest], axis=2)
-    joined, d_query = lax.optimization_barrier((joined, d_query))
-    joined = lax.psum_scatter(joined, "col", scatter_dimension=0, tiled=False)
+    d_query, d_kv, d_chosen, large_grad = lax.optimization_barrier(
+        (d_query, d_kv, d_chosen, large_grad)
+    )
+    large_grad = lax.psum_scatter(large_grad, "col", scatter_dimension=0, tiled=False)
+    large_grad = row_major(large_grad)
     if sub == 1:
         d_kv = [d_kv[0], lax.ppermute(d_kv[1], "dp", swap)]
     else:
@@ -1068,12 +1054,12 @@
         place, near, x_rows, d_query.reshape(rows, dp, feat, tokens), d_kv
     )
     dx_part = lax.all_to_all(dx_part, "row", 0, 0, tiled=True)
-    dx_part, joined = lax.optimization_barrier((dx_part, joined))
-    joined = joined.astype(f32)
+    dx_part, large_grad = lax.optimization_barrier((dx_part, large_grad))
+    large_grad = large_grad.astype(f32)
     dx = dy_one + jnp.sum(dx_part.astype(f32), axis=0)
     x_moved = home_cols(dx.astype(bf16))
 
-    d_chosen = jnp.sum(d_chosen.astype(f32), axis=0).astype(bf16)
+    d_chosen = sum(piece.astype(f32) for piece in d_chosen).astype(bf16)
     if sub > 1:
         d_chosen = lax.psum_scatter(
             d_chosen.reshape(sub, width, c_tokens), "col", scatter_dimension=0, tiled=True,
@@ -1094,10 +1080,9 @@
     x_grad = home_cores(x_moved).astype(f32)
 
     qkv = with_core(g_qkv, lax.ppermute(qkv_other, "dp", swap))
-    qkv_grad = lax.psum_scatter(
-        qkv.reshape(cols, part_width, -1), "col", scatter_dimension=0, tiled=False
-    ).astype(f32)
-    large_grad, rest = joined[:, : 2 * units], joined[:, 2 * units :]
+    last = jnp.concatenate([rest, qkv.reshape(cols, part_width, -1)], axis=2)
+    last = lax.psum_scatter(last, "col", scatter_dimension=0, tiled=False).astype(f32)
+    rest, qkv_grad = last[:, :512], last[:, 512:]
 
     return (
         home_cores(block_out),

time: 542 us -> 519 us (0.958)
  waiting for transfers between devices: 143 us -> 124 us
  Pallas kernels: 229 us -> 219 us
  starting transfers between devices: 63.2 us -> 73.2 us
  other arithmetic: 40.3 us -> 33.8 us
    ppermute x12, waiting for transfers between devices: 72.6 us -> 63.2 us  [send(): return lax.ppermute(v, 'row', [(i, i ^ k) for i in range(rows)])]
    unnamed x9 -> x10, waiting for transfers between devices: 9.47 us -> 0.14 us
    all_to_all x3, starting transfers between devices: 12.5 us -> 20.1 us  [home_cols(): return lax.all_to_all(value, 'col', 0, 0, tiled=True)]
    convert_element_type x4 -> x3, other arithmetic: 15.1 us -> 8.14 us  [with_core(): return (own.astype(f32) + got.astype(f32)).astype(bf16)]
    unnamed x87 -> x83, local copies, waits for them, and re-layouts: 14.8 us -> 13.3 us
  transfers between devices with their start and end apart: 42 -> 44, of which waited for: 18 -> 14; matrix products, arithmetic and copies ran while one was open for 11% -> 12% of each run, Pallas kernels for 35% -> 35%
where the time goes in v7:
time: 519 us; the launch traced here: 510 us
  Pallas kernels  219 us (42%)
  waiting for transfers between devices  124 us (24%)
  starting transfers between devices  73.2 us (14%)
  other arithmetic  33.8 us (7%)
  local copies, waits for them, and re-layouts  29.3 us (6%)
  between operations  15.9 us (3%)
  matrix products  13.1 us (3%)
    pallas_call x2, Pallas kernels, attend_back(): pl.pallas_call(functools.partial(attend_back_kernel, sources=len(kv_list)...  68.7 us
    ppermute x12, waiting for transfers between devices, send(): return lax.ppermute(v, 'row', [(i, i ^ k) for i in range(rows)])  63.2 us
    pallas_call x2, Pallas kernels, attend(): pl.pallas_call(functools.partial(attend_kernel, sources=len(kv_list), n_q...  39.9 us
    pallas_call x1, Pallas kernels, middle(): pl.pallas_call(middle_kernel, grid=(2 * groups,), in_specs=[whole(normed_...  38.9 us
    all_to_all x3, waiting for transfers between devices, across_cols(): lax.all_to_all(value, 'col', 0, 0, tiled=True)  28.3 us
    pallas_call x1, Pallas kernels, small_grads(): pl.pallas_call(functools.partial(small_grads_kernel, paired=paired), grid...  23.5 us
    all_to_all x3, starting transfers between devices, home_cols(): return lax.all_to_all(value, 'col', 0, 0, tiled=True)  20.1 us
    all_to_all x3, starting transfers between devices, across_cols(): lax.all_to_all(value, 'col', 0, 0, tiled=True)  17.6 us
  transfers between devices with their start and end apart: 44, of which 14 were waited for; matrix products, arithmetic and copies ran while one was open for 12% of the time, Pallas kernels for 35%

profile of v7, /device:TPU:0, one launch (start us, length us, event | category | flops | bytes accessed | tf_op | source)
XLA Modules:
  0.0 510.2 jit_solution(3134454423887722974)
XLA Ops:
  15.0 6.4 %all-to-all-start = ((bf16[4,192,512]{2,1,0:T(8,128)(2,1)}), bf16[4,192,512]{2,1,0:T(8,128)(2,1)}, u32[]{:S(2)}, u32[]{:S(2)}) async-start(bf16[4,192,512]{2,1,0:T(8,128)(2,1)} %pad_maximum_fusion.1), calls=%async_computation | async-start | bytes 1572864 | tf_op jit(solution)/shard_map/all_to_all | solution.py:874
  22.1 28.3 %all-to-all-done = bf16[4,192,512]{2,1,0:T(8,128)(2,1)} async-done(((bf16[4,192,512]{2,1,0:T(8,128)(2,1)}), bf16[4,192,512]{2,1,0:T(8,128)(2,1)}, u32[]{:S(2)}, u32[]{:S(2)}) %all-to-all-start) | async-done | bytes 786464 | tf_op jit(solution)/shard_map/all_to_all | solution.py:874
  50.5 1.5 collective-permute-start.2
  53.5 18.0 %collective-permute-done.2.refs_2_ = bf16[768,512]{1,0:T(8,128)(2,1)S(1)} collective-permute-done((bf16[768,512]{1,0:T(8,128)(2,1)}, bf16[768,512]{1,0:T(8,128)(2,1)S(1)}, u32[]{:S(2)}, u32[]{:S(2)}) %collective-permute-start.2) | collective-permute-done | bytes 786464 | tf_op jit(solution)/shard_map/ppermute | solution.py:885
  78.3 10.5 %collective-permute-done.3 = bf16[384,512]{1,0:T(8,128)(2,1)S(1)} collective-permute-done((bf16[384,512]{1,0:T(8,128)(2,1)}, bf16[384,512]{1,0:T(8,128)(2,1)S(1)}, u32[]{:S(2)}, u32[]{:S(2)}) %collective-permute-start.3) | collective-permute-done | bytes 393248 | tf_op jit(solution)/shard_map/ppermute | solution.py:885
  89.6 1.8 constant_dynamic-update-slice_fusion.refs_3_
  91.4 6.6 %project.1 = (bf16[4,2,96,512]{3,2,1,0:T(8,128)(2,1)}, bf16[4,2,2,96,512]{4,3,2,1,0:T(8,128)(2,1)}) custom-call(s32[2]{0:T(128)} %pad_add_fusion.2.place_ref, bf16[2,768,384]{2,1,0:T(8,128)(2,1)} %bitcast.106, bf16[768,512]{1,0:T(8,128)(2,1)} %bitcast.refs_0_.x_ref, bf16[768,512]{1,0:T(8,128)(2,1)} %copy-done.20, bf16[768,512]{1,0:T(8,128)(2,1)} %copy-done.19, ...), custom_call_target="tpu_custom_call" | custom-call | tf_op jit(solution)/shard_map/project/pallas_call | solution.py:351
  98.1 1.6 fusion.5
  101.9 1.9 broadcast_select_fusion.12
  103.8 1.9 all-reduce.1
  107.8 3.4 all-to-all-start.2
  111.2 27.0 %self_attention.1 = (bf16[4,2,3,32,512]{4,3,2,1,0:T(8,128)(2,1)}, f32[3,4,1,512]{3,2,1,0:T(1,128)S(1)}) custom-call(s32[13]{0:T(128)S(1)} %pad_add_fusion.1.refs_0_, bf16[4,2,3,32,512]{4,3,2,1,0:T(8,128)(2,1)S(1)} %bitcast.83, bf16[4,2,2,3,32,512]{5,4,3,2,1,0:T(8,128)(2,1)S(1)} %bitcast.82, bf16[4,2,2,3,32,512]{5,4,3,2,1,0:T(8,128)(2,1)} %collective-permute-done.5.refs_3_), custom_call_target="tpu_custom_call" | custom-call | flops 12884901888 | bytes 6291456 | tf_op jit(solution)/shard_map/self_attention/pallas_call | solution.py:239
  138.2 4.1 all-to-all-start.1
  143.5 10.2 %all-to-all-done.1 = bf16[4,2,3,32,512]{4,3,2,1,0:T(8,128)(2,1)S(1)} async-done(((bf16[4,2,3,32,512]{4,3,2,1,0:T(8,128)(2,1)}), bf16[4,2,3,32,512]{4,3,2,1,0:T(8,128)(2,1)S(1)}, u32[]{:S(2)}, u32[]{:S(2)}) %all-to-all-start.1) | async-done | bytes 786464 | tf_op jit(solution)/shard_map/all_to_all | solution.py:966
  153.7 7.9 %all-to-all-start.3 = ((bf16[4,192,512]{2,1,0:T(8,128)(2,1)}), bf16[4,192,512]{2,1,0:T(8,128)(2,1)}, u32[]{:S(2)}, u32[]{:S(2)}) async-start(bf16[4,192,512]{2,1,0:T(8,128)(2,1)} %pad_maximum_fusion.2), calls=%async_computation.3 | async-start | bytes 1572864 | tf_op jit(solution)/shard_map/all_to_all | solution.py:874
  162.1 1.5 collective-permute-start.9
  165.1 6.8 %collective-permute-done.9 = bf16[2,768,128]{2,1,0:T(8,128)(2,1)S(1)} collective-permute-done((bf16[2,768,128]{2,1,0:T(8,128)(2,1)S(1)}, bf16[2,768,128]{2,1,0:T(8,128)(2,1)S(1)}, u32[]{:S(2)}, u32[]{:S(2)}) %collective-permute-start.9) | collective-permute-done | bytes 393248 | tf_op jit(solution)/shard_map/ppermute | solution.py:885
  173.3 2.6 collective-permute-done.8
  177.5 1.8 collective-permute-done.10
  179.3 2.3 collective-permute-done.11
  182.9 8.9 %cross_kv.1 = bf16[8,192,1024]{2,1,0:T(8,128)(2,1)} custom-call(bf16[8,768,512]{2,1,0:T(8,128)(2,1)} %bitcast.91, bf16[8,768,128]{2,1,0:T(8,128)(2,1)} %copy-done.18), custom_call_target="tpu_custom_call" | custom-call | tf_op jit(solution)/shard_map/cross_kv/pallas_call | solution.py:459
  191.8 8.9 %after_self.1 = (f32[768,512]{1,0:T(8,128)}, f32[1,512]{1,0:T(1,128)}, bf16[768,512]{1,0:T(8,128)(2,1)}, bf16[8,96,512]{2,1,0:T(8,128)(2,1)}) custom-call(bf16[768,512]{1,0:T(8,128)(2,1)} %bitcast.refs_0_.x_ref, bf16[4,2,96,512]{3,2,1,0:T(8,128)(2,1)} %bitcast.100, bf16[8,768,512]{2,1,0:T(8,128)(2,1)} %bitcast.92), custom_call_target="tpu_custom_call" | custom-call | tf_op jit(solution)/shard_map/after_self/pallas_call | solution.py:507
  201.9 12.9 %cross_attention.1 = (bf16[1,2,4,3,32,512]{5,4,3,2,1,0:T(8,128)(2,1)S(1)}, f32[12,1,1,512]{3,2,1,0:T(1,128)S(1)}) custom-call(s32[13]{0:T(128)S(1)} %pad_add_fusion.1.refs_0_, bf16[1,2,4,3,32,512]{5,4,3,2,1,0:T(8,128)(2,1)S(1)} %bitcast.85, bf16[1,2,4,2,3,32,1024]{6,5,4,3,2,1,0:T(8,128)(2,1)S(1)} %bitcast.76), custom_call_target="tpu_custom_call" | custom-call | flops 3221225472 | bytes 6291456 | tf_op jit(solution)/shard_map/cross_attention/pallas_call | solution.py:239
  215.8 7.1 %all-gather.11.cloned.1.call-done = bf16[6144,768]{1,0:T(8,128)(2,1)} async-done(((bf16[192,768]{1,0:T(8,128)(2,1)}), bf16[6144,768]{1,0:T(8,128)(2,1)}) %all-gather.11.cloned.1.call-update) | async-done | bytes 9437200 | tf_op jit(solution)/shard_map/all_gather | solution.py:938
  222.9 38.9 %middle.1 = (bf16[768,512]{1,0:T(8,128)(2,1)}, bf16[8,96,512]{2,1,0:T(8,128)(2,1)}, f32[768,512]{1,0:T(8,128)}, bf16[768,512]{1,0:T(8,128)(2,1)}, bf16[8,768,768...) custom-call(f32[768,512]{1,0:T(8,128)} %get-tuple-element.83.normed_one_ref.normed_ref, ...), custom_call_target="tpu_custom_call" | custom-call | flops 14495514624 | bytes 37748736 | tf_op jit(solution)/shard_map/middle/pallas_call | solution.py:624
  261.9 3.6 all-to-all-start.4
  265.8 21.4 %cross_attention_back.1 = (bf16[1,2,4,3,32,512]{5,4,3,2,1,0:T(8,128)(2,1)S(1)}, bf16[1,2,4,2,3,32,1024]{6,5,4,3,2,1,0:T(8,128)(2,1)}) custom-call(s32[13]{0:T(128)S(1)} %pad_add_fusion.1.refs_0_, bf16[1,2,4,3,32,512]{5,4,3,2,1,0:T(8,128)(2,1)S(1)} %bitcast.86, bf16[1,2,4,2,3,32,1024]{6,5,4,3,2,1,0:T(8,128)(2,1)} %bitcast.75, ...), custom_call_target="tpu_custom_call" | custom-call | flops 8053063680 | bytes 6291456 | tf_op jit(solution)/shard_map/cross_attention_back/pallas_call | solution.py:260
  288.1 10.6 %before_self.1 = (bf16[4,2,96,512]{3,2,1,0:T(8,128)(2,1)}, bf16[768,512]{1,0:T(8,128)(2,1)}, f32[768,512]{1,0:T(8,128)}, f32[768,128]{1,0:T(8,128)}) custom-call(bf16[8,96,512]{2,1,0:T(8,128)(2,1)} %bitcast.78, bf16[8,768,512]{2,1,0:T(8,128)(2,1)} %bitcast.94, f32[768,512]{1,0:T(8,128)} %get-tuple-element.96.dy_ref, ...), custom_call_target="tpu_custom_call" | custom-call | tf_op jit(solution)/shard_map/before_self/pallas_call | solution.py:692
  298.8 3.5 all-to-all-start.5
  302.3 23.5 %small_grads.1 = (bf16[4,768,512]{2,1,0:T(8,128)(2,1)}, bf16[4,768,512]{2,1,0:T(8,128)(2,1)}, bf16[4,768,128]{2,1,0:T(8,128)(2,1)}, bf16[4,768,128]{2,1,0:T(8,128)(2,1)}) custom-call(s32[2]{0:T(128)} %pad_add_fusion.2.place_ref, bf16[8,768,512]{2,1,0:T(8,128)(2,1)} %bitcast.95, bf16[8,768,128]{2,1,0:T(8,128)(2,1)} %copy-done.18, ...), custom_call_target="tpu_custom_call" | custom-call | flops 6643777536 | bytes 12582912 | tf_op jit(solution)/shard_map/small_grads/pallas_call | solution.py:784
  326.3 6.5 %collective-permute-done.15 = bf16[4,768,128]{2,1,0:T(8,128)(2,1)S(1)} collective-permute-done((bf16[4,768,128]{2,1,0:T(8,128)(2,1)}, bf16[4,768,128]{2,1,0:T(8,128)(2,1)S(1)}, u32[]{:S(2)}, u32[]{:S(2)}) %collective-permute-start.15) | collective-permute-done | bytes 786464 | tf_op jit(solution)/shard_map/ppermute | solution.py:1020
  334.2 4.6 add_convert_fusion
  339.2 2.9 collective-permute-start.18
  342.7 47.2 %self_attention_back.1 = (bf16[4,2,3,32,512]{4,3,2,1,0:T(8,128)(2,1)S(1)}, f32[4,2,2,3,32,512]{5,4,3,2,1,0:T(8,128)}, bf16[4,2,2,3,32,512]{5,4,3,2,1,0:T(8,128)(2,1)S(1)}) custom-call(s32[13]{0:T(128)S(1)} %pad_add_fusion.1.refs_0_, bf16[4,2,3,32,512]{4,3,2,1,0:T(8,128)(2,1)S(1)} %bitcast.84, bf16[4,2,2,3,32,512]{5,4,3,2,1,0:T(8,128)(2,1)} %bitcast.81, ...), custom_call_target="tpu_custom_call" | custom-call | flops 32212254720 | bytes 6291456 | tf_op jit(solution)/shard_map/self_attention_back/pallas_call | solution.py:260
  392.2 1.9 add_convert_fusion.4
  394.1 11.6 %all-to-all-start.8 = ((bf16[4,192,128]{2,1,0:T(8,128)(2,1)}), bf16[4,192,128]{2,1,0:T(8,128)(2,1)S(1)}, u32[]{:S(2)}, u32[]{:S(2)}) async-start(bf16[4,192,128]{2,1,0:T(8,128)(2,1)} %bitcast.44), calls=%async_computation.10 | async-start | bytes 393216 | tf_op jit(solution)/shard_map/all_to_all | solution.py:894
  405.8 12.5 %project_back.1 = (bf16[4,768,512]{2,1,0:T(8,128)(2,1)}, bf16[768,384]{1,0:T(8,128)(2,1)}, bf16[768,384]{1,0:T(8,128)(2,1)}) custom-call(s32[2]{0:T(128)} %pad_add_fusion.2.place_ref, bf16[2,768,384]{2,1,0:T(8,128)(2,1)} %bitcast.107, bf16[768,512]{1,0:T(8,128)(2,1)} %bitcast.refs_0_.x_ref, bf16[768,512]{1,0:T(8,128)(2,1)} %copy-done.20, ...), custom_call_target="tpu_custom_call" | custom-call | flops 3623878656 | bytes 16777216 | tf_op jit(solution)/shard_map/project_back/pallas_call | solution.py:412
  418.3 4.0 all-to-all-start.6
  422.7 1.9 broadcast_select_fusion.3
  425.2 2.2 copy.50
  427.4 2.2 add_convert_fusion.3
  429.6 2.2 copy.51
  431.8 3.0 pad_maximum_fusion
  436.3 2.1 collective-permute-start.22
  442.0 21.1 %collective-permute-done.22 = bf16[2,192,256]{2,1,0:T(8,128)(2,1)S(1)} collective-permute-done((bf16[2,192,256]{2,1,0:T(8,128)(2,1)S(1)}, bf16[2,192,256]{2,1,0:T(8,128)(2,1)S(1)}, u32[]{:S(2)}, u32[]{:S(2)}) %collective-permute-start.22) | collective-permute-done | bytes 196640 | tf_op jit(solution)/shard_map/ppermute | solution.py:885
  469.3 4.8 all-to-all-start.7
  474.9 11.4 %fusion = f32[2,192,4096]{2,1,0:T(8,128)} fusion(bf16[2,192,1024]{2,1,0:T(8,128)(2,1)} %maximum_dynamic-update-slice_fusion, s32[2,1024]{1,0:T(2,128)S(1)} %pad_add_fusion), kind=kOutput, calls=%fused_computation.1 | convolution fusion | flops 3229614080 | bytes 7086080 | tf_op jit(solution)/shard_map/swp,spn->swn/dot_general | solution.py:827
  490.3 7.0 %all-to-all-done.7 = bf16[4,192,512]{2,1,0:T(8,128)(2,1)} async-done(((bf16[4,192,512]{2,1,0:T(8,128)(2,1)}), bf16[4,192,512]{2,1,0:T(8,128)(2,1)}, u32[]{:S(2)}, u32[]{:S(2)}) %all-to-all-start.7) | async-done | bytes 786464 | tf_op jit(solution)/shard_map/all_to_all | solution.py:894
  (209 shorter events, 59.2 us)
Async XLA Ops:
  7.2 90.9 %copy-start = (bf16[2,192,4096]{2,1,0:T(8,128)(2,1)S(1)}, bf16[2,192,4096]{2,1,0:T(8,128)(2,1)}, u32[]{:S(2)}) copy-start(bf16[2,192,4096]{2,1,0:T(8,128)(2,1)} %param.15) | copy-start | bytes 9437188
  7.2 84.2 %all-gather.7.cloned.1.call-start = ((), (), s32[]{:S(2)}) async-start(), calls=%async_computation.17 | async-start | bytes 1327104 | tf_op jit(solution)/shard_map/all_gather | solution.py:917
  9.2 172.6 %all-gather.9.cloned.1.call-start = ((), (), s32[]{:S(2)}) async-start(), calls=%async_computation.18 | async-start | bytes 6488064 | tf_op jit(solution)/shard_map/all_gather | solution.py:938
  10.5 1.9 collective-permute-start
  15.0 35.5 %all-to-all-start = ((bf16[4,192,512]{2,1,0:T(8,128)(2,1)}), bf16[4,192,512]{2,1,0:T(8,128)(2,1)}, u32[]{:S(2)}, u32[]{:S(2)}) async-start(bf16[4,192,512]{2,1,0:T(8,128)(2,1)} %pad_maximum_fusion.1), calls=%async_computation | async-start | bytes 1572864 | tf_op jit(solution)/shard_map/all_to_all | solution.py:874
  21.4 201.5 %all-gather.11.cloned.1.call-start = ((), (), s32[]{:S(2)}) async-start(), calls=%async_computation.19 | async-start | bytes 9732096 | tf_op jit(solution)/shard_map/all_gather | solution.py:938
  50.5 21.1 %collective-permute-start.2 = (bf16[768,512]{1,0:T(8,128)(2,1)}, bf16[768,512]{1,0:T(8,128)(2,1)S(1)}, u32[]{:S(2)}, u32[]{:S(2)}) collective-permute-start(bf16[768,512]{1,0:T(8,128)(2,1)} %bitcast.refs_0_.x_ref), channel_id=1, source_target_pairs={{0,8},{4,12},{8,0},{12,4},{1,9},{5,13},{9,1},{13,5},{2,10},{6,14},... | collective-permute-start | bytes 2359304 | tf_op jit(solution)/shard_map/ppermute | solution.py:885
  52.0 22.6 %collective-permute-start.1 = (bf16[768,512]{1,0:T(8,128)(2,1)}, bf16[768,512]{1,0:T(8,128)(2,1)S(1)}, u32[]{:S(2)}, u32[]{:S(2)}) collective-permute-start(bf16[768,512]{1,0:T(8,128)(2,1)} %bitcast.refs_0_.x_ref), channel_id=1, source_target_pairs={{0,4},{4,0},{8,12},{12,8},{1,5},{5,1},{9,13},{13,9},{2,6},{6,2},{1... | collective-permute-start | bytes 2359304 | tf_op jit(solution)/shard_map/ppermute | solution.py:885
  73.2 15.7 %collective-permute-start.3 = (bf16[384,512]{1,0:T(8,128)(2,1)}, bf16[384,512]{1,0:T(8,128)(2,1)S(1)}, u32[]{:S(2)}, u32[]{:S(2)}) collective-permute-start(bf16[384,512]{1,0:T(8,128)(2,1)} %slice.128), channel_id=1, source_target_pairs={{0,4},{4,0},{8,12},{12,8},{1,5},{5,1},{9,13},{13,9},{2,6},{6,2},{1... | collective-permute-start | bytes 1179656 | tf_op jit(solution)/shard_map/ppermute | solution.py:885
  76.3 13.3 %collective-permute-start.4 = (bf16[384,512]{1,0:T(8,128)(2,1)}, bf16[384,512]{1,0:T(8,128)(2,1)}, u32[]{:S(2)}, u32[]{:S(2)}) collective-permute-start(bf16[384,512]{1,0:T(8,128)(2,1)} %slice.129), channel_id=1, source_target_pairs={{0,8},{4,12},{8,0},{12,4},{1,9},{5,13},{9,1},{13,5},{2,10},{6,14},... | collective-permute-start | bytes 1179656 | tf_op jit(solution)/shard_map/ppermute | solution.py:885
  98.1 13.1 %collective-permute-start.5 = (bf16[4,2,2,3,32,512]{5,4,3,2,1,0:T(8,128)(2,1)}, bf16[4,2,2,3,32,512]{5,4,3,2,1,0:T(8,128)(2,1)}, u32[]{:S(2)}, u32[]{:S(2)}) collective-permute-start(bf16[4,2,2,3,32,512]{5,4,3,2,1,0:T(8,128)(2,1)} %bitcast.80), channel_id=1, source_target_pairs={{0,16},{16,0},{1,17},{17,1},{2,18},{18,2},{3,19},{19,3},{4,20},{20... | collective-permute-start | bytes 4718600 | tf_op jit(solution)/shard_map/ppermute | solution.py:954
  99.8 11.4 %copy-start.4 = (bf16[4,2,2,96,512]{4,3,2,1,0:T(8,128)(2,1)S(1)}, bf16[4,2,2,96,512]{4,3,2,1,0:T(8,128)(2,1)}, u32[]{:S(2)}) copy-start(bf16[4,2,2,96,512]{4,3,2,1,0:T(8,128)(2,1)} %get-tuple-element.76) | copy-start | bytes 4718596
  99.8 7.3 %collective-permute-start.6 = (bf16[2,192,128]{2,1,0:T(8,128)(2,1)S(1)}, bf16[2,192,128]{2,1,0:T(8,128)(2,1)S(1)}, u32[]{:S(2)}, u32[]{:S(2)}) collective-permute-start(bf16[2,192,128]{2,1,0:T(8,128)(2,1)S(1)} %broadcast_select_fusion.18), channel_id=1, source_target_pairs={{0,16},{16,0},{1,17},{17,1},{2,18},{18,2},{3,19},{19,3},{4,20},{20... | collective-permute-start | bytes 294920 | tf_op jit(solution)/shard_map/ppermute | solution.py:861
  103.8 38.7 %collective-permute-start.12 = (bf16[2,192,512]{2,1,0:T(8,128)(2,1)}, bf16[2,192,512]{2,1,0:T(8,128)(2,1)S(1)}, u32[]{:S(2)}, u32[]{:S(2)}) collective-permute-start(bf16[2,192,512]{2,1,0:T(8,128)(2,1)} %broadcast_select_fusion.12), channel_id=1, source_target_pairs={{0,16},{16,0},{1,17},{17,1},{2,18},{18,2},{3,19},{19,3},{4,20},{20... | collective-permute-start | bytes 1179656 | tf_op jit(solution)/shard_map/ppermute | solution.py:861
  107.8 30.4 %all-to-all-start.2 = ((bf16[4,192,128]{2,1,0:T(8,128)(2,1)}), bf16[4,192,128]{2,1,0:T(8,128)(2,1)S(1)}, u32[]{:S(2)}, u32[]{:S(2)}) async-start(bf16[4,192,128]{2,1,0:T(8,128)(2,1)} %pad_maximum_fusion.6), calls=%async_computation.2 | async-start | bytes 393216 | tf_op jit(solution)/shard_map/all_to_all | solution.py:874
  138.2 15.5 %all-to-all-start.1 = ((bf16[4,2,3,32,512]{4,3,2,1,0:T(8,128)(2,1)}), bf16[4,2,3,32,512]{4,3,2,1,0:T(8,128)(2,1)S(1)}, u32[]{:S(2)}, u32[]{:S(2)}) async-start(bf16[4,2,3,32,512]{4,3,2,1,0:T(8,128)(2,1)} %get-tuple-element.77.refs_5_), calls=%async_computation.1 | async-start | bytes 1572864 | tf_op jit(solution)/shard_map/all_to_all | solution.py:966
  142.3 19.7 %collective-permute-start.7 = (bf16[768,128]{1,0:T(8,128)(2,1)S(1)}, bf16[768,128]{1,0:T(8,128)(2,1)S(1)}, u32[]{:S(2)}, u32[]{:S(2)}) collective-permute-start(bf16[768,128]{1,0:T(8,128)(2,1)S(1)} %bitcast.103), channel_id=1, source_target_pairs={{0,16},{16,0},{1,17},{17,1},{2,18},{18,2},{3,19},{19,3},{4,20},{20... | collective-permute-start | bytes 589832 | tf_op jit(solution)/shard_map/ppermute | solution.py:981
  153.7 11.4 %copy-start.17 = (bf16[4,2,3,32,512]{4,3,2,1,0:T(8,128)(2,1)}, bf16[4,2,3,32,512]{4,3,2,1,0:T(8,128)(2,1)S(1)}, u32[]{:S(2)}) copy-start(bf16[4,2,3,32,512]{4,3,2,1,0:T(8,128)(2,1)S(1)} %all-to-all-done.1) | copy-start | bytes 2359300
  153.7 62.1 %all-to-all-start.3 = ((bf16[4,192,512]{2,1,0:T(8,128)(2,1)}), bf16[4,192,512]{2,1,0:T(8,128)(2,1)}, u32[]{:S(2)}, u32[]{:S(2)}) async-start(bf16[4,192,512]{2,1,0:T(8,128)(2,1)} %pad_maximum_fusion.2), calls=%async_computation.3 | async-start | bytes 1572864 | tf_op jit(solution)/shard_map/all_to_all | solution.py:874
  161.6 126.6 %reduce-scatter.10.cloned.1.call-start = ((), (), s32[]{:S(2)}) async-start(), calls=%async_computation.14 | async-start | bytes 14155776 | tf_op jit(solution)/shard_map/reduce_scatter | solution.py:999
  162.1 9.9 %collective-permute-start.9 = (bf16[2,768,128]{2,1,0:T(8,128)(2,1)S(1)}, bf16[2,768,128]{2,1,0:T(8,128)(2,1)S(1)}, u32[]{:S(2)}, u32[]{:S(2)}) collective-permute-start(bf16[2,768,128]{2,1,0:T(8,128)(2,1)S(1)} %pad_maximum_fusion.4), channel_id=1, source_target_pairs={{0,8},{4,12},{8,0},{12,4},{1,9},{5,13},{9,1},{13,5},{2,10},{6,14},... | collective-permute-start | bytes 1179656 | tf_op jit(solution)/shard_map/ppermute | solution.py:885
  163.6 12.3 %collective-permute-start.8 = (bf16[2,768,128]{2,1,0:T(8,128)(2,1)S(1)}, bf16[2,768,128]{2,1,0:T(8,128)(2,1)S(1)}, u32[]{:S(2)}, u32[]{:S(2)}) collective-permute-start(bf16[2,768,128]{2,1,0:T(8,128)(2,1)S(1)} %pad_maximum_fusion.4), channel_id=1, source_target_pairs={{0,4},{4,0},{8,12},{12,8},{1,5},{5,1},{9,13},{13,9},{2,6},{6,2},{1... | collective-permute-start | bytes 1179656 | tf_op jit(solution)/shard_map/ppermute | solution.py:885
  172.0 7.3 %collective-permute-start.10 = (bf16[1,768,128]{2,1,0:T(8,128)(2,1)S(1)}, bf16[1,768,128]{2,1,0:T(8,128)(2,1)S(1)}, u32[]{:S(2)}, u32[]{:S(2)}) collective-permute-start(bf16[1,768,128]{2,1,0:T(8,128)(2,1)S(1)} %slice.132), channel_id=1, source_target_pairs={{0,4},{4,0},{8,12},{12,8},{1,5},{5,1},{9,13},{13,9},{2,6},{6,2},{1... | collective-permute-start | bytes 589832 | tf_op jit(solution)/shard_map/ppermute | solution.py:885
  175.9 5.7 %collective-permute-start.11 = (bf16[1,768,128]{2,1,0:T(8,128)(2,1)S(1)}, bf16[1,768,128]{2,1,0:T(8,128)(2,1)S(1)}, u32[]{:S(2)}, u32[]{:S(2)}) collective-permute-start(bf16[1,768,128]{2,1,0:T(8,128)(2,1)S(1)} %slice.133), channel_id=1, source_target_pairs={{0,8},{4,12},{8,0},{12,4},{1,9},{5,13},{9,1},{13,5},{2,10},{6,14},... | collective-permute-start | bytes 589832 | tf_op jit(solution)/shard_map/ppermute | solution.py:885
  261.9 26.2 %all-to-all-start.4 = ((bf16[4,192,512]{2,1,0:T(8,128)(2,1)}), bf16[4,192,512]{2,1,0:T(8,128)(2,1)S(1)}, u32[]{:S(2)}, u32[]{:S(2)}) async-start(bf16[4,192,512]{2,1,0:T(8,128)(2,1)} %bitcast.111), calls=%async_computation.5 | async-start | bytes 1572864 | tf_op jit(solution)/shard_map/all_to_all | solution.py:894
  265.5 126.7 %reduce-scatter.16.cloned.1.call-start = ((), (), s32[]{:S(2)}) async-start(), calls=%async_computation.20 | async-start | bytes 5898240
  298.8 27.0 %all-to-all-start.5 = ((bf16[4,2,96,512]{3,2,1,0:T(8,128)(2,1)}), bf16[4,2,96,512]{3,2,1,0:T(8,128)(2,1)S(1)}, u32[]{:S(2)}, u32[]{:S(2)}) async-start(bf16[4,2,96,512]{3,2,1,0:T(8,128)(2,1)} %get-tuple-element.99), calls=%async_computation.6 | async-start | bytes 1572864 | tf_op jit(solution)/shard_map/all_to_all | solution.py:1011
  302.3 122.9 %reduce-scatter.18.cloned.1.call-start = ((), (), s32[]{:S(2)}) async-start(), calls=%async_computation.21 | async-start | bytes 3932160
  325.8 8.4 %collective-permute-start.14 = (bf16[4,768,512]{2,1,0:T(8,128)(2,1)}, bf16[4,768,512]{2,1,0:T(8,128)(2,1)S(1)}, u32[]{:S(2)}, u32[]{:S(2)}) collective-permute-start(bf16[4,768,512]{2,1,0:T(8,128)(2,1)} %get-tuple-element.112), channel_id=1, source_target_pairs={{0,16},{16,0},{1,17},{17,1},{2,18},{18,2},{3,19},{19,3},{4,20},{20... | collective-permute-start | bytes 9437192 | tf_op jit(solution)/shard_map/ppermute | solution.py:1019
  326.2 6.6 %collective-permute-start.15 = (bf16[4,768,128]{2,1,0:T(8,128)(2,1)}, bf16[4,768,128]{2,1,0:T(8,128)(2,1)S(1)}, u32[]{:S(2)}, u32[]{:S(2)}) collective-permute-start(bf16[4,768,128]{2,1,0:T(8,128)(2,1)} %get-tuple-element.115), channel_id=1, source_target_pairs={{0,16},{16,0},{1,17},{17,1},{2,18},{18,2},{3,19},{19,3},{4,20},{20... | collective-permute-start | bytes 2359304 | tf_op jit(solution)/shard_map/ppermute | solution.py:1020
  338.8 127.9 %reduce-scatter.12.cloned.1.call-start = ((), (), s32[]{:S(2)}) async-start(), calls=%async_computation.15 | async-start | bytes 1474560 | tf_op jit(solution)/shard_map/reduce_scatter | solution.py:1040
  339.2 51.7 %collective-permute-start.18 = (bf16[768,128]{1,0:T(8,128)(2,1)S(1)}, bf16[768,128]{1,0:T(8,128)(2,1)S(1)}, u32[]{:S(2)}, u32[]{:S(2)}) collective-permute-start(bf16[768,128]{1,0:T(8,128)(2,1)S(1)} %get-tuple-element.167), channel_id=1, source_target_pairs={{0,12},{4,8},{8,4},{12,0},{1,13},{5,9},{9,5},{13,1},{2,14},{6,10},... | collective-permute-start | bytes 589832 | tf_op jit(solution)/shard_map/ppermute | solution.py:1026
  342.1 48.8 %collective-permute-start.17 = (bf16[768,128]{1,0:T(8,128)(2,1)S(1)}, bf16[768,128]{1,0:T(8,128)(2,1)S(1)}, u32[]{:S(2)}, u32[]{:S(2)}) collective-permute-start(bf16[768,128]{1,0:T(8,128)(2,1)S(1)} %get-tuple-element.168), channel_id=1, source_target_pairs={{0,8},{4,12},{8,0},{12,4},{1,9},{5,13},{9,1},{13,5},{2,10},{6,14},... | collective-permute-start | bytes 589832 | tf_op jit(solution)/shard_map/ppermute | solution.py:1026
  342.6 49.6 %collective-permute-start.16 = (bf16[768,128]{1,0:T(8,128)(2,1)S(1)}, bf16[768,128]{1,0:T(8,128)(2,1)}, u32[]{:S(2)}, u32[]{:S(2)}) collective-permute-start(bf16[768,128]{1,0:T(8,128)(2,1)S(1)} %get-tuple-element.169), channel_id=1, source_target_pairs={{0,4},{4,0},{8,12},{12,8},{1,5},{5,1},{9,13},{13,9},{2,6},{6,2},{1... | collective-permute-start | bytes 589832 | tf_op jit(solution)/shard_map/ppermute | solution.py:1026
  392.2 13.6 %collective-permute-start.19 = (bf16[4,2,2,3,32,512]{5,4,3,2,1,0:T(8,128)(2,1)S(1)}, bf16[4,2,2,3,32,512]{5,4,3,2,1,0:T(8,128)(2,1)}, u32[]{:S(2)}, u32[]{:S(2)}) collective-permute-start(bf16[4,2,2,3,32,512]{5,4,3,2,1,0:T(8,128)(2,1)S(1)} %get-tuple-element.125), channel_id=1, source_target_pairs={{0,16},{16,0},{1,17},{17,1},{2,18},{18,2},{3,19},{19,3},{4,20},{20... | collective-permute-start | bytes 4718600 | tf_op jit(solution)/shard_map/ppermute | solution.py:1043
  394.1 24.2 %all-to-all-start.8 = ((bf16[4,192,128]{2,1,0:T(8,128)(2,1)}), bf16[4,192,128]{2,1,0:T(8,128)(2,1)S(1)}, u32[]{:S(2)}, u32[]{:S(2)}) async-start(bf16[4,192,128]{2,1,0:T(8,128)(2,1)} %bitcast.44), calls=%async_computation.10 | async-start | bytes 393216 | tf_op jit(solution)/shard_map/all_to_all | solution.py:894
  418.3 48.4 %all-to-all-start.6 = ((bf16[4,768,512]{2,1,0:T(8,128)(2,1)}), bf16[4,768,512]{2,1,0:T(8,128)(2,1)S(1)}, u32[]{:S(2)}, u32[]{:S(2)}) async-start(bf16[4,768,512]{2,1,0:T(8,128)(2,1)} %get-tuple-element.126), calls=%async_computation.7 | async-start | bytes 6291456 | tf_op jit(solution)/shard_map/all_to_all | solution.py:1056
  422.3 65.5 %reduce-scatter.14.cloned.1.call-start = ((), (), s32[]{:S(2)}) async-start(), calls=%async_computation.16 | async-start | bytes 2293760 | tf_op jit(solution)/shard_map/reduce_scatter | solution.py:1084
  422.6 4.8 collective-permute-start.26
  424.6 15.3 %collective-permute-start.13 = (bf16[2,192,512]{2,1,0:T(8,128)(2,1)}, bf16[2,192,512]{2,1,0:T(8,128)(2,1)}, u32[]{:S(2)}, u32[]{:S(2)}) collective-permute-start(bf16[2,192,512]{2,1,0:T(8,128)(2,1)} %broadcast_select_fusion.3), channel_id=1, source_target_pairs={{0,16},{16,0},{1,17},{17,1},{2,18},{18,2},{3,19},{19,3},{4,20},{20... | collective-permute-start | bytes 1179656 | tf_op jit(solution)/shard_map/ppermute | solution.py:903
  425.1 9.8 %collective-permute-start.20 = (bf16[2,192,128]{2,1,0:T(8,128)(2,1)S(1)}, bf16[2,192,128]{2,1,0:T(8,128)(2,1)S(1)}, u32[]{:S(2)}, u32[]{:S(2)}) collective-permute-start(bf16[2,192,128]{2,1,0:T(8,128)(2,1)S(1)} %broadcast_select_fusion.21), channel_id=1, source_target_pairs={{0,16},{16,0},{1,17},{17,1},{2,18},{18,2},{3,19},{19,3},{4,20},{20... | collective-permute-start | bytes 294920 | tf_op jit(solution)/shard_map/ppermute | solution.py:903
  436.3 26.7 %collective-permute-start.22 = (bf16[2,192,256]{2,1,0:T(8,128)(2,1)S(1)}, bf16[2,192,256]{2,1,0:T(8,128)(2,1)S(1)}, u32[]{:S(2)}, u32[]{:S(2)}) collective-permute-start(bf16[2,192,256]{2,1,0:T(8,128)(2,1)S(1)} %pad_maximum_fusion.7), channel_id=1, source_target_pairs={{0,8},{4,12},{8,0},{12,4},{1,9},{5,13},{9,1},{13,5},{2,10},{6,14},... | collective-permute-start | bytes 589832 | tf_op jit(solution)/shard_map/ppermute | solution.py:885
  438.4 26.1 %collective-permute-start.21 = (bf16[2,192,256]{2,1,0:T(8,128)(2,1)S(1)}, bf16[2,192,256]{2,1,0:T(8,128)(2,1)S(1)}, u32[]{:S(2)}, u32[]{:S(2)}) collective-permute-start(bf16[2,192,256]{2,1,0:T(8,128)(2,1)S(1)} %pad_maximum_fusion.7), channel_id=1, source_target_pairs={{0,4},{4,0},{8,12},{12,8},{1,5},{5,1},{9,13},{13,9},{2,6},{6,2},{1... | collective-permute-start | bytes 589832 | tf_op jit(solution)/shard_map/ppermute | solution.py:885
  463.1 11.0 %collective-permute-start.23 = (bf16[1,192,256]{2,1,0:T(8,128)(2,1)S(1)}, bf16[1,192,256]{2,1,0:T(8,128)(2,1)S(1)}, u32[]{:S(2)}, u32[]{:S(2)}) collective-permute-start(bf16[1,192,256]{2,1,0:T(8,128)(2,1)S(1)} %slice.136), channel_id=1, source_target_pairs={{0,4},{4,0},{8,12},{12,8},{1,5},{5,1},{9,13},{13,9},{2,6},{6,2},{1... | collective-permute-start | bytes 294920 | tf_op jit(solution)/shard_map/ppermute | solution.py:885
  464.6 9.5 %collective-permute-start.24 = (bf16[1,192,256]{2,1,0:T(8,128)(2,1)S(1)}, bf16[1,192,256]{2,1,0:T(8,128)(2,1)S(1)}, u32[]{:S(2)}, u32[]{:S(2)}) collective-permute-start(bf16[1,192,256]{2,1,0:T(8,128)(2,1)S(1)} %slice.137), channel_id=1, source_target_pairs={{0,8},{4,12},{8,0},{12,4},{1,9},{5,13},{9,1},{13,5},{2,10},{6,14},... | collective-permute-start | bytes 294920 | tf_op jit(solution)/shard_map/ppermute | solution.py:885
  469.3 28.0 %all-to-all-start.7 = ((bf16[4,192,512]{2,1,0:T(8,128)(2,1)}), bf16[4,192,512]{2,1,0:T(8,128)(2,1)}, u32[]{:S(2)}, u32[]{:S(2)}) async-start(bf16[4,192,512]{2,1,0:T(8,128)(2,1)} %bitcast.43), calls=%async_computation.9 | async-start | bytes 1572864 | tf_op jit(solution)/shard_map/all_to_all | solution.py:894
  474.9 11.4 %copy-start.22 = (bf16[1,192,768]{2,1,0:T(8,128)(2,1)S(1)}, bf16[1,192,768]{2,1,0:T(8,128)(2,1)}, u32[]{:S(2)}) copy-start(bf16[1,192,768]{2,1,0:T(8,128)(2,1)} %reduce-scatter.12.cloned.1.call-done) | copy-start | bytes 884740
  498.5 1.8 collective-permute-start.25
  (32 other events, 114.8 us)
Sparse Core Ops, SparseCore 0:
  10.2 32.9 all-gather.6
  46.6 80.6 all-gather.8
  130.7 92.1 all-gather.10
  262.0 15.8 reduce-scatter.9
  288.3 74.3 reduce-scatter.15
  365.5 43.8 reduce-scatter.17
  411.7 29.3 reduce-scatter.11
  443.4 41.5 reduce-scatter.13
